TPU v7x, 32 devices: a whole 2x2x4 slice. The times are simulated.
32 devices in a mesh: sector: 8 (over z, y), radial: 4 (over x, core).
Axes of the slice: x: 2, y: 2, z: 4, core: 2. Of those that a mesh axis runs over, the one named last changes fastest.
Arguments:
- density: float32 [1024, 64, 128], P('sector', 'radial'), may hold values from 0.4 to 1.2
- swirl: float32 [1024, 64, 128], P('sector', 'radial'), may hold values from -4 to 4
- heat_rate: float32 [1024, 64, 128], P('sector', 'radial'), may hold values from 0.1 to 3
- acoustic: float32 [3, 1024, 128], P(None, 'sector'), may hold values from -5 to 5
- mode_impedance: float32 [513], replicated, may hold values from 0.05 to 8
- mouth_azimuth: int32 [16], replicated, may hold values from 0 to 56, as said below
- mouth_radius: int32 [16], replicated, may hold values from 0 to 56, as said below
Outputs:
- density_next: float32 [1024, 64, 128], P('sector', 'radial')
- pressure: float32 [1024, 64, 128], P('sector', 'radial')
- acoustic_next: float32 [3, 1024, 128], P(None, 'sector')
Inputs may be any that keep to these rules, and one draw needn't show every extreme that they name: Burner b's mouth starts at azimuthal cell b * 64 + mouth_azimuth[b] and spans 8 cells. Burner b's mouth spans radial cells mouth_radius[b] to mouth_radius[b] + 7.
All inputs are finite; a program needn't handle non-finite values.
Results may differ from a plain program's by a relative error of at most 0.00018.
Values sent between devices are 32-bit elements; how exact they have to be, the bound alone decides.
No kernel may reach another device: no remote copies, remote signals or barrier semaphores. Data moves between devices by JAX's collectives and lax.ppermute only.
A program may use at most 128 MiB of HBM per device.

v0:
```python
import math

import jax
import jax.numpy as jnp
from jax import lax
from jax.sharding import PartitionSpec as P

BURNERS = 16
MOUTH = 8
SWEEPS = 4
SUBSTEPS = 8


time_step = 0.2
diffusion = 0.05
inflow_rate = 0.5
wave_speed = 0.5
heat_coupling = 0.5
feedback = 0.5


def passed_along(value, axis, steps):
    count = lax.axis_size(axis)
    pairs = [(source, (source + steps) % count) for source in range(count)]
    return lax.ppermute(value, axis, pairs)


def padded(cells, sides, width, closed):
    for axis, dim in sides:
        count = lax.axis_size(axis)
        ends = count if closed else count - 1
        head = lax.slice_in_dim(cells, 0, width, axis=dim)
        tail = lax.slice_in_dim(cells, cells.shape[dim] - width, cells.shape[dim], axis=dim)
        cells = jnp.concatenate(
            [
                lax.ppermute(tail, axis, [(i, (i + 1) % count) for i in range(ends)]),
                cells,
                lax.ppermute(head, axis, [((i + 1) % count, i) for i in range(ends)]),
            ],
            axis=dim,
        )
    return cells


def axial_pair(field):
    zeros = jnp.zeros_like(field[:, :, :1])
    return jnp.concatenate([field[:, :, 1:], zeros], 2) + jnp.concatenate(
        [zeros, field[:, :, :-1]], 2
    )


def mode_order(mode_rows, n_theta):
    half = n_theta // 2
    return jnp.where(mode_rows <= half, mode_rows, mode_rows - half)


def spectral_basis(mode_rows, theta_cols, n_theta):
    half = n_theta // 2
    order = mode_order(mode_rows, n_theta)
    phase = order[:, None] * theta_cols[None, :] % n_theta
    angle = phase.astype(jnp.float32) * (2.0 * math.pi / n_theta)
    return jnp.where((mode_rows <= half)[:, None], jnp.cos(angle), jnp.sin(angle))


def inverse_weight(mode_rows, n_theta):
    half = n_theta // 2
    edge = (mode_rows == 0) | (mode_rows == half)
    return jnp.where(edge, 1.0, 2.0).astype(jnp.float32) / n_theta


def row_blocks(n_theta):
    count = max(n_theta // 512, 1)
    return (count, n_theta // count)


def forward_transform(columns):
    n_theta = columns.shape[0]
    count, size = row_blocks(n_theta)
    theta_cols = jnp.arange(n_theta, dtype=jnp.int32)

    def forward_one_block(block):
        mode_rows = block * size + jnp.arange(size, dtype=jnp.int32)
        basis = spectral_basis(mode_rows, theta_cols, n_theta)
        return jnp.dot(
            basis, columns, precision=lax.Precision.HIGHEST, preferred_element_type=jnp.float32
        )

    result = lax.map(forward_one_block, jnp.arange(count, dtype=jnp.int32))
    return result.reshape(n_theta, columns.shape[1])


def inverse_transform(columns):
    n_theta = columns.shape[0]
    count, size = row_blocks(n_theta)
    mode_rows = jnp.arange(n_theta, dtype=jnp.int32)
    weighted = columns * inverse_weight(mode_rows, n_theta)[:, None]

    def inverse_one_block(block):
        theta_cols = block * size + jnp.arange(size, dtype=jnp.int32)
        basis = spectral_basis(mode_rows, theta_cols, n_theta)
        return lax.dot_general(
            basis,
            weighted,
            (((0,), (0,)), ((), ())),
            precision=lax.Precision.HIGHEST,
            preferred_element_type=jnp.float32,
        )

    result = lax.map(inverse_one_block, jnp.arange(count, dtype=jnp.int32))
    return result.reshape(n_theta, columns.shape[1])


def forward_items(items):
    width = items.shape[2]
    return forward_transform(items.reshape(items.shape[0], width)).reshape(items.shape[0], 1, width)


def inverse_items(items):
    width = items.shape[2]
    return inverse_transform(items.reshape(items.shape[0], width)).reshape(items.shape[0], 1, width)


def advance(wave_press, wave_along, wave_axial, source, fetch_above, fetch_below):
    zeros = jnp.zeros_like(wave_press[:, :1])
    for substep in range(SUBSTEPS):
        above = fetch_above(wave_press[:1])
        press_up = jnp.concatenate([wave_press[1:], above], 0)
        press_axial = jnp.concatenate([wave_press[:, 1:], zeros], 1)
        wave_along = wave_along - wave_speed * (press_up - wave_press)
        wave_axial = wave_axial - wave_speed * (press_axial - wave_press)
        below = fetch_below(wave_along[-1:])
        along_down = jnp.concatenate([below, wave_along[:-1]], 0)
        axial_down = jnp.concatenate([zeros, wave_axial[:, :-1]], 1)
        wave_press = (
            wave_press
            - wave_speed * (wave_along - along_down + (wave_axial - axial_down))
            + heat_coupling * source
        )
    return jnp.stack([wave_press, wave_along, wave_axial])


def shards(density, swirl, heat_rate, acoustic, mode_impedance, mouth_azimuth, mouth_radius):
    sectors = lax.axis_size("sector")
    radials = lax.axis_size("radial")
    cells_theta, cells_radius, cells_axial = density.shape
    n_theta = cells_theta * sectors
    n_radius = cells_radius * radials
    sector_index = lax.axis_index("sector")
    radial_index = lax.axis_index("radial")
    theta_global = sector_index * cells_theta + jnp.arange(cells_theta, dtype=jnp.int32)
    radius_global = radial_index * cells_radius + jnp.arange(cells_radius, dtype=jnp.int32)
    theta_start = jnp.arange(BURNERS, dtype=jnp.int32) * (n_theta // BURNERS) + mouth_azimuth
    inside_theta = (
        (theta_global[None, :] >= theta_start[:, None])
        & (theta_global[None, :] < theta_start[:, None] + MOUTH)
    ).astype(jnp.float32)
    inside_radius = (
        (radius_global[None, :] >= mouth_radius[:, None])
        & (radius_global[None, :] < mouth_radius[:, None] + MOUTH)
    ).astype(jnp.float32)
    mouth_mask = lax.dot_general(
        inside_theta, inside_radius, (((0,), (0,)), ((), ())), preferred_element_type=jnp.float32
    )
    heat_field = heat_rate * density * density
    local_heat = jnp.sum(heat_field, axis=1) / n_radius
    rows = cells_theta // radials
    source = lax.psum_scatter(local_heat, "radial", scatter_dimension=0, tiled=True)
    own_block = lax.dynamic_slice_in_dim(acoustic, radial_index * rows, rows, 1)

    def fetch_above(row):
        return passed_along(row, ("sector", "radial"), -1)

    def fetch_below(row):
        return passed_along(row, ("sector", "radial"), 1)

    portion = advance(own_block[0], own_block[1], own_block[2], source, fetch_above, fetch_below)
    acoustic_next = lax.all_gather(portion, "radial", axis=1, tiled=True)
    swirl_flux = swirl * density
    azimuth_ext = padded(jnp.stack([density, swirl_flux]), (("sector", 1),), 1, True)
    radial_ext = padded(density, (("radial", 1),), 1, False)
    twice = 2.0 * density
    laplace = (
        azimuth_ext[0, 2:]
        + azimuth_ext[0, :-2]
        - twice
        + (radial_ext[:, 2:] + radial_ext[:, :-2] - twice)
        + (axial_pair(density) - twice)
    )
    advection = -0.5 * (azimuth_ext[1, 2:] - azimuth_ext[1, :-2])
    density_next = (
        density
        + time_step * (advection + diffusion * laplace)
        + inflow_rate * mouth_mask[:, :, None] * (1.0 - density)
    )
    forcing = (density_next - density) / time_step + feedback * acoustic_next[0][:, None, :]
    columns = cells_radius * cells_axial // sectors
    spectral = forward_items(
        lax.all_to_all(
            forcing.reshape(cells_theta, sectors, columns),
            "sector",
            split_axis=1,
            concat_axis=0,
            tiled=True,
        )
    )
    mode_block = lax.all_to_all(
        spectral, "sector", split_axis=0, concat_axis=1, tiled=True
    ).reshape(cells_theta, cells_radius, cells_axial)
    mode_rows = sector_index * cells_theta + jnp.arange(cells_theta, dtype=jnp.int32)
    order = mode_order(mode_rows, n_theta)
    table_index = jnp.arange(mode_impedance.shape[0], dtype=jnp.int32)
    selector = (order[:, None] == table_index[None, :]).astype(jnp.float32)
    impedance_rows = jnp.dot(
        selector,
        mode_impedance,
        precision=lax.Precision.HIGHEST,
        preferred_element_type=jnp.float32,
    )
    shifted = 2.0 - 2.0 * jnp.cos(order.astype(jnp.float32) * (2.0 * math.pi / n_theta))
    diagonal = (4.0 + shifted + impedance_rows)[:, None, None]
    solution = mode_block / diagonal
    for sweep in range(SWEEPS - 1):
        solution_ext = padded(solution, (("radial", 1),), 1, False)
        solution = (
            mode_block + (solution_ext[:, 2:] + solution_ext[:, :-2]) + axial_pair(solution)
        ) / diagonal
    gathered = inverse_items(
        lax.all_to_all(
            solution.reshape(cells_theta, sectors, columns),
            "sector",
            split_axis=1,
            concat_axis=0,
            tiled=True,
        )
    )
    pressure = lax.all_to_all(gathered, "sector", split_axis=0, concat_axis=1, tiled=True).reshape(
        cells_theta, cells_radius, cells_axial
    )
    return (density_next, pressure, acoustic_next)


def solution(mesh):
    return jax.shard_map(
        shards,
        mesh=mesh,
        in_specs=(
            P("sector", "radial", None),
            P("sector", "radial", None),
            P("sector", "radial", None),
            P(None, "sector", None),
            P(),
            P(),
            P(),
        ),
        out_specs=(
            P("sector", "radial", None),
            P("sector", "radial", None),
            P(None, "sector", None),
        ),
        check_vma=False,
    )
```

profile of v0, /device:TPU:0, one launch (start us, length us, event | category | flops | bytes accessed | tf_op | source)
XLA Modules:
  0.0 344.7 jit_solution(12204324801520040112)
XLA Ops:
  8.0 6.4 %collective-permute-start.4 = (f32[1,128]{1,0:T(1,128)S(1)}, f32[1,128]{1,0:T(1,128)S(1)}, u32[]{:S(2)}, u32[]{:S(2)}) collective-permute-start(f32[1,128]{1,0:T(1,128)S(1)} %fusion.155), channel_id=1, source_target_pairs={{0,31},{1,0},{2,1},{3,2},{4,3},{5,4},{6,5},{7,6},{8,7},{9,8},{10,9... | collective-permute-start | bytes 1544 | tf_op jit(solution)/shard_map/ppermute | solution.py:25
  14.4 1.8 fusion.63
  19.2 5.8 %collective-permute-done.5 = f32[1,128]{1,0:T(1,128)S(1)} collective-permute-done((f32[1,128]{1,0:T(1,128)S(1)}, f32[1,128]{1,0:T(1,128)S(1)}, u32[]{:S(2)}, u32[]{:S(2)}) %collective-permute-start.5) | collective-permute-done | bytes 544 | tf_op jit(solution)/shard_map/ppermute | solution.py:25
  25.0 8.2 %reduce-scatter.2.cloned.1.call-done = f32[32,128]{1,0:T(8,128)} async-done(((f32[128,128]{1,0:T(8,128)}), f32[32,128]{1,0:T(8,128)}) %reduce-scatter.2.cloned.1.call-update) | async-done | bytes 16400 | tf_op jit(solution)/shard_map/reduce_scatter | solution.py:167
  34.1 3.1 collective-permute-start.6
  38.6 6.6 %collective-permute-done.7 = f32[1,128]{1,0:T(1,128)S(1)} collective-permute-done((f32[1,128]{1,0:T(1,128)S(1)}, f32[1,128]{1,0:T(1,128)S(1)}, u32[]{:S(2)}, u32[]{:S(2)}) %collective-permute-start.7) | collective-permute-done | bytes 544 | tf_op jit(solution)/shard_map/ppermute | solution.py:25
  47.4 6.6 %collective-permute-done.9 = f32[1,128]{1,0:T(1,128)S(1)} collective-permute-done((f32[1,128]{1,0:T(1,128)S(1)}, f32[1,128]{1,0:T(1,128)S(1)}, u32[]{:S(2)}, u32[]{:S(2)}) %collective-permute-start.9) | collective-permute-done | bytes 544 | tf_op jit(solution)/shard_map/ppermute | solution.py:25
  55.2 1.6 copy.46
  57.6 6.0 %collective-permute-done.11 = f32[1,128]{1,0:T(1,128)S(1)} collective-permute-done((f32[1,128]{1,0:T(1,128)S(1)}, f32[1,128]{1,0:T(1,128)S(1)}, u32[]{:S(2)}, u32[]{:S(2)}) %collective-permute-start.11) | collective-permute-done | bytes 544 | tf_op jit(solution)/shard_map/ppermute | solution.py:25
  63.7 2.8 slice_maximum_fusion
  66.4 2.2 copy.48
  68.7 2.2 copy.50
  70.9 2.0 collective-permute-start.1
  74.4 3.0 collective-permute-start.3
  77.5 2.2 collective-permute-done.13
  79.8 1.4 collective-permute-start.14
  81.2 1.5 fusion.164
  82.9 6.6 %collective-permute-done.15 = f32[1,128]{1,0:T(1,128)S(1)} collective-permute-done((f32[1,128]{1,0:T(1,128)S(1)}, f32[1,128]{1,0:T(1,128)S(1)}, u32[]{:S(2)}, u32[]{:S(2)}) %collective-permute-start.15) | collective-permute-done | bytes 544 | tf_op jit(solution)/shard_map/ppermute | solution.py:25
  90.9 6.6 %collective-permute-done.17 = f32[1,128]{1,0:T(1,128)S(1)} collective-permute-done((f32[1,128]{1,0:T(1,128)S(1)}, f32[1,128]{1,0:T(1,128)S(1)}, u32[]{:S(2)}, u32[]{:S(2)}) %collective-permute-start.17) | collective-permute-done | bytes 544 | tf_op jit(solution)/shard_map/ppermute | solution.py:25
  99.2 2.0 copy.49
  101.3 2.0 copy.51
  103.3 2.3 collective-permute-done.19
  105.6 5.6 %all_gather.3 = f32[3,128,128]{2,1,0:T(8,128)S(1)} all-gather(f32[3,32,128]{2,1,0:T(8,128)S(1)} %pad_maximum_fusion.13), channel_id=1, replica_groups=mesh['sector'=8,'radial'=4] {'radial'}, dimensions={1}, use_global_device_ids=true | all-gather | bytes 245760 | tf_op jit(solution)/shard_map/all_gather | solution.py:177
  111.3 4.5 %multiply_add_fusion = (f32[128,16,128]{0,2,1:T(8,128)}, f32[128,16,128]{0,2,1:T(8,128)S(1)}) fusion(f32[128,16,128]{0,2,1:T(8,128)S(1)} %copy.59, f32[128,128]{0,1:T(8,128)S(1)} %copy.62, f32[128,16]{0,1:T(8,128)S(1)} %convolution_multiply_fusion, f32[128,16,127]{0,2,1:T(8,128)} %get-tuple-element.225, f32[128,16,127]{0,2,1:T(8,128)} %get-tuple-element.224, ...), kind=kLoop, calls=%fused_computation.111 | loop fusion | flops 8126464 | bytes 7561216 | tf_op jit(solution)/shard_map/add | solution.py:195
  115.9 2.5 copy.63
  118.4 3.6 %all-to-all-start = ((f32[128,8,256]{2,0,1:T(8,128)}), f32[128,8,256]{2,0,1:T(8,128)S(1)}, u32[]{:S(2)}, u32[]{:S(2)}) async-start(f32[128,8,256]{2,0,1:T(8,128)} %copy.63), calls=%async_computation.1 | async-start | bytes 2097152 | tf_op jit(solution)/shard_map/all_to_all | solution.py:198
  122.0 26.5 %all-to-all-done = f32[128,8,256]{2,0,1:T(8,128)S(1)} async-done(((f32[128,8,256]{2,0,1:T(8,128)}), f32[128,8,256]{2,0,1:T(8,128)S(1)}, u32[]{:S(2)}, u32[]{:S(2)}) %all-to-all-start) | async-done | bytes 1048608 | tf_op jit(solution)/shard_map/all_to_all | solution.py:198
  148.5 40.4 %while.27 = (s32[]{:T(128)}, f32[2,512,256]{2,1,0:T(8,128)S(1)}, s32[2]{0:T(128)S(1)}, f32[1024,256]{1,0:T(8,128)S(1)}, s32[]{:T(128)}, /*index=5*/s32[1]{0:T(128)}) while((s32[]{:T(128)}, f32[2,512,256]{2,1,0:T(8,128)S(1)}, s32[2]{0:T(128)S(1)}, f32[1024,256]{1,0:T(8,128)S(1)}, s32[]{:T(128)}, /*index=5*/s32[1]{0:T(128)}) %tuple.93), condition=%wide.region_3.4_spmd.clone, body=%wide.region_2.3_spmd.clone.sunk | while | flops 1618480128 | bytes 1578089 | solution.py:88
  149.8 18.9 %fusion.178 = f32[2,512,256]{2,1,0:T(8,128)S(1)} fusion(f32[2,512,256]{2,1,0:T(8,128)S(1)} %get-tuple-element.299, s32[]{:T(128)} %get-tuple-element.298, f32[1024,256]{1,0:T(8,128)S(1)} %get-tuple-element.307, s32[512]{0:T(512)S(1)} %add_select_fusion.4, pred[512]{0:T(512)(128)(4,1)S(1)} %fusion.177), kind=kOutput, calls=%fused_computation.17.clone.1 | convolution fusion | flops 1618477056 | bytes 1575428 | tf_op jit(solution)/shard_map/while/body/eval_jaxpr/dot_general | solution.py:84
  170.0 18.9 %fusion.178 = f32[2,512,256]{2,1,0:T(8,128)S(1)} fusion(f32[2,512,256]{2,1,0:T(8,128)S(1)} %get-tuple-element.299, s32[]{:T(128)} %get-tuple-element.298, f32[1024,256]{1,0:T(8,128)S(1)} %get-tuple-element.307, s32[512]{0:T(512)S(1)} %add_select_fusion.4, pred[512]{0:T(512)(128)(4,1)S(1)} %fusion.177), kind=kOutput, calls=%fused_computation.17.clone.1 | convolution fusion | flops 1618477056 | bytes 1575428 | tf_op jit(solution)/shard_map/while/body/eval_jaxpr/dot_general | solution.py:84
  188.9 2.0 reshape_reshape.6
  190.9 3.6 %all-to-all-start.1 = ((f32[1024,1,256]{2,1,0:T(1,128)}), f32[1024,1,256]{2,1,0:T(1,128)S(1)}, u32[]{:S(2)}, u32[]{:S(2)}) async-start(f32[1024,1,256]{2,1,0:T(1,128)} %reshape_reshape.6), calls=%async_computation.2 | async-start | bytes 2097152 | tf_op jit(solution)/shard_map/all_to_all | solution.py:206
  194.9 25.6 %all-to-all-done.1 = f32[1024,1,256]{2,1,0:T(1,128)S(1)} async-done(((f32[1024,1,256]{2,1,0:T(1,128)}), f32[1024,1,256]{2,1,0:T(1,128)S(1)}, u32[]{:S(2)}, u32[]{:S(2)}) %all-to-all-start.1) | async-done | bytes 1048608 | tf_op jit(solution)/shard_map/all_to_all | solution.py:206
  221.1 1.3 collective-permute-start.20
  222.4 3.0 collective-permute-start.21
  228.1 4.0 %collective-permute-start.23 = (f32[128,1,128]{0,2,1:T(8,128)S(1)}, f32[128,1,128]{0,2,1:T(8,128)S(1)}, u32[]{:S(2)}, u32[]{:S(2)}) collective-permute-start(f32[128,1,128]{0,2,1:T(8,128)S(1)} %get-tuple-element.217), channel_id=1, source_target_pairs={{0,1},{1,2},{2,3},{4,5},{5,6},{6,7},{8,9},{9,10},{10,11},{12,13},{... | collective-permute-start | bytes 196616 | tf_op jit(solution)/shard_map/ppermute | solution.py:36
  234.8 5.3 %collective-permute-start.25 = (f32[128,1,128]{0,2,1:T(8,128)S(1)}, f32[128,1,128]{0,2,1:T(8,128)S(1)}, u32[]{:S(2)}, u32[]{:S(2)}) collective-permute-start(f32[128,1,128]{0,2,1:T(8,128)S(1)} %get-tuple-element.213), channel_id=1, source_target_pairs={{0,1},{1,2},{2,3},{4,5},{5,6},{6,7},{8,9},{9,10},{10,11},{12,13},{... | collective-permute-start | bytes 196616 | tf_op jit(solution)/shard_map/ppermute | solution.py:36
  241.0 1.4 fusion.67
  242.4 3.8 %all-to-all-start.2 = ((f32[128,8,256]{0,2,1:T(8,128)}), f32[128,8,256]{0,2,1:T(8,128)S(1)}, u32[]{:S(2)}, u32[]{:S(2)}) async-start(f32[128,8,256]{0,2,1:T(8,128)} %bitcast.112), calls=%async_computation.3 | async-start | bytes 2097152 | tf_op jit(solution)/shard_map/all_to_all | solution.py:228
  246.2 26.4 %all-to-all-done.2 = f32[128,8,256]{0,2,1:T(8,128)S(1)} async-done(((f32[128,8,256]{0,2,1:T(8,128)}), f32[128,8,256]{0,2,1:T(8,128)S(1)}, u32[]{:S(2)}, u32[]{:S(2)}) %all-to-all-start.2) | async-done | bytes 1048608 | tf_op jit(solution)/shard_map/all_to_all | solution.py:228
  274.2 28.4 %while.28 = (s32[]{:T(128)}, f32[2,512,256]{2,1,0:T(8,128)S(1)}, s32[2]{0:T(128)S(1)}, f32[1024,256]{1,0:T(8,128)}, s32[]{:T(128)}, /*index=5*/s32[1]{0:T(128)}) while((s32[]{:T(128)}, f32[2,512,256]{2,1,0:T(8,128)S(1)}, s32[2]{0:T(128)S(1)}, f32[1024,256]{1,0:T(8,128)}, s32[]{:T(128)}, /*index=5*/s32[1]{0:T(128)}) %tuple.86), condition=%wide.region_5.6_spmd.clone.clone, body=%wide.region_4.5_spmd.clone.clone.sunk | while | flops 1618481664 | bytes 1587301 | solution.py:109
  275.7 12.8 %fusion.181 = f32[2,512,256]{2,1,0:T(8,128)S(1)} fusion(f32[2,512,256]{2,1,0:T(8,128)S(1)} %get-tuple-element.317, s32[]{:T(128)} %get-tuple-element.316, f32[1024,256]{1,0:T(8,128)} %get-tuple-element.325, s32[512]{0:T(512)S(1)} %iota_add_fusion.6, s32[1024]{0:T(1024)S(1)} %iota_select_fusion.2, pred[1024]{0:T(1024)(128)(4,1)S(1)} %iota_compare_fusion.6), kind=kOutput, calls=%fused_computation.47.clone.1 | convolution fusion | flops 1618477056 | bytes 1580036 | tf_op jit(solution)/shard_map/while/body/eval_jaxpr/dot_general | solution.py:101
  289.8 12.8 %fusion.181 = f32[2,512,256]{2,1,0:T(8,128)S(1)} fusion(f32[2,512,256]{2,1,0:T(8,128)S(1)} %get-tuple-element.317, s32[]{:T(128)} %get-tuple-element.316, f32[1024,256]{1,0:T(8,128)} %get-tuple-element.325, s32[512]{0:T(512)S(1)} %iota_add_fusion.6, s32[1024]{0:T(1024)S(1)} %iota_select_fusion.2, pred[1024]{0:T(1024)(128)(4,1)S(1)} %iota_compare_fusion.6), kind=kOutput, calls=%fused_computation.47.clone.1 | convolution fusion | flops 1618477056 | bytes 1580036 | tf_op jit(solution)/shard_map/while/body/eval_jaxpr/dot_general | solution.py:101
  302.6 2.0 reshape_reshape.7
  304.7 4.2 %all-to-all-start.3 = ((f32[1024,1,256]{2,1,0:T(1,128)}), f32[1024,1,256]{2,1,0:T(1,128)S(1)}, u32[]{:S(2)}, u32[]{:S(2)}) async-start(f32[1024,1,256]{2,1,0:T(1,128)} %reshape_reshape.7), calls=%async_computation.4 | async-start | bytes 2097152 | tf_op jit(solution)/shard_map/all_to_all | solution.py:236
  308.9 1.4 copy.67
  310.3 25.1 %all-to-all-done.3 = f32[1024,1,256]{2,1,0:T(1,128)S(1)} async-done(((f32[1024,1,256]{2,1,0:T(1,128)}), f32[1024,1,256]{2,1,0:T(1,128)S(1)}, u32[]{:S(2)}, u32[]{:S(2)}) %all-to-all-start.3) | async-done | bytes 1048608 | tf_op jit(solution)/shard_map/all_to_all | solution.py:236
  335.8 1.4 copy.68
  (146 shorter events, 27.4 us)
Async XLA Ops:
  7.2 47.6 %copy-start = (f32[128,16,128]{2,1,0:T(8,128)S(1)}, f32[128,16,128]{2,1,0:T(8,128)}, u32[]{:S(2)}) copy-start(f32[128,16,128]{2,1,0:T(8,128)} %param.11) | copy-start | bytes 3145732
  7.2 26.1 %reduce-scatter.2.cloned.1.call-start = ((), (), s32[]{:S(2)}) async-start(), calls=%async_computation.5 | async-start | bytes 81920 | tf_op jit(solution)/shard_map/reduce_scatter | solution.py:167
  8.0 9.6 %collective-permute-start.4 = (f32[1,128]{1,0:T(1,128)S(1)}, f32[1,128]{1,0:T(1,128)S(1)}, u32[]{:S(2)}, u32[]{:S(2)}) collective-permute-start(f32[1,128]{1,0:T(1,128)S(1)} %fusion.155), channel_id=1, source_target_pairs={{0,31},{1,0},{2,1},{3,2},{4,3},{5,4},{6,5},{7,6},{8,7},{9,8},{10,9... | collective-permute-start | bytes 1544 | tf_op jit(solution)/shard_map/ppermute | solution.py:25
  18.4 6.6 %collective-permute-start.5 = (f32[1,128]{1,0:T(1,128)S(1)}, f32[1,128]{1,0:T(1,128)S(1)}, u32[]{:S(2)}, u32[]{:S(2)}) collective-permute-start(f32[1,128]{1,0:T(1,128)S(1)} %slice.356), channel_id=1, source_target_pairs={{0,1},{1,2},{2,3},{3,4},{4,5},{5,6},{6,7},{7,8},{8,9},{9,10},{10,1... | collective-permute-start | bytes 1544 | tf_op jit(solution)/shard_map/ppermute | solution.py:25
  34.1 4.4 %collective-permute-start.6 = (f32[1,128]{1,0:T(1,128)S(1)}, f32[1,128]{1,0:T(1,128)S(1)}, u32[]{:S(2)}, u32[]{:S(2)}) collective-permute-start(f32[1,128]{1,0:T(1,128)S(1)} %slice.361), channel_id=1, source_target_pairs={{0,31},{1,0},{2,1},{3,2},{4,3},{5,4},{6,5},{7,6},{8,7},{9,8},{10,9... | collective-permute-start | bytes 1544 | tf_op jit(solution)/shard_map/ppermute | solution.py:25
  38.5 6.6 %collective-permute-start.7 = (f32[1,128]{1,0:T(1,128)S(1)}, f32[1,128]{1,0:T(1,128)S(1)}, u32[]{:S(2)}, u32[]{:S(2)}) collective-permute-start(f32[1,128]{1,0:T(1,128)S(1)} %slice.362), channel_id=1, source_target_pairs={{0,1},{1,2},{2,3},{3,4},{4,5},{5,6},{6,7},{7,8},{8,9},{9,10},{10,1... | collective-permute-start | bytes 1544 | tf_op jit(solution)/shard_map/ppermute | solution.py:25
  46.0 1.3 collective-permute-start.8
  47.3 6.6 %collective-permute-start.9 = (f32[1,128]{1,0:T(1,128)S(1)}, f32[1,128]{1,0:T(1,128)S(1)}, u32[]{:S(2)}, u32[]{:S(2)}) collective-permute-start(f32[1,128]{1,0:T(1,128)S(1)} %slice.368), channel_id=1, source_target_pairs={{0,1},{1,2},{2,3},{3,4},{4,5},{5,6},{6,7},{7,8},{8,9},{9,10},{10,1... | collective-permute-start | bytes 1544 | tf_op jit(solution)/shard_map/ppermute | solution.py:25
  54.8 2.1 collective-permute-start.10
  56.8 6.8 %copy-start.1 = (f32[32,128]{1,0:T(8,128)S(1)}, f32[32,128]{1,0:T(8,128)}, u32[]{:S(2)}) copy-start(f32[32,128]{1,0:T(8,128)} %reduce-scatter.2.cloned.1.call-done) | copy-start | bytes 49156
  56.9 6.6 %collective-permute-start.11 = (f32[1,128]{1,0:T(1,128)S(1)}, f32[1,128]{1,0:T(1,128)S(1)}, u32[]{:S(2)}, u32[]{:S(2)}) collective-permute-start(f32[1,128]{1,0:T(1,128)S(1)} %slice.374), channel_id=1, source_target_pairs={{0,1},{1,2},{2,3},{3,4},{4,5},{5,6},{6,7},{7,8},{8,9},{9,10},{10,1... | collective-permute-start | bytes 1544 | tf_op jit(solution)/shard_map/ppermute | solution.py:25
  63.7 9.3 %collective-permute-start.12 = (f32[1,128]{1,0:T(1,128)S(1)}, f32[1,128]{1,0:T(1,128)S(1)}, u32[]{:S(2)}, u32[]{:S(2)}) collective-permute-start(f32[1,128]{1,0:T(1,128)S(1)} %slice.379), channel_id=1, source_target_pairs={{0,31},{1,0},{2,1},{3,2},{4,3},{5,4},{6,5},{7,6},{8,7},{9,8},{10,9... | collective-permute-start | bytes 1544 | tf_op jit(solution)/shard_map/ppermute | solution.py:25
  68.7 30.6 %collective-permute-start = (f32[2,1,16,128]{3,2,1,0:T(8,128)S(1)}, f32[2,1,16,128]{3,2,1,0:T(8,128)S(1)}, u32[]{:S(2)}, u32[]{:S(2)}) collective-permute-start(f32[2,1,16,128]{3,2,1,0:T(8,128)S(1)} %copy.48), channel_id=1, source_target_pairs={{4,0},{8,4},{12,8},{16,12},{20,16},{24,20},{28,24},{0,28},{5,1},{9... | collective-permute-start | bytes 49160 | tf_op jit(solution)/shard_map/ppermute | solution.py:38
  70.9 30.4 %collective-permute-start.1 = (f32[2,1,16,128]{3,2,1,0:T(8,128)S(1)}, f32[2,1,16,128]{3,2,1,0:T(8,128)S(1)}, u32[]{:S(2)}, u32[]{:S(2)}) collective-permute-start(f32[2,1,16,128]{3,2,1,0:T(8,128)S(1)} %copy.50), channel_id=1, source_target_pairs={{0,4},{4,8},{8,12},{12,16},{16,20},{20,24},{24,28},{28,0},{1,5},{5... | collective-permute-start | bytes 49160 | tf_op jit(solution)/shard_map/ppermute | solution.py:36
  73.0 6.6 %collective-permute-start.13 = (f32[1,128]{1,0:T(1,128)S(1)}, f32[1,128]{1,0:T(1,128)S(1)}, u32[]{:S(2)}, u32[]{:S(2)}) collective-permute-start(f32[1,128]{1,0:T(1,128)S(1)} %slice.380), channel_id=1, source_target_pairs={{0,1},{1,2},{2,3},{3,4},{4,5},{5,6},{6,7},{7,8},{8,9},{9,10},{10,1... | collective-permute-start | bytes 1544 | tf_op jit(solution)/shard_map/ppermute | solution.py:25
  73.1 38.2 %collective-permute-start.2 = (f32[128,1,128]{0,2,1:T(8,128)S(1)}, f32[128,1,128]{0,2,1:T(8,128)S(1)}, u32[]{:S(2)}, u32[]{:S(2)}) collective-permute-start(f32[128,1,128]{0,2,1:T(8,128)S(1)} %get-tuple-element.222), channel_id=1, source_target_pairs={{1,0},{2,1},{3,2},{5,4},{6,5},{7,6},{9,8},{10,9},{11,10},{13,12},{... | collective-permute-start | bytes 196616 | tf_op jit(solution)/shard_map/ppermute | solution.py:38
  74.4 36.9 %collective-permute-start.3 = (f32[128,1,128]{0,2,1:T(8,128)S(1)}, f32[128,1,128]{0,2,1:T(8,128)S(1)}, u32[]{:S(2)}, u32[]{:S(2)}) collective-permute-start(f32[128,1,128]{0,2,1:T(8,128)S(1)} %get-tuple-element.223), channel_id=1, source_target_pairs={{0,1},{1,2},{2,3},{4,5},{5,6},{6,7},{8,9},{9,10},{10,11},{12,13},{... | collective-permute-start | bytes 196616 | tf_op jit(solution)/shard_map/ppermute | solution.py:36
  79.8 3.1 copy-start.3
  79.8 9.8 %copy-start.4 = (s32[16]{0:T(128)S(1)}, s32[16]{0:T(128)}, u32[]{:S(2)}) copy-start(s32[16]{0:T(128)} %param.17) | copy-start | bytes 196
  79.8 3.0 collective-permute-start.14
  82.8 6.6 %collective-permute-start.15 = (f32[1,128]{1,0:T(1,128)S(1)}, f32[1,128]{1,0:T(1,128)S(1)}, u32[]{:S(2)}, u32[]{:S(2)}) collective-permute-start(f32[1,128]{1,0:T(1,128)S(1)} %slice.386), channel_id=1, source_target_pairs={{0,1},{1,2},{2,3},{3,4},{4,5},{5,6},{6,7},{7,8},{8,9},{9,10},{10,1... | collective-permute-start | bytes 1544 | tf_op jit(solution)/shard_map/ppermute | solution.py:25
  89.5 1.3 collective-permute-start.16
  90.8 6.6 %collective-permute-start.17 = (f32[1,128]{1,0:T(1,128)S(1)}, f32[1,128]{1,0:T(1,128)S(1)}, u32[]{:S(2)}, u32[]{:S(2)}) collective-permute-start(f32[1,128]{1,0:T(1,128)S(1)} %slice.392), channel_id=1, source_target_pairs={{0,1},{1,2},{2,3},{3,4},{4,5},{5,6},{6,7},{7,8},{8,9},{9,10},{10,1... | collective-permute-start | bytes 1544 | tf_op jit(solution)/shard_map/ppermute | solution.py:25
  97.6 1.3 collective-permute-start.18
  98.9 6.6 %collective-permute-start.19 = (f32[1,128]{1,0:T(1,128)S(1)}, f32[1,128]{1,0:T(1,128)S(1)}, u32[]{:S(2)}, u32[]{:S(2)}) collective-permute-start(f32[1,128]{1,0:T(1,128)S(1)} %slice.398), channel_id=1, source_target_pairs={{0,1},{1,2},{2,3},{3,4},{4,5},{5,6},{6,7},{7,8},{8,9},{9,10},{10,1... | collective-permute-start | bytes 1544 | tf_op jit(solution)/shard_map/ppermute | solution.py:25
  118.4 30.0 %all-to-all-start = ((f32[128,8,256]{2,0,1:T(8,128)}), f32[128,8,256]{2,0,1:T(8,128)S(1)}, u32[]{:S(2)}, u32[]{:S(2)}) async-start(f32[128,8,256]{2,0,1:T(8,128)} %copy.63), calls=%async_computation.1 | async-start | bytes 2097152 | tf_op jit(solution)/shard_map/all_to_all | solution.py:198
  188.9 5.7 %copy-start.2 = (f32[513]{0:T(1024)S(1)}, f32[513]{0:T(1024)}, u32[]{:S(2)}) copy-start(f32[513]{0:T(1024)} %param.15) | copy-start | bytes 6160
  190.9 29.6 %all-to-all-start.1 = ((f32[1024,1,256]{2,1,0:T(1,128)}), f32[1024,1,256]{2,1,0:T(1,128)S(1)}, u32[]{:S(2)}, u32[]{:S(2)}) async-start(f32[1024,1,256]{2,1,0:T(1,128)} %reshape_reshape.6), calls=%async_computation.2 | async-start | bytes 2097152 | tf_op jit(solution)/shard_map/all_to_all | solution.py:206
  221.1 4.5 %collective-permute-start.20 = (f32[128,1,128]{0,2,1:T(8,128)S(1)}, f32[128,1,128]{0,2,1:T(8,128)S(1)}, u32[]{:S(2)}, u32[]{:S(2)}) collective-permute-start(f32[128,1,128]{0,2,1:T(8,128)S(1)} %get-tuple-element.220), channel_id=1, source_target_pairs={{1,0},{2,1},{3,2},{5,4},{6,5},{7,6},{9,8},{10,9},{11,10},{13,12},{... | collective-permute-start | bytes 196616 | tf_op jit(solution)/shard_map/ppermute | solution.py:38
  222.4 3.9 %collective-permute-start.21 = (f32[128,1,128]{0,2,1:T(8,128)S(1)}, f32[128,1,128]{0,2,1:T(8,128)S(1)}, u32[]{:S(2)}, u32[]{:S(2)}) collective-permute-start(f32[128,1,128]{0,2,1:T(8,128)S(1)} %get-tuple-element.221), channel_id=1, source_target_pairs={{0,1},{1,2},{2,3},{4,5},{5,6},{6,7},{8,9},{9,10},{10,11},{12,13},{... | collective-permute-start | bytes 196616 | tf_op jit(solution)/shard_map/ppermute | solution.py:36
  226.8 5.6 %collective-permute-start.22 = (f32[128,1,128]{0,2,1:T(8,128)S(1)}, f32[128,1,128]{0,2,1:T(8,128)S(1)}, u32[]{:S(2)}, u32[]{:S(2)}) collective-permute-start(f32[128,1,128]{0,2,1:T(8,128)S(1)} %get-tuple-element.216), channel_id=1, source_target_pairs={{1,0},{2,1},{3,2},{5,4},{6,5},{7,6},{9,8},{10,9},{11,10},{13,12},{... | collective-permute-start | bytes 196616 | tf_op jit(solution)/shard_map/ppermute | solution.py:38
  228.1 4.9 %collective-permute-start.23 = (f32[128,1,128]{0,2,1:T(8,128)S(1)}, f32[128,1,128]{0,2,1:T(8,128)S(1)}, u32[]{:S(2)}, u32[]{:S(2)}) collective-permute-start(f32[128,1,128]{0,2,1:T(8,128)S(1)} %get-tuple-element.217), channel_id=1, source_target_pairs={{0,1},{1,2},{2,3},{4,5},{5,6},{6,7},{8,9},{9,10},{10,11},{12,13},{... | collective-permute-start | bytes 196616 | tf_op jit(solution)/shard_map/ppermute | solution.py:36
  233.5 6.8 %collective-permute-start.24 = (f32[128,1,128]{0,2,1:T(8,128)S(1)}, f32[128,1,128]{0,2,1:T(8,128)S(1)}, u32[]{:S(2)}, u32[]{:S(2)}) collective-permute-start(f32[128,1,128]{0,2,1:T(8,128)S(1)} %get-tuple-element.212), channel_id=1, source_target_pairs={{1,0},{2,1},{3,2},{5,4},{6,5},{7,6},{9,8},{10,9},{11,10},{13,12},{... | collective-permute-start | bytes 196616 | tf_op jit(solution)/shard_map/ppermute | solution.py:38
  234.8 6.2 %collective-permute-start.25 = (f32[128,1,128]{0,2,1:T(8,128)S(1)}, f32[128,1,128]{0,2,1:T(8,128)S(1)}, u32[]{:S(2)}, u32[]{:S(2)}) collective-permute-start(f32[128,1,128]{0,2,1:T(8,128)S(1)} %get-tuple-element.213), channel_id=1, source_target_pairs={{0,1},{1,2},{2,3},{4,5},{5,6},{6,7},{8,9},{9,10},{10,11},{12,13},{... | collective-permute-start | bytes 196616 | tf_op jit(solution)/shard_map/ppermute | solution.py:36
  242.4 30.3 %all-to-all-start.2 = ((f32[128,8,256]{0,2,1:T(8,128)}), f32[128,8,256]{0,2,1:T(8,128)S(1)}, u32[]{:S(2)}, u32[]{:S(2)}) async-start(f32[128,8,256]{0,2,1:T(8,128)} %bitcast.112), calls=%async_computation.3 | async-start | bytes 2097152 | tf_op jit(solution)/shard_map/all_to_all | solution.py:228
  304.7 30.7 %all-to-all-start.3 = ((f32[1024,1,256]{2,1,0:T(1,128)}), f32[1024,1,256]{2,1,0:T(1,128)S(1)}, u32[]{:S(2)}, u32[]{:S(2)}) async-start(f32[1024,1,256]{2,1,0:T(1,128)} %reshape_reshape.7), calls=%async_computation.4 | async-start | bytes 2097152 | tf_op jit(solution)/shard_map/all_to_all | solution.py:236
Sparse Core Ops, SparseCore 0:
  17.0 16.2 reduce-scatter.1
where the time goes:
time: 346 us; the launch traced here: 345 us
  waiting for transfers between devices  161 us (47%)
  matrix products  64 us (18%)
  starting transfers between devices  49.9 us (14%)
  local copies, waits for them, and re-layouts  28.5 us (8%)
  other arithmetic  17.9 us (5%)
  between operations  14.6 us (4%)
  blocking collectives  5.59 us (2%)
    ppermute x16, waiting for transfers between devices, passed_along(): return lax.ppermute(value, axis, pairs)  47.4 us
    dot_general x2, matrix products, forward_one_block(): jnp.dot(basis, columns, precision=lax.Precision.HIGHEST, preferred_elemen...  37.8 us
    all_to_all x1, waiting for transfers between devices, shards(): lax.all_to_all(forcing.reshape(cells_theta, sectors, columns), 'sector',...  26.5 us
    all_to_all x1, waiting for transfers between devices, shards(): lax.all_to_all(solution.reshape(cells_theta, sectors, columns), 'sector',...  26.4 us
    dot_general x2, matrix products, inverse_one_block(): lax.dot_general(basis, weighted, (((0,), (0,)), ((), ())), precision=lax....  25.6 us
    all_to_all x1, waiting for transfers between devices, shards(): lax.all_to_all(spectral, 'sector', split_axis=0, concat_axis=1, tiled=True)  25.6 us
    all_to_all x1, waiting for transfers between devices, shards(): lax.all_to_all(gathered, 'sector', split_axis=0, concat_axis=1, tiled=True)  25.1 us
    ppermute x5, starting transfers between devices, padded(): lax.ppermute(tail, axis, [(i, (i + 1) % count) for i in range(ends)])  17.5 us
  transfers between devices with their start and end apart: 31, of which 20 were waited for; matrix products, arithmetic and copies ran while one was open for 7% of the time, Pallas kernels for 0%

commit v1 on v0

v1 whole, which is shorter than its diff:
```python
import math

import jax
import jax.numpy as jnp
import numpy as np
from jax import lax
from jax.experimental import pallas as pl
from jax.experimental.pallas import tpu as pltpu
from jax.sharding import PartitionSpec as P

BURNERS = 16
MOUTH = 8
SWEEPS = 4
SUBSTEPS = 8

time_step = 0.2
diffusion = 0.05
inflow_rate = 0.5
wave_speed = 0.5
heat_coupling = 0.5
feedback = 0.5

F32 = jnp.float32
BF16 = jnp.bfloat16
HALO = SWEEPS - 1
EDGE = 8
VMEM = pl.BlockSpec(memory_space=pltpu.VMEM)
SMEM = pl.BlockSpec(memory_space=pltpu.SMEM)
ANY = pl.BlockSpec(memory_space=pl.ANY)


def halves(table):
    high = table.astype(BF16)
    low = (table - high.astype(np.float64)).astype(BF16)
    return high, low


def axial_tables(cells):
    index = np.arange(1, cells + 1, dtype=np.float64)
    basis = math.sqrt(2.0 / (cells + 1)) * np.sin(
        np.pi * ((index[:, None] * index[None, :]) % (2 * (cells + 1))) / (cells + 1)
    )
    return basis, 2.0 * np.cos(np.pi * index / (cells + 1))


def mode_classes(n_theta):
    half = n_theta // 2
    multiples = np.arange(0, half, 4)
    first = (
        np.concatenate([multiples, [half], multiples[1:]]),
        np.concatenate([np.zeros(len(multiples) + 1), np.ones(len(multiples) - 1)]),
    )
    twos = np.arange(2, half, 4)
    second = (np.concatenate([twos, twos]), np.repeat([0, 1], len(twos)))
    ones, threes = np.arange(1, half, 4), np.arange(3, half, 4)
    third = (np.concatenate([ones, threes, ones, threes]), np.repeat([0, 1], half // 2))
    return first, second, third


def azimuth_tables(n_theta):
    bases = []
    for (order, odd), rows in zip(mode_classes(n_theta), (n_theta // 4, n_theta // 4, n_theta // 2)):
        phase = (np.arange(rows)[:, None] * order[None, :].astype(np.int64)) % n_theta
        angle = phase * (2.0 * np.pi / n_theta)
        bases.append(np.where(odd[None, :] == 0, np.cos(angle), np.sin(angle)))
    return bases


def diagonal_tables(n_theta):
    half = n_theta // 2
    order = np.concatenate([part[0] for part in mode_classes(n_theta)])
    shifted = 2.0 - 2.0 * np.cos(order * (2.0 * np.pi / n_theta))
    weight = np.where((order == 0) | (order == half), 1.0, 2.0) / n_theta
    return (4.0 + shifted).astype(np.float32), weight.astype(np.float32)


def mode_rows(impedance):
    half = impedance.shape[0] - 1
    by_four = impedance[:half].reshape(half // 4, 4).T
    q0, q1, q2, q3 = by_four[0], by_four[1], by_four[2], by_four[3]
    first = jnp.concatenate([impedance[half:], q0[1:]])
    return jnp.concatenate([q0, first, q2, q2, q1, q3, q1, q3])


def split(value):
    high = value.astype(BF16)
    return high, (value - high.astype(F32)).astype(BF16)


def product(left, right, dims):
    def one(a, b):
        return lax.dot_general(a, b, (dims, ((), ())), preferred_element_type=F32)

    return one(left[0], right[0]) + (one(left[1], right[0]) + one(left[0], right[1]))


NN = ((1,), (0,))
NT = ((1,), (1,))


def edges_kernel(density, swirl, heat_rate, acoustic, heat, first, last, head, tail):
    cells_theta, cells_radius, _ = density.shape
    total = None
    for r in range(cells_radius):
        rho = density[:, r, :]
        term = heat_rate[:, r, :] * rho * rho
        total = term if total is None else total + term
    heat[...] = total
    first[...] = density[:, 0, :]
    last[...] = density[:, cells_radius - 1, :]
    for out, row, begin in ((head, 0, 0), (tail, cells_theta - 1, cells_theta - EDGE)):
        rho = density[row]
        out[0:cells_radius] = rho
        out[cells_radius : 2 * cells_radius] = rho * swirl[row]
        for k in range(3):
            at = 2 * cells_radius + k * EDGE
            out[at : at + EDGE] = acoustic[k, begin : begin + EDGE]


def flow_kernel(
    chunks, n_theta, mouth_azimuth, mouth_radius, density, swirl, above, below, inner, outer,
    basis_high, basis_low, density_next, *rest
):
    sends, forcing = rest[:chunks], rest[chunks]
    sectors = lax.axis_size("sector")
    radials = lax.axis_size("radial")
    sector = lax.axis_index("sector")
    radial = lax.axis_index("radial")
    cells_theta, cells_radius, cells_axial = density.shape
    shape = (cells_radius, cells_axial)
    rows = lax.broadcasted_iota(jnp.int32, shape, 0)
    lanes = lax.broadcasted_iota(jnp.int32, shape, 1)
    has_inner = (radial > 0).astype(F32)
    has_outer = (radial < radials - 1).astype(F32)
    segment = n_theta // BURNERS
    part = min(segment, cells_theta)

    row_above = above[0:cells_radius], above[cells_radius : 2 * cells_radius]
    row_below = below[0:cells_radius], below[cells_radius : 2 * cells_radius]

    def at(t):
        if t < 0:
            return row_below
        if t >= cells_theta:
            return row_above
        rho = density[t]
        return rho, rho * swirl[t]

    window = [at(-1), at(0)]
    for t in range(cells_theta):
        window.append(at(t + 1))
        (rho_down, flux_down), (rho, _), (rho_up, flux_up) = window
        window = window[1:]
        if t % part == 0:
            burner = (sector * cells_theta + t) // segment
            start = burner * segment + mouth_azimuth[burner] - sector * cells_theta
            radius = mouth_radius[burner] - radial * cells_radius
            mouth = ((rows >= radius) & (rows < radius + MOUTH)).astype(F32) * inflow_rate
        open_here = ((start <= t) & (t < start + MOUTH)).astype(F32)
        gain = mouth * open_here
        r_up = jnp.where(
            rows == cells_radius - 1,
            jnp.broadcast_to(outer[t : t + 1, :] * has_outer, shape),
            pltpu.roll(rho, cells_radius - 1, 0),
        )
        r_down = jnp.where(
            rows == 0,
            jnp.broadcast_to(inner[t : t + 1, :] * has_inner, shape),
            pltpu.roll(rho, 1, 0),
        )
        z_up = jnp.where(lanes == cells_axial - 1, 0.0, pltpu.roll(rho, cells_axial - 1, 1))
        z_down = jnp.where(lanes == 0, 0.0, pltpu.roll(rho, 1, 1))
        twice = 2.0 * rho
        laplace = (rho_up + rho_down - twice) + (r_up + r_down - twice) + (z_up + z_down - twice)
        advection = -0.5 * (flux_up - flux_down)
        flow = advection + diffusion * laplace
        inflow = gain * (1.0 - rho)
        density_next[t] = rho + time_step * flow + inflow
        forcing[t] = flow + inflow * (1.0 / time_step)

    basis = basis_high[...], basis_low[...]
    own = cells_axial // sectors
    each = own // chunks
    for r in range(cells_radius):
        modes = product(basis, split(forcing[:, r, :]), NT)
        for d in range(sectors):
            for c in range(chunks):
                begin = d * own + c * each
                sends[c][d, r * each : (r + 1) * each, :] = modes[begin : begin + each]


def acoustic_kernel(
    n_radius, columns, acoustic, above, below, source, source_above, source_below, basis_high,
    basis_low, send_in, acoustic_next, send, staged, sem
):
    cells_theta, cells_axial = source.shape
    skip = above.shape[0] - 3 * EDGE

    def extended(k):
        begin = skip + k * EDGE
        return jnp.concatenate(
            [below[begin : begin + EDGE], acoustic[k], above[begin : begin + EDGE]], 0
        )

    press, along, axial = extended(0), extended(1), extended(2)
    heat = jnp.concatenate([source_below[...], source[...], source_above[...]], 0)
    heat = heat * (heat_coupling / n_radius)
    count = press.shape[0]
    lanes = lax.broadcasted_iota(jnp.int32, press.shape, 1)
    for _ in range(SUBSTEPS):
        press_up = pltpu.roll(press, count - 1, 0)
        press_axial = jnp.where(lanes == cells_axial - 1, 0.0, pltpu.roll(press, cells_axial - 1, 1))
        along = along - wave_speed * (press_up - press)
        axial = axial - wave_speed * (press_axial - press)
        along_down = pltpu.roll(along, 1, 0)
        axial_down = jnp.where(lanes == 0, 0.0, pltpu.roll(axial, 1, 1))
        press = press - wave_speed * ((along - along_down) + (axial - axial_down)) + heat
    own = slice(EDGE, EDGE + cells_theta)
    acoustic_next[0] = press[own]
    acoustic_next[1] = along[own]
    acoustic_next[2] = axial[own]
    modes = product((basis_high[...], basis_low[...]), split(feedback * press[own]), NT)
    staged[...] = modes.reshape(staged.shape)
    copy = pltpu.make_async_copy(
        staged, send.at[:, pl.ds(columns, staged.shape[1]), :], sem
    )
    copy.start()
    copy.wait()


def forward_kernel(edge, columns, received, w0h, w0l, w1h, w1l, w2h, w2l, modes, first, last):
    blocks = received.shape[0]
    quarter = blocks // 4

    def joined(parts):
        return jnp.concatenate(parts, 1) if len(parts) > 1 else parts[0]

    pieces = [received[s] for s in range(blocks)]
    half = blocks // 2
    even = [pieces[s] + pieces[s + half] for s in range(half)]
    odd = [pieces[s] - pieces[s + half] for s in range(half)]
    both = [even[s] + even[s + quarter] for s in range(quarter)]
    apart = [even[s] - even[s + quarter] for s in range(quarter)]
    at = 0
    for parts, wh, wl in ((both, w0h, w0l), (apart, w1h, w1l), (odd, w2h, w2l)):
        width = wh.shape[1]
        out = product(split(joined(parts)), (wh[...], wl[...]), NN)
        modes[:, at : at + width] = out
        first[:, at : at + width] = out[:edge]
        last[:, at : at + width] = out[columns - edge : columns]
        at += width


def solve_kernel(
    chunk, chunks, modes, inner, outer, wave, inverse, scaled, axial, w0h, w0l, w1h, w1l, w2h,
    w2l, send, solved
):
    radials = lax.axis_size("radial")
    radial = lax.axis_index("radial")
    sector = lax.axis_index("sector")
    n_theta = modes.shape[1]
    each = axial.shape[1] // chunks
    cells_radius = inner.shape[0] // each // HALO
    cells_radius = send.shape[1] // each
    has_inner = (radial > 0).astype(F32)
    has_outer = (radial < radials - 1).astype(F32)
    eigen = axial[sector][chunk * each : (chunk + 1) * each, :]
    step = eigen.shape[1]
    total = cells_radius + 2 * HALO
    for block in range(n_theta // step):
        lane = slice(block * step, (block + 1) * step)
        inv = jnp.broadcast_to(inverse[:, lane], (each, step))
        inv_inner, inv_outer = inv * has_inner, inv * has_outer
        last_scale = jnp.broadcast_to(scaled[:, lane], (each, step))
        add = wave[chunk * each : (chunk + 1) * each, lane]

        def row_of(i):
            if i < HALO:
                return inner[i * each : (i + 1) * each, lane]
            i -= HALO
            if i < cells_radius:
                return modes[i * each : (i + 1) * each, lane]
            i -= cells_radius
            return outer[i * each : (i + 1) * each, lane]

        def scale_of(i):
            if i < HALO:
                return inv_inner
            return inv if i < HALO + cells_radius else inv_outer

        right = [row_of(i) + add for i in range(total)]
        x = [right[i] * scale_of(i) for i in range(total)]
        for sweep in range(1, SWEEPS):
            fresh = [None] * total
            for i in range(sweep, total - sweep):
                scale = last_scale if sweep == SWEEPS - 1 else scale_of(i)
                fresh[i] = (right[i] + (x[i + 1] + x[i - 1]) + eigen * x[i]) * scale
            x = fresh
        for i in range(cells_radius):
            solved[i * each : (i + 1) * each, lane] = x[i + HALO]

    sectors = send.shape[0]
    width = send.shape[2]
    n0, n1 = w0h.shape[1], w1h.shape[1]
    value = split(solved[:, :n0])
    both = product(value, (w0h[...], w0l[...]), NT)
    value = split(solved[:, n0 : n0 + n1])
    apart = product(value, (w1h[...], w1l[...]), NT)
    value = split(solved[:, n0 + n1 :])
    odd = product(value, (w2h[...], w2l[...]), NT)
    even = jnp.concatenate([both + apart, both - apart], 1)
    for s in range(sectors // 2):
        lane = slice(s * width, (s + 1) * width)
        send[s] = even[:, lane] + odd[:, lane]
        send[s + sectors // 2] = even[:, lane] - odd[:, lane]


def pressure_kernel(chunks, *refs):
    received, (basis_high, basis_low, pressure) = refs[:chunks], refs[chunks:]
    cells_radius = pressure.shape[1]
    sectors = received[0].shape[0]
    each = received[0].shape[1] // cells_radius
    basis = basis_high[...], basis_low[...]
    for r in range(cells_radius):
        rows = [
            received[c][d, r * each : (r + 1) * each, :]
            for d in range(sectors)
            for c in range(chunks)
        ]
        modes = jnp.concatenate(rows, 0)
        pressure[:, r, :] = product(split(modes.T), basis, NN)


def call(kernel, outs, ins, scratch=(), **more):
    flops = more.pop("flops", 0)
    moved = sum(math.prod(o.shape) * 4 for o in outs)
    return pl.pallas_call(
        kernel,
        out_shape=outs,
        in_specs=ins,
        out_specs=more.pop("out_specs", [VMEM] * len(outs)),
        scratch_shapes=list(scratch),
        cost_estimate=pl.CostEstimate(flops=flops, bytes_accessed=3 * moved, transcendentals=0),
        compiler_params=pltpu.CompilerParams(vmem_limit_bytes=40 * 1024 * 1024),
        **more,
    )


def shape(*dims):
    return jax.ShapeDtypeStruct(dims, F32)


def shifted(value, axis, steps):
    count = lax.axis_size(axis)
    return lax.ppermute(value, axis, [(i, (i + steps) % count) for i in range(count)])


def exchanged(value):
    return lax.all_to_all(value, "sector", split_axis=0, concat_axis=0, tiled=True)


def shards(density, swirl, heat_rate, acoustic, mode_impedance, mouth_azimuth, mouth_radius):
    sectors = lax.axis_size("sector")
    radials = lax.axis_size("radial")
    cells_theta, cells_radius, cells_axial = density.shape
    n_theta = cells_theta * sectors
    n_radius = cells_radius * radials
    own = cells_axial // sectors
    chunks = max(1, min(2, own // 8))
    each = own // chunks
    columns = cells_radius * each
    edge = HALO * each

    basis, eigen = axial_tables(cells_axial)
    basis_high, basis_low = (jnp.asarray(t) for t in halves(basis))
    eigen = jnp.asarray(
        np.broadcast_to(eigen.reshape(sectors, own, 1), (sectors, own, 128)).astype(np.float32)
    )
    tables = []
    for table in azimuth_tables(n_theta):
        tables += [jnp.asarray(t) for t in halves(table)]
    fixed, weight = diagonal_tables(n_theta)
    inverse = (1.0 / (jnp.asarray(fixed) + mode_rows(mode_impedance)))[None, :]
    scaled = inverse * jnp.asarray(weight)[None, :]

    packed = 2 * cells_radius + 3 * EDGE
    row_block = shape(cells_theta, cells_axial)
    heat, first, last, head, tail = call(
        edges_kernel,
        [row_block] * 3 + [shape(packed, cells_axial)] * 2,
        [VMEM] * 4,
    )(density, swirl, heat_rate, acoustic)
    above = shifted(head, "sector", -1)
    below = shifted(tail, "sector", 1)
    outer = shifted(first, "radial", -1)
    inner = shifted(last, "radial", 1)

    step = 1
    while step < radials:
        heat = heat + lax.ppermute(heat, "radial", [(i, i ^ step) for i in range(radials)])
        step *= 2
    source_above = shifted(heat[:EDGE], "sector", -1)
    source_below = shifted(heat[-EDGE:], "sector", 1)

    sent = [shape(sectors, columns, cells_theta)] * (chunks - 1)
    sent.append(shape(sectors, columns + own, cells_theta))
    density_next, *sends = call(
        lambda *refs: flow_kernel(chunks, n_theta, *refs),
        [shape(*density.shape)] + sent,
        [SMEM] * 2 + [VMEM] * 8,
        [pltpu.VMEM(density.shape, F32)],
    )(mouth_azimuth, mouth_radius, density, swirl, above, below, inner, outer, basis_high, basis_low)

    acoustic_next, sends[-1] = call(
        lambda *refs: acoustic_kernel(n_radius, columns, *refs),
        [shape(*acoustic.shape), sent[-1]],
        [VMEM] * 8 + [ANY],
        [pltpu.VMEM((sectors, own, cells_theta), F32), pltpu.SemaphoreType.DMA],
        out_specs=[VMEM, ANY],
        input_output_aliases={8: 1},
    )(acoustic, above, below, heat, source_above, source_below, basis_high, basis_low, sends[-1])

    received = [exchanged(value) for value in sends]
    modes = []
    for c in range(chunks):
        count = received[c].shape[1]
        c_modes, c_first, c_last = call(
            lambda *refs: forward_kernel(edge, columns, *refs),
            [shape(count, n_theta), shape(edge, n_theta), shape(edge, n_theta)],
            [VMEM] * 7,
        )(received[c], *tables)
        modes.append((c_modes, shifted(c_last, "radial", 1), shifted(c_first, "radial", -1)))
    wave = modes[-1][0][columns:]

    results = []
    for c in range(chunks):
        (send,) = call(
            lambda *refs: solve_kernel(c, chunks, *refs),
            [shape(sectors, columns, cells_theta)],
            [VMEM] * 13,
            [pltpu.VMEM((columns, n_theta), F32)],
        )(*modes[c], wave, inverse, scaled, eigen, *tables)
        results.append(exchanged(send))

    (pressure,) = call(
        lambda *refs: pressure_kernel(chunks, *refs),
        [shape(*density.shape)],
        [VMEM] * (chunks + 2),
    )(*results, basis_high, basis_low)
    return density_next, pressure, acoustic_next


def solution(mesh):
    return jax.shard_map(
        shards,
        mesh=mesh,
        in_specs=(
            P("sector", "radial", None),
            P("sector", "radial", None),
            P("sector", "radial", None),
            P(None, "sector", None),
            P(),
            P(),
            P(),
        ),
        out_specs=(
            P("sector", "radial", None),
            P("sector", "radial", None),
            P(None, "sector", None),
        ),
        check_vma=False,
    )
```

time: 346 us -> 109 us (0.32)
  waiting for transfers between devices: 161 us -> 36.6 us
  matrix products: 64 us -> 0 us
  starting transfers between devices: 49.9 us -> 28.6 us
  local copies, waits for them, and re-layouts: 28.5 us -> 8.63 us
  other arithmetic: 17.9 us -> 0.02 us
  Pallas kernels: 0 us -> 16.5 us
  between operations: 14.6 us -> 0.91 us
  blocking collectives: 5.59 us -> 17.2 us
    all_to_all x4 -> x3, waiting for transfers between devices: 104 us -> 17.4 us  [exchanged(): lax.all_to_all(value, 'sector', split_axis=0, concat_axis=0, tiled=True)]
    dot_general x6 -> x0, matrix products: 64 us -> none  [the longest x2 37.8 us: forward_one_block(): jnp.dot(basis, columns, precision=lax.Precision.HIGHEST, preferred_elemen...]
    ppermute x26 -> x12, waiting for transfers between devices: 49.4 us -> 19.2 us  [the longest x10 15.2 us: shifted(): lax.ppermute(value, axis, [(i, (i + steps) % count) for i in range(count)])]
    all_to_all x0 -> x1, blocking collectives: none -> 17.2 us  [exchanged(): lax.all_to_all(value, 'sector', split_axis=0, concat_axis=0, tiled=True)]
    ppermute x26 -> x12, starting transfers between devices: 34.6 us -> 17.6 us  [the longest x10 16 us: shifted(): lax.ppermute(value, axis, [(i, (i + steps) % count) for i in range(count)])]
    pallas_call x0 -> x8, Pallas kernels: none -> 16.5 us  [the longest x1 5.72 us: shards(): call(lambda *refs: flow_kernel(chunks, n_theta, *refs), [shape(*density.s...]
    reduce_scatter x1 -> x0, waiting for transfers between devices: 8.24 us -> none  [shards(): lax.psum_scatter(local_heat, 'radial', scatter_dimension=0, tiled=True)]
    slice x42 -> x7, local copies, waits for them, and re-layouts: 8.72 us -> 0.85 us  [the longest x2 0.61 us: mode_rows(): first = jnp.concatenate([impedance[half:], q0[1:]])]
  transfers between devices with their start and end apart: 31 -> 15, of which waited for: 20 -> 9; matrix products, arithmetic and copies ran while one was open for 7% -> 1% of each run, Pallas kernels for 0% -> 5%
where the time goes in v1:
time: 109 us; the launch traced here: 108 us
  waiting for transfers between devices  36.6 us (34%)
  starting transfers between devices  28.6 us (26%)
  blocking collectives  17.2 us (16%)
  Pallas kernels  16.5 us (15%)
  local copies, waits for them, and re-layouts  8.63 us (8%)
    all_to_all x3, waiting for transfers between devices, exchanged(): lax.all_to_all(value, 'sector', split_axis=0, concat_axis=0, tiled=True)  17.4 us
    all_to_all x1, blocking collectives, exchanged(): lax.all_to_all(value, 'sector', split_axis=0, concat_axis=0, tiled=True)  17.2 us
    ppermute x10, starting transfers between devices, shifted(): lax.ppermute(value, axis, [(i, (i + steps) % count) for i in range(count)])  16 us
    ppermute x10, waiting for transfers between devices, shifted(): lax.ppermute(value, axis, [(i, (i + steps) % count) for i in range(count)])  15.2 us
    all_to_all x3, starting transfers between devices, exchanged(): lax.all_to_all(value, 'sector', split_axis=0, concat_axis=0, tiled=True)  11 us
    unnamed x50, local copies, waits for them, and re-layouts  7.03 us
    pallas_call x1, Pallas kernels, shards(): call(lambda *refs: flow_kernel(chunks, n_theta, *refs), [shape(*density.s...  5.72 us
    ppermute x2, waiting for transfers between devices, shards(): lax.ppermute(heat, 'radial', [(i, i ^ step) for i in range(radials)])  4.02 us
  transfers between devices with their start and end apart: 15, of which 9 were waited for; matrix products, arithmetic and copies ran while one was open for 1% of the time, Pallas kernels for 5%

profile of v1, /device:TPU:0, one launch (start us, length us, event | category | flops | bytes accessed | tf_op | source)
XLA Modules:
  0.0 108.4 jit_solution(9927071796036118048)
XLA Ops:
  0.6 1.2 %copy-done.2 = f32[128,16,128]{2,1,0:T(8,128)S(1)} copy-done((f32[128,16,128]{2,1,0:T(8,128)S(1)}, f32[128,16,128]{2,1,0:T(8,128)}, u32[]{:S(2)}) %copy-start.2) | copy-done | bytes 1048600
  1.9 1.2 %copy-done.3 = f32[128,16,128]{2,1,0:T(8,128)S(1)} copy-done((f32[128,16,128]{2,1,0:T(8,128)S(1)}, f32[128,16,128]{2,1,0:T(8,128)}, u32[]{:S(2)}) %copy-start.3) | copy-done | bytes 1048600
  3.1 1.2 %copy-done.8 = f32[128,16,128]{2,1,0:T(8,128)S(1)} copy-done((f32[128,16,128]{2,1,0:T(8,128)S(1)}, f32[128,16,128]{2,1,0:T(8,128)}, u32[]{:S(2)}) %copy-start.8) | copy-done | bytes 1048600
  4.3 0.9 copy-done.9
  5.2 0.9 shard_map.193
  6.1 0.5 collective-permute-start.2
  6.7 2.0 %collective-permute-start.3 = (f32[128,128]{1,0:T(8,128)S(1)}, f32[128,128]{1,0:T(8,128)S(1)}, u32[]{:S(2)}, u32[]{:S(2)}) collective-permute-start(f32[128,128]{1,0:T(8,128)S(1)} %get-tuple-element.22), channel_id=1, source_target_pairs={{0,3},{1,0},{2,1},{3,2},{4,7},{5,4},{6,5},{7,6},{8,11},{9,8},{10,9... | collective-permute-start | bytes 196616 | tf_op jit(solution)/shard_map/ppermute | solution.py:355
  8.7 5.3 %collective-permute-start = (f32[56,128]{1,0:T(8,128)S(1)}, f32[56,128]{1,0:T(8,128)S(1)}, u32[]{:S(2)}, u32[]{:S(2)}) collective-permute-start(f32[56,128]{1,0:T(8,128)S(1)} %get-tuple-element.19), channel_id=1, source_target_pairs={{0,28},{4,0},{8,4},{12,8},{16,12},{20,16},{24,20},{28,24},{1,29},{... | collective-permute-start | bytes 86024 | tf_op jit(solution)/shard_map/ppermute | solution.py:355
  14.0 1.6 %collective-permute-done.refs_4_.refs_1_ = f32[56,128]{1,0:T(8,128)S(1)} collective-permute-done((f32[56,128]{1,0:T(8,128)S(1)}, f32[56,128]{1,0:T(8,128)S(1)}, u32[]{:S(2)}, u32[]{:S(2)}) %collective-permute-start) | collective-permute-done | bytes 28704 | tf_op jit(solution)/shard_map/ppermute | solution.py:355
  15.5 5.0 %collective-permute-done.1.refs_5_.refs_2_ = f32[56,128]{1,0:T(8,128)S(1)} collective-permute-done((f32[56,128]{1,0:T(8,128)S(1)}, f32[56,128]{1,0:T(8,128)S(1)}, u32[]{:S(2)}, u32[]{:S(2)}) %collective-permute-start.1) | collective-permute-done | bytes 28704 | tf_op jit(solution)/shard_map/ppermute | solution.py:355
  20.6 5.7 %shard_map.194 = (f32[128,16,128]{2,1,0:T(8,128)}, f32[8,128,128]{2,1,0:T(8,128)}, f32[8,144,128]{2,1,0:T(8,128)}) custom-call(s32[16]{0:T(128)S(1)} %copy-done.16, s32[16]{0:T(128)S(1)} %copy-done.17, f32[128,16,128]{2,1,0:T(8,128)S(1)} %copy-done.2, f32[128,16,128]{2,1,0:T(8,128)S(1)} %copy-done.3, f32[56,128]{1,0:T(8,128)S(1)} %collective-permute-done.refs_4_.refs_1_, ...), custom_call_target="tpu_custom_call" | custom-call | bytes 6488064 | tf_op jit(solution)/shard_map/pallas_call | solution.py:407
  26.3 3.5 %all-to-all-start = ((f32[8,128,128]{2,1,0:T(8,128)}), f32[8,128,128]{2,1,0:T(8,128)S(1)}, u32[]{:S(2)}, u32[]{:S(2)}) async-start(f32[8,128,128]{2,1,0:T(8,128)} %get-tuple-element.24), calls=%async_computation | async-start | bytes 1048576 | tf_op jit(solution)/shard_map/all_to_all | solution.py:359
  29.8 0.1 collective-permute-start.6
  29.9 1.2 %collective-permute-done.6 = f32[128,128]{1,0:T(8,128)S(1)} collective-permute-done((f32[128,128]{1,0:T(8,128)S(1)}, f32[128,128]{1,0:T(8,128)S(1)}, u32[]{:S(2)}, u32[]{:S(2)}) %collective-permute-start.6) | collective-permute-done | bytes 65568 | tf_op jit(solution)/shard_map/ppermute | solution.py:400
  31.1 1.6 %collective-permute-start.7 = (f32[128,128]{1,0:T(8,128)S(1)}, f32[128,128]{1,0:T(8,128)S(1)}, u32[]{:S(2)}, u32[]{:S(2)}) collective-permute-start(f32[128,128]{1,0:T(8,128)S(1)} %add.9), channel_id=1, source_target_pairs={{0,2},{1,3},{2,0},{3,1},{4,6},{5,7},{6,4},{7,5},{8,10},{9,11},{10,... | collective-permute-start | bytes 196616 | tf_op jit(solution)/shard_map/ppermute | solution.py:400
  32.7 2.8 %collective-permute-done.7 = f32[128,128]{1,0:T(8,128)S(1)} collective-permute-done((f32[128,128]{1,0:T(8,128)S(1)}, f32[128,128]{1,0:T(8,128)S(1)}, u32[]{:S(2)}, u32[]{:S(2)}) %collective-permute-start.7) | collective-permute-done | bytes 65568 | tf_op jit(solution)/shard_map/ppermute | solution.py:400
  35.5 4.6 %collective-permute-start.8 = (f32[8,128]{1,0:T(8,128)S(1)}, f32[8,128]{1,0:T(8,128)S(1)}, u32[]{:S(2)}, u32[]{:S(2)}) collective-permute-start(f32[8,128]{1,0:T(8,128)S(1)} %get-tuple-element.40), channel_id=1, source_target_pairs={{0,28},{4,0},{8,4},{12,8},{16,12},{20,16},{24,20},{28,24},{1,29},{... | collective-permute-start | bytes 12296 | tf_op jit(solution)/shard_map/ppermute | solution.py:355
  40.1 1.3 %collective-permute-done.8.refs_4_ = f32[8,128]{1,0:T(8,128)S(1)} collective-permute-done((f32[8,128]{1,0:T(8,128)S(1)}, f32[8,128]{1,0:T(8,128)S(1)}, u32[]{:S(2)}, u32[]{:S(2)}) %collective-permute-start.8) | collective-permute-done | bytes 4128 | tf_op jit(solution)/shard_map/ppermute | solution.py:355
  41.5 5.0 %collective-permute-done.9.refs_5_ = f32[8,128]{1,0:T(8,128)S(1)} collective-permute-done((f32[8,128]{1,0:T(8,128)S(1)}, f32[8,128]{1,0:T(8,128)S(1)}, u32[]{:S(2)}, u32[]{:S(2)}) %collective-permute-start.9) | collective-permute-done | bytes 4128 | tf_op jit(solution)/shard_map/ppermute | solution.py:355
  46.5 2.7 %shard_map.196 = (f32[3,128,128]{2,1,0:T(8,128)}, f32[8,144,128]{2,1,0:T(8,128)}) custom-call(f32[3,128,128]{2,1,0:T(8,128)S(1)} %copy-done.10, f32[56,128]{1,0:T(8,128)S(1)} %collective-permute-done.refs_4_.refs_1_, f32[56,128]{1,0:T(8,128)S(1)} %collective-permute-done.1.refs_5_.refs_2_, ...), custom_call_target="tpu_custom_call", output_to_operand_aliasing={{1}: (8, {})} | custom-call | bytes 2359296 | tf_op jit(solution)/shard_map/pallas_call | solution.py:414
  49.2 0.0 copy-start
  49.2 0.0 copy-start.1
  49.2 0.0 copy-start.7
  49.2 3.7 %all-to-all-start.1 = ((f32[8,144,128]{2,1,0:T(8,128)}), f32[8,144,128]{2,1,0:T(8,128)S(1)}, u32[]{:S(2)}, u32[]{:S(2)}) async-start(f32[8,144,128]{2,1,0:T(8,128)} %get-tuple-element.30), calls=%async_computation.1 | async-start | bytes 1179648 | tf_op jit(solution)/shard_map/all_to_all | solution.py:359
  52.9 0.5 slice.39
  53.4 0.1 reshape.11
  53.5 0.1 slice_reduce_fusion.3
  53.7 0.2 slice_reduce_fusion
  53.9 0.6 concatenate.3
  54.6 0.0 copy-done.4
  54.6 0.1 copy-done.5
  54.6 1.1 %shard_map.195 = (f32[128,1024]{1,0:T(8,128)S(1)}, f32[24,1024]{1,0:T(8,128)}, f32[24,1024]{1,0:T(8,128)}) custom-call(f32[8,128,128]{2,1,0:T(8,128)S(1)} %all-to-all-done.refs_0_, bf16[256,256]{1,0:T(8,128)(2,1)S(1)} %copy-done.4, bf16[256,256]{1,0:T(8,128)(2,1)S(1)} %copy-done.5, bf16[256,256]{1,0:T(8,128)(2,1)S(1)} %copy-done.6, ...), custom_call_target="tpu_custom_call" | custom-call | bytes 2162688 | tf_op jit(solution)/shard_map/pallas_call | solution.py:427
  55.8 0.8 copy-done.11
  56.6 1.7 %collective-permute-start.5 = (f32[24,1024]{1,0:T(8,128)}, f32[24,1024]{1,0:T(8,128)}, u32[]{:S(2)}, u32[]{:S(2)}) collective-permute-start(f32[24,1024]{1,0:T(8,128)} %get-tuple-element.27), channel_id=1, source_target_pairs={{0,3},{1,0},{2,1},{3,2},{4,7},{5,4},{6,5},{7,6},{8,11},{9,8},{10,9... | collective-permute-start | bytes 294920 | tf_op jit(solution)/shard_map/ppermute | solution.py:355
  58.3 8.7 %all-to-all-done.1.refs_0_ = f32[8,144,128]{2,1,0:T(8,128)S(1)} async-done(((f32[8,144,128]{2,1,0:T(8,128)}), f32[8,144,128]{2,1,0:T(8,128)S(1)}, u32[]{:S(2)}, u32[]{:S(2)}) %all-to-all-start.1) | async-done | bytes 589856 | tf_op jit(solution)/shard_map/all_to_all | solution.py:359
  67.0 0.5 shard_map.197
  67.6 0.6 copy-done.20
  68.2 0.6 copy-done.18
  68.8 0.2 copy-done.15
  69.1 2.6 %shard_map.198 = f32[8,128,128]{2,1,0:T(8,128)} custom-call(f32[128,1024]{1,0:T(8,128)S(1)} %copy-done.12, f32[24,1024]{1,0:T(8,128)S(1)} %collective-permute-done.4.refs_1_, f32[24,1024]{1,0:T(8,128)} %collective-permute-done.5.refs_2_, f32[16,1024]{1,0:T(8,128)S(1)} %slice.36.refs_3_, f32[1,1024]{1,0:T(1,128)S(1)} %bitcast.5, f32[1,1024]{1,0:T(1,128)S(1)} %bitcast.3, ...), custom_call_target="tpu_custom_call" | custom-call | bytes 1572864 | tf_op jit(solution)/shard_map/pallas_call | solution.py:437
  71.7 3.8 %all-to-all-start.2 = ((f32[8,128,128]{2,1,0:T(8,128)}), f32[8,128,128]{2,1,0:T(8,128)S(1)}, u32[]{:S(2)}, u32[]{:S(2)}) async-start(f32[8,128,128]{2,1,0:T(8,128)} %shard_map.198), calls=%async_computation.2 | async-start | bytes 1048576 | tf_op jit(solution)/shard_map/all_to_all | solution.py:359
  75.5 0.1 collective-permute-start.10
  75.6 1.7 %collective-permute-start.11 = (f32[24,1024]{1,0:T(8,128)S(1)}, f32[24,1024]{1,0:T(8,128)S(1)}, u32[]{:S(2)}, u32[]{:S(2)}) collective-permute-start(f32[24,1024]{1,0:T(8,128)S(1)} %copy-done.19), channel_id=1, source_target_pairs={{0,3},{1,0},{2,1},{3,2},{4,7},{5,4},{6,5},{7,6},{8,11},{9,8},{10,9... | collective-permute-start | bytes 294920 | tf_op jit(solution)/shard_map/ppermute | solution.py:355
  77.3 2.3 %collective-permute-done.10.refs_1_ = f32[24,1024]{1,0:T(8,128)S(1)} collective-permute-done((f32[24,1024]{1,0:T(8,128)S(1)}, f32[24,1024]{1,0:T(8,128)S(1)}, u32[]{:S(2)}, u32[]{:S(2)}) %collective-permute-start.10) | collective-permute-done | bytes 98336 | tf_op jit(solution)/shard_map/ppermute | solution.py:355
  79.6 0.9 shard_map.199
  80.6 8.7 %all-to-all-done.2.refs_0_ = f32[8,128,128]{2,1,0:T(8,128)S(1)} async-done(((f32[8,128,128]{2,1,0:T(8,128)}), f32[8,128,128]{2,1,0:T(8,128)S(1)}, u32[]{:S(2)}, u32[]{:S(2)}) %all-to-all-start.2) | async-done | bytes 524320 | tf_op jit(solution)/shard_map/all_to_all | solution.py:359
  89.3 17.2 %all_to_all.20.refs_1_ = f32[8,128,128]{2,1,0:T(8,128)S(1)} all-to-all(f32[8,128,128]{2,1,0:T(8,128)S(1)} %shard_map.199), channel_id=1, replica_groups=mesh['sector'=8,'radial'=4] {'sector'}, dimensions={0} | all-to-all | bytes 1048576 | tf_op jit(solution)/shard_map/all_to_all | solution.py:359
  106.4 2.0 %shard_map.200 = f32[128,16,128]{2,1,0:T(8,128)} custom-call(f32[8,128,128]{2,1,0:T(8,128)S(1)} %all-to-all-done.2.refs_0_, f32[8,128,128]{2,1,0:T(8,128)S(1)} %all_to_all.20.refs_1_, bf16[128,128]{1,0:T(8,128)(2,1)S(1)} %copy-done.13, bf16[128,128]{1,0:T(8,128)(2,1)S(1)} %copy-done.14), custom_call_target="tpu_custom_call" | custom-call | bytes 3145728 | tf_op jit(solution)/shard_map/pallas_call | solution.py:445
  (53 shorter events, 0.1 us)
Async XLA Ops:
  0.6 1.2 %copy-start.2 = (f32[128,16,128]{2,1,0:T(8,128)S(1)}, f32[128,16,128]{2,1,0:T(8,128)}, u32[]{:S(2)}) copy-start(f32[128,16,128]{2,1,0:T(8,128)} %refs_2_.4) | copy-start | bytes 3145732
  1.9 1.2 %copy-start.3 = (f32[128,16,128]{2,1,0:T(8,128)S(1)}, f32[128,16,128]{2,1,0:T(8,128)}, u32[]{:S(2)}) copy-start(f32[128,16,128]{2,1,0:T(8,128)} %refs_3_.4) | copy-start | bytes 3145732
  3.1 1.2 %copy-start.8 = (f32[128,16,128]{2,1,0:T(8,128)S(1)}, f32[128,16,128]{2,1,0:T(8,128)}, u32[]{:S(2)}) copy-start(f32[128,16,128]{2,1,0:T(8,128)} %heat_rate.1) | copy-start | bytes 3145732
  4.3 0.9 copy-start.9
  5.2 15.3 %copy-start.13 = (bf16[128,128]{1,0:T(8,128)(2,1)S(1)}, bf16[128,128]{1,0:T(8,128)(2,1)}, u32[]{:S(2)}) copy-start(bf16[128,128]{1,0:T(8,128)(2,1)} %constant.24.clone.refs_8_.refs_6_.refs_2_) | copy-start | bytes 98308
  5.2 15.3 %copy-start.14 = (bf16[128,128]{1,0:T(8,128)(2,1)S(1)}, bf16[128,128]{1,0:T(8,128)(2,1)}, u32[]{:S(2)}) copy-start(bf16[128,128]{1,0:T(8,128)(2,1)} %constant.25.clone.refs_9_.refs_7_.refs_3_) | copy-start | bytes 98308
  6.1 14.4 %collective-permute-start.2 = (f32[128,128]{1,0:T(8,128)S(1)}, f32[128,128]{1,0:T(8,128)S(1)}, u32[]{:S(2)}, u32[]{:S(2)}) collective-permute-start(f32[128,128]{1,0:T(8,128)S(1)} %get-tuple-element.21), channel_id=1, source_target_pairs={{0,1},{1,2},{2,3},{3,0},{4,5},{5,6},{6,7},{7,4},{8,9},{9,10},{10,1... | collective-permute-start | bytes 196616 | tf_op jit(solution)/shard_map/ppermute | solution.py:355
  6.7 13.9 %collective-permute-start.3 = (f32[128,128]{1,0:T(8,128)S(1)}, f32[128,128]{1,0:T(8,128)S(1)}, u32[]{:S(2)}, u32[]{:S(2)}) collective-permute-start(f32[128,128]{1,0:T(8,128)S(1)} %get-tuple-element.22), channel_id=1, source_target_pairs={{0,3},{1,0},{2,1},{3,2},{4,7},{5,4},{6,5},{7,6},{8,11},{9,8},{10,9... | collective-permute-start | bytes 196616 | tf_op jit(solution)/shard_map/ppermute | solution.py:355
  8.7 11.9 %copy-start.16 = (s32[16]{0:T(128)S(1)}, s32[16]{0:T(128)}, u32[]{:S(2)}) copy-start(s32[16]{0:T(128)} %refs_0_.2) | copy-start | bytes 196
  8.7 11.9 %copy-start.17 = (s32[16]{0:T(128)S(1)}, s32[16]{0:T(128)}, u32[]{:S(2)}) copy-start(s32[16]{0:T(128)} %refs_1_.3) | copy-start | bytes 196
  8.7 6.9 %collective-permute-start = (f32[56,128]{1,0:T(8,128)S(1)}, f32[56,128]{1,0:T(8,128)S(1)}, u32[]{:S(2)}, u32[]{:S(2)}) collective-permute-start(f32[56,128]{1,0:T(8,128)S(1)} %get-tuple-element.19), channel_id=1, source_target_pairs={{0,28},{4,0},{8,4},{12,8},{16,12},{20,16},{24,20},{28,24},{1,29},{... | collective-permute-start | bytes 86024 | tf_op jit(solution)/shard_map/ppermute | solution.py:355
  14.0 6.6 %collective-permute-start.1 = (f32[56,128]{1,0:T(8,128)S(1)}, f32[56,128]{1,0:T(8,128)S(1)}, u32[]{:S(2)}, u32[]{:S(2)}) collective-permute-start(f32[56,128]{1,0:T(8,128)S(1)} %get-tuple-element.20), channel_id=1, source_target_pairs={{0,4},{4,8},{8,12},{12,16},{16,20},{20,24},{24,28},{28,0},{1,5},{5... | collective-permute-start | bytes 86024 | tf_op jit(solution)/shard_map/ppermute | solution.py:355
  26.3 22.8 %all-to-all-start = ((f32[8,128,128]{2,1,0:T(8,128)}), f32[8,128,128]{2,1,0:T(8,128)S(1)}, u32[]{:S(2)}, u32[]{:S(2)}) async-start(f32[8,128,128]{2,1,0:T(8,128)} %get-tuple-element.24), calls=%async_computation | async-start | bytes 1048576 | tf_op jit(solution)/shard_map/all_to_all | solution.py:359
  29.8 16.6 %copy-start.10 = (f32[3,128,128]{2,1,0:T(8,128)S(1)}, f32[3,128,128]{2,1,0:T(8,128)}, u32[]{:S(2)}) copy-start(f32[3,128,128]{2,1,0:T(8,128)} %refs_0_.3) | copy-start | bytes 589828
  29.8 1.3 %collective-permute-start.6 = (f32[128,128]{1,0:T(8,128)S(1)}, f32[128,128]{1,0:T(8,128)S(1)}, u32[]{:S(2)}, u32[]{:S(2)}) collective-permute-start(f32[128,128]{1,0:T(8,128)S(1)} %get-tuple-element.28), channel_id=1, source_target_pairs={{0,1},{1,0},{2,3},{3,2},{4,5},{5,4},{6,7},{7,6},{8,9},{9,8},{10,11... | collective-permute-start | bytes 196616 | tf_op jit(solution)/shard_map/ppermute | solution.py:400
  31.1 4.3 %collective-permute-start.7 = (f32[128,128]{1,0:T(8,128)S(1)}, f32[128,128]{1,0:T(8,128)S(1)}, u32[]{:S(2)}, u32[]{:S(2)}) collective-permute-start(f32[128,128]{1,0:T(8,128)S(1)} %add.9), channel_id=1, source_target_pairs={{0,2},{1,3},{2,0},{3,1},{4,6},{5,7},{6,4},{7,5},{8,10},{9,11},{10,... | collective-permute-start | bytes 196616 | tf_op jit(solution)/shard_map/ppermute | solution.py:400
  35.5 6.0 %collective-permute-start.8 = (f32[8,128]{1,0:T(8,128)S(1)}, f32[8,128]{1,0:T(8,128)S(1)}, u32[]{:S(2)}, u32[]{:S(2)}) collective-permute-start(f32[8,128]{1,0:T(8,128)S(1)} %get-tuple-element.40), channel_id=1, source_target_pairs={{0,28},{4,0},{8,4},{12,8},{16,12},{20,16},{24,20},{28,24},{1,29},{... | collective-permute-start | bytes 12296 | tf_op jit(solution)/shard_map/ppermute | solution.py:355
  40.1 6.3 %collective-permute-start.9 = (f32[8,128]{1,0:T(8,128)S(1)}, f32[8,128]{1,0:T(8,128)S(1)}, u32[]{:S(2)}, u32[]{:S(2)}) collective-permute-start(f32[8,128]{1,0:T(8,128)S(1)} %get-tuple-element.39), channel_id=1, source_target_pairs={{0,4},{4,8},{8,12},{12,16},{16,20},{20,24},{24,28},{28,0},{1,5},{5... | collective-permute-start | bytes 12296 | tf_op jit(solution)/shard_map/ppermute | solution.py:355
  46.4 7.0 %slice-start = ((f32[513]{0:T(1024)}), f32[512]{0:T(512)S(1)}, s32[]{:S(2)}) async-start(f32[513]{0:T(1024)} %param.22), calls=%async_computation.4 | async-start | bytes 4096 | tf_op jit(solution)/shard_map/slice | solution.py:79
  49.1 3.7 %copy-start.22 = (f32[513]{0:T(1024)S(1)}, f32[513]{0:T(1024)}, u32[]{:S(2)}) copy-start(f32[513]{0:T(1024)} %param.22) | copy-start | bytes 6160
  49.2 5.4 %copy-start = (bf16[512,512]{1,0:T(8,128)(2,1)S(1)}, bf16[512,512]{1,0:T(8,128)(2,1)}, u32[]{:S(2)}) copy-start(bf16[512,512]{1,0:T(8,128)(2,1)} %constant.31.clone.refs_5_.refs_11_) | copy-start | bytes 1572868
  49.2 5.4 %copy-start.1 = (bf16[512,512]{1,0:T(8,128)(2,1)S(1)}, bf16[512,512]{1,0:T(8,128)(2,1)}, u32[]{:S(2)}) copy-start(bf16[512,512]{1,0:T(8,128)(2,1)} %constant.32.clone.refs_6_.refs_12_) | copy-start | bytes 1572868
  49.2 5.4 %copy-start.7 = (bf16[256,256]{1,0:T(8,128)(2,1)S(1)}, bf16[256,256]{1,0:T(8,128)(2,1)}, u32[]{:S(2)}) copy-start(bf16[256,256]{1,0:T(8,128)(2,1)} %constant.30.clone.refs_4_.refs_10_) | copy-start | bytes 393220
  49.2 17.8 %all-to-all-start.1 = ((f32[8,144,128]{2,1,0:T(8,128)}), f32[8,144,128]{2,1,0:T(8,128)S(1)}, u32[]{:S(2)}, u32[]{:S(2)}) async-start(f32[8,144,128]{2,1,0:T(8,128)} %get-tuple-element.30), calls=%async_computation.1 | async-start | bytes 1179648 | tf_op jit(solution)/shard_map/all_to_all | solution.py:359
  53.4 1.1 %copy-start.6 = (bf16[256,256]{1,0:T(8,128)(2,1)S(1)}, bf16[256,256]{1,0:T(8,128)(2,1)}, u32[]{:S(2)}) copy-start(bf16[256,256]{1,0:T(8,128)(2,1)} %constant.29.clone.refs_3_.refs_9_) | copy-start | bytes 393220
  53.6 0.9 copy-start.4
  53.6 1.0 copy-start.5
  54.6 3.7 %copy-start.23 = (f32[1024]{0:T(1024)S(1)}, f32[1024]{0:T(1024)}, u32[]{:S(2)}) copy-start(f32[1024]{0:T(1024)} %constant.33.clone) | copy-start | bytes 12292
  54.6 3.7 %copy-start.24 = (f32[1024]{0:T(1024)S(1)}, f32[1024]{0:T(1024)}, u32[]{:S(2)}) copy-start(f32[1024]{0:T(1024)} %constant.34.clone) | copy-start | bytes 12292
  55.8 0.8 copy-start.11
  56.6 11.7 %collective-permute-start.4 = (f32[24,1024]{1,0:T(8,128)}, f32[24,1024]{1,0:T(8,128)S(1)}, u32[]{:S(2)}, u32[]{:S(2)}) collective-permute-start(f32[24,1024]{1,0:T(8,128)} %get-tuple-element.26), channel_id=1, source_target_pairs={{0,1},{1,2},{2,3},{3,0},{4,5},{5,6},{6,7},{7,4},{8,9},{9,10},{10,1... | collective-permute-start | bytes 294920 | tf_op jit(solution)/shard_map/ppermute | solution.py:355
  56.6 12.3 %collective-permute-start.5 = (f32[24,1024]{1,0:T(8,128)}, f32[24,1024]{1,0:T(8,128)}, u32[]{:S(2)}, u32[]{:S(2)}) collective-permute-start(f32[24,1024]{1,0:T(8,128)} %get-tuple-element.27), channel_id=1, source_target_pairs={{0,3},{1,0},{2,1},{3,2},{4,7},{5,4},{6,5},{7,6},{8,11},{9,8},{10,9... | collective-permute-start | bytes 294920 | tf_op jit(solution)/shard_map/ppermute | solution.py:355
  58.3 10.5 %copy-start.12 = (f32[128,1024]{1,0:T(8,128)S(1)}, f32[128,1024]{1,0:T(8,128)}, u32[]{:S(2)}) copy-start(f32[128,1024]{1,0:T(8,128)} %copy-done.11) | copy-start | bytes 1572868
  67.5 0.6 copy-start.20
  68.2 0.6 copy-start.18
  68.2 0.9 copy-start.15
  71.7 3.8 %copy-start.21 = (f32[24,1024]{1,0:T(8,128)S(1)}, f32[24,1024]{1,0:T(8,128)}, u32[]{:S(2)}) copy-start(f32[24,1024]{1,0:T(8,128)} %copy-done.20) | copy-start | bytes 294916
  71.7 3.9 %copy-start.19 = (f32[24,1024]{1,0:T(8,128)S(1)}, f32[24,1024]{1,0:T(8,128)}, u32[]{:S(2)}) copy-start(f32[24,1024]{1,0:T(8,128)} %copy-done.18) | copy-start | bytes 294916
  71.7 17.5 %all-to-all-start.2 = ((f32[8,128,128]{2,1,0:T(8,128)}), f32[8,128,128]{2,1,0:T(8,128)S(1)}, u32[]{:S(2)}, u32[]{:S(2)}) async-start(f32[8,128,128]{2,1,0:T(8,128)} %shard_map.198), calls=%async_computation.2 | async-start | bytes 1048576 | tf_op jit(solution)/shard_map/all_to_all | solution.py:359
  75.5 4.1 %collective-permute-start.10 = (f32[24,1024]{1,0:T(8,128)S(1)}, f32[24,1024]{1,0:T(8,128)S(1)}, u32[]{:S(2)}, u32[]{:S(2)}) collective-permute-start(f32[24,1024]{1,0:T(8,128)S(1)} %copy-done.21), channel_id=1, source_target_pairs={{0,1},{1,2},{2,3},{3,0},{4,5},{5,6},{6,7},{7,4},{8,9},{9,10},{10,1... | collective-permute-start | bytes 294920 | tf_op jit(solution)/shard_map/ppermute | solution.py:355
  75.6 4.0 %collective-permute-start.11 = (f32[24,1024]{1,0:T(8,128)S(1)}, f32[24,1024]{1,0:T(8,128)S(1)}, u32[]{:S(2)}, u32[]{:S(2)}) collective-permute-start(f32[24,1024]{1,0:T(8,128)S(1)} %copy-done.19), channel_id=1, source_target_pairs={{0,3},{1,0},{2,1},{3,2},{4,7},{5,4},{6,5},{7,6},{8,11},{9,8},{10,9... | collective-permute-start | bytes 294920 | tf_op jit(solution)/shard_map/ppermute | solution.py:355

commit v2 on v1

v2 whole, which is shorter than its diff:
```python
import math

import jax
import jax.numpy as jnp
import numpy as np
from jax import lax
from jax.experimental import pallas as pl
from jax.experimental.pallas import tpu as pltpu
from jax.sharding import PartitionSpec as P

BURNERS = 16
MOUTH = 8
SWEEPS = 4
SUBSTEPS = 8

time_step = 0.2
diffusion = 0.05
inflow_rate = 0.5
wave_speed = 0.5
heat_coupling = 0.5
feedback = 0.5

F32 = jnp.float32
BF16 = jnp.bfloat16
HALO = SWEEPS - 1
EDGE = 8
VMEM = pl.BlockSpec(memory_space=pltpu.VMEM)
SMEM = pl.BlockSpec(memory_space=pltpu.SMEM)
HBM = pl.BlockSpec(memory_space=pltpu.HBM)


def halves(table):
    high = table.astype(BF16)
    low = (table - high.astype(np.float64)).astype(BF16)
    return high, low


def axial_tables(cells):
    index = np.arange(1, cells + 1, dtype=np.float64)
    basis = math.sqrt(2.0 / (cells + 1)) * np.sin(
        np.pi * ((index[:, None] * index[None, :]) % (2 * (cells + 1))) / (cells + 1)
    )
    return basis, 2.0 * np.cos(np.pi * index / (cells + 1))


def mode_classes(n_theta):
    half = n_theta // 2
    multiples = np.arange(0, half, 4)
    first = (
        np.concatenate([multiples, [half], multiples[1:]]),
        np.concatenate([np.zeros(len(multiples) + 1), np.ones(len(multiples) - 1)]),
    )
    twos = np.arange(2, half, 4)
    second = (np.concatenate([twos, twos]), np.repeat([0, 1], len(twos)))
    ones, threes = np.arange(1, half, 4), np.arange(3, half, 4)
    third = (np.concatenate([ones, threes, ones, threes]), np.repeat([0, 1], half // 2))
    return first, second, third


def azimuth_tables(n_theta):
    bases = []
    for (order, odd), rows in zip(mode_classes(n_theta), (n_theta // 4, n_theta // 4, n_theta // 2)):
        phase = (np.arange(rows)[:, None] * order[None, :].astype(np.int64)) % n_theta
        angle = phase * (2.0 * np.pi / n_theta)
        bases.append(np.where(odd[None, :] == 0, np.cos(angle), np.sin(angle)))
    return bases


def diagonal_tables(n_theta):
    half = n_theta // 2
    order = np.concatenate([part[0] for part in mode_classes(n_theta)])
    shifted = 2.0 - 2.0 * np.cos(order * (2.0 * np.pi / n_theta))
    weight = np.where((order == 0) | (order == half), 1.0, 2.0) / n_theta
    return (4.0 + shifted).astype(np.float32), weight.astype(np.float32)


def mode_rows(impedance):
    half = impedance.shape[0] - 1
    by_four = impedance[:half].reshape(half // 4, 4).T
    q0, q1, q2, q3 = by_four[0], by_four[1], by_four[2], by_four[3]
    first = jnp.concatenate([impedance[half:], q0[1:]])
    return jnp.concatenate([q0, first, q2, q2, q1, q3, q1, q3])


def split(value):
    high = value.astype(BF16)
    return high, (value - high.astype(F32)).astype(BF16)


def product(left, right, dims):
    def one(a, b):
        return lax.dot_general(a, b, (dims, ((), ())), preferred_element_type=F32)

    return one(left[0], right[0]) + (one(left[1], right[0]) + one(left[0], right[1]))


NN = ((1,), (0,))
NT = ((1,), (1,))


def edges_kernel(
    density, swirl, heat_rate, acoustic, first, last, head, tail, rho, rate, spin, wave, sems
):
    cells_theta, cells_radius, _ = density.shape
    copies = []

    def fetch(source, target):
        copy = pltpu.make_async_copy(source, target, sems.at[len(copies)])
        copy.start()
        copies.append(copy)

    for side, begin, row in ((0, 0, 0), (1, cells_theta - EDGE, cells_theta - 1)):
        fetch(density.at[pl.ds(begin, EDGE)], rho.at[side])
        fetch(heat_rate.at[pl.ds(begin, EDGE)], rate.at[side])
        fetch(swirl.at[pl.ds(row, 1)], spin.at[side])
        fetch(acoustic.at[:, pl.ds(begin, EDGE)], wave.at[side])
    fetch(density.at[:, 0, :], first)
    fetch(density.at[:, cells_radius - 1, :], last)
    for copy in copies:
        copy.wait()
    for side, out, row in ((0, head, 0), (1, tail, EDGE - 1)):
        edge = rho[side, row]
        out[0:cells_radius] = edge
        out[cells_radius : 2 * cells_radius] = edge * spin[side, 0]
        at = 2 * cells_radius
        for k in range(3):
            out[at : at + EDGE] = wave[side, k]
            at += EDGE
        heat = jnp.sum(rate[side] * rho[side] * rho[side], axis=1)
        out[at : at + EDGE] = heat


def flow_kernel(n_theta, mouth_azimuth, mouth_radius, density, swirl, heat_rate, forcing, heat):
    sector = lax.axis_index("sector")
    radial = lax.axis_index("radial")
    cells_theta, cells_radius, cells_axial = density.shape
    shape = (cells_radius, cells_axial)
    rows = lax.broadcasted_iota(jnp.int32, shape, 0)
    lanes = lax.broadcasted_iota(jnp.int32, shape, 1)
    segment = n_theta // BURNERS
    part = min(segment, cells_theta)
    zero = jnp.zeros(shape, F32)

    def at(t):
        if t < 0 or t >= cells_theta:
            return zero, zero
        rho = density[t]
        return rho, rho * swirl[t]

    window = [at(-1), at(0)]
    for t in range(cells_theta):
        window.append(at(t + 1))
        (rho_down, flux_down), (rho, _), (rho_up, flux_up) = window
        window = window[1:]
        if t % part == 0:
            burner = (sector * cells_theta + t) // segment
            start = burner * segment + mouth_azimuth[burner] - sector * cells_theta
            radius = mouth_radius[burner] - radial * cells_radius
            mouth = ((rows >= radius) & (rows < radius + MOUTH)).astype(F32)
            mouth = mouth * (inflow_rate / time_step)
        gain = mouth * ((start <= t) & (t < start + MOUTH)).astype(F32)
        r_up = jnp.where(rows == cells_radius - 1, 0.0, pltpu.roll(rho, cells_radius - 1, 0))
        r_down = jnp.where(rows == 0, 0.0, pltpu.roll(rho, 1, 0))
        z_up = jnp.where(lanes == cells_axial - 1, 0.0, pltpu.roll(rho, cells_axial - 1, 1))
        z_down = jnp.where(lanes == 0, 0.0, pltpu.roll(rho, 1, 1))
        twice = 2.0 * rho
        laplace = (rho_up + rho_down - twice) + (r_up + r_down - twice) + (z_up + z_down - twice)
        forcing[t] = -0.5 * (flux_up - flux_down) + diffusion * laplace + gain * (1.0 - rho)

    total = None
    for r in range(cells_radius):
        rho = density[:, r, :]
        term = heat_rate[:, r, :] * rho * rho
        total = term if total is None else total + term
    heat[...] = total


def own_basis(basis, own, begin, each):
    sectors = lax.axis_size("sector")
    sector = lax.axis_index("sector")
    rows = [
        basis[pl.ds(pl.multiple_of((sector ^ k) * own + begin, 8), each), :]
        for k in range(sectors)
    ]
    return jnp.concatenate(rows, 0)


def sine_modes(basis, fields):
    high, low = split(basis)
    count = high.shape[0]
    left = jnp.concatenate(
        [jnp.concatenate([high, high], 1), jnp.concatenate([low, jnp.zeros_like(low)], 1)], 0
    )
    right = jnp.concatenate([jnp.concatenate(split(field), 1) for field in fields], 0)
    out = lax.dot_general(left, right, (NT, ((), ())), preferred_element_type=F32)
    return out[:count] + out[count:]


def spread(slots, forcing, basis, own, begin, each):
    cells_theta, cells_radius, _ = forcing.shape
    mine = own_basis(basis, own, begin, each)
    for r in range(0, cells_radius, 2):
        modes = sine_modes(mine, [forcing[:, r + i, :] for i in range(2)])
        for i in range(2):
            lane = slice(i * cells_theta, (i + 1) * cells_theta)
            for k, slot in enumerate(slots):
                slot[(r + i) * each : (r + i + 1) * each, :] = modes[
                    k * each : (k + 1) * each, lane
                ]


def first_kernel(
    each, n_radius, partial, heat, acoustic, above, below, inner, outer, basis, forcing, state,
    *slots
):
    radials = lax.axis_size("radial")
    radial = lax.axis_index("radial")
    cells_theta, cells_radius, cells_axial = partial.shape
    shape = (cells_radius, cells_axial)
    sectors = len(slots)
    own = cells_axial // sectors
    columns = cells_radius * each
    forcing[...] = partial[...]
    rho, flux = slice(0, cells_radius), slice(cells_radius, 2 * cells_radius)
    forcing[0] = forcing[0] + (0.5 * below[flux] + diffusion * below[rho])
    forcing[cells_theta - 1] = forcing[cells_theta - 1] + (
        diffusion * above[rho] - 0.5 * above[flux]
    )
    inside = diffusion * (radial > 0).astype(F32)
    outside = diffusion * (radial < radials - 1).astype(F32)
    forcing[:, 0, :] = forcing[:, 0, :] + inside * inner[...]
    forcing[:, cells_radius - 1, :] = forcing[:, cells_radius - 1, :] + outside * outer[...]
    spread(slots, forcing, basis, own, 0, each)

    skip = 2 * cells_radius
    share = (radial == 0).astype(F32)

    def extended(k):
        rows = slice(skip + k * EDGE, skip + (k + 1) * EDGE)
        middle = acoustic[k] if k < 3 else heat[...]
        return jnp.concatenate([below[rows], middle, above[rows]], 0)

    press, along, axial = extended(0) * share, extended(1) * share, extended(2) * share
    warm = extended(3) * (heat_coupling / n_radius)
    count = press.shape[0]
    lanes = lax.broadcasted_iota(jnp.int32, press.shape, 1)
    for _ in range(SUBSTEPS):
        press_up = pltpu.roll(press, count - 1, 0)
        press_axial = jnp.where(lanes == cells_axial - 1, 0.0, pltpu.roll(press, cells_axial - 1, 1))
        along = along - wave_speed * (press_up - press)
        axial = axial - wave_speed * (press_axial - press)
        along_down = pltpu.roll(along, 1, 0)
        axial_down = jnp.where(lanes == 0, 0.0, pltpu.roll(axial, 1, 1))
        press = press - wave_speed * ((along - along_down) + (axial - axial_down)) + warm
    middle = slice(EDGE, EDGE + cells_theta)
    state[0] = press[middle]
    state[1] = along[middle]
    state[2] = axial[middle]
    modes = sine_modes(own_basis(basis, own, 0, own), [feedback * press[middle]])
    for k, slot in enumerate(slots):
        slot[columns : columns + own, :] = modes[k * own : (k + 1) * own]


def next_kernel(chunk, each, forcing, basis, *slots):
    own = forcing.shape[2] // len(slots)
    spread(slots, forcing, basis, own, chunk * each, each)


def forward_kernel(edge, columns, sectors, *refs):
    received, refs = refs[:sectors], refs[sectors:]
    tables, refs = refs[:6], refs[6:]
    outs, pieces = refs[:-1], refs[-1]
    modes, first, last = outs[:3]
    sector = lax.axis_index("sector")
    for k in range(sectors):
        pieces[sector ^ k] = received[k][...]
    quarter, half = sectors // 4, sectors // 2

    def joined(parts):
        return jnp.concatenate(parts, 1) if len(parts) > 1 else parts[0]

    values = [pieces[s] for s in range(sectors)]
    even = [values[s] + values[s + half] for s in range(half)]
    odd = [values[s] - values[s + half] for s in range(half)]
    both = [even[s] + even[s + quarter] for s in range(quarter)]
    apart = [even[s] - even[s + quarter] for s in range(quarter)]
    at = 0
    for i, parts in enumerate((both, apart, odd)):
        wh, wl = tables[2 * i : 2 * i + 2]
        lane = slice(at, at + wh.shape[1])
        out = product(split(joined(parts)), (wh[...], wl[...]), NN)
        modes[:, lane] = out[:columns]
        first[:, lane] = out[:edge]
        last[:, lane] = out[columns - edge : columns]
        if len(outs) > 3:
            outs[3][:, lane] = out[columns:]
        at += wh.shape[1]


def solve_kernel(
    chunk, each, modes, inner, outer, wave, inverse, scaled, axial, w0h, w0l, w1h, w1l, w2h,
    w2l, *refs
):
    slots, solved, pieces = refs[:-2], refs[-2], refs[-1]
    radials = lax.axis_size("radial")
    radial = lax.axis_index("radial")
    sector = lax.axis_index("sector")
    columns, n_theta = modes.shape
    cells_radius = columns // each
    has_inner = (radial > 0).astype(F32)
    has_outer = (radial < radials - 1).astype(F32)
    eigen = axial[sector][chunk * each : (chunk + 1) * each, :]
    step = eigen.shape[1]
    total = cells_radius + 2 * HALO
    for block in range(n_theta // step):
        lane = slice(block * step, (block + 1) * step)
        inv = jnp.broadcast_to(inverse[:, lane], (each, step))
        inv_inner, inv_outer = inv * has_inner, inv * has_outer
        last_scale = jnp.broadcast_to(scaled[:, lane], (each, step))
        add = wave[chunk * each : (chunk + 1) * each, lane]

        def row_of(i):
            if i < HALO:
                return inner[i * each : (i + 1) * each, lane]
            i -= HALO
            if i < cells_radius:
                return modes[i * each : (i + 1) * each, lane]
            i -= cells_radius
            return outer[i * each : (i + 1) * each, lane]

        def scale_of(i):
            if i < HALO:
                return inv_inner
            return inv if i < HALO + cells_radius else inv_outer

        right = [row_of(i) + add for i in range(total)]
        x = [right[i] * scale_of(i) for i in range(total)]
        for sweep in range(1, SWEEPS):
            fresh = [None] * total
            for i in range(sweep, total - sweep):
                scale = last_scale if sweep == SWEEPS - 1 else scale_of(i)
                fresh[i] = (right[i] + (x[i + 1] + x[i - 1]) + eigen * x[i]) * scale
            x = fresh
        for i in range(cells_radius):
            solved[i * each : (i + 1) * each, lane] = x[i + HALO]

    sectors = len(slots)
    width = pieces.shape[2]
    n0, n1 = w0h.shape[1], w1h.shape[1]
    both = product(split(solved[:, :n0]), (w0h[...], w0l[...]), NT)
    apart = product(split(solved[:, n0 : n0 + n1]), (w1h[...], w1l[...]), NT)
    odd = product(split(solved[:, n0 + n1 :]), (w2h[...], w2l[...]), NT)
    even = jnp.concatenate([both + apart, both - apart], 1)
    for s in range(sectors // 2):
        lane = slice(s * width, (s + 1) * width)
        pieces[s] = even[:, lane] + odd[:, lane]
        pieces[s + sectors // 2] = even[:, lane] - odd[:, lane]
    for k, slot in enumerate(slots):
        slot[...] = pieces[sector ^ k]


def pressure_kernel(chunks, *refs):
    received, (basis, pressure) = refs[:-2], refs[-2:]
    sectors = len(received) // chunks
    cells_radius = pressure.shape[1]
    each = received[0].shape[0] // cells_radius
    high, low = split(own_basis(basis, each * chunks, 0, each * chunks))
    right = jnp.concatenate(
        [jnp.concatenate([high, low], 1), jnp.concatenate([high, jnp.zeros_like(low)], 1)], 0
    )
    cells_axial = high.shape[1]
    for r in range(cells_radius):
        rows = [
            received[c * sectors + k][r * each : (r + 1) * each, :]
            for k in range(sectors)
            for c in range(chunks)
        ]
        modes = jnp.concatenate(rows, 0)
        left = jnp.concatenate(split(modes.T), 1)
        out = lax.dot_general(left, right, (NN, ((), ())), preferred_element_type=F32)
        pressure[:, r, :] = out[:, :cells_axial] + out[:, cells_axial:]


def call(kernel, outs, ins, scratch=(), **more):
    moved = sum(math.prod(o.shape) * 4 for o in outs)
    return pl.pallas_call(
        kernel,
        out_shape=outs,
        in_specs=ins,
        out_specs=[VMEM] * len(outs),
        scratch_shapes=list(scratch),
        cost_estimate=pl.CostEstimate(flops=0, bytes_accessed=3 * moved, transcendentals=0),
        compiler_params=pltpu.CompilerParams(vmem_limit_bytes=24 * 1024 * 1024),
        **more,
    )


def shape(*dims):
    return jax.ShapeDtypeStruct(dims, F32)


def shifted(value, axis, steps):
    count = lax.axis_size(axis)
    return lax.ppermute(value, axis, [(i, (i + steps) % count) for i in range(count)])


def swapped(value, axis, bits):
    return lax.ppermute(value, axis, [(i, i ^ bits) for i in range(lax.axis_size(axis))])


def summed(value, axis):
    step = 1
    while step < lax.axis_size(axis):
        value = value + swapped(value, axis, step)
        step *= 2
    return value


def exchanged(slots):
    return [slots[0]] + [swapped(slots[k], "sector", k) for k in range(1, len(slots))]


def shards(density, swirl, heat_rate, acoustic, mode_impedance, mouth_azimuth, mouth_radius):
    sectors = lax.axis_size("sector")
    radials = lax.axis_size("radial")
    cells_theta, cells_radius, cells_axial = density.shape
    n_theta = cells_theta * sectors
    n_radius = cells_radius * radials
    own = cells_axial // sectors
    chunks = max(1, min(2, own // 8))
    each = own // chunks
    columns = cells_radius * each
    edge = HALO * each

    basis, eigen = axial_tables(cells_axial)
    basis = jnp.asarray(basis.astype(np.float32))
    eigen = jnp.asarray(
        np.broadcast_to(eigen.reshape(sectors, own, 1), (sectors, own, 128)).astype(np.float32)
    )
    tables = []
    for table in azimuth_tables(n_theta):
        tables += [jnp.asarray(t) for t in halves(table)]
    fixed, weight = diagonal_tables(n_theta)
    inverse = (1.0 / (jnp.asarray(fixed) + mode_rows(mode_impedance)))[None, :]
    scaled = inverse * jnp.asarray(weight)[None, :]

    packed = 2 * cells_radius + 4 * EDGE
    row_block = shape(cells_theta, cells_axial)
    first, last, head, tail = call(
        edges_kernel,
        [row_block] * 2 + [shape(packed, cells_axial)] * 2,
        [HBM] * 4,
        [
            pltpu.VMEM((2, EDGE, cells_radius, cells_axial), F32),
            pltpu.VMEM((2, EDGE, cells_radius, cells_axial), F32),
            pltpu.VMEM((2, 1, cells_radius, cells_axial), F32),
            pltpu.VMEM((2, 3, EDGE, cells_axial), F32),
            pltpu.SemaphoreType.DMA((10,)),
        ],
    )(density, swirl, heat_rate, acoustic)
    above = shifted(head, "sector", -1)
    below = shifted(tail, "sector", 1)
    outer = shifted(first, "radial", -1)
    inner = shifted(last, "radial", 1)

    partial, heat = call(
        lambda *refs: flow_kernel(n_theta, *refs),
        [shape(*density.shape), row_block],
        [SMEM] * 2 + [VMEM] * 3,
    )(mouth_azimuth, mouth_radius, density, swirl, heat_rate)

    forcing, state, *slots = call(
        lambda *refs: first_kernel(each, n_radius, *refs),
        [shape(*density.shape), shape(*acoustic.shape)]
        + [shape(columns + own, cells_theta)] * sectors,
        [VMEM] * 8,
    )(partial, heat, acoustic, above, below, inner, outer, basis)
    received = [exchanged(slots)]
    for c in range(1, chunks):
        slots = call(
            lambda *refs: next_kernel(c, each, *refs),
            [shape(columns, cells_theta)] * sectors,
            [VMEM] * 2,
        )(forcing, basis)
        received.append(exchanged(slots))
    density_next = density + time_step * forcing

    modes, wave = [], None
    for c in range(chunks):
        count = received[c][0].shape[0]
        outs = [shape(columns, n_theta), shape(edge, n_theta), shape(edge, n_theta)]
        if c == 0:
            outs.append(shape(own, n_theta))
        c_modes, c_first, c_last, *waves = call(
            lambda *refs: forward_kernel(edge, columns, sectors, *refs),
            outs,
            [VMEM] * (sectors + 6),
            [pltpu.VMEM((sectors, count, cells_theta), F32)],
        )(*received[c], *tables)
        if c == 0:
            wave = summed(waves[0], "radial")
        modes.append((c_modes, shifted(c_last, "radial", 1), shifted(c_first, "radial", -1)))

    results = []
    for c in range(chunks):
        slots = call(
            lambda *refs: solve_kernel(c, each, *refs),
            [shape(columns, cells_theta)] * sectors,
            [VMEM] * 13,
            [pltpu.VMEM((columns, n_theta), F32), pltpu.VMEM((sectors, columns, cells_theta), F32)],
        )(*modes[c], wave, inverse, scaled, eigen, *tables)
        results += exchanged(slots)
    acoustic_next = summed(state, "radial")

    (pressure,) = call(
        lambda *refs: pressure_kernel(chunks, *refs),
        [shape(*density.shape)],
        [VMEM] * (chunks * sectors + 1),
    )(*results, basis)
    return density_next, pressure, acoustic_next


def solution(mesh):
    return jax.shard_map(
        shards,
        mesh=mesh,
        in_specs=(
            P("sector", "radial", None),
            P("sector", "radial", None),
            P("sector", "radial", None),
            P(None, "sector", None),
            P(),
            P(),
            P(),
        ),
        out_specs=(
            P("sector", "radial", None),
            P("sector", "radial", None),
            P(None, "sector", None),
        ),
        check_vma=False,
    )
```

time: 109 us -> 116 us (1.064)
  starting transfers between devices: 28.6 us -> 55.6 us
  waiting for transfers between devices: 36.6 us -> 12.2 us
  blocking collectives: 17.2 us -> 0 us
  local copies, waits for them, and re-layouts: 8.63 us -> 23.2 us
  other arithmetic: 0.02 us -> 3.38 us
  Pallas kernels: 16.5 us -> 19.6 us
    ppermute x2 -> x32, starting transfers between devices: 1.63 us -> 44.3 us  [swapped(): lax.ppermute(value, axis, [(i, i ^ bits) for i in range(lax.axis_size(axi...]
    all_to_all x3 -> x0, waiting for transfers between devices: 17.4 us -> none  [exchanged(): lax.all_to_all(value, 'sector', split_axis=0, concat_axis=0, tiled=True)]
    all_to_all x1 -> x0, blocking collectives: 17.2 us -> none  [exchanged(): lax.all_to_all(value, 'sector', split_axis=0, concat_axis=0, tiled=True)]
    ppermute x10 -> x8, waiting for transfers between devices: 15.2 us -> 2.76 us  [shifted(): lax.ppermute(value, axis, [(i, (i + steps) % count) for i in range(count)])]
    unnamed x50 -> x90, local copies, waits for them, and re-layouts: 7.03 us -> 19.2 us
    all_to_all x3 -> x0, starting transfers between devices: 11 us -> none  [exchanged(): lax.all_to_all(value, 'sector', split_axis=0, concat_axis=0, tiled=True)]
    ppermute x2 -> x32, waiting for transfers between devices: 4.02 us -> 9.44 us  [swapped(): lax.ppermute(value, axis, [(i, i ^ bits) for i in range(lax.axis_size(axi...]
    ppermute x10 -> x8, starting transfers between devices: 16 us -> 11.4 us  [shifted(): lax.ppermute(value, axis, [(i, (i + steps) % count) for i in range(count)])]
  transfers between devices with their start and end apart: 15 -> 40, of which waited for: 9 -> 8; matrix products, arithmetic and copies ran while one was open for 1% -> 6% of each run, Pallas kernels for 5% -> 12%
where the time goes in v2:
time: 116 us; the launch traced here: 115 us
  starting transfers between devices  55.6 us (48%)
  local copies, waits for them, and re-layouts  23.2 us (20%)
  Pallas kernels  19.6 us (17%)
  waiting for transfers between devices  12.2 us (11%)
  other arithmetic  3.38 us (3%)
    ppermute x32, starting transfers between devices, swapped(): lax.ppermute(value, axis, [(i, i ^ bits) for i in range(lax.axis_size(axi...  44.3 us
    unnamed x90, local copies, waits for them, and re-layouts  19.2 us
    ppermute x8, starting transfers between devices, shifted(): lax.ppermute(value, axis, [(i, (i + steps) % count) for i in range(count)])  11.4 us
    ppermute x32, waiting for transfers between devices, swapped(): lax.ppermute(value, axis, [(i, i ^ bits) for i in range(lax.axis_size(axi...  9.44 us
    pallas_call x1, Pallas kernels, shards(): call(lambda *refs: first_kernel(each, n_radius, *refs), [shape(*density.s...  4.71 us
    pallas_call x1, Pallas kernels, shards(): call(lambda *refs: flow_kernel(n_theta, *refs), [shape(*density.shape), r...  3.83 us
    pallas_call x1, Pallas kernels, shards(): call(lambda *refs: next_kernel(c, each, *refs), [shape(columns, cells_the...  3.5 us
    pallas_call x2, Pallas kernels, shards(): call(lambda *refs: forward_kernel(edge, columns, sectors, *refs), outs, [...  3.11 us
  transfers between devices with their start and end apart: 40, of which 8 were waited for; matrix products, arithmetic and copies ran while one was open for 6% of the time, Pallas kernels for 12%

profile of v2, /device:TPU:0, one launch (start us, length us, event | category | flops | bytes accessed | tf_op | source)
XLA Modules:
  0.0 115.0 jit_solution(11490754035482842485)
XLA Ops:
  0.6 1.2 %copy-done = f32[128,16,128]{2,1,0:T(8,128)S(1)} copy-done((f32[128,16,128]{2,1,0:T(8,128)S(1)}, f32[128,16,128]{2,1,0:T(8,128)}, u32[]{:S(2)}) %copy-start) | copy-done | bytes 1048600
  1.9 1.2 %copy-done.4 = f32[128,16,128]{2,1,0:T(8,128)S(1)} copy-done((f32[128,16,128]{2,1,0:T(8,128)S(1)}, f32[128,16,128]{2,1,0:T(8,128)}, u32[]{:S(2)}) %copy-start.4) | copy-done | bytes 1048600
  3.1 1.2 %copy-done.5 = f32[128,16,128]{2,1,0:T(8,128)S(1)} copy-done((f32[128,16,128]{2,1,0:T(8,128)S(1)}, f32[128,16,128]{2,1,0:T(8,128)}, u32[]{:S(2)}) %copy-start.5) | copy-done | bytes 1048600
  4.3 0.9 copy-done.11
  6.4 2.0 %collective-permute-start.3 = (f32[128,128]{1,0:T(8,128)S(1)}, f32[128,128]{1,0:T(8,128)S(1)}, u32[]{:S(2)}, u32[]{:S(2)}) collective-permute-start(f32[128,128]{1,0:T(8,128)S(1)} %get-tuple-element.55), channel_id=1, source_target_pairs={{0,3},{1,0},{2,1},{3,2},{4,7},{5,4},{6,5},{7,6},{8,11},{9,8},{10,9... | collective-permute-start | bytes 196616 | tf_op jit(solution)/shard_map/ppermute | solution.py:404
  8.3 5.3 %collective-permute-start = (f32[64,128]{1,0:T(8,128)S(1)}, f32[64,128]{1,0:T(8,128)S(1)}, u32[]{:S(2)}, u32[]{:S(2)}) collective-permute-start(f32[64,128]{1,0:T(8,128)S(1)} %get-tuple-element.52), channel_id=1, source_target_pairs={{0,28},{4,0},{8,4},{12,8},{16,12},{20,16},{24,20},{28,24},{1,29},{... | collective-permute-start | bytes 98312 | tf_op jit(solution)/shard_map/ppermute | solution.py:404
  13.7 3.8 %shard_map.184 = (f32[128,16,128]{2,1,0:T(8,128)S(1)}, f32[128,128]{1,0:T(8,128)S(1)}) custom-call(s32[16]{0:T(128)S(1)} %copy-done.35, s32[16]{0:T(128)S(1)} %copy-done.36, f32[128,16,128]{2,1,0:T(8,128)S(1)} %copy-done.1, f32[128,16,128]{2,1,0:T(8,128)S(1)} %copy-done.4, f32[128,16,128]{2,1,0:T(8,128)S(1)} %copy-done.5), custom_call_target="tpu_custom_call" | custom-call | bytes 3342336 | tf_op jit(solution)/shard_map/pallas_call | solution.py:466
  17.5 2.7 %collective-permute-done.1.refs_4_ = f32[64,128]{1,0:T(8,128)S(1)} collective-permute-done((f32[64,128]{1,0:T(8,128)S(1)}, f32[64,128]{1,0:T(8,128)S(1)}, u32[]{:S(2)}, u32[]{:S(2)}) %collective-permute-start.1) | collective-permute-done | bytes 32800 | tf_op jit(solution)/shard_map/ppermute | solution.py:404
  20.3 4.7 %shard_map.186 = (f32[128,16,128]{2,1,0:T(8,128)S(1)}, f32[3,128,128]{2,1,0:T(8,128)S(1)}, f32[144,128]{1,0:T(8,128)S(1)}, f32[144,128]{1,0:T(8,128)S(1)}, f32[1...) custom-call(f32[128,16,128]{2,1,0:T(8,128)S(1)} %get-tuple-element.5, ...), custom_call_target="tpu_custom_call" | custom-call | bytes 5505024 | tf_op jit(solution)/shard_map/pallas_call | solution.py:472
  26.4 2.0 %collective-permute-start.10 = (f32[144,128]{1,0:T(8,128)S(1)}, f32[144,128]{1,0:T(8,128)S(1)}, u32[]{:S(2)}, u32[]{:S(2)}) collective-permute-start(f32[144,128]{1,0:T(8,128)S(1)} %get-tuple-element.64), channel_id=1, source_target_pairs={{0,28},{4,24},{8,20},{12,16},{16,12},{20,8},{24,4},{28,0},{1,29},{... | collective-permute-start | bytes 221192 | tf_op jit(solution)/shard_map/ppermute | solution.py:408
  28.4 3.5 %collective-permute-start.6 = (f32[144,128]{1,0:T(8,128)}, f32[144,128]{1,0:T(8,128)}, u32[]{:S(2)}, u32[]{:S(2)}) collective-permute-start(f32[144,128]{1,0:T(8,128)} %get-tuple-element.60), channel_id=1, source_target_pairs={{0,12},{4,8},{8,4},{12,0},{16,28},{20,24},{24,20},{28,16},{1,13},{... | collective-permute-start | bytes 221192 | tf_op jit(solution)/shard_map/ppermute | solution.py:408
  32.2 1.7 %collective-permute-done.10.refs_7_ = f32[144,128]{1,0:T(8,128)S(1)} collective-permute-done((f32[144,128]{1,0:T(8,128)S(1)}, f32[144,128]{1,0:T(8,128)S(1)}, u32[]{:S(2)}, u32[]{:S(2)}) %collective-permute-start.10) | collective-permute-done | bytes 73760 | tf_op jit(solution)/shard_map/ppermute | solution.py:408
  35.5 3.3 %collective-permute-start.9 = (f32[144,128]{1,0:T(8,128)}, f32[144,128]{1,0:T(8,128)}, u32[]{:S(2)}, u32[]{:S(2)}) collective-permute-start(f32[144,128]{1,0:T(8,128)} %get-tuple-element.63), channel_id=1, source_target_pairs={{0,24},{4,28},{8,16},{12,20},{16,8},{20,12},{24,0},{28,4},{1,25},{... | collective-permute-start | bytes 221192 | tf_op jit(solution)/shard_map/ppermute | solution.py:408
  40.0 0.8 copy-done.14
  40.9 3.5 %shard_map.189 = (f32[128,128]{1,0:T(8,128)S(1)}, f32[128,128]{1,0:T(8,128)S(1)}, f32[128,128]{1,0:T(8,128)S(1)}, f32[128,128]{1,0:T(8,128)S(1)}, f32[128,128]{1...) custom-call(f32[128,16,128]{2,1,0:T(8,128)S(1)} %get-tuple-element.56.refs_0_, ...), custom_call_target="tpu_custom_call" | custom-call | bytes 1572864 | tf_op jit(solution)/shard_map/pallas_call | solution.py:480
  45.0 1.3 %collective-permute-start.23 = (f32[128,128]{1,0:T(8,128)S(1)}, f32[128,128]{1,0:T(8,128)S(1)}, u32[]{:S(2)}, u32[]{:S(2)}) collective-permute-start(f32[128,128]{1,0:T(8,128)S(1)} %get-tuple-element.79), channel_id=1, source_target_pairs={{0,8},{4,12},{8,0},{12,4},{16,24},{20,28},{24,16},{28,20},{1,9},{5... | collective-permute-start | bytes 196616 | tf_op jit(solution)/shard_map/ppermute | solution.py:408
  46.3 2.2 %collective-permute-start.24 = (f32[128,128]{1,0:T(8,128)S(1)}, f32[128,128]{1,0:T(8,128)S(1)}, u32[]{:S(2)}, u32[]{:S(2)}) collective-permute-start(f32[128,128]{1,0:T(8,128)S(1)} %get-tuple-element.80), channel_id=1, source_target_pairs={{0,12},{4,8},{8,4},{12,0},{16,28},{20,24},{24,20},{28,16},{1,13},{... | collective-permute-start | bytes 196616 | tf_op jit(solution)/shard_map/ppermute | solution.py:408
  48.5 0.9 copy-done.9
  49.4 0.9 copy-done.22
  50.3 0.9 copy-done.24
  51.2 0.9 copy-done.26
  52.1 1.6 %shard_map.187 = (f32[128,1024]{1,0:T(8,128)S(1)}, f32[24,1024]{1,0:T(8,128)S(1)}, f32[24,1024]{1,0:T(8,128)S(1)}, f32[16,1024]{1,0:T(8,128)S(1)}) custom-call(f32[144,128]{1,0:T(8,128)S(1)} %copy-done.22, f32[144,128]{1,0:T(8,128)S(1)} %copy-done.26, f32[144,128]{1,0:T(8,128)} %collective-permute-done.5.refs_2_, f32[144,128]{1,0:T(8,128)} %collective-permute-done.6.refs_3_, ...), custom_call_target="tpu_custom_call" | custom-call | bytes 2359296 | tf_op jit(solution)/shard_map/pallas_call | solution.py:494
  55.8 1.9 %collective-permute-start.26 = (f32[128,128]{1,0:T(8,128)}, f32[128,128]{1,0:T(8,128)}, u32[]{:S(2)}, u32[]{:S(2)}) collective-permute-start(f32[128,128]{1,0:T(8,128)} %get-tuple-element.82), channel_id=1, source_target_pairs={{0,20},{4,16},{8,28},{12,24},{16,4},{20,0},{24,12},{28,8},{1,21},{... | collective-permute-start | bytes 196616 | tf_op jit(solution)/shard_map/ppermute | solution.py:408
  59.0 2.5 %collective-permute-start.27 = (f32[128,128]{1,0:T(8,128)}, f32[128,128]{1,0:T(8,128)}, u32[]{:S(2)}, u32[]{:S(2)}) collective-permute-start(f32[128,128]{1,0:T(8,128)} %get-tuple-element.83), channel_id=1, source_target_pairs={{0,24},{4,28},{8,16},{12,20},{16,8},{20,12},{24,0},{28,4},{1,25},{... | collective-permute-start | bytes 196616 | tf_op jit(solution)/shard_map/ppermute | solution.py:408
  62.1 2.7 %collective-permute-start.28 = (f32[128,128]{1,0:T(8,128)}, f32[128,128]{1,0:T(8,128)}, u32[]{:S(2)}, u32[]{:S(2)}) collective-permute-start(f32[128,128]{1,0:T(8,128)} %get-tuple-element.84), channel_id=1, source_target_pairs={{0,28},{4,24},{8,20},{12,16},{16,12},{20,8},{24,4},{28,0},{1,29},{... | collective-permute-start | bytes 196616 | tf_op jit(solution)/shard_map/ppermute | solution.py:408
  65.5 1.5 %collective-permute-start.14 = (f32[16,1024]{1,0:T(8,128)}, f32[16,1024]{1,0:T(8,128)}, u32[]{:S(2)}, u32[]{:S(2)}) collective-permute-start(f32[16,1024]{1,0:T(8,128)} %add.19), channel_id=1, source_target_pairs={{0,2},{1,3},{2,0},{3,1},{4,6},{5,7},{6,4},{7,5},{8,10},{9,11},{10,... | collective-permute-start | bytes 196616 | tf_op jit(solution)/shard_map/ppermute | solution.py:408
  67.7 1.3 %concatenate.3 = f32[1024]{0:T(1024)S(1)} concatenate(f32[128]{0:T(128)} %get-tuple-element.100, f32[1]{0:T(128)} %slice.27, f32[127]{0:T(128)} %slice_reduce_fusion.3, f32[128]{0:T(128)S(1)} %get-tuple-element.99, f32[128]{0:T(128)S(1)} %get-tuple-element.99, f32[128]{0:T(128)S(1)} %get-tuple-element.98, f32[128]{0:T(128)S(1)} %get-tuple-element.97, f32[128]{0:T(128)S(1)} %get-tuple-element.98, ...), dimensions={0} | concatenate | bytes 8192 | tf_op jit(solution)/shard_map/concatenate | solution.py:82
  69.5 0.9 copy-done.10
  73.8 1.5 %shard_map.190 = (f32[128,1024]{1,0:T(8,128)S(1)}, f32[24,1024]{1,0:T(8,128)S(1)}, f32[24,1024]{1,0:T(8,128)S(1)}) custom-call(f32[128,128]{1,0:T(8,128)S(1)} %copy-done.28, f32[128,128]{1,0:T(8,128)S(1)} %copy-done.30, f32[128,128]{1,0:T(8,128)S(1)} %copy-done.32, f32[128,128]{1,0:T(8,128)S(1)} %copy-done.34, f32[128,128]{1,0:T(8,128)} %collective-permute-done.25.refs_4_, ...), custom_call_target="tpu_custom_call" | custom-call | bytes 2162688 | tf_op jit(solution)/shard_map/pallas_call | solution.py:494
  75.3 1.7 %collective-permute-start.30 = (f32[24,1024]{1,0:T(8,128)S(1)}, f32[24,1024]{1,0:T(8,128)S(1)}, u32[]{:S(2)}, u32[]{:S(2)}) collective-permute-start(f32[24,1024]{1,0:T(8,128)S(1)} %get-tuple-element.87), channel_id=1, source_target_pairs={{0,3},{1,0},{2,1},{3,2},{4,7},{5,4},{6,5},{7,6},{8,11},{9,8},{10,9... | collective-permute-start | bytes 294920 | tf_op jit(solution)/shard_map/ppermute | solution.py:404
  77.1 1.7 %collective-permute-start.12 = (f32[24,1024]{1,0:T(8,128)S(1)}, f32[24,1024]{1,0:T(8,128)S(1)}, u32[]{:S(2)}, u32[]{:S(2)}) collective-permute-start(f32[24,1024]{1,0:T(8,128)S(1)} %copy-done.38), channel_id=1, source_target_pairs={{0,3},{1,0},{2,1},{3,2},{4,7},{5,4},{6,5},{7,6},{8,11},{9,8},{10,9... | collective-permute-start | bytes 294920 | tf_op jit(solution)/shard_map/ppermute | solution.py:404
  78.8 0.9 add.20.refs_3_
  79.8 1.0 shard_map.191
  80.9 2.8 %collective-permute-start.32 = (f32[128,128]{1,0:T(8,128)S(1)}, f32[128,128]{1,0:T(8,128)S(1)}, u32[]{:S(2)}, u32[]{:S(2)}) collective-permute-start(f32[128,128]{1,0:T(8,128)S(1)} %get-tuple-element.90), channel_id=1, source_target_pairs={{0,8},{4,12},{8,0},{12,4},{16,24},{20,28},{24,16},{28,20},{1,9},{5... | collective-permute-start | bytes 196616 | tf_op jit(solution)/shard_map/ppermute | solution.py:408
  84.4 2.0 %collective-permute-start.34 = (f32[128,128]{1,0:T(8,128)S(1)}, f32[128,128]{1,0:T(8,128)S(1)}, u32[]{:S(2)}, u32[]{:S(2)}) collective-permute-start(f32[128,128]{1,0:T(8,128)S(1)} %get-tuple-element.92), channel_id=1, source_target_pairs={{0,16},{4,20},{8,24},{12,28},{16,0},{20,4},{24,8},{28,12},{1,17},{... | collective-permute-start | bytes 196616 | tf_op jit(solution)/shard_map/ppermute | solution.py:408
  86.5 1.1 collective-permute-start.35
  87.6 1.0 shard_map.188
  88.6 2.5 %collective-permute-start.36 = (f32[128,128]{1,0:T(8,128)S(1)}, f32[128,128]{1,0:T(8,128)S(1)}, u32[]{:S(2)}, u32[]{:S(2)}) collective-permute-start(f32[128,128]{1,0:T(8,128)S(1)} %get-tuple-element.94), channel_id=1, source_target_pairs={{0,24},{4,28},{8,16},{12,20},{16,8},{20,12},{24,0},{28,4},{1,25},{... | collective-permute-start | bytes 196616 | tf_op jit(solution)/shard_map/ppermute | solution.py:408
  91.1 2.1 %collective-permute-start.37 = (f32[128,128]{1,0:T(8,128)S(1)}, f32[128,128]{1,0:T(8,128)S(1)}, u32[]{:S(2)}, u32[]{:S(2)}) collective-permute-start(f32[128,128]{1,0:T(8,128)S(1)} %get-tuple-element.95), channel_id=1, source_target_pairs={{0,28},{4,24},{8,20},{12,16},{16,12},{20,8},{24,4},{28,0},{1,29},{... | collective-permute-start | bytes 196616 | tf_op jit(solution)/shard_map/ppermute | solution.py:408
  94.2 2.2 %collective-permute-done.35.refs_13_ = f32[128,128]{1,0:T(8,128)S(1)} collective-permute-done((f32[128,128]{1,0:T(8,128)S(1)}, f32[128,128]{1,0:T(8,128)S(1)}, u32[]{:S(2)}, u32[]{:S(2)}) %collective-permute-start.35) | collective-permute-done | bytes 65568 | tf_op jit(solution)/shard_map/ppermute | solution.py:408
  96.7 1.9 %collective-permute-start.39 = (f32[3,128,128]{2,1,0:T(8,128)S(1)}, f32[3,128,128]{2,1,0:T(8,128)S(1)}, u32[]{:S(2)}, u32[]{:S(2)}) collective-permute-start(f32[3,128,128]{2,1,0:T(8,128)S(1)} %add.22), channel_id=1, source_target_pairs={{0,2},{1,3},{2,0},{3,1},{4,6},{5,7},{6,4},{7,5},{8,10},{9,11},{10,... | collective-permute-start | bytes 589832 | tf_op jit(solution)/shard_map/ppermute | solution.py:408
  98.8 3.3 %collective-permute-start.18 = (f32[128,128]{1,0:T(8,128)S(1)}, f32[128,128]{1,0:T(8,128)S(1)}, u32[]{:S(2)}, u32[]{:S(2)}) collective-permute-start(f32[128,128]{1,0:T(8,128)S(1)} %get-tuple-element.73), channel_id=1, source_target_pairs={{0,16},{4,20},{8,24},{12,28},{16,0},{20,4},{24,8},{28,12},{1,17},{... | collective-permute-start | bytes 196616 | tf_op jit(solution)/shard_map/ppermute | solution.py:408
  102.4 1.8 %collective-permute-start.20 = (f32[128,128]{1,0:T(8,128)S(1)}, f32[128,128]{1,0:T(8,128)S(1)}, u32[]{:S(2)}, u32[]{:S(2)}) collective-permute-start(f32[128,128]{1,0:T(8,128)S(1)} %get-tuple-element.75), channel_id=1, source_target_pairs={{0,24},{4,28},{8,16},{12,20},{16,8},{20,12},{24,0},{28,4},{1,25},{... | collective-permute-start | bytes 196616 | tf_op jit(solution)/shard_map/ppermute | solution.py:408
  104.3 2.5 %collective-permute-start.21 = (f32[128,128]{1,0:T(8,128)S(1)}, f32[128,128]{1,0:T(8,128)S(1)}, u32[]{:S(2)}, u32[]{:S(2)}) collective-permute-start(f32[128,128]{1,0:T(8,128)S(1)} %get-tuple-element.76), channel_id=1, source_target_pairs={{0,28},{4,24},{8,20},{12,16},{16,12},{20,8},{24,4},{28,0},{1,29},{... | collective-permute-start | bytes 196616 | tf_op jit(solution)/shard_map/ppermute | solution.py:408
  106.8 1.1 multiply_add_fusion
  107.9 2.0 %collective-permute-done.18.refs_4_ = f32[128,128]{1,0:T(8,128)S(1)} collective-permute-done((f32[128,128]{1,0:T(8,128)S(1)}, f32[128,128]{1,0:T(8,128)S(1)}, u32[]{:S(2)}, u32[]{:S(2)}) %collective-permute-start.18) | collective-permute-done | bytes 65568 | tf_op jit(solution)/shard_map/ppermute | solution.py:408
  109.9 2.4 %collective-permute-done.19.refs_5_ = f32[128,128]{1,0:T(8,128)S(1)} collective-permute-done((f32[128,128]{1,0:T(8,128)S(1)}, f32[128,128]{1,0:T(8,128)S(1)}, u32[]{:S(2)}, u32[]{:S(2)}) %collective-permute-start.19) | collective-permute-done | bytes 65568 | tf_op jit(solution)/shard_map/ppermute | solution.py:408
  112.4 1.9 %shard_map.192 = f32[128,16,128]{2,1,0:T(8,128)} custom-call(f32[128,128]{1,0:T(8,128)S(1)} %get-tuple-element.69.refs_0_, f32[128,128]{1,0:T(8,128)S(1)} %collective-permute-done.15.refs_1_, f32[128,128]{1,0:T(8,128)S(1)} %collective-permute-done.16.refs_2_, f32[128,128]{1,0:T(8,128)S(1)} %collective-permute-done.17.refs_3_, ...), custom_call_target="tpu_custom_call" | custom-call | bytes 3145728 | tf_op jit(solution)/shard_map/pallas_call | solution.py:515
  (144 shorter events, 19.0 us)
Async XLA Ops:
  5.2 8.4 %copy-start.1 = (f32[128,16,128]{2,1,0:T(8,128)S(1)}, f32[128,16,128]{2,1,0:T(8,128)}, u32[]{:S(2)}) copy-start(f32[128,16,128]{2,1,0:T(8,128)} %density.1) | copy-start | bytes 3145732
  5.8 14.5 %collective-permute-start.2 = (f32[128,128]{1,0:T(8,128)S(1)}, f32[128,128]{1,0:T(8,128)S(1)}, u32[]{:S(2)}, u32[]{:S(2)}) collective-permute-start(f32[128,128]{1,0:T(8,128)S(1)} %get-tuple-element.54), channel_id=1, source_target_pairs={{0,1},{1,2},{2,3},{3,0},{4,5},{5,6},{6,7},{7,4},{8,9},{9,10},{10,1... | collective-permute-start | bytes 196616 | tf_op jit(solution)/shard_map/ppermute | solution.py:404
  6.4 13.9 %collective-permute-start.3 = (f32[128,128]{1,0:T(8,128)S(1)}, f32[128,128]{1,0:T(8,128)S(1)}, u32[]{:S(2)}, u32[]{:S(2)}) collective-permute-start(f32[128,128]{1,0:T(8,128)S(1)} %get-tuple-element.55), channel_id=1, source_target_pairs={{0,3},{1,0},{2,1},{3,2},{4,7},{5,4},{6,5},{7,6},{8,11},{9,8},{10,9... | collective-permute-start | bytes 196616 | tf_op jit(solution)/shard_map/ppermute | solution.py:404
  8.3 9.2 %collective-permute-start = (f32[64,128]{1,0:T(8,128)S(1)}, f32[64,128]{1,0:T(8,128)S(1)}, u32[]{:S(2)}, u32[]{:S(2)}) collective-permute-start(f32[64,128]{1,0:T(8,128)S(1)} %get-tuple-element.52), channel_id=1, source_target_pairs={{0,28},{4,0},{8,4},{12,8},{16,12},{20,16},{24,20},{28,24},{1,29},{... | collective-permute-start | bytes 98312 | tf_op jit(solution)/shard_map/ppermute | solution.py:404
  13.7 6.6 %collective-permute-start.1 = (f32[64,128]{1,0:T(8,128)S(1)}, f32[64,128]{1,0:T(8,128)S(1)}, u32[]{:S(2)}, u32[]{:S(2)}) collective-permute-start(f32[64,128]{1,0:T(8,128)S(1)} %get-tuple-element.53), channel_id=1, source_target_pairs={{0,4},{4,8},{8,12},{12,16},{16,20},{20,24},{24,28},{28,0},{1,5},{5... | collective-permute-start | bytes 98312 | tf_op jit(solution)/shard_map/ppermute | solution.py:404
  20.3 28.2 %copy-start.6 = (bf16[256,256]{1,0:T(8,128)(2,1)S(1)}, bf16[256,256]{1,0:T(8,128)(2,1)}, u32[]{:S(2)}) copy-start(bf16[256,256]{1,0:T(8,128)(2,1)} %constant.26.clone.refs_8_.refs_7_) | copy-start | bytes 393220
  20.3 28.2 %copy-start.7 = (bf16[256,256]{1,0:T(8,128)(2,1)S(1)}, bf16[256,256]{1,0:T(8,128)(2,1)}, u32[]{:S(2)}) copy-start(bf16[256,256]{1,0:T(8,128)(2,1)} %constant.27.clone.refs_9_.refs_8_) | copy-start | bytes 393220
  20.3 28.2 %copy-start.8 = (bf16[256,256]{1,0:T(8,128)(2,1)S(1)}, bf16[256,256]{1,0:T(8,128)(2,1)}, u32[]{:S(2)}) copy-start(bf16[256,256]{1,0:T(8,128)(2,1)} %constant.28.clone.refs_10_.refs_9_) | copy-start | bytes 393220
  26.4 7.5 %collective-permute-start.10 = (f32[144,128]{1,0:T(8,128)S(1)}, f32[144,128]{1,0:T(8,128)S(1)}, u32[]{:S(2)}, u32[]{:S(2)}) collective-permute-start(f32[144,128]{1,0:T(8,128)S(1)} %get-tuple-element.64), channel_id=1, source_target_pairs={{0,28},{4,24},{8,20},{12,16},{16,12},{20,8},{24,4},{28,0},{1,29},{... | collective-permute-start | bytes 221192 | tf_op jit(solution)/shard_map/ppermute | solution.py:408
  28.4 6.5 %collective-permute-start.4 = (f32[144,128]{1,0:T(8,128)S(1)}, f32[144,128]{1,0:T(8,128)S(1)}, u32[]{:S(2)}, u32[]{:S(2)}) collective-permute-start(f32[144,128]{1,0:T(8,128)S(1)} %get-tuple-element.58), channel_id=1, source_target_pairs={{0,4},{4,0},{8,12},{12,8},{16,20},{20,16},{24,28},{28,24},{1,5},{5... | collective-permute-start | bytes 221192 | tf_op jit(solution)/shard_map/ppermute | solution.py:408
  28.4 16.6 %collective-permute-start.5 = (f32[144,128]{1,0:T(8,128)}, f32[144,128]{1,0:T(8,128)}, u32[]{:S(2)}, u32[]{:S(2)}) collective-permute-start(f32[144,128]{1,0:T(8,128)} %get-tuple-element.59), channel_id=1, source_target_pairs={{0,8},{4,12},{8,0},{12,4},{16,24},{20,28},{24,16},{28,20},{1,9},{5... | collective-permute-start | bytes 221192 | tf_op jit(solution)/shard_map/ppermute | solution.py:408
  28.4 16.6 %collective-permute-start.6 = (f32[144,128]{1,0:T(8,128)}, f32[144,128]{1,0:T(8,128)}, u32[]{:S(2)}, u32[]{:S(2)}) collective-permute-start(f32[144,128]{1,0:T(8,128)} %get-tuple-element.60), channel_id=1, source_target_pairs={{0,12},{4,8},{8,4},{12,0},{16,28},{20,24},{24,20},{28,16},{1,13},{... | collective-permute-start | bytes 221192 | tf_op jit(solution)/shard_map/ppermute | solution.py:408
  31.8 14.5 %collective-permute-start.7 = (f32[144,128]{1,0:T(8,128)}, f32[144,128]{1,0:T(8,128)}, u32[]{:S(2)}, u32[]{:S(2)}) collective-permute-start(f32[144,128]{1,0:T(8,128)} %get-tuple-element.61), channel_id=1, source_target_pairs={{0,16},{4,20},{8,24},{12,28},{16,0},{20,4},{24,8},{28,12},{1,17},{... | collective-permute-start | bytes 221192 | tf_op jit(solution)/shard_map/ppermute | solution.py:408
  34.5 14.0 %collective-permute-start.8 = (f32[144,128]{1,0:T(8,128)}, f32[144,128]{1,0:T(8,128)}, u32[]{:S(2)}, u32[]{:S(2)}) collective-permute-start(f32[144,128]{1,0:T(8,128)} %get-tuple-element.62), channel_id=1, source_target_pairs={{0,20},{4,16},{8,28},{12,24},{16,4},{20,0},{24,12},{28,8},{1,21},{... | collective-permute-start | bytes 221192 | tf_op jit(solution)/shard_map/ppermute | solution.py:408
  35.5 13.0 %collective-permute-start.9 = (f32[144,128]{1,0:T(8,128)}, f32[144,128]{1,0:T(8,128)}, u32[]{:S(2)}, u32[]{:S(2)}) collective-permute-start(f32[144,128]{1,0:T(8,128)} %get-tuple-element.63), channel_id=1, source_target_pairs={{0,24},{4,28},{8,16},{12,20},{16,8},{20,12},{24,0},{28,4},{1,25},{... | collective-permute-start | bytes 221192 | tf_op jit(solution)/shard_map/ppermute | solution.py:408
  40.9 7.7 %copy-start.3 = (bf16[512,512]{1,0:T(8,128)(2,1)S(1)}, bf16[512,512]{1,0:T(8,128)(2,1)}, u32[]{:S(2)}) copy-start(bf16[512,512]{1,0:T(8,128)(2,1)} %constant.31.clone.refs_13_.refs_12_) | copy-start | bytes 1572868
  45.0 13.4 %collective-permute-start.22 = (f32[128,128]{1,0:T(8,128)S(1)}, f32[128,128]{1,0:T(8,128)S(1)}, u32[]{:S(2)}, u32[]{:S(2)}) collective-permute-start(f32[128,128]{1,0:T(8,128)S(1)} %get-tuple-element.78), channel_id=1, source_target_pairs={{0,4},{4,0},{8,12},{12,8},{16,20},{20,16},{24,28},{28,24},{1,5},{5... | collective-permute-start | bytes 196616 | tf_op jit(solution)/shard_map/ppermute | solution.py:408
  45.0 16.5 %collective-permute-start.23 = (f32[128,128]{1,0:T(8,128)S(1)}, f32[128,128]{1,0:T(8,128)S(1)}, u32[]{:S(2)}, u32[]{:S(2)}) collective-permute-start(f32[128,128]{1,0:T(8,128)S(1)} %get-tuple-element.79), channel_id=1, source_target_pairs={{0,8},{4,12},{8,0},{12,4},{16,24},{20,28},{24,16},{28,20},{1,9},{5... | collective-permute-start | bytes 196616 | tf_op jit(solution)/shard_map/ppermute | solution.py:408
  46.3 18.5 %collective-permute-start.24 = (f32[128,128]{1,0:T(8,128)S(1)}, f32[128,128]{1,0:T(8,128)S(1)}, u32[]{:S(2)}, u32[]{:S(2)}) collective-permute-start(f32[128,128]{1,0:T(8,128)S(1)} %get-tuple-element.80), channel_id=1, source_target_pairs={{0,12},{4,8},{8,4},{12,0},{16,28},{20,24},{24,20},{28,16},{1,13},{... | collective-permute-start | bytes 196616 | tf_op jit(solution)/shard_map/ppermute | solution.py:408
  54.5 1.3 %collective-permute-start.13 = (f32[16,1024]{1,0:T(8,128)S(1)}, f32[16,1024]{1,0:T(8,128)S(1)}, u32[]{:S(2)}, u32[]{:S(2)}) collective-permute-start(f32[16,1024]{1,0:T(8,128)S(1)} %get-tuple-element.68), channel_id=1, source_target_pairs={{0,1},{1,0},{2,3},{3,2},{4,5},{5,4},{6,7},{7,6},{8,9},{9,8},{10,11... | collective-permute-start | bytes 196616 | tf_op jit(solution)/shard_map/ppermute | solution.py:408
  55.3 13.7 %collective-permute-start.25 = (f32[128,128]{1,0:T(8,128)}, f32[128,128]{1,0:T(8,128)}, u32[]{:S(2)}, u32[]{:S(2)}) collective-permute-start(f32[128,128]{1,0:T(8,128)} %get-tuple-element.81), channel_id=1, source_target_pairs={{0,16},{4,20},{8,24},{12,28},{16,0},{20,4},{24,8},{28,12},{1,17},{... | collective-permute-start | bytes 196616 | tf_op jit(solution)/shard_map/ppermute | solution.py:408
  55.8 13.2 %collective-permute-start.26 = (f32[128,128]{1,0:T(8,128)}, f32[128,128]{1,0:T(8,128)}, u32[]{:S(2)}, u32[]{:S(2)}) collective-permute-start(f32[128,128]{1,0:T(8,128)} %get-tuple-element.82), channel_id=1, source_target_pairs={{0,20},{4,16},{8,28},{12,24},{16,4},{20,0},{24,12},{28,8},{1,21},{... | collective-permute-start | bytes 196616 | tf_op jit(solution)/shard_map/ppermute | solution.py:408
  59.0 10.0 %collective-permute-start.27 = (f32[128,128]{1,0:T(8,128)}, f32[128,128]{1,0:T(8,128)}, u32[]{:S(2)}, u32[]{:S(2)}) collective-permute-start(f32[128,128]{1,0:T(8,128)} %get-tuple-element.83), channel_id=1, source_target_pairs={{0,24},{4,28},{8,16},{12,20},{16,8},{20,12},{24,0},{28,4},{1,25},{... | collective-permute-start | bytes 196616 | tf_op jit(solution)/shard_map/ppermute | solution.py:408
  62.1 7.4 %collective-permute-start.28 = (f32[128,128]{1,0:T(8,128)}, f32[128,128]{1,0:T(8,128)}, u32[]{:S(2)}, u32[]{:S(2)}) collective-permute-start(f32[128,128]{1,0:T(8,128)} %get-tuple-element.84), channel_id=1, source_target_pairs={{0,28},{4,24},{8,20},{12,16},{16,12},{20,8},{24,4},{28,0},{1,29},{... | collective-permute-start | bytes 196616 | tf_op jit(solution)/shard_map/ppermute | solution.py:408
  65.5 11.6 %collective-permute-start.14 = (f32[16,1024]{1,0:T(8,128)}, f32[16,1024]{1,0:T(8,128)}, u32[]{:S(2)}, u32[]{:S(2)}) collective-permute-start(f32[16,1024]{1,0:T(8,128)} %add.19), channel_id=1, source_target_pairs={{0,2},{1,3},{2,0},{3,1},{4,6},{5,7},{6,4},{7,5},{8,10},{9,11},{10,... | collective-permute-start | bytes 196616 | tf_op jit(solution)/shard_map/ppermute | solution.py:408
  69.0 17.5 %collective-permute-start.38 = (f32[3,128,128]{2,1,0:T(8,128)}, f32[3,128,128]{2,1,0:T(8,128)S(1)}, u32[]{:S(2)}, u32[]{:S(2)}) collective-permute-start(f32[3,128,128]{2,1,0:T(8,128)} %copy-done.19), channel_id=1, source_target_pairs={{0,1},{1,0},{2,3},{3,2},{4,5},{5,4},{6,7},{7,6},{8,9},{9,8},{10,11... | collective-permute-start | bytes 589832 | tf_op jit(solution)/shard_map/ppermute | solution.py:408
  75.3 4.5 %collective-permute-start.29 = (f32[24,1024]{1,0:T(8,128)S(1)}, f32[24,1024]{1,0:T(8,128)S(1)}, u32[]{:S(2)}, u32[]{:S(2)}) collective-permute-start(f32[24,1024]{1,0:T(8,128)S(1)} %get-tuple-element.86), channel_id=1, source_target_pairs={{0,1},{1,2},{2,3},{3,0},{4,5},{5,6},{6,7},{7,4},{8,9},{9,10},{10,1... | collective-permute-start | bytes 294920 | tf_op jit(solution)/shard_map/ppermute | solution.py:404
  75.3 4.5 %collective-permute-start.30 = (f32[24,1024]{1,0:T(8,128)S(1)}, f32[24,1024]{1,0:T(8,128)S(1)}, u32[]{:S(2)}, u32[]{:S(2)}) collective-permute-start(f32[24,1024]{1,0:T(8,128)S(1)} %get-tuple-element.87), channel_id=1, source_target_pairs={{0,3},{1,0},{2,1},{3,2},{4,7},{5,4},{6,5},{7,6},{8,11},{9,8},{10,9... | collective-permute-start | bytes 294920 | tf_op jit(solution)/shard_map/ppermute | solution.py:404
  77.1 6.7 %collective-permute-start.11 = (f32[24,1024]{1,0:T(8,128)S(1)}, f32[24,1024]{1,0:T(8,128)S(1)}, u32[]{:S(2)}, u32[]{:S(2)}) collective-permute-start(f32[24,1024]{1,0:T(8,128)S(1)} %copy-done.40), channel_id=1, source_target_pairs={{0,1},{1,2},{2,3},{3,0},{4,5},{5,6},{6,7},{7,4},{8,9},{9,10},{10,1... | collective-permute-start | bytes 294920 | tf_op jit(solution)/shard_map/ppermute | solution.py:404
  77.1 7.4 %collective-permute-start.12 = (f32[24,1024]{1,0:T(8,128)S(1)}, f32[24,1024]{1,0:T(8,128)S(1)}, u32[]{:S(2)}, u32[]{:S(2)}) collective-permute-start(f32[24,1024]{1,0:T(8,128)S(1)} %copy-done.38), channel_id=1, source_target_pairs={{0,3},{1,0},{2,1},{3,2},{4,7},{5,4},{6,5},{7,6},{8,11},{9,8},{10,9... | collective-permute-start | bytes 294920 | tf_op jit(solution)/shard_map/ppermute | solution.py:404
  79.8 7.8 %copy-start.17 = (f32[128,1024]{1,0:T(8,128)S(1)}, f32[128,1024]{1,0:T(8,128)}, u32[]{:S(2)}) copy-start(f32[128,1024]{1,0:T(8,128)} %copy-done.16) | copy-start | bytes 1572868
  80.8 7.8 %collective-permute-start.31 = (f32[128,128]{1,0:T(8,128)S(1)}, f32[128,128]{1,0:T(8,128)S(1)}, u32[]{:S(2)}, u32[]{:S(2)}) collective-permute-start(f32[128,128]{1,0:T(8,128)S(1)} %get-tuple-element.89), channel_id=1, source_target_pairs={{0,4},{4,0},{8,12},{12,8},{16,20},{20,16},{24,28},{28,24},{1,5},{5... | collective-permute-start | bytes 196616 | tf_op jit(solution)/shard_map/ppermute | solution.py:408
  80.9 10.2 %collective-permute-start.32 = (f32[128,128]{1,0:T(8,128)S(1)}, f32[128,128]{1,0:T(8,128)S(1)}, u32[]{:S(2)}, u32[]{:S(2)}) collective-permute-start(f32[128,128]{1,0:T(8,128)S(1)} %get-tuple-element.90), channel_id=1, source_target_pairs={{0,8},{4,12},{8,0},{12,4},{16,24},{20,28},{24,16},{28,20},{1,9},{5... | collective-permute-start | bytes 196616 | tf_op jit(solution)/shard_map/ppermute | solution.py:408
  83.7 9.4 %collective-permute-start.33 = (f32[128,128]{1,0:T(8,128)S(1)}, f32[128,128]{1,0:T(8,128)S(1)}, u32[]{:S(2)}, u32[]{:S(2)}) collective-permute-start(f32[128,128]{1,0:T(8,128)S(1)} %get-tuple-element.91), channel_id=1, source_target_pairs={{0,12},{4,8},{8,4},{12,0},{16,28},{20,24},{24,20},{28,16},{1,13},{... | collective-permute-start | bytes 196616 | tf_op jit(solution)/shard_map/ppermute | solution.py:408
  84.4 9.5 %collective-permute-start.34 = (f32[128,128]{1,0:T(8,128)S(1)}, f32[128,128]{1,0:T(8,128)S(1)}, u32[]{:S(2)}, u32[]{:S(2)}) collective-permute-start(f32[128,128]{1,0:T(8,128)S(1)} %get-tuple-element.92), channel_id=1, source_target_pairs={{0,16},{4,20},{8,24},{12,28},{16,0},{20,4},{24,8},{28,12},{1,17},{... | collective-permute-start | bytes 196616 | tf_op jit(solution)/shard_map/ppermute | solution.py:408
  86.5 9.9 %collective-permute-start.35 = (f32[128,128]{1,0:T(8,128)S(1)}, f32[128,128]{1,0:T(8,128)S(1)}, u32[]{:S(2)}, u32[]{:S(2)}) collective-permute-start(f32[128,128]{1,0:T(8,128)S(1)} %get-tuple-element.93), channel_id=1, source_target_pairs={{0,20},{4,16},{8,28},{12,24},{16,4},{20,0},{24,12},{28,8},{1,21},{... | collective-permute-start | bytes 196616 | tf_op jit(solution)/shard_map/ppermute | solution.py:408
  87.6 9.1 %copy-start.20 = (f32[3,128,128]{2,1,0:T(8,128)S(1)}, f32[3,128,128]{2,1,0:T(8,128)}, u32[]{:S(2)}) copy-start(f32[3,128,128]{2,1,0:T(8,128)} %copy-done.19) | copy-start | bytes 589828
  88.6 8.1 %collective-permute-start.36 = (f32[128,128]{1,0:T(8,128)S(1)}, f32[128,128]{1,0:T(8,128)S(1)}, u32[]{:S(2)}, u32[]{:S(2)}) collective-permute-start(f32[128,128]{1,0:T(8,128)S(1)} %get-tuple-element.94), channel_id=1, source_target_pairs={{0,24},{4,28},{8,16},{12,20},{16,8},{20,12},{24,0},{28,4},{1,25},{... | collective-permute-start | bytes 196616 | tf_op jit(solution)/shard_map/ppermute | solution.py:408
  91.1 7.7 %collective-permute-start.37 = (f32[128,128]{1,0:T(8,128)S(1)}, f32[128,128]{1,0:T(8,128)S(1)}, u32[]{:S(2)}, u32[]{:S(2)}) collective-permute-start(f32[128,128]{1,0:T(8,128)S(1)} %get-tuple-element.95), channel_id=1, source_target_pairs={{0,28},{4,24},{8,20},{12,16},{16,12},{20,8},{24,4},{28,0},{1,29},{... | collective-permute-start | bytes 196616 | tf_op jit(solution)/shard_map/ppermute | solution.py:408
  93.2 8.9 %collective-permute-start.15 = (f32[128,128]{1,0:T(8,128)S(1)}, f32[128,128]{1,0:T(8,128)S(1)}, u32[]{:S(2)}, u32[]{:S(2)}) collective-permute-start(f32[128,128]{1,0:T(8,128)S(1)} %get-tuple-element.70), channel_id=1, source_target_pairs={{0,4},{4,0},{8,12},{12,8},{16,20},{20,16},{24,28},{28,24},{1,5},{5... | collective-permute-start | bytes 196616 | tf_op jit(solution)/shard_map/ppermute | solution.py:408
  94.0 8.5 %collective-permute-start.16 = (f32[128,128]{1,0:T(8,128)S(1)}, f32[128,128]{1,0:T(8,128)S(1)}, u32[]{:S(2)}, u32[]{:S(2)}) collective-permute-start(f32[128,128]{1,0:T(8,128)S(1)} %get-tuple-element.71), channel_id=1, source_target_pairs={{0,8},{4,12},{8,0},{12,4},{16,24},{20,28},{24,16},{28,20},{1,9},{5... | collective-permute-start | bytes 196616 | tf_op jit(solution)/shard_map/ppermute | solution.py:408
  96.4 7.9 %collective-permute-start.17 = (f32[128,128]{1,0:T(8,128)S(1)}, f32[128,128]{1,0:T(8,128)S(1)}, u32[]{:S(2)}, u32[]{:S(2)}) collective-permute-start(f32[128,128]{1,0:T(8,128)S(1)} %get-tuple-element.72), channel_id=1, source_target_pairs={{0,12},{4,8},{8,4},{12,0},{16,28},{20,24},{24,20},{28,16},{1,13},{... | collective-permute-start | bytes 196616 | tf_op jit(solution)/shard_map/ppermute | solution.py:408
  96.7 17.6 %collective-permute-start.39 = (f32[3,128,128]{2,1,0:T(8,128)S(1)}, f32[3,128,128]{2,1,0:T(8,128)S(1)}, u32[]{:S(2)}, u32[]{:S(2)}) collective-permute-start(f32[3,128,128]{2,1,0:T(8,128)S(1)} %add.22), channel_id=1, source_target_pairs={{0,2},{1,3},{2,0},{3,1},{4,6},{5,7},{6,4},{7,5},{8,10},{9,11},{10,... | collective-permute-start | bytes 589832 | tf_op jit(solution)/shard_map/ppermute | solution.py:408
  98.8 11.1 %collective-permute-start.18 = (f32[128,128]{1,0:T(8,128)S(1)}, f32[128,128]{1,0:T(8,128)S(1)}, u32[]{:S(2)}, u32[]{:S(2)}) collective-permute-start(f32[128,128]{1,0:T(8,128)S(1)} %get-tuple-element.73), channel_id=1, source_target_pairs={{0,16},{4,20},{8,24},{12,28},{16,0},{20,4},{24,8},{28,12},{1,17},{... | collective-permute-start | bytes 196616 | tf_op jit(solution)/shard_map/ppermute | solution.py:408
  102.1 10.3 %collective-permute-start.19 = (f32[128,128]{1,0:T(8,128)S(1)}, f32[128,128]{1,0:T(8,128)S(1)}, u32[]{:S(2)}, u32[]{:S(2)}) collective-permute-start(f32[128,128]{1,0:T(8,128)S(1)} %get-tuple-element.74), channel_id=1, source_target_pairs={{0,20},{4,16},{8,28},{12,24},{16,4},{20,0},{24,12},{28,8},{1,21},{... | collective-permute-start | bytes 196616 | tf_op jit(solution)/shard_map/ppermute | solution.py:408
  102.4 9.9 %collective-permute-start.20 = (f32[128,128]{1,0:T(8,128)S(1)}, f32[128,128]{1,0:T(8,128)S(1)}, u32[]{:S(2)}, u32[]{:S(2)}) collective-permute-start(f32[128,128]{1,0:T(8,128)S(1)} %get-tuple-element.75), channel_id=1, source_target_pairs={{0,24},{4,28},{8,16},{12,20},{16,8},{20,12},{24,0},{28,4},{1,25},{... | collective-permute-start | bytes 196616 | tf_op jit(solution)/shard_map/ppermute | solution.py:408
  104.3 8.1 %copy-start.15 = (f32[128,128]{1,0:T(8,128)S(1)}, f32[128,128]{1,0:T(8,128)}, u32[]{:S(2)}) copy-start(f32[128,128]{1,0:T(8,128)} %constant.24.clone.refs_7_.refs_1_.refs_16_) | copy-start | bytes 196612
  104.3 8.1 %collective-permute-start.21 = (f32[128,128]{1,0:T(8,128)S(1)}, f32[128,128]{1,0:T(8,128)S(1)}, u32[]{:S(2)}, u32[]{:S(2)}) collective-permute-start(f32[128,128]{1,0:T(8,128)S(1)} %get-tuple-element.76), channel_id=1, source_target_pairs={{0,28},{4,24},{8,20},{12,16},{16,12},{20,8},{24,4},{28,0},{1,29},{... | collective-permute-start | bytes 196616 | tf_op jit(solution)/shard_map/ppermute | solution.py:408
  (38 other events, 81.6 us)

commit v3 on v2

--- a/solution.py
+++ b/solution.py
@@ -99,9 +99,12 @@
 
 
 def edges_kernel(
-    density, swirl, heat_rate, acoustic, first, last, head, tail, rho, rate, spin, wave, sems
+    density, swirl, heat_rate, acoustic, radial_pair, radial_link, sector_pair, sector_link, rho,
+    rate, spin, wave, rim, sems
 ):
     cells_theta, cells_radius, _ = density.shape
+    radial_odd = lax.axis_index("radial") % 2
+    sector_odd = lax.axis_index("sector") % 2
     copies = []
 
     def fetch(source, target):
@@ -114,12 +117,14 @@
         fetch(heat_rate.at[pl.ds(begin, EDGE)], rate.at[side])
         fetch(swirl.at[pl.ds(row, 1)], spin.at[side])
         fetch(acoustic.at[:, pl.ds(begin, EDGE)], wave.at[side])
-    fetch(density.at[:, 0, :], first)
-    fetch(density.at[:, cells_radius - 1, :], last)
+    fetch(density.at[:, 0, :], rim.at[0])
+    fetch(density.at[:, cells_radius - 1, :], rim.at[1])
     for copy in copies:
         copy.wait()
-    for side, out, row in ((0, head, 0), (1, tail, EDGE - 1)):
-        edge = rho[side, row]
+    radial_pair[...] = rim[1 - radial_odd]
+    radial_link[...] = rim[radial_odd]
+    for out, side in ((sector_pair, 1 - sector_odd), (sector_link, sector_odd)):
+        edge = jnp.where(side == 0, rho[0, 0], rho[1, EDGE - 1])
         out[0:cells_radius] = edge
         out[cells_radius : 2 * cells_radius] = edge * spin[side, 0]
         at = 2 * cells_radius
@@ -130,7 +135,13 @@
         out[at : at + EDGE] = heat
 
 
-def flow_kernel(n_theta, mouth_azimuth, mouth_radius, density, swirl, heat_rate, forcing, heat):
+PIECES = 4
+
+
+def flow_kernel(
+    n_theta, mouth_azimuth, mouth_radius, density_in, swirl_in, heat_rate_in, forcing, heat,
+    density, swirl, heat_rate, sems
+):
     sector = lax.axis_index("sector")
     radial = lax.axis_index("radial")
     cells_theta, cells_radius, cells_axial = density.shape
@@ -140,10 +151,24 @@
     segment = n_theta // BURNERS
     part = min(segment, cells_theta)
     zero = jnp.zeros(shape, F32)
+    piece = cells_theta // PIECES
+    copies = {}
+    for i in range(PIECES):
+        rows_here = pl.ds(i * piece, piece)
+        for k, (source, target) in enumerate(
+            ((density_in, density), (swirl_in, swirl), (heat_rate_in, heat_rate))
+        ):
+            copies[k, i] = pltpu.make_async_copy(
+                source.at[rows_here], target.at[rows_here], sems.at[k, i]
+            )
+            copies[k, i].start()
 
     def at(t):
         if t < 0 or t >= cells_theta:
             return zero, zero
+        if t % piece == 0:
+            copies[0, t // piece].wait()
+            copies[1, t // piece].wait()
         rho = density[t]
         return rho, rho * swirl[t]
 
@@ -167,6 +192,8 @@
         laplace = (rho_up + rho_down - twice) + (r_up + r_down - twice) + (z_up + z_down - twice)
         forcing[t] = -0.5 * (flux_up - flux_down) + diffusion * laplace + gain * (1.0 - rho)
 
+    for i in range(PIECES):
+        copies[2, i].wait()
     total = None
     for r in range(cells_radius):
         rho = density[:, r, :]
@@ -175,16 +202,6 @@
     heat[...] = total
 
 
-def own_basis(basis, own, begin, each):
-    sectors = lax.axis_size("sector")
-    sector = lax.axis_index("sector")
-    rows = [
-        basis[pl.ds(pl.multiple_of((sector ^ k) * own + begin, 8), each), :]
-        for k in range(sectors)
-    ]
-    return jnp.concatenate(rows, 0)
-
-
 def sine_modes(basis, fields):
     high, low = split(basis)
     count = high.shape[0]
@@ -196,30 +213,38 @@
     return out[:count] + out[count:]
 
 
-def spread(slots, forcing, basis, own, begin, each):
+def spread(send, forcing, basis, own, begin, each):
     cells_theta, cells_radius, _ = forcing.shape
-    mine = own_basis(basis, own, begin, each)
+    sectors = send.shape[0]
+    mine = [basis[d * own + begin : d * own + begin + each, :] for d in range(sectors)]
+    mine = jnp.concatenate(mine, 0)
     for r in range(0, cells_radius, 2):
         modes = sine_modes(mine, [forcing[:, r + i, :] for i in range(2)])
         for i in range(2):
             lane = slice(i * cells_theta, (i + 1) * cells_theta)
-            for k, slot in enumerate(slots):
-                slot[(r + i) * each : (r + i + 1) * each, :] = modes[
-                    k * each : (k + 1) * each, lane
+            for d in range(sectors):
+                send[d, (r + i) * each : (r + i + 1) * each, :] = modes[
+                    d * each : (d + 1) * each, lane
                 ]
 
 
 def first_kernel(
-    each, n_radius, partial, heat, acoustic, above, below, inner, outer, basis, forcing, state,
-    *slots
+    each, n_radius, partial, heat, acoustic, radial_pair, radial_link, sector_pair, sector_link,
+    basis, forcing, state, send
 ):
     radials = lax.axis_size("radial")
     radial = lax.axis_index("radial")
     cells_theta, cells_radius, cells_axial = partial.shape
     shape = (cells_radius, cells_axial)
-    sectors = len(slots)
+    sectors = send.shape[0]
     own = cells_axial // sectors
     columns = cells_radius * each
+    sector_odd = lax.axis_index("sector") % 2 == 1
+    radial_odd = radial % 2 == 1
+    above = jnp.where(sector_odd, sector_link[...], sector_pair[...])
+    below = jnp.where(sector_odd, sector_pair[...], sector_link[...])
+    outer = jnp.where(radial_odd, radial_link[...], radial_pair[...])
+    inner = jnp.where(radial_odd, radial_pair[...], radial_link[...])
     forcing[...] = partial[...]
     rho, flux = slice(0, cells_radius), slice(cells_radius, 2 * cells_radius)
     forcing[0] = forcing[0] + (0.5 * below[flux] + diffusion * below[rho])
@@ -228,9 +253,9 @@
     )
     inside = diffusion * (radial > 0).astype(F32)
     outside = diffusion * (radial < radials - 1).astype(F32)
-    forcing[:, 0, :] = forcing[:, 0, :] + inside * inner[...]
-    forcing[:, cells_radius - 1, :] = forcing[:, cells_radius - 1, :] + outside * outer[...]
-    spread(slots, forcing, basis, own, 0, each)
+    forcing[:, 0, :] = forcing[:, 0, :] + inside * inner
+    forcing[:, cells_radius - 1, :] = forcing[:, cells_radius - 1, :] + outside * outer
+    spread(send, forcing, basis, own, 0, each)
 
     skip = 2 * cells_radius
     share = (radial == 0).astype(F32)
@@ -256,30 +281,27 @@
     state[0] = press[middle]
     state[1] = along[middle]
     state[2] = axial[middle]
-    modes = sine_modes(own_basis(basis, own, 0, own), [feedback * press[middle]])
-    for k, slot in enumerate(slots):
-        slot[columns : columns + own, :] = modes[k * own : (k + 1) * own]
-
-
-def next_kernel(chunk, each, forcing, basis, *slots):
-    own = forcing.shape[2] // len(slots)
-    spread(slots, forcing, basis, own, chunk * each, each)
-
-
-def forward_kernel(edge, columns, sectors, *refs):
-    received, refs = refs[:sectors], refs[sectors:]
-    tables, refs = refs[:6], refs[6:]
-    outs, pieces = refs[:-1], refs[-1]
-    modes, first, last = outs[:3]
-    sector = lax.axis_index("sector")
-    for k in range(sectors):
-        pieces[sector ^ k] = received[k][...]
+    modes = sine_modes(basis[...], [feedback * press[middle]])
+    for d in range(sectors):
+        send[d, columns : columns + own, :] = modes[d * own : (d + 1) * own]
+
+
+def next_kernel(chunk, each, forcing, basis, send):
+    own = forcing.shape[2] // send.shape[0]
+    spread(send, forcing, basis, own, chunk * each, each)
+
+
+def forward_kernel(edge, columns, received, *refs):
+    tables, outs = refs[:6], refs[6:]
+    modes, pair, link = outs[:3]
+    sectors = received.shape[0]
+    radial_odd = lax.axis_index("radial") % 2 == 1
     quarter, half = sectors // 4, sectors // 2
 
     def joined(parts):
         return jnp.concatenate(parts, 1) if len(parts) > 1 else parts[0]
 
-    values = [pieces[s] for s in range(sectors)]
+    values = [received[s] for s in range(sectors)]
     even = [values[s] + values[s + half] for s in range(half)]
     odd = [values[s] - values[s + half] for s in range(half)]
     both = [even[s] + even[s + quarter] for s in range(quarter)]
@@ -290,18 +312,18 @@
         lane = slice(at, at + wh.shape[1])
         out = product(split(joined(parts)), (wh[...], wl[...]), NN)
         modes[:, lane] = out[:columns]
-        first[:, lane] = out[:edge]
-        last[:, lane] = out[columns - edge : columns]
+        first, last = out[:edge], out[columns - edge : columns]
+        pair[:, lane] = jnp.where(radial_odd, first, last)
+        link[:, lane] = jnp.where(radial_odd, last, first)
         if len(outs) > 3:
             outs[3][:, lane] = out[columns:]
         at += wh.shape[1]
 
 
 def solve_kernel(
-    chunk, each, modes, inner, outer, wave, inverse, scaled, axial, w0h, w0l, w1h, w1l, w2h,
-    w2l, *refs
+    chunk, each, modes, pair, link, wave, inverse, scaled, axial, w0h, w0l, w1h, w1l, w2h, w2l,
+    send, solved
 ):
-    slots, solved, pieces = refs[:-2], refs[-2], refs[-1]
     radials = lax.axis_size("radial")
     radial = lax.axis_index("radial")
     sector = lax.axis_index("sector")
@@ -309,6 +331,7 @@
     cells_radius = columns // each
     has_inner = (radial > 0).astype(F32)
     has_outer = (radial < radials - 1).astype(F32)
+    radial_odd = radial % 2 == 1
     eigen = axial[sector][chunk * each : (chunk + 1) * each, :]
     step = eigen.shape[1]
     total = cells_radius + 2 * HALO
@@ -320,13 +343,13 @@
         add = wave[chunk * each : (chunk + 1) * each, lane]
 
         def row_of(i):
-            if i < HALO:
-                return inner[i * each : (i + 1) * each, lane]
             i -= HALO
-            if i < cells_radius:
+            if 0 <= i < cells_radius:
                 return modes[i * each : (i + 1) * each, lane]
-            i -= cells_radius
-            return outer[i * each : (i + 1) * each, lane]
+            odd_one, even_one = (pair, link) if i < 0 else (link, pair)
+            i = i + HALO if i < 0 else i - cells_radius
+            rows = slice(i * each, (i + 1) * each)
+            return jnp.where(radial_odd, odd_one[rows, lane], even_one[rows, lane])
 
         def scale_of(i):
             if i < HALO:
@@ -344,8 +367,7 @@
         for i in range(cells_radius):
             solved[i * each : (i + 1) * each, lane] = x[i + HALO]
 
-    sectors = len(slots)
-    width = pieces.shape[2]
+    sectors, _, width = send.shape
     n0, n1 = w0h.shape[1], w1h.shape[1]
     both = product(split(solved[:, :n0]), (w0h[...], w0l[...]), NT)
     apart = product(split(solved[:, n0 : n0 + n1]), (w1h[...], w1l[...]), NT)
@@ -353,26 +375,24 @@
     even = jnp.concatenate([both + apart, both - apart], 1)
     for s in range(sectors // 2):
         lane = slice(s * width, (s + 1) * width)
-        pieces[s] = even[:, lane] + odd[:, lane]
-        pieces[s + sectors // 2] = even[:, lane] - odd[:, lane]
-    for k, slot in enumerate(slots):
-        slot[...] = pieces[sector ^ k]
+        send[s] = even[:, lane] + odd[:, lane]
+        send[s + sectors // 2] = even[:, lane] - odd[:, lane]
 
 
 def pressure_kernel(chunks, *refs):
     received, (basis, pressure) = refs[:-2], refs[-2:]
-    sectors = len(received) // chunks
+    sectors = received[0].shape[0]
     cells_radius = pressure.shape[1]
-    each = received[0].shape[0] // cells_radius
-    high, low = split(own_basis(basis, each * chunks, 0, each * chunks))
+    each = received[0].shape[1] // cells_radius
+    high, low = split(basis[...])
     right = jnp.concatenate(
         [jnp.concatenate([high, low], 1), jnp.concatenate([high, jnp.zeros_like(low)], 1)], 0
     )
     cells_axial = high.shape[1]
     for r in range(cells_radius):
         rows = [
-            received[c * sectors + k][r * each : (r + 1) * each, :]
-            for k in range(sectors)
+            received[c][d, r * each : (r + 1) * each, :]
+            for d in range(sectors)
             for c in range(chunks)
         ]
         modes = jnp.concatenate(rows, 0)
@@ -381,7 +401,7 @@
         pressure[:, r, :] = out[:, :cells_axial] + out[:, cells_axial:]
 
 
-def call(kernel, outs, ins, scratch=(), **more):
+def call(kernel, outs, ins, scratch=(), limit=24 * 1024 * 1024, **more):
     moved = sum(math.prod(o.shape) * 4 for o in outs)
     return pl.pallas_call(
         kernel,
@@ -390,7 +410,7 @@
         out_specs=[VMEM] * len(outs),
         scratch_shapes=list(scratch),
         cost_estimate=pl.CostEstimate(flops=0, bytes_accessed=3 * moved, transcendentals=0),
-        compiler_params=pltpu.CompilerParams(vmem_limit_bytes=24 * 1024 * 1024),
+        compiler_params=pltpu.CompilerParams(vmem_limit_bytes=limit),
         **more,
     )
 
@@ -399,9 +419,12 @@
     return jax.ShapeDtypeStruct(dims, F32)
 
 
-def shifted(value, axis, steps):
+def paired(pair, link, axis, closed):
     count = lax.axis_size(axis)
-    return lax.ppermute(value, axis, [(i, (i + steps) % count) for i in range(count)])
+    first = [(i, i ^ 1) for i in range(count)]
+    second = [(i, (i + 1) % count) for i in range(1, count if closed else count - 1, 2)]
+    second += [(j, i) for i, j in second]
+    return lax.ppermute(pair, axis, first), lax.ppermute(link, axis, second)
 
 
 def swapped(value, axis, bits):
@@ -416,8 +439,8 @@
     return value
 
 
-def exchanged(slots):
-    return [slots[0]] + [swapped(slots[k], "sector", k) for k in range(1, len(slots))]
+def exchanged(value):
+    return lax.all_to_all(value, "sector", split_axis=0, concat_axis=0, tiled=True)
 
 
 def shards(density, swirl, heat_rate, acoustic, mode_impedance, mouth_azimuth, mouth_radius):
@@ -446,7 +469,7 @@
 
     packed = 2 * cells_radius + 4 * EDGE
     row_block = shape(cells_theta, cells_axial)
-    first, last, head, tail = call(
+    edges = call(
         edges_kernel,
         [row_block] * 2 + [shape(packed, cells_axial)] * 2,
         [HBM] * 4,
@@ -455,67 +478,64 @@
             pltpu.VMEM((2, EDGE, cells_radius, cells_axial), F32),
             pltpu.VMEM((2, 1, cells_radius, cells_axial), F32),
             pltpu.VMEM((2, 3, EDGE, cells_axial), F32),
+            pltpu.VMEM((2, cells_theta, cells_axial), F32),
             pltpu.SemaphoreType.DMA((10,)),
         ],
+        limit=None,
     )(density, swirl, heat_rate, acoustic)
-    above = shifted(head, "sector", -1)
-    below = shifted(tail, "sector", 1)
-    outer = shifted(first, "radial", -1)
-    inner = shifted(last, "radial", 1)
+    sector_halo = paired(edges[2], edges[3], "sector", True)
+    radial_halo = paired(edges[0], edges[1], "radial", False)
 
     partial, heat = call(
         lambda *refs: flow_kernel(n_theta, *refs),
         [shape(*density.shape), row_block],
-        [SMEM] * 2 + [VMEM] * 3,
+        [SMEM] * 2 + [HBM] * 3,
+        [pltpu.VMEM(density.shape, F32)] * 3 + [pltpu.SemaphoreType.DMA((3, PIECES))],
+        limit=None,
     )(mouth_azimuth, mouth_radius, density, swirl, heat_rate)
 
-    forcing, state, *slots = call(
+    forcing, state, send = call(
         lambda *refs: first_kernel(each, n_radius, *refs),
-        [shape(*density.shape), shape(*acoustic.shape)]
-        + [shape(columns + own, cells_theta)] * sectors,
+        [shape(*density.shape), shape(*acoustic.shape), shape(sectors, columns + own, cells_theta)],
         [VMEM] * 8,
-    )(partial, heat, acoustic, above, below, inner, outer, basis)
-    received = [exchanged(slots)]
+    )(partial, heat, acoustic, *radial_halo, *sector_halo, basis)
+    received = [exchanged(send)]
     for c in range(1, chunks):
-        slots = call(
+        (send,) = call(
             lambda *refs: next_kernel(c, each, *refs),
-            [shape(columns, cells_theta)] * sectors,
+            [shape(sectors, columns, cells_theta)],
             [VMEM] * 2,
         )(forcing, basis)
-        received.append(exchanged(slots))
+        received.append(exchanged(send))
     density_next = density + time_step * forcing
 
     modes, wave = [], None
     for c in range(chunks):
-        count = received[c][0].shape[0]
         outs = [shape(columns, n_theta), shape(edge, n_theta), shape(edge, n_theta)]
         if c == 0:
             outs.append(shape(own, n_theta))
-        c_modes, c_first, c_last, *waves = call(
-            lambda *refs: forward_kernel(edge, columns, sectors, *refs),
-            outs,
-            [VMEM] * (sectors + 6),
-            [pltpu.VMEM((sectors, count, cells_theta), F32)],
-        )(*received[c], *tables)
+        c_modes, pair, link, *waves = call(
+            lambda *refs: forward_kernel(edge, columns, *refs), outs, [VMEM] * 7
+        )(received[c], *tables)
         if c == 0:
             wave = summed(waves[0], "radial")
-        modes.append((c_modes, shifted(c_last, "radial", 1), shifted(c_first, "radial", -1)))
+        modes.append((c_modes, *paired(pair, link, "radial", False)))
 
     results = []
     for c in range(chunks):
-        slots = call(
+        (send,) = call(
             lambda *refs: solve_kernel(c, each, *refs),
-            [shape(columns, cells_theta)] * sectors,
+            [shape(sectors, columns, cells_theta)],
             [VMEM] * 13,
-            [pltpu.VMEM((columns, n_theta), F32), pltpu.VMEM((sectors, columns, cells_theta), F32)],
+            [pltpu.VMEM((columns, n_theta), F32)],
         )(*modes[c], wave, inverse, scaled, eigen, *tables)
-        results += exchanged(slots)
+        results.append(exchanged(send))
     acoustic_next = summed(state, "radial")
 
     (pressure,) = call(
         lambda *refs: pressure_kernel(chunks, *refs),
         [shape(*density.shape)],
-        [VMEM] * (chunks * sectors + 1),
+        [VMEM] * (chunks + 1),
     )(*results, basis)
     return density_next, pressure, acoustic_next
 

time: 116 us -> 110 us (0.948)
  waiting for transfers between devices: 12.2 us -> 47 us
  starting transfers between devices: 55.6 us -> 28.6 us
  local copies, waits for them, and re-layouts: 23.2 us -> 11.3 us
  other arithmetic: 3.38 us -> 1.86 us
    ppermute x32 -> x4, starting transfers between devices: 44.3 us -> 4.24 us  [swapped(): lax.ppermute(value, axis, [(i, i ^ bits) for i in range(lax.axis_size(axi...]
    all_to_all x0 -> x4, waiting for transfers between devices: none -> 35.7 us  [exchanged(): lax.all_to_all(value, 'sector', split_axis=0, concat_axis=0, tiled=True)]
    all_to_all x0 -> x4, starting transfers between devices: none -> 15.6 us  [exchanged(): lax.all_to_all(value, 'sector', split_axis=0, concat_axis=0, tiled=True)]
    unnamed x90 -> x50, local copies, waits for them, and re-layouts: 19.2 us -> 9.02 us
    ppermute x8, starting transfers between devices: 11.4 us -> 8.76 us  [paired(): return (lax.ppermute(pair, axis, first), lax.ppermute(link, axis, second))]
    ppermute x8, waiting for transfers between devices: 2.76 us -> 0.84 us  [paired(): return (lax.ppermute(pair, axis, first), lax.ppermute(link, axis, second))]
    pallas_call x5, Pallas kernels: 8.58 us -> 6.76 us  [the longest x1 2.8 us: shards(): call(lambda *refs: next_kernel(c, each, *refs), [shape(sectors, columns,...]
    add x4, other arithmetic: 2.27 us -> 0.75 us  [summed(): value = value + swapped(value, axis, step)]
  transfers between devices with their start and end apart: 40 -> 16, of which waited for: 8 -> 8; matrix products, arithmetic and copies ran while one was open for 6% -> 4% of each run, Pallas kernels for 12% -> 9%
where the time goes in v3:
time: 110 us; the launch traced here: 109 us
  waiting for transfers between devices  47 us (43%)
  starting transfers between devices  28.6 us (26%)
  Pallas kernels  19.5 us (18%)
  local copies, waits for them, and re-layouts  11.3 us (10%)
  other arithmetic  1.86 us (2%)
    all_to_all x4, waiting for transfers between devices, exchanged(): lax.all_to_all(value, 'sector', split_axis=0, concat_axis=0, tiled=True)  35.7 us
    all_to_all x4, starting transfers between devices, exchanged(): lax.all_to_all(value, 'sector', split_axis=0, concat_axis=0, tiled=True)  15.6 us
    ppermute x4, waiting for transfers between devices, swapped(): lax.ppermute(value, axis, [(i, i ^ bits) for i in range(lax.axis_size(axi...  10.5 us
    unnamed x50, local copies, waits for them, and re-layouts  9.02 us
    ppermute x8, starting transfers between devices, paired(): return (lax.ppermute(pair, axis, first), lax.ppermute(link, axis, second))  8.76 us
    pallas_call x1, Pallas kernels, shards(): call(lambda *refs: first_kernel(each, n_radius, *refs), [shape(*density.s...  4.81 us
    ppermute x4, starting transfers between devices, swapped(): lax.ppermute(value, axis, [(i, i ^ bits) for i in range(lax.axis_size(axi...  4.24 us
    pallas_call x1, Pallas kernels, shards(): call(lambda *refs: flow_kernel(n_theta, *refs), [shape(*density.shape), r...  4.22 us
  transfers between devices with their start and end apart: 16, of which 8 were waited for; matrix products, arithmetic and copies ran while one was open for 4% of the time, Pallas kernels for 9%

profile of v3, /device:TPU:0, one launch (start us, length us, event | category | flops | bytes accessed | tf_op | source)
XLA Modules:
  0.0 109.3 jit_solution(16765558000649964415)
XLA Ops:
  0.6 1.8 %shard_map.185 = (f32[128,128]{1,0:T(8,128)}, f32[128,128]{1,0:T(8,128)}, f32[64,128]{1,0:T(8,128)}, f32[64,128]{1,0:T(8,128)}) custom-call(f32[128,16,128]{2,1,0:T(8,128)} %density.1, f32[128,16,128]{2,1,0:T(8,128)} %swirl.1, f32[128,16,128]{2,1,0:T(8,128)} %heat_rate.1, f32[3,128,128]{2,1,0:T(8,128)} %refs_2_.6), custom_call_target="tpu_custom_call" | custom-call | bytes 589824 | tf_op jit(solution)/shard_map/pallas_call | solution.py:472
  2.5 0.6 collective-permute-start
  3.0 0.7 collective-permute-start.1
  3.7 2.6 %collective-permute-start.2 = (f32[64,128]{1,0:T(8,128)}, f32[64,128]{1,0:T(8,128)S(1)}, u32[]{:S(2)}, u32[]{:S(2)}) collective-permute-start(f32[64,128]{1,0:T(8,128)} %get-tuple-element.23), channel_id=1, source_target_pairs={{0,4},{4,0},{8,12},{12,8},{16,20},{20,16},{24,28},{28,24},{1,5},{5... | collective-permute-start | bytes 98312 | tf_op jit(solution)/shard_map/ppermute | solution.py:427
  6.3 3.5 %collective-permute-start.3 = (f32[64,128]{1,0:T(8,128)}, f32[64,128]{1,0:T(8,128)S(1)}, u32[]{:S(2)}, u32[]{:S(2)}) collective-permute-start(f32[64,128]{1,0:T(8,128)} %get-tuple-element.24), channel_id=1, source_target_pairs={{4,8},{12,16},{20,24},{28,0},{8,4},{16,12},{24,20},{0,28},{5,9},{1... | collective-permute-start | bytes 98312 | tf_op jit(solution)/shard_map/ppermute | solution.py:427
  9.8 4.2 %shard_map.184 = (f32[128,16,128]{2,1,0:T(8,128)}, f32[128,128]{1,0:T(8,128)}) custom-call(s32[16]{0:T(128)} %refs_0_.1, s32[16]{0:T(128)} %refs_1_.4, f32[128,16,128]{2,1,0:T(8,128)} %density.1, f32[128,16,128]{2,1,0:T(8,128)} %swirl.1, f32[128,16,128]{2,1,0:T(8,128)} %heat_rate.1), custom_call_target="tpu_custom_call" | custom-call | bytes 3342336 | tf_op jit(solution)/shard_map/pallas_call | solution.py:489
  14.1 1.2 %copy-done.9 = f32[128,16,128]{2,1,0:T(8,128)S(1)} copy-done((f32[128,16,128]{2,1,0:T(8,128)S(1)}, f32[128,16,128]{2,1,0:T(8,128)}, u32[]{:S(2)}) %copy-start.9) | copy-done | bytes 1048600
  15.3 0.8 copy-done.15
  16.2 4.8 %shard_map.186 = (f32[128,16,128]{2,1,0:T(8,128)S(1)}, f32[3,128,128]{2,1,0:T(8,128)S(1)}, f32[8,144,128]{2,1,0:T(8,128)}) custom-call(f32[128,16,128]{2,1,0:T(8,128)S(1)} %copy-done.9, f32[128,128]{1,0:T(8,128)S(1)} %copy-done.15, f32[3,128,128]{2,1,0:T(8,128)S(1)} %copy-done.10, f32[128,128]{1,0:T(8,128)S(1)} %collective-permute-done.refs_3_, ...), custom_call_target="tpu_custom_call" | custom-call | bytes 5505024 | tf_op jit(solution)/shard_map/pallas_call | solution.py:497
  21.0 3.8 %all-to-all-start = ((f32[8,144,128]{2,1,0:T(8,128)}), f32[8,144,128]{2,1,0:T(8,128)S(1)}, u32[]{:S(2)}, u32[]{:S(2)}) async-start(f32[8,144,128]{2,1,0:T(8,128)} %get-tuple-element.26), calls=%async_computation | async-start | bytes 1179648 | tf_op jit(solution)/shard_map/all_to_all | solution.py:443
  24.9 2.8 %shard_map.189 = f32[8,128,128]{2,1,0:T(8,128)S(1)} custom-call(f32[128,16,128]{2,1,0:T(8,128)S(1)} %get-tuple-element.25.refs_0_, f32[128,128]{1,0:T(8,128)S(1)} %copy-done.11), custom_call_target="tpu_custom_call" | custom-call | bytes 1572864 | tf_op jit(solution)/shard_map/pallas_call | solution.py:504
  27.7 0.8 copy-done.6
  28.5 12.7 %all-to-all-done.refs_0_ = f32[8,144,128]{2,1,0:T(8,128)S(1)} async-done(((f32[8,144,128]{2,1,0:T(8,128)}), f32[8,144,128]{2,1,0:T(8,128)S(1)}, u32[]{:S(2)}, u32[]{:S(2)}) %all-to-all-start) | async-done | bytes 589856 | tf_op jit(solution)/shard_map/all_to_all | solution.py:443
  41.2 4.5 %all-to-all-start.2 = ((f32[8,128,128]{2,1,0:T(8,128)}), f32[8,128,128]{2,1,0:T(8,128)}, u32[]{:S(2)}, u32[]{:S(2)}) async-start(f32[8,128,128]{2,1,0:T(8,128)} %copy-done.6), calls=%async_computation.2 | async-start | bytes 1048576 | tf_op jit(solution)/shard_map/all_to_all | solution.py:443
  45.7 0.6 slice.27
  46.3 0.1 reshape.11
  46.4 0.6 copy-done.19
  47.0 0.8 slice_reduce_fusion
  47.8 0.1 copy-done.2
  48.0 0.5 shard_map.187
  48.5 0.8 copy-done.12
  49.3 0.6 copy-done.16
  49.9 0.6 copy-done.17
  50.6 0.4 collective-permute-start.6
  51.1 0.6 copy-done.24
  51.7 0.7 concatenate.3
  52.5 8.5 %all-to-all-done.2.refs_0_ = f32[8,128,128]{2,1,0:T(8,128)} async-done(((f32[8,128,128]{2,1,0:T(8,128)}), f32[8,128,128]{2,1,0:T(8,128)}, u32[]{:S(2)}, u32[]{:S(2)}) %all-to-all-start.2) | async-done | bytes 524320 | tf_op jit(solution)/shard_map/all_to_all | solution.py:443
  61.0 1.5 %shard_map.190 = (f32[128,1024]{1,0:T(8,128)S(1)}, f32[24,1024]{1,0:T(8,128)S(1)}, f32[24,1024]{1,0:T(8,128)S(1)}) custom-call(f32[8,128,128]{2,1,0:T(8,128)} %all-to-all-done.2.refs_0_, bf16[256,256]{1,0:T(8,128)(2,1)S(1)} %copy-done.2, bf16[256,256]{1,0:T(8,128)(2,1)S(1)} %copy-done.3, bf16[256,256]{1,0:T(8,128)(2,1)S(1)} %copy-done.4, ...), custom_call_target="tpu_custom_call" | custom-call | bytes 2162688 | tf_op jit(solution)/shard_map/pallas_call | solution.py:517
  62.7 0.7 collective-permute-start.9
  63.4 3.5 %collective-permute-start.7 = (f32[16,1024]{1,0:T(8,128)S(1)}, f32[16,1024]{1,0:T(8,128)S(1)}, u32[]{:S(2)}, u32[]{:S(2)}) collective-permute-start(f32[16,1024]{1,0:T(8,128)S(1)} %add.19), channel_id=1, source_target_pairs={{0,2},{1,3},{2,0},{3,1},{4,6},{5,7},{6,4},{7,5},{8,10},{9,11},{10,... | collective-permute-start | bytes 196616 | tf_op jit(solution)/shard_map/ppermute | solution.py:431
  66.9 3.4 %collective-permute-done.7 = f32[16,1024]{1,0:T(8,128)S(1)} collective-permute-done((f32[16,1024]{1,0:T(8,128)S(1)}, f32[16,1024]{1,0:T(8,128)S(1)}, u32[]{:S(2)}, u32[]{:S(2)}) %collective-permute-start.7) | collective-permute-done | bytes 65568 | tf_op jit(solution)/shard_map/ppermute | solution.py:431
  70.4 1.0 shard_map.191
  71.4 0.8 copy-done.8
  72.1 3.6 %all-to-all-start.3 = ((f32[8,128,128]{2,1,0:T(8,128)}), f32[8,128,128]{2,1,0:T(8,128)S(1)}, u32[]{:S(2)}, u32[]{:S(2)}) async-start(f32[8,128,128]{2,1,0:T(8,128)} %copy-done.8), calls=%async_computation.3 | async-start | bytes 1048576 | tf_op jit(solution)/shard_map/all_to_all | solution.py:443
  75.8 0.7 collective-permute-start.5
  76.5 0.8 collective-permute-done.4.refs_1_
  77.3 1.0 copy-done.13
  78.3 1.0 shard_map.188
  79.3 0.8 copy-done.7
  80.1 9.5 %all-to-all-done.3.refs_1_ = f32[8,128,128]{2,1,0:T(8,128)S(1)} async-done(((f32[8,128,128]{2,1,0:T(8,128)}), f32[8,128,128]{2,1,0:T(8,128)S(1)}, u32[]{:S(2)}, u32[]{:S(2)}) %all-to-all-start.3) | async-done | bytes 524320 | tf_op jit(solution)/shard_map/all_to_all | solution.py:443
  89.6 3.6 %all-to-all-start.1 = ((f32[8,128,128]{2,1,0:T(8,128)}), f32[8,128,128]{2,1,0:T(8,128)S(1)}, u32[]{:S(2)}, u32[]{:S(2)}) async-start(f32[8,128,128]{2,1,0:T(8,128)} %copy-done.7), calls=%async_computation.1 | async-start | bytes 1048576 | tf_op jit(solution)/shard_map/all_to_all | solution.py:443
  93.2 1.4 %collective-permute-done.10 = f32[3,128,128]{2,1,0:T(8,128)S(1)} collective-permute-done((f32[3,128,128]{2,1,0:T(8,128)S(1)}, f32[3,128,128]{2,1,0:T(8,128)S(1)}, u32[]{:S(2)}, u32[]{:S(2)}) %collective-permute-start.10) | collective-permute-done | bytes 196640 | tf_op jit(solution)/shard_map/ppermute | solution.py:431
  94.7 0.3 collective-permute-start.11
  95.0 1.1 %multiply_add_fusion = f32[128,16,128]{2,1,0:T(8,128)} fusion(f32[128,16,128]{2,1,0:T(8,128)S(1)} %copy-done.18, f32[128,16,128]{2,1,0:T(8,128)S(1)} %get-tuple-element.25.refs_0_), kind=kLoop, calls=%fused_computation | loop fusion | flops 524288 | bytes 3145728 | tf_op jit(solution)/shard_map/add | solution.py:510
  96.1 5.6 %collective-permute-done.11 = f32[3,128,128]{2,1,0:T(8,128)S(1)} collective-permute-done((f32[3,128,128]{2,1,0:T(8,128)S(1)}, f32[3,128,128]{2,1,0:T(8,128)S(1)}, u32[]{:S(2)}, u32[]{:S(2)}) %collective-permute-start.11) | collective-permute-done | bytes 196640 | tf_op jit(solution)/shard_map/ppermute | solution.py:431
  101.7 0.7 add.23
  102.4 5.0 %all-to-all-done.1.refs_0_ = f32[8,128,128]{2,1,0:T(8,128)S(1)} async-done(((f32[8,128,128]{2,1,0:T(8,128)}), f32[8,128,128]{2,1,0:T(8,128)S(1)}, u32[]{:S(2)}, u32[]{:S(2)}) %all-to-all-start.1) | async-done | bytes 524320 | tf_op jit(solution)/shard_map/all_to_all | solution.py:443
  107.4 1.9 %shard_map.192 = f32[128,16,128]{2,1,0:T(8,128)} custom-call(f32[8,128,128]{2,1,0:T(8,128)S(1)} %all-to-all-done.1.refs_0_, f32[8,128,128]{2,1,0:T(8,128)S(1)} %all-to-all-done.3.refs_1_, f32[128,128]{1,0:T(8,128)S(1)} %copy-done.11), custom_call_target="tpu_custom_call" | custom-call | bytes 3145728 | tf_op jit(solution)/shard_map/pallas_call | solution.py:535
  (56 shorter events, 0.4 us)
Async XLA Ops:
  2.5 11.6 %collective-permute-start = (f32[128,128]{1,0:T(8,128)}, f32[128,128]{1,0:T(8,128)S(1)}, u32[]{:S(2)}, u32[]{:S(2)}) collective-permute-start(f32[128,128]{1,0:T(8,128)} %get-tuple-element.21), channel_id=1, source_target_pairs={{0,1},{1,0},{2,3},{3,2},{4,5},{5,4},{6,7},{7,6},{8,9},{9,8},{10,11... | collective-permute-start | bytes 196616 | tf_op jit(solution)/shard_map/ppermute | solution.py:427
  3.0 11.1 %collective-permute-start.1 = (f32[128,128]{1,0:T(8,128)}, f32[128,128]{1,0:T(8,128)S(1)}, u32[]{:S(2)}, u32[]{:S(2)}) collective-permute-start(f32[128,128]{1,0:T(8,128)} %get-tuple-element.22), channel_id=1, source_target_pairs={{1,2},{2,1},{5,6},{6,5},{9,10},{10,9},{13,14},{14,13},{17,18},{18,... | collective-permute-start | bytes 196616 | tf_op jit(solution)/shard_map/ppermute | solution.py:427
  3.7 10.4 %collective-permute-start.2 = (f32[64,128]{1,0:T(8,128)}, f32[64,128]{1,0:T(8,128)S(1)}, u32[]{:S(2)}, u32[]{:S(2)}) collective-permute-start(f32[64,128]{1,0:T(8,128)} %get-tuple-element.23), channel_id=1, source_target_pairs={{0,4},{4,0},{8,12},{12,8},{16,20},{20,16},{24,28},{28,24},{1,5},{5... | collective-permute-start | bytes 98312 | tf_op jit(solution)/shard_map/ppermute | solution.py:427
  6.3 7.8 %copy-start.10 = (f32[3,128,128]{2,1,0:T(8,128)S(1)}, f32[3,128,128]{2,1,0:T(8,128)}, u32[]{:S(2)}) copy-start(f32[3,128,128]{2,1,0:T(8,128)} %refs_2_.6) | copy-start | bytes 589828
  6.3 7.8 %copy-start.11 = (f32[128,128]{1,0:T(8,128)S(1)}, f32[128,128]{1,0:T(8,128)}, u32[]{:S(2)}) copy-start(f32[128,128]{1,0:T(8,128)} %constant.24.clone.refs_7_.refs_1_.refs_2_) | copy-start | bytes 196612
  6.3 7.8 %collective-permute-start.3 = (f32[64,128]{1,0:T(8,128)}, f32[64,128]{1,0:T(8,128)S(1)}, u32[]{:S(2)}, u32[]{:S(2)}) collective-permute-start(f32[64,128]{1,0:T(8,128)} %get-tuple-element.24), channel_id=1, source_target_pairs={{4,8},{12,16},{20,24},{28,0},{8,4},{16,12},{24,20},{0,28},{5,9},{1... | collective-permute-start | bytes 98312 | tf_op jit(solution)/shard_map/ppermute | solution.py:427
  14.1 1.2 %copy-start.9 = (f32[128,16,128]{2,1,0:T(8,128)S(1)}, f32[128,16,128]{2,1,0:T(8,128)}, u32[]{:S(2)}) copy-start(f32[128,16,128]{2,1,0:T(8,128)} %get-tuple-element.19.refs_0_) | copy-start | bytes 3145732
  15.3 0.8 copy-start.15
  21.0 20.2 %all-to-all-start = ((f32[8,144,128]{2,1,0:T(8,128)}), f32[8,144,128]{2,1,0:T(8,128)S(1)}, u32[]{:S(2)}, u32[]{:S(2)}) async-start(f32[8,144,128]{2,1,0:T(8,128)} %get-tuple-element.26), calls=%async_computation | async-start | bytes 1179648 | tf_op jit(solution)/shard_map/all_to_all | solution.py:443
  24.8 21.4 %slice-start = ((f32[513]{0:T(1024)}), f32[512]{0:T(512)S(1)}, s32[]{:S(2)}) async-start(f32[513]{0:T(1024)} %param.21), calls=%async_computation.4 | async-start | bytes 4096 | tf_op jit(solution)/shard_map/slice | solution.py:79
  24.8 22.9 %copy-start.4 = (bf16[256,256]{1,0:T(8,128)(2,1)S(1)}, bf16[256,256]{1,0:T(8,128)(2,1)}, u32[]{:S(2)}) copy-start(bf16[256,256]{1,0:T(8,128)(2,1)} %constant.28.clone.refs_3_.refs_9_) | copy-start | bytes 393220
  24.8 22.9 %copy-start.5 = (bf16[256,256]{1,0:T(8,128)(2,1)S(1)}, bf16[256,256]{1,0:T(8,128)(2,1)}, u32[]{:S(2)}) copy-start(bf16[256,256]{1,0:T(8,128)(2,1)} %constant.29.clone.refs_4_.refs_10_) | copy-start | bytes 393220
  27.7 0.8 copy-start.6
  28.5 17.2 %copy-start.21 = (f32[513]{0:T(1024)S(1)}, f32[513]{0:T(1024)}, u32[]{:S(2)}) copy-start(f32[513]{0:T(1024)} %param.21) | copy-start | bytes 6160
  28.5 19.3 %copy-start = (bf16[512,512]{1,0:T(8,128)(2,1)S(1)}, bf16[512,512]{1,0:T(8,128)(2,1)}, u32[]{:S(2)}) copy-start(bf16[512,512]{1,0:T(8,128)(2,1)} %constant.30.clone.refs_5_.refs_11_) | copy-start | bytes 1572868
  28.5 19.3 %copy-start.1 = (bf16[512,512]{1,0:T(8,128)(2,1)S(1)}, bf16[512,512]{1,0:T(8,128)(2,1)}, u32[]{:S(2)}) copy-start(bf16[512,512]{1,0:T(8,128)(2,1)} %constant.31.clone.refs_6_.refs_12_) | copy-start | bytes 1572868
  41.2 19.9 %all-to-all-start.2 = ((f32[8,128,128]{2,1,0:T(8,128)}), f32[8,128,128]{2,1,0:T(8,128)}, u32[]{:S(2)}, u32[]{:S(2)}) async-start(f32[8,128,128]{2,1,0:T(8,128)} %copy-done.6), calls=%async_computation.2 | async-start | bytes 1048576 | tf_op jit(solution)/shard_map/all_to_all | solution.py:443
  46.4 0.6 copy-start.19
  47.0 0.9 copy-start.2
  47.0 1.0 copy-start.3
  48.0 3.0 %copy-start.20 = (f32[128,4]{1,0:T(8,128)S(1)}, f32[128,4]{1,0:T(8,128)}, u32[]{:S(2)}) copy-start(f32[128,4]{1,0:T(8,128)} %copy-done.19) | copy-start | bytes 6148
  48.5 0.8 copy-start.12
  49.3 0.6 copy-start.16
  49.9 0.6 copy-start.17
  50.6 12.8 %collective-permute-start.6 = (f32[16,1024]{1,0:T(8,128)S(1)}, f32[16,1024]{1,0:T(8,128)S(1)}, u32[]{:S(2)}, u32[]{:S(2)}) collective-permute-start(f32[16,1024]{1,0:T(8,128)S(1)} %get-tuple-element.30), channel_id=1, source_target_pairs={{0,1},{1,0},{2,3},{3,2},{4,5},{5,4},{6,7},{7,6},{8,9},{9,8},{10,11... | collective-permute-start | bytes 196616 | tf_op jit(solution)/shard_map/ppermute | solution.py:431
  51.1 0.6 copy-start.24
  62.6 7.8 %collective-permute-start.8 = (f32[24,1024]{1,0:T(8,128)S(1)}, f32[24,1024]{1,0:T(8,128)S(1)}, u32[]{:S(2)}, u32[]{:S(2)}) collective-permute-start(f32[24,1024]{1,0:T(8,128)S(1)} %get-tuple-element.32), channel_id=1, source_target_pairs={{0,1},{1,0},{2,3},{3,2},{4,5},{5,4},{6,7},{7,6},{8,9},{9,8},{10,11... | collective-permute-start | bytes 294920 | tf_op jit(solution)/shard_map/ppermute | solution.py:427
  62.6 4.3 %copy-start.22 = (f32[1024]{0:T(1024)S(1)}, f32[1024]{0:T(1024)}, u32[]{:S(2)}) copy-start(f32[1024]{0:T(1024)} %constant.32.clone) | copy-start | bytes 12292
  62.7 4.3 %copy-start.23 = (f32[1024]{0:T(1024)S(1)}, f32[1024]{0:T(1024)}, u32[]{:S(2)}) copy-start(f32[1024]{0:T(1024)} %constant.33.clone) | copy-start | bytes 12292
  62.7 7.7 %collective-permute-start.9 = (f32[24,1024]{1,0:T(8,128)S(1)}, f32[24,1024]{1,0:T(8,128)S(1)}, u32[]{:S(2)}, u32[]{:S(2)}) collective-permute-start(f32[24,1024]{1,0:T(8,128)S(1)} %get-tuple-element.33), channel_id=1, source_target_pairs={{1,2},{2,1},{5,6},{6,5},{9,10},{10,9},{13,14},{14,13},{17,18},{18,... | collective-permute-start | bytes 294920 | tf_op jit(solution)/shard_map/ppermute | solution.py:427
  63.4 7.0 %collective-permute-start.7 = (f32[16,1024]{1,0:T(8,128)S(1)}, f32[16,1024]{1,0:T(8,128)S(1)}, u32[]{:S(2)}, u32[]{:S(2)}) collective-permute-start(f32[16,1024]{1,0:T(8,128)S(1)} %add.19), channel_id=1, source_target_pairs={{0,2},{1,3},{2,0},{3,1},{4,6},{5,7},{6,4},{7,5},{8,10},{9,11},{10,... | collective-permute-start | bytes 196616 | tf_op jit(solution)/shard_map/ppermute | solution.py:431
  66.9 3.5 %copy-start.14 = (f32[8,16,128]{2,1,0:T(8,128)S(1)}, f32[8,16,128]{2,1,0:T(8,128)}, u32[]{:S(2)}) copy-start(f32[8,16,128]{2,1,0:T(8,128)} %constant.25.clone.refs_6_) | copy-start | bytes 196612
  71.4 0.8 copy-start.8
  72.1 17.5 %all-to-all-start.3 = ((f32[8,128,128]{2,1,0:T(8,128)}), f32[8,128,128]{2,1,0:T(8,128)S(1)}, u32[]{:S(2)}, u32[]{:S(2)}) async-start(f32[8,128,128]{2,1,0:T(8,128)} %copy-done.8), calls=%async_computation.3 | async-start | bytes 1048576 | tf_op jit(solution)/shard_map/all_to_all | solution.py:443
  75.8 1.5 %collective-permute-start.4 = (f32[24,1024]{1,0:T(8,128)}, f32[24,1024]{1,0:T(8,128)S(1)}, u32[]{:S(2)}, u32[]{:S(2)}) collective-permute-start(f32[24,1024]{1,0:T(8,128)} %copy-done.17), channel_id=1, source_target_pairs={{0,1},{1,0},{2,3},{3,2},{4,5},{5,4},{6,7},{7,6},{8,9},{9,8},{10,11... | collective-permute-start | bytes 294920 | tf_op jit(solution)/shard_map/ppermute | solution.py:427
  75.8 1.5 %collective-permute-start.5 = (f32[24,1024]{1,0:T(8,128)}, f32[24,1024]{1,0:T(8,128)S(1)}, u32[]{:S(2)}, u32[]{:S(2)}) collective-permute-start(f32[24,1024]{1,0:T(8,128)} %copy-done.16), channel_id=1, source_target_pairs={{1,2},{2,1},{5,6},{6,5},{9,10},{10,9},{13,14},{14,13},{17,18},{18,... | collective-permute-start | bytes 294920 | tf_op jit(solution)/shard_map/ppermute | solution.py:427
  77.3 1.0 copy-start.13
  79.3 0.8 copy-start.7
  80.1 14.9 %copy-start.18 = (f32[128,16,128]{2,1,0:T(8,128)S(1)}, f32[128,16,128]{2,1,0:T(8,128)}, u32[]{:S(2)}) copy-start(f32[128,16,128]{2,1,0:T(8,128)} %density.1) | copy-start | bytes 3145732
  89.6 17.8 %all-to-all-start.1 = ((f32[8,128,128]{2,1,0:T(8,128)}), f32[8,128,128]{2,1,0:T(8,128)S(1)}, u32[]{:S(2)}, u32[]{:S(2)}) async-start(f32[8,128,128]{2,1,0:T(8,128)} %copy-done.7), calls=%async_computation.1 | async-start | bytes 1048576 | tf_op jit(solution)/shard_map/all_to_all | solution.py:443
  93.2 1.4 %collective-permute-start.10 = (f32[3,128,128]{2,1,0:T(8,128)S(1)}, f32[3,128,128]{2,1,0:T(8,128)S(1)}, u32[]{:S(2)}, u32[]{:S(2)}) collective-permute-start(f32[3,128,128]{2,1,0:T(8,128)S(1)} %get-tuple-element.34), channel_id=1, source_target_pairs={{0,1},{1,0},{2,3},{3,2},{4,5},{5,4},{6,7},{7,6},{8,9},{9,8},{10,11... | collective-permute-start | bytes 589832 | tf_op jit(solution)/shard_map/ppermute | solution.py:431
  94.7 7.0 %collective-permute-start.11 = (f32[3,128,128]{2,1,0:T(8,128)S(1)}, f32[3,128,128]{2,1,0:T(8,128)S(1)}, u32[]{:S(2)}, u32[]{:S(2)}) collective-permute-start(f32[3,128,128]{2,1,0:T(8,128)S(1)} %add.22), channel_id=1, source_target_pairs={{0,2},{1,3},{2,0},{3,1},{4,6},{5,7},{6,4},{7,5},{8,10},{9,11},{10,... | collective-permute-start | bytes 589832 | tf_op jit(solution)/shard_map/ppermute | solution.py:431

commit v4 on v3

--- a/solution.py
+++ b/solution.py
@@ -98,13 +98,24 @@
 NT = ((1,), (1,))
 
 
-def edges_kernel(
-    density, swirl, heat_rate, acoustic, radial_pair, radial_link, sector_pair, sector_link, rho,
-    rate, spin, wave, rim, sems
-):
+def rim_kernel(density, pair, link, rim, sems):
+    cells_radius = density.shape[1]
+    odd = lax.axis_index("radial") % 2
+    copies = [
+        pltpu.make_async_copy(density.at[:, row, :], rim.at[side], sems.at[side])
+        for side, row in ((0, 0), (1, cells_radius - 1))
+    ]
+    for copy in copies:
+        copy.start()
+    for copy in copies:
+        copy.wait()
+    pair[...] = rim[1 - odd]
+    link[...] = rim[odd]
+
+
+def pack_kernel(density, swirl, acoustic, heat, pair, link, rho, spin, wave, sems):
     cells_theta, cells_radius, _ = density.shape
-    radial_odd = lax.axis_index("radial") % 2
-    sector_odd = lax.axis_index("sector") % 2
+    odd = lax.axis_index("sector") % 2
     copies = []
 
     def fetch(source, target):
@@ -113,35 +124,23 @@
         copies.append(copy)
 
     for side, begin, row in ((0, 0, 0), (1, cells_theta - EDGE, cells_theta - 1)):
-        fetch(density.at[pl.ds(begin, EDGE)], rho.at[side])
-        fetch(heat_rate.at[pl.ds(begin, EDGE)], rate.at[side])
+        fetch(density.at[pl.ds(row, 1)], rho.at[side])
         fetch(swirl.at[pl.ds(row, 1)], spin.at[side])
         fetch(acoustic.at[:, pl.ds(begin, EDGE)], wave.at[side])
-    fetch(density.at[:, 0, :], rim.at[0])
-    fetch(density.at[:, cells_radius - 1, :], rim.at[1])
     for copy in copies:
         copy.wait()
-    radial_pair[...] = rim[1 - radial_odd]
-    radial_link[...] = rim[radial_odd]
-    for out, side in ((sector_pair, 1 - sector_odd), (sector_link, sector_odd)):
-        edge = jnp.where(side == 0, rho[0, 0], rho[1, EDGE - 1])
+    for out, side in ((pair, 1 - odd), (link, odd)):
+        edge = rho[side, 0]
         out[0:cells_radius] = edge
         out[cells_radius : 2 * cells_radius] = edge * spin[side, 0]
         at = 2 * cells_radius
         for k in range(3):
             out[at : at + EDGE] = wave[side, k]
             at += EDGE
-        heat = jnp.sum(rate[side] * rho[side] * rho[side], axis=1)
-        out[at : at + EDGE] = heat
-
-
-PIECES = 4
-
-
-def flow_kernel(
-    n_theta, mouth_azimuth, mouth_radius, density_in, swirl_in, heat_rate_in, forcing, heat,
-    density, swirl, heat_rate, sems
-):
+        out[at : at + EDGE] = jnp.where(side == 0, heat[:EDGE], heat[cells_theta - EDGE :])
+
+
+def flow_kernel(n_theta, mouth_azimuth, mouth_radius, density, swirl, heat_rate, forcing, heat):
     sector = lax.axis_index("sector")
     radial = lax.axis_index("radial")
     cells_theta, cells_radius, cells_axial = density.shape
@@ -151,24 +150,10 @@
     segment = n_theta // BURNERS
     part = min(segment, cells_theta)
     zero = jnp.zeros(shape, F32)
-    piece = cells_theta // PIECES
-    copies = {}
-    for i in range(PIECES):
-        rows_here = pl.ds(i * piece, piece)
-        for k, (source, target) in enumerate(
-            ((density_in, density), (swirl_in, swirl), (heat_rate_in, heat_rate))
-        ):
-            copies[k, i] = pltpu.make_async_copy(
-                source.at[rows_here], target.at[rows_here], sems.at[k, i]
-            )
-            copies[k, i].start()
 
     def at(t):
         if t < 0 or t >= cells_theta:
             return zero, zero
-        if t % piece == 0:
-            copies[0, t // piece].wait()
-            copies[1, t // piece].wait()
         rho = density[t]
         return rho, rho * swirl[t]
 
@@ -192,8 +177,6 @@
         laplace = (rho_up + rho_down - twice) + (r_up + r_down - twice) + (z_up + z_down - twice)
         forcing[t] = -0.5 * (flux_up - flux_down) + diffusion * laplace + gain * (1.0 - rho)
 
-    for i in range(PIECES):
-        copies[2, i].wait()
     total = None
     for r in range(cells_radius):
         rho = density[:, r, :]
@@ -213,59 +196,57 @@
     return out[:count] + out[count:]
 
 
-def spread(send, forcing, basis, own, begin, each):
-    cells_theta, cells_radius, _ = forcing.shape
+def spread_kernel(partial, partial_heat, pair, link, basis, forcing, heat, send):
+    radials = lax.axis_size("radial")
+    radial = lax.axis_index("radial")
+    cells_theta, cells_radius, cells_axial = partial.shape
     sectors = send.shape[0]
-    mine = [basis[d * own + begin : d * own + begin + each, :] for d in range(sectors)]
-    mine = jnp.concatenate(mine, 0)
+    own = cells_axial // sectors
+    odd = radial % 2 == 1
+    inner = jnp.where(odd, pair[...], link[...]) * (diffusion * (radial > 0).astype(F32))
+    outer = jnp.where(odd, link[...], pair[...]) * (diffusion * (radial < radials - 1).astype(F32))
+    forcing[...] = partial[...]
+    forcing[:, 0, :] = forcing[:, 0, :] + inner
+    forcing[:, cells_radius - 1, :] = forcing[:, cells_radius - 1, :] + outer
+    heat[...] = partial_heat[...]
+    mine = basis[...]
     for r in range(0, cells_radius, 2):
         modes = sine_modes(mine, [forcing[:, r + i, :] for i in range(2)])
         for i in range(2):
             lane = slice(i * cells_theta, (i + 1) * cells_theta)
             for d in range(sectors):
-                send[d, (r + i) * each : (r + i + 1) * each, :] = modes[
-                    d * each : (d + 1) * each, lane
+                send[d, (r + i) * own : (r + i + 1) * own, :] = modes[
+                    d * own : (d + 1) * own, lane
                 ]
 
 
-def first_kernel(
-    each, n_radius, partial, heat, acoustic, radial_pair, radial_link, sector_pair, sector_link,
-    basis, forcing, state, send
+def late_kernel(
+    n_radius, density, forcing, heat, acoustic, pair, link, basis, density_next, acoustic_next,
+    *slots
 ):
-    radials = lax.axis_size("radial")
-    radial = lax.axis_index("radial")
-    cells_theta, cells_radius, cells_axial = partial.shape
-    shape = (cells_radius, cells_axial)
-    sectors = send.shape[0]
+    sector = lax.axis_index("sector")
+    cells_theta, cells_radius, cells_axial = density.shape
+    sectors = len(slots)
     own = cells_axial // sectors
-    columns = cells_radius * each
-    sector_odd = lax.axis_index("sector") % 2 == 1
-    radial_odd = radial % 2 == 1
-    above = jnp.where(sector_odd, sector_link[...], sector_pair[...])
-    below = jnp.where(sector_odd, sector_pair[...], sector_link[...])
-    outer = jnp.where(radial_odd, radial_link[...], radial_pair[...])
-    inner = jnp.where(radial_odd, radial_pair[...], radial_link[...])
-    forcing[...] = partial[...]
+    odd = sector % 2 == 1
+    above = jnp.where(odd, link[...], pair[...])
+    below = jnp.where(odd, pair[...], link[...])
     rho, flux = slice(0, cells_radius), slice(cells_radius, 2 * cells_radius)
-    forcing[0] = forcing[0] + (0.5 * below[flux] + diffusion * below[rho])
-    forcing[cells_theta - 1] = forcing[cells_theta - 1] + (
-        diffusion * above[rho] - 0.5 * above[flux]
-    )
-    inside = diffusion * (radial > 0).astype(F32)
-    outside = diffusion * (radial < radials - 1).astype(F32)
-    forcing[:, 0, :] = forcing[:, 0, :] + inside * inner
-    forcing[:, cells_radius - 1, :] = forcing[:, cells_radius - 1, :] + outside * outer
-    spread(send, forcing, basis, own, 0, each)
+    first = 0.5 * below[flux] + diffusion * below[rho]
+    last = diffusion * above[rho] - 0.5 * above[flux]
+    density_next[...] = density[...] + time_step * forcing[...]
+    density_next[0] = density[0] + time_step * (forcing[0] + first)
+    end = cells_theta - 1
+    density_next[end] = density[end] + time_step * (forcing[end] + last)
 
     skip = 2 * cells_radius
-    share = (radial == 0).astype(F32)
 
     def extended(k):
         rows = slice(skip + k * EDGE, skip + (k + 1) * EDGE)
         middle = acoustic[k] if k < 3 else heat[...]
         return jnp.concatenate([below[rows], middle, above[rows]], 0)
 
-    press, along, axial = extended(0) * share, extended(1) * share, extended(2) * share
+    press, along, axial = extended(0), extended(1), extended(2)
     warm = extended(3) * (heat_coupling / n_radius)
     count = press.shape[0]
     lanes = lax.broadcasted_iota(jnp.int32, press.shape, 1)
@@ -278,30 +259,49 @@
         axial_down = jnp.where(lanes == 0, 0.0, pltpu.roll(axial, 1, 1))
         press = press - wave_speed * ((along - along_down) + (axial - axial_down)) + warm
     middle = slice(EDGE, EDGE + cells_theta)
-    state[0] = press[middle]
-    state[1] = along[middle]
-    state[2] = axial[middle]
-    modes = sine_modes(basis[...], [feedback * press[middle]])
-    for d in range(sectors):
-        send[d, columns : columns + own, :] = modes[d * own : (d + 1) * own]
-
-
-def next_kernel(chunk, each, forcing, basis, send):
-    own = forcing.shape[2] // send.shape[0]
-    spread(send, forcing, basis, own, chunk * each, each)
-
-
-def forward_kernel(edge, columns, received, *refs):
-    tables, outs = refs[:6], refs[6:]
-    modes, pair, link = outs[:3]
-    sectors = received.shape[0]
+    acoustic_next[0] = press[middle]
+    acoustic_next[1] = along[middle]
+    acoustic_next[2] = axial[middle]
+    mine = jnp.concatenate(
+        [basis[pl.ds(pl.multiple_of((sector ^ k) * own, 8), own), :] for k in range(sectors)], 0
+    )
+    blank = jnp.zeros((cells_theta - 2 * cells_radius, cells_axial), F32)
+    edges = jnp.concatenate([first, last, blank], 0)
+    modes = sine_modes(mine, [feedback * press[middle], edges])
+    for k, slot in enumerate(slots):
+        rows = slice(k * own, (k + 1) * own)
+        slot[:own] = modes[rows, :cells_theta]
+        slot[own:] = modes[rows, cells_theta:]
+
+
+def forward_kernel(edge, received, *refs):
+    sectors, columns, cells_theta = received.shape
+    slots, refs = refs[:sectors], refs[sectors:]
+    tables, (modes, pair, link, wave), late = refs[:6], refs[6:10], refs[10]
+    own = wave.shape[0]
+    cells_radius = columns // own
+    sector = lax.axis_index("sector")
     radial_odd = lax.axis_index("radial") % 2 == 1
+    for k in range(sectors):
+        late[sector ^ k] = slots[k][...]
+    lanes = lax.broadcasted_iota(jnp.int32, (own, cells_theta), 1)
+
+    def value(s):
+        extra = late[s, own:]
+        rows = []
+        for r in range(cells_radius):
+            first = jnp.where(lanes == 0, extra[:, r : r + 1], 0.0)
+            at = cells_radius + r
+            both = jnp.where(lanes == cells_theta - 1, extra[:, at : at + 1], first)
+            rows.append(received[s, r * own : (r + 1) * own, :] + both)
+        return jnp.concatenate(rows + [late[s, :own]], 0)
+
     quarter, half = sectors // 4, sectors // 2
 
     def joined(parts):
         return jnp.concatenate(parts, 1) if len(parts) > 1 else parts[0]
 
-    values = [received[s] for s in range(sectors)]
+    values = [value(s) for s in range(sectors)]
     even = [values[s] + values[s + half] for s in range(half)]
     odd = [values[s] - values[s + half] for s in range(half)]
     both = [even[s] + even[s + quarter] for s in range(quarter)]
@@ -315,24 +315,24 @@
         first, last = out[:edge], out[columns - edge : columns]
         pair[:, lane] = jnp.where(radial_odd, first, last)
         link[:, lane] = jnp.where(radial_odd, last, first)
-        if len(outs) > 3:
-            outs[3][:, lane] = out[columns:]
+        wave[:, lane] = out[columns:]
         at += wh.shape[1]
 
 
 def solve_kernel(
-    chunk, each, modes, pair, link, wave, inverse, scaled, axial, w0h, w0l, w1h, w1l, w2h, w2l,
+    modes, pair, link, wave, inverse, scaled, axial, w0h, w0l, w1h, w1l, w2h, w2l,
     send, solved
 ):
     radials = lax.axis_size("radial")
     radial = lax.axis_index("radial")
     sector = lax.axis_index("sector")
     columns, n_theta = modes.shape
+    each = axial.shape[1]
     cells_radius = columns // each
     has_inner = (radial > 0).astype(F32)
     has_outer = (radial < radials - 1).astype(F32)
     radial_odd = radial % 2 == 1
-    eigen = axial[sector][chunk * each : (chunk + 1) * each, :]
+    eigen = axial[sector]
     step = eigen.shape[1]
     total = cells_radius + 2 * HALO
     for block in range(n_theta // step):
@@ -340,7 +340,7 @@
         inv = jnp.broadcast_to(inverse[:, lane], (each, step))
         inv_inner, inv_outer = inv * has_inner, inv * has_outer
         last_scale = jnp.broadcast_to(scaled[:, lane], (each, step))
-        add = wave[chunk * each : (chunk + 1) * each, lane]
+        add = wave[:, lane]
 
         def row_of(i):
             i -= HALO
@@ -379,22 +379,17 @@
         send[s + sectors // 2] = even[:, lane] - odd[:, lane]
 
 
-def pressure_kernel(chunks, *refs):
-    received, (basis, pressure) = refs[:-2], refs[-2:]
-    sectors = received[0].shape[0]
+def pressure_kernel(received, basis, pressure):
+    sectors = received.shape[0]
     cells_radius = pressure.shape[1]
-    each = received[0].shape[1] // cells_radius
+    own = received.shape[1] // cells_radius
     high, low = split(basis[...])
     right = jnp.concatenate(
         [jnp.concatenate([high, low], 1), jnp.concatenate([high, jnp.zeros_like(low)], 1)], 0
     )
     cells_axial = high.shape[1]
     for r in range(cells_radius):
-        rows = [
-            received[c][d, r * each : (r + 1) * each, :]
-            for d in range(sectors)
-            for c in range(chunks)
-        ]
+        rows = [received[d, r * own : (r + 1) * own, :] for d in range(sectors)]
         modes = jnp.concatenate(rows, 0)
         left = jnp.concatenate(split(modes.T), 1)
         out = lax.dot_general(left, right, (NN, ((), ())), preferred_element_type=F32)
@@ -450,10 +445,8 @@
     n_theta = cells_theta * sectors
     n_radius = cells_radius * radials
     own = cells_axial // sectors
-    chunks = max(1, min(2, own // 8))
-    each = own // chunks
-    columns = cells_radius * each
-    edge = HALO * each
+    columns = cells_radius * own
+    edge = HALO * own
 
     basis, eigen = axial_tables(cells_axial)
     basis = jnp.asarray(basis.astype(np.float32))
@@ -469,74 +462,60 @@
 
     packed = 2 * cells_radius + 4 * EDGE
     row_block = shape(cells_theta, cells_axial)
-    edges = call(
-        edges_kernel,
-        [row_block] * 2 + [shape(packed, cells_axial)] * 2,
-        [HBM] * 4,
-        [
-            pltpu.VMEM((2, EDGE, cells_radius, cells_axial), F32),
-            pltpu.VMEM((2, EDGE, cells_radius, cells_axial), F32),
-            pltpu.VMEM((2, 1, cells_radius, cells_axial), F32),
-            pltpu.VMEM((2, 3, EDGE, cells_axial), F32),
-            pltpu.VMEM((2, cells_theta, cells_axial), F32),
-            pltpu.SemaphoreType.DMA((10,)),
-        ],
+    pair, link = call(
+        rim_kernel,
+        [row_block] * 2,
+        [HBM],
+        [pltpu.VMEM((2, cells_theta, cells_axial), F32), pltpu.SemaphoreType.DMA((2,))],
         limit=None,
-    )(density, swirl, heat_rate, acoustic)
-    sector_halo = paired(edges[2], edges[3], "sector", True)
-    radial_halo = paired(edges[0], edges[1], "radial", False)
+    )(density)
+    radial_halo = paired(pair, link, "radial", False)
 
     partial, heat = call(
         lambda *refs: flow_kernel(n_theta, *refs),
         [shape(*density.shape), row_block],
-        [SMEM] * 2 + [HBM] * 3,
-        [pltpu.VMEM(density.shape, F32)] * 3 + [pltpu.SemaphoreType.DMA((3, PIECES))],
-        limit=None,
+        [SMEM] * 2 + [VMEM] * 3,
     )(mouth_azimuth, mouth_radius, density, swirl, heat_rate)
-
-    forcing, state, send = call(
-        lambda *refs: first_kernel(each, n_radius, *refs),
-        [shape(*density.shape), shape(*acoustic.shape), shape(sectors, columns + own, cells_theta)],
-        [VMEM] * 8,
-    )(partial, heat, acoustic, *radial_halo, *sector_halo, basis)
-    received = [exchanged(send)]
-    for c in range(1, chunks):
-        (send,) = call(
-            lambda *refs: next_kernel(c, each, *refs),
-            [shape(sectors, columns, cells_theta)],
-            [VMEM] * 2,
-        )(forcing, basis)
-        received.append(exchanged(send))
-    density_next = density + time_step * forcing
-
-    modes, wave = [], None
-    for c in range(chunks):
-        outs = [shape(columns, n_theta), shape(edge, n_theta), shape(edge, n_theta)]
-        if c == 0:
-            outs.append(shape(own, n_theta))
-        c_modes, pair, link, *waves = call(
-            lambda *refs: forward_kernel(edge, columns, *refs), outs, [VMEM] * 7
-        )(received[c], *tables)
-        if c == 0:
-            wave = summed(waves[0], "radial")
-        modes.append((c_modes, *paired(pair, link, "radial", False)))
-
-    results = []
-    for c in range(chunks):
-        (send,) = call(
-            lambda *refs: solve_kernel(c, each, *refs),
-            [shape(sectors, columns, cells_theta)],
-            [VMEM] * 13,
-            [pltpu.VMEM((columns, n_theta), F32)],
-        )(*modes[c], wave, inverse, scaled, eigen, *tables)
-        results.append(exchanged(send))
-    acoustic_next = summed(state, "radial")
-
-    (pressure,) = call(
-        lambda *refs: pressure_kernel(chunks, *refs),
-        [shape(*density.shape)],
-        [VMEM] * (chunks + 1),
-    )(*results, basis)
+    forcing, heat, send = call(
+        spread_kernel,
+        [shape(*density.shape), row_block, shape(sectors, columns, cells_theta)],
+        [VMEM] * 5,
+    )(partial, heat, *radial_halo, basis)
+    received = exchanged(send)
+
+    heat = summed(heat, "radial")
+    pair, link = call(
+        pack_kernel,
+        [shape(packed, cells_axial)] * 2,
+        [HBM] * 3 + [VMEM],
+        [
+            pltpu.VMEM((2, 1, cells_radius, cells_axial), F32),
+            pltpu.VMEM((2, 1, cells_radius, cells_axial), F32),
+            pltpu.VMEM((2, 3, EDGE, cells_axial), F32),
+            pltpu.SemaphoreType.DMA((6,)),
+        ],
+    )(density, swirl, acoustic, heat)
+    density_next, acoustic_next, *slots = call(
+        lambda *refs: late_kernel(n_radius, *refs),
+        [shape(*density.shape), shape(*acoustic.shape)] + [shape(2 * own, cells_theta)] * sectors,
+        [VMEM] * 7,
+    )(density, forcing, heat, acoustic, *paired(pair, link, "sector", True), basis)
+    slots = [slots[0]] + [swapped(slots[k], "sector", k) for k in range(1, sectors)]
+
+    modes, pair, link, wave = call(
+        lambda *refs: forward_kernel(edge, *refs),
+        [shape(columns, n_theta)] + [shape(edge, n_theta)] * 2 + [shape(own, n_theta)],
+        [VMEM] * (sectors + 7),
+        [pltpu.VMEM((sectors, 2 * own, cells_theta), F32)],
+    )(received, *slots, *tables)
+    (send,) = call(
+        solve_kernel,
+        [shape(sectors, columns, cells_theta)],
+        [VMEM] * 13,
+        [pltpu.VMEM((columns, n_theta), F32)],
+    )(modes, *paired(pair, link, "radial", False), wave, inverse, scaled, eigen, *tables)
+
+    (pressure,) = call(pressure_kernel, [shape(*density.shape)], [VMEM] * 2)(exchanged(send), basis)
     return density_next, pressure, acoustic_next
 
 

time: 110 us -> 106 us (0.964); the launches traced: 109 us -> 104 us
  waiting for transfers between devices: 47 us -> 15.7 us
  blocking collectives: 0 us -> 27.8 us
  starting transfers between devices: 28.6 us -> 32.7 us
  Pallas kernels: 19.5 us -> 16.6 us
  other arithmetic: 1.86 us -> 0.03 us
    all_to_all x4 -> x1, waiting for transfers between devices: 35.7 us -> 0.01 us  [exchanged(): lax.all_to_all(value, 'sector', split_axis=0, concat_axis=0, tiled=True)]
    all_to_all x0 -> x1, blocking collectives: none -> 27.8 us  [exchanged(): lax.all_to_all(value, 'sector', split_axis=0, concat_axis=0, tiled=True)]
    ppermute x4 -> x9, starting transfers between devices: 4.24 us -> 18.8 us  [swapped(): lax.ppermute(value, axis, [(i, i ^ bits) for i in range(lax.axis_size(axi...]
    all_to_all x4 -> x1, starting transfers between devices: 15.6 us -> 6.97 us  [exchanged(): lax.all_to_all(value, 'sector', split_axis=0, concat_axis=0, tiled=True)]
    ppermute x8 -> x6, waiting for transfers between devices: 0.84 us -> 8.73 us  [paired(): return (lax.ppermute(pair, axis, first), lax.ppermute(link, axis, second))]
    ppermute x4 -> x9, waiting for transfers between devices: 10.5 us -> 6.99 us  [swapped(): lax.ppermute(value, axis, [(i, i ^ bits) for i in range(lax.axis_size(axi...]
    pallas_call x8 -> x7, Pallas kernels: 15.3 us -> 12.7 us  [the longest x1 3.07 us: shards(): call(spread_kernel, [shape(*density.shape), row_block, shape(sectors, col...]
    ppermute x8 -> x6, starting transfers between devices: 8.76 us -> 6.96 us  [paired(): return (lax.ppermute(pair, axis, first), lax.ppermute(link, axis, second))]
  transfers between devices with their start and end apart: 16 -> 16, of which waited for: 8 -> 6; matrix products, arithmetic and copies ran while one was open for 4% -> 2% of each run, Pallas kernels for 9% -> 7%
where the time goes in v4:
time: 106 us; the launch traced here: 104 us
  starting transfers between devices  32.7 us (31%)
  blocking collectives  27.8 us (26%)
  Pallas kernels  16.6 us (16%)
  waiting for transfers between devices  15.7 us (15%)
  local copies, waits for them, and re-layouts  10.4 us (10%)
    all_to_all x1, blocking collectives, exchanged(): lax.all_to_all(value, 'sector', split_axis=0, concat_axis=0, tiled=True)  27.8 us
    ppermute x9, starting transfers between devices, swapped(): lax.ppermute(value, axis, [(i, i ^ bits) for i in range(lax.axis_size(axi...  18.8 us
    ppermute x6, waiting for transfers between devices, paired(): return (lax.ppermute(pair, axis, first), lax.ppermute(link, axis, second))  8.73 us
    unnamed x44, local copies, waits for them, and re-layouts  8.05 us
    ppermute x9, waiting for transfers between devices, swapped(): lax.ppermute(value, axis, [(i, i ^ bits) for i in range(lax.axis_size(axi...  6.99 us
    all_to_all x1, starting transfers between devices, exchanged(): lax.all_to_all(value, 'sector', split_axis=0, concat_axis=0, tiled=True)  6.97 us
    ppermute x6, starting transfers between devices, paired(): return (lax.ppermute(pair, axis, first), lax.ppermute(link, axis, second))  6.96 us
    pallas_call x1, Pallas kernels, shards(): call(lambda *refs: flow_kernel(n_theta, *refs), [shape(*density.shape), r...  3.84 us
  transfers between devices with their start and end apart: 16, of which 6 were waited for; matrix products, arithmetic and copies ran while one was open for 2% of the time, Pallas kernels for 7%

profile of v4, /device:TPU:0, one launch (start us, length us, event | category | flops | bytes accessed | tf_op | source)
XLA Modules:
  0.0 104.1 jit_solution(9336278492717058766)
XLA Ops:
  0.6 1.6 %shard_map.185 = (f32[128,128]{1,0:T(8,128)}, f32[128,128]{1,0:T(8,128)}) custom-call(f32[128,16,128]{2,1,0:T(8,128)} %refs_0_.3), custom_call_target="tpu_custom_call" | custom-call | bytes 393216 | tf_op jit(solution)/shard_map/pallas_call | solution.py:465
  2.3 0.0 copy-start.16
  2.3 0.0 copy-start.17
  2.3 0.6 collective-permute-start
  2.9 0.7 collective-permute-start.1
  3.6 0.0 copy-start.1
  3.6 1.2 %copy-done.1 = f32[128,16,128]{2,1,0:T(8,128)S(1)} copy-done((f32[128,16,128]{2,1,0:T(8,128)S(1)}, f32[128,16,128]{2,1,0:T(8,128)}, u32[]{:S(2)}) %copy-start.1) | copy-done | bytes 1048600
  4.8 1.2 %copy-done.5 = f32[128,16,128]{2,1,0:T(8,128)S(1)} copy-done((f32[128,16,128]{2,1,0:T(8,128)S(1)}, f32[128,16,128]{2,1,0:T(8,128)}, u32[]{:S(2)}) %copy-start.5) | copy-done | bytes 1048600
  6.0 3.8 %shard_map.184 = (f32[128,16,128]{2,1,0:T(8,128)S(1)}, f32[128,128]{1,0:T(8,128)S(1)}) custom-call(s32[16]{0:T(128)S(1)} %copy-done.16, s32[16]{0:T(128)S(1)} %copy-done.17, f32[128,16,128]{2,1,0:T(8,128)S(1)} %copy-done, f32[128,16,128]{2,1,0:T(8,128)S(1)} %copy-done.1, f32[128,16,128]{2,1,0:T(8,128)S(1)} %copy-done.5), custom_call_target="tpu_custom_call" | custom-call | bytes 3342336 | tf_op jit(solution)/shard_map/pallas_call | solution.py:474
  9.9 0.0 collective-permute-done.pair
  9.9 3.1 %shard_map.186 = (f32[128,16,128]{2,1,0:T(8,128)S(1)}, f32[128,128]{1,0:T(8,128)S(1)}, f32[8,256,128]{2,1,0:T(8,128)S(1)}) custom-call(f32[128,16,128]{2,1,0:T(8,128)S(1)} %get-tuple-element.26.partial, f32[128,128]{1,0:T(8,128)S(1)} %get-tuple-element.27.partial_heat, f32[128,128]{1,0:T(8,128)S(1)} %collective-permute-done.pair, ...), custom_call_target="tpu_custom_call" | custom-call | bytes 6488064 | tf_op jit(solution)/shard_map/pallas_call | solution.py:479
  13.0 1.0 copy-done.6
  14.0 1.0 copy-done.7
  14.9 7.0 %all-to-all-start = ((f32[8,256,128]{2,1,0:T(8,128)}), f32[8,256,128]{2,1,0:T(8,128)S(1)}, u32[]{:S(2)}, u32[]{:S(2)}) async-start(f32[8,256,128]{2,1,0:T(8,128)} %copy-done.6), calls=%async_computation | async-start | bytes 2097152 | tf_op jit(solution)/shard_map/all_to_all | solution.py:438
  21.9 2.6 %collective-permute-start.2 = (f32[128,128]{1,0:T(8,128)S(1)}, f32[128,128]{1,0:T(8,128)S(1)}, u32[]{:S(2)}, u32[]{:S(2)}) collective-permute-start(f32[128,128]{1,0:T(8,128)S(1)} %get-tuple-element.31), channel_id=1, source_target_pairs={{0,1},{1,0},{2,3},{3,2},{4,5},{5,4},{6,7},{7,6},{8,9},{9,8},{10,11... | collective-permute-start | bytes 196616 | tf_op jit(solution)/shard_map/ppermute | solution.py:426
  24.5 0.9 collective-permute-done.2
  25.5 1.2 %collective-permute-start.3 = (f32[128,128]{1,0:T(8,128)S(1)}, f32[128,128]{1,0:T(8,128)S(1)}, u32[]{:S(2)}, u32[]{:S(2)}) collective-permute-start(f32[128,128]{1,0:T(8,128)S(1)} %add.9), channel_id=1, source_target_pairs={{0,2},{1,3},{2,0},{3,1},{4,6},{5,7},{6,4},{7,5},{8,10},{9,11},{10,... | collective-permute-start | bytes 196616 | tf_op jit(solution)/shard_map/ppermute | solution.py:426
  26.7 3.2 %collective-permute-done.3 = f32[128,128]{1,0:T(8,128)S(1)} collective-permute-done((f32[128,128]{1,0:T(8,128)S(1)}, f32[128,128]{1,0:T(8,128)S(1)}, u32[]{:S(2)}, u32[]{:S(2)}) %collective-permute-start.3) | collective-permute-done | bytes 65568 | tf_op jit(solution)/shard_map/ppermute | solution.py:426
  29.9 0.8 shard_map.187
  30.7 1.7 %collective-permute-start.4 = (f32[64,128]{1,0:T(8,128)}, f32[64,128]{1,0:T(8,128)S(1)}, u32[]{:S(2)}, u32[]{:S(2)}) collective-permute-start(f32[64,128]{1,0:T(8,128)} %get-tuple-element.32), channel_id=1, source_target_pairs={{0,4},{4,0},{8,12},{12,8},{16,20},{20,16},{24,28},{28,24},{1,5},{5... | collective-permute-start | bytes 98312 | tf_op jit(solution)/shard_map/ppermute | solution.py:422
  32.4 3.3 %collective-permute-start.5 = (f32[64,128]{1,0:T(8,128)}, f32[64,128]{1,0:T(8,128)S(1)}, u32[]{:S(2)}, u32[]{:S(2)}) collective-permute-start(f32[64,128]{1,0:T(8,128)} %get-tuple-element.33), channel_id=1, source_target_pairs={{4,8},{12,16},{20,24},{28,0},{8,4},{16,12},{24,20},{0,28},{5,9},{1... | collective-permute-start | bytes 98312 | tf_op jit(solution)/shard_map/ppermute | solution.py:422
  35.7 0.7 reshape.11
  36.4 0.0 collective-permute-done.4.refs_4_
  36.4 8.0 %collective-permute-done.5.refs_5_ = f32[64,128]{1,0:T(8,128)S(1)} collective-permute-done((f32[64,128]{1,0:T(8,128)}, f32[64,128]{1,0:T(8,128)S(1)}, u32[]{:S(2)}, u32[]{:S(2)}) %collective-permute-start.5) | collective-permute-done | bytes 32800 | tf_op jit(solution)/shard_map/ppermute | solution.py:422
  44.4 1.2 %copy-done.8 = f32[128,16,128]{2,1,0:T(8,128)S(1)} copy-done((f32[128,16,128]{2,1,0:T(8,128)S(1)}, f32[128,16,128]{2,1,0:T(8,128)}, u32[]{:S(2)}) %copy-start.8) | copy-done | bytes 1048600
  45.7 2.5 %shard_map.188 = (f32[128,16,128]{2,1,0:T(8,128)}, f32[3,128,128]{2,1,0:T(8,128)}, f32[32,128]{1,0:T(8,128)S(1)}, f32[32,128]{1,0:T(8,128)}, f32[32,128]{1,0:T(8...) custom-call(f32[128,16,128]{2,1,0:T(8,128)S(1)} %copy-done, ...), custom_call_target="tpu_custom_call" | custom-call | bytes 4128768 | tf_op jit(solution)/shard_map/pallas_call | solution.py:498
  48.1 1.3 %collective-permute-start.10 = (f32[32,128]{1,0:T(8,128)S(1)}, f32[32,128]{1,0:T(8,128)S(1)}, u32[]{:S(2)}, u32[]{:S(2)}) collective-permute-start(f32[32,128]{1,0:T(8,128)S(1)} %get-tuple-element.41), channel_id=1, source_target_pairs={{0,20},{4,16},{8,28},{12,24},{16,4},{20,0},{24,12},{28,8},{1,21},{... | collective-permute-start | bytes 49160 | tf_op jit(solution)/shard_map/ppermute | solution.py:426
  49.5 7.1 %collective-permute-start.11 = (f32[32,128]{1,0:T(8,128)S(1)}, f32[32,128]{1,0:T(8,128)S(1)}, u32[]{:S(2)}, u32[]{:S(2)}) collective-permute-start(f32[32,128]{1,0:T(8,128)S(1)} %get-tuple-element.42), channel_id=1, source_target_pairs={{0,24},{4,28},{8,16},{12,20},{16,8},{20,12},{24,0},{28,4},{1,25},{... | collective-permute-start | bytes 49160 | tf_op jit(solution)/shard_map/ppermute | solution.py:426
  56.6 0.2 slice_reduce_fusion
  56.8 3.0 %collective-permute-start.12 = (f32[32,128]{1,0:T(8,128)}, f32[32,128]{1,0:T(8,128)S(1)}, u32[]{:S(2)}, u32[]{:S(2)}) collective-permute-start(f32[32,128]{1,0:T(8,128)} %get-tuple-element.43), channel_id=1, source_target_pairs={{0,28},{4,24},{8,20},{12,16},{16,12},{20,8},{24,4},{28,0},{1,29},{... | collective-permute-start | bytes 49160 | tf_op jit(solution)/shard_map/ppermute | solution.py:426
  59.9 0.0 collective-permute-start.7
  59.9 3.5 %collective-permute-start.8 = (f32[32,128]{1,0:T(8,128)}, f32[32,128]{1,0:T(8,128)S(1)}, u32[]{:S(2)}, u32[]{:S(2)}) collective-permute-start(f32[32,128]{1,0:T(8,128)} %get-tuple-element.39), channel_id=1, source_target_pairs={{0,12},{4,8},{8,4},{12,0},{16,28},{20,24},{24,20},{28,16},{1,13},{... | collective-permute-start | bytes 49160 | tf_op jit(solution)/shard_map/ppermute | solution.py:426
  63.4 0.1 slice_reduce_fusion.3
  63.5 0.6 copy-done.19
  64.0 0.6 slice.27
  64.6 0.7 concatenate.3
  65.3 0.3 collective-permute-done.8.refs_4_
  65.6 2.6 %collective-permute-done.9.refs_5_ = f32[32,128]{1,0:T(8,128)S(1)} collective-permute-done((f32[32,128]{1,0:T(8,128)}, f32[32,128]{1,0:T(8,128)S(1)}, u32[]{:S(2)}, u32[]{:S(2)}) %collective-permute-start.9) | collective-permute-done | bytes 16416 | tf_op jit(solution)/shard_map/ppermute | solution.py:426
  68.2 0.0 copy-start.13
  68.2 0.9 copy-done.13
  69.1 0.9 copy-done.14
  70.1 1.6 %shard_map.189 = (f32[256,1024]{1,0:T(8,128)S(1)}, f32[48,1024]{1,0:T(8,128)S(1)}, f32[48,1024]{1,0:T(8,128)S(1)}, f32[16,1024]{1,0:T(8,128)S(1)}) custom-call(f32[8,256,128]{2,1,0:T(8,128)S(1)} %all-to-all-done.refs_0_, f32[32,128]{1,0:T(8,128)S(1)} %get-tuple-element.36.refs_1_, f32[32,128]{1,0:T(8,128)S(1)} %collective-permute-done.6.refs_2_, ...), custom_call_target="tpu_custom_call" | custom-call | bytes 4521984 | tf_op jit(solution)/shard_map/pallas_call | solution.py:505
  71.6 0.1 collective-permute-start.13
  71.7 0.7 collective-permute-start.14
  72.4 0.7 collective-permute-done.13.pair
  73.1 1.3 %shard_map.190 = f32[8,256,128]{2,1,0:T(8,128)S(1)} custom-call(f32[256,1024]{1,0:T(8,128)S(1)} %get-tuple-element.44.modes, f32[48,1024]{1,0:T(8,128)S(1)} %collective-permute-done.13.pair, f32[48,1024]{1,0:T(8,128)S(1)} %collective-permute-done.14.link, f32[16,1024]{1,0:T(8,128)S(1)} %get-tuple-element.47.wave, f32[1,1024]{1,0:T(1,128)S(1)} %bitcast.4, ...), custom_call_target="tpu_custom_call" | custom-call | bytes 3145728 | tf_op jit(solution)/shard_map/pallas_call | solution.py:511
  74.5 27.8 %all_to_all.10.received = f32[8,256,128]{2,1,0:T(8,128)S(1)} all-to-all(f32[8,256,128]{2,1,0:T(8,128)S(1)} %shard_map.190), channel_id=1, replica_groups=mesh['sector'=8,'radial'=4] {'sector'}, dimensions={0} | all-to-all | bytes 2097152 | tf_op jit(solution)/shard_map/all_to_all | solution.py:438
  102.2 1.9 %shard_map.191 = f32[128,16,128]{2,1,0:T(8,128)} custom-call(f32[8,256,128]{2,1,0:T(8,128)S(1)} %all_to_all.10.received, f32[128,128]{1,0:T(8,128)S(1)} %copy-done.10), custom_call_target="tpu_custom_call" | custom-call | bytes 3145728 | tf_op jit(solution)/shard_map/pallas_call | solution.py:518
  (47 shorter events, 0.1 us)
Async XLA Ops:
  0.6 2.9 %copy-start = (f32[128,16,128]{2,1,0:T(8,128)S(1)}, f32[128,16,128]{2,1,0:T(8,128)}, u32[]{:S(2)}) copy-start(f32[128,16,128]{2,1,0:T(8,128)} %refs_0_.3) | copy-start | bytes 3145732
  2.3 1.3 %copy-start.16 = (s32[16]{0:T(128)S(1)}, s32[16]{0:T(128)}, u32[]{:S(2)}) copy-start(s32[16]{0:T(128)} %refs_0_.2) | copy-start | bytes 196
  2.3 1.3 %copy-start.17 = (s32[16]{0:T(128)S(1)}, s32[16]{0:T(128)}, u32[]{:S(2)}) copy-start(s32[16]{0:T(128)} %refs_1_.1) | copy-start | bytes 196
  2.3 7.6 %collective-permute-start = (f32[128,128]{1,0:T(8,128)}, f32[128,128]{1,0:T(8,128)S(1)}, u32[]{:S(2)}, u32[]{:S(2)}) collective-permute-start(f32[128,128]{1,0:T(8,128)} %get-tuple-element.28), channel_id=1, source_target_pairs={{0,1},{1,0},{2,3},{3,2},{4,5},{5,4},{6,7},{7,6},{8,9},{9,8},{10,11... | collective-permute-start | bytes 196616 | tf_op jit(solution)/shard_map/ppermute | solution.py:422
  2.9 7.0 %collective-permute-start.1 = (f32[128,128]{1,0:T(8,128)}, f32[128,128]{1,0:T(8,128)S(1)}, u32[]{:S(2)}, u32[]{:S(2)}) collective-permute-start(f32[128,128]{1,0:T(8,128)} %get-tuple-element.29), channel_id=1, source_target_pairs={{1,2},{2,1},{5,6},{6,5},{9,10},{10,9},{13,14},{14,13},{17,18},{18,... | collective-permute-start | bytes 196616 | tf_op jit(solution)/shard_map/ppermute | solution.py:422
  3.6 1.2 %copy-start.1 = (f32[128,16,128]{2,1,0:T(8,128)S(1)}, f32[128,16,128]{2,1,0:T(8,128)}, u32[]{:S(2)}) copy-start(f32[128,16,128]{2,1,0:T(8,128)} %swirl.1) | copy-start | bytes 3145732
  4.8 1.2 %copy-start.5 = (f32[128,16,128]{2,1,0:T(8,128)S(1)}, f32[128,16,128]{2,1,0:T(8,128)}, u32[]{:S(2)}) copy-start(f32[128,16,128]{2,1,0:T(8,128)} %refs_4_.1) | copy-start | bytes 3145732
  6.0 3.9 %copy-start.10 = (f32[128,128]{1,0:T(8,128)S(1)}, f32[128,128]{1,0:T(8,128)}, u32[]{:S(2)}) copy-start(f32[128,128]{1,0:T(8,128)} %constant.22.clone.basis.refs_6_) | copy-start | bytes 196612
  13.0 1.0 copy-start.6
  14.0 1.0 copy-start.7
  14.9 15.0 %copy-start.2 = (f32[128,16,128]{2,1,0:T(8,128)S(1)}, f32[128,16,128]{2,1,0:T(8,128)}, u32[]{:S(2)}) copy-start(f32[128,16,128]{2,1,0:T(8,128)} %swirl.1) | copy-start | bytes 3145732
  14.9 53.3 %all-to-all-start = ((f32[8,256,128]{2,1,0:T(8,128)}), f32[8,256,128]{2,1,0:T(8,128)S(1)}, u32[]{:S(2)}, u32[]{:S(2)}) async-start(f32[8,256,128]{2,1,0:T(8,128)} %copy-done.6), calls=%async_computation | async-start | bytes 2097152 | tf_op jit(solution)/shard_map/all_to_all | solution.py:438
  21.9 8.0 %copy-start.9 = (f32[3,128,128]{2,1,0:T(8,128)S(1)}, f32[3,128,128]{2,1,0:T(8,128)}, u32[]{:S(2)}) copy-start(f32[3,128,128]{2,1,0:T(8,128)} %refs_3_.3) | copy-start | bytes 589828
  21.9 3.5 %collective-permute-start.2 = (f32[128,128]{1,0:T(8,128)S(1)}, f32[128,128]{1,0:T(8,128)S(1)}, u32[]{:S(2)}, u32[]{:S(2)}) collective-permute-start(f32[128,128]{1,0:T(8,128)S(1)} %get-tuple-element.31), channel_id=1, source_target_pairs={{0,1},{1,0},{2,3},{3,2},{4,5},{5,4},{6,7},{7,6},{8,9},{9,8},{10,11... | collective-permute-start | bytes 196616 | tf_op jit(solution)/shard_map/ppermute | solution.py:426
  25.5 4.4 %collective-permute-start.3 = (f32[128,128]{1,0:T(8,128)S(1)}, f32[128,128]{1,0:T(8,128)S(1)}, u32[]{:S(2)}, u32[]{:S(2)}) collective-permute-start(f32[128,128]{1,0:T(8,128)S(1)} %add.9), channel_id=1, source_target_pairs={{0,2},{1,3},{2,0},{3,1},{4,6},{5,7},{6,4},{7,5},{8,10},{9,11},{10,... | collective-permute-start | bytes 196616 | tf_op jit(solution)/shard_map/ppermute | solution.py:426
  30.7 5.7 %collective-permute-start.4 = (f32[64,128]{1,0:T(8,128)}, f32[64,128]{1,0:T(8,128)S(1)}, u32[]{:S(2)}, u32[]{:S(2)}) collective-permute-start(f32[64,128]{1,0:T(8,128)} %get-tuple-element.32), channel_id=1, source_target_pairs={{0,4},{4,0},{8,12},{12,8},{16,20},{20,16},{24,28},{28,24},{1,5},{5... | collective-permute-start | bytes 98312 | tf_op jit(solution)/shard_map/ppermute | solution.py:422
  32.4 3.3 %slice-start = ((f32[513]{0:T(1024)}), f32[512]{0:T(512)S(1)}, s32[]{:S(2)}) async-start(f32[513]{0:T(1024)} %param.21), calls=%async_computation.2 | async-start | bytes 4096 | tf_op jit(solution)/shard_map/slice | solution.py:79
  32.4 12.0 %collective-permute-start.5 = (f32[64,128]{1,0:T(8,128)}, f32[64,128]{1,0:T(8,128)S(1)}, u32[]{:S(2)}, u32[]{:S(2)}) collective-permute-start(f32[64,128]{1,0:T(8,128)} %get-tuple-element.33), channel_id=1, source_target_pairs={{4,8},{12,16},{20,24},{28,0},{8,4},{16,12},{24,20},{0,28},{5,9},{1... | collective-permute-start | bytes 98312 | tf_op jit(solution)/shard_map/ppermute | solution.py:422
  44.4 1.2 %copy-start.8 = (f32[128,16,128]{2,1,0:T(8,128)S(1)}, f32[128,16,128]{2,1,0:T(8,128)}, u32[]{:S(2)}) copy-start(f32[128,16,128]{2,1,0:T(8,128)} %copy-done.7) | copy-start | bytes 3145732
  45.6 10.9 %copy-start.18 = (f32[128,4]{1,0:T(8,128)S(1)}, f32[128,4]{1,0:T(8,128)}, u32[]{:S(2)}) copy-start(f32[128,4]{1,0:T(8,128)} %reshape.11) | copy-start | bytes 6148
  45.7 22.6 %copy-start.3 = (bf16[512,512]{1,0:T(8,128)(2,1)S(1)}, bf16[512,512]{1,0:T(8,128)(2,1)}, u32[]{:S(2)}) copy-start(bf16[512,512]{1,0:T(8,128)(2,1)} %constant.28.clone.refs_13_.w2h) | copy-start | bytes 1572868
  45.7 22.6 %copy-start.4 = (bf16[512,512]{1,0:T(8,128)(2,1)S(1)}, bf16[512,512]{1,0:T(8,128)(2,1)}, u32[]{:S(2)}) copy-start(bf16[512,512]{1,0:T(8,128)(2,1)} %constant.29.clone.refs_14_.w2l) | copy-start | bytes 1572868
  48.1 11.7 %collective-permute-start.10 = (f32[32,128]{1,0:T(8,128)S(1)}, f32[32,128]{1,0:T(8,128)S(1)}, u32[]{:S(2)}, u32[]{:S(2)}) collective-permute-start(f32[32,128]{1,0:T(8,128)S(1)} %get-tuple-element.41), channel_id=1, source_target_pairs={{0,20},{4,16},{8,28},{12,24},{16,4},{20,0},{24,12},{28,8},{1,21},{... | collective-permute-start | bytes 49160 | tf_op jit(solution)/shard_map/ppermute | solution.py:426
  49.5 13.9 %collective-permute-start.11 = (f32[32,128]{1,0:T(8,128)S(1)}, f32[32,128]{1,0:T(8,128)S(1)}, u32[]{:S(2)}, u32[]{:S(2)}) collective-permute-start(f32[32,128]{1,0:T(8,128)S(1)} %get-tuple-element.42), channel_id=1, source_target_pairs={{0,24},{4,28},{8,16},{12,20},{16,8},{20,12},{24,0},{28,4},{1,25},{... | collective-permute-start | bytes 49160 | tf_op jit(solution)/shard_map/ppermute | solution.py:426
  56.6 11.6 %copy-start.11 = (bf16[256,256]{1,0:T(8,128)(2,1)S(1)}, bf16[256,256]{1,0:T(8,128)(2,1)}, u32[]{:S(2)}) copy-start(bf16[256,256]{1,0:T(8,128)(2,1)} %constant.24.clone.refs_9_.w0h) | copy-start | bytes 393220
  56.6 11.6 %copy-start.12 = (bf16[256,256]{1,0:T(8,128)(2,1)S(1)}, bf16[256,256]{1,0:T(8,128)(2,1)}, u32[]{:S(2)}) copy-start(bf16[256,256]{1,0:T(8,128)(2,1)} %constant.25.clone.refs_10_.w0l) | copy-start | bytes 393220
  56.8 8.5 %collective-permute-start.12 = (f32[32,128]{1,0:T(8,128)}, f32[32,128]{1,0:T(8,128)S(1)}, u32[]{:S(2)}, u32[]{:S(2)}) collective-permute-start(f32[32,128]{1,0:T(8,128)} %get-tuple-element.43), channel_id=1, source_target_pairs={{0,28},{4,24},{8,20},{12,16},{16,12},{20,8},{24,4},{28,0},{1,29},{... | collective-permute-start | bytes 49160 | tf_op jit(solution)/shard_map/ppermute | solution.py:426
  59.9 5.5 %collective-permute-start.6 = (f32[32,128]{1,0:T(8,128)}, f32[32,128]{1,0:T(8,128)S(1)}, u32[]{:S(2)}, u32[]{:S(2)}) collective-permute-start(f32[32,128]{1,0:T(8,128)} %get-tuple-element.37), channel_id=1, source_target_pairs={{0,4},{4,0},{8,12},{12,8},{16,20},{20,16},{24,28},{28,24},{1,5},{5... | collective-permute-start | bytes 49160 | tf_op jit(solution)/shard_map/ppermute | solution.py:426
  59.9 5.5 %collective-permute-start.7 = (f32[32,128]{1,0:T(8,128)}, f32[32,128]{1,0:T(8,128)S(1)}, u32[]{:S(2)}, u32[]{:S(2)}) collective-permute-start(f32[32,128]{1,0:T(8,128)} %get-tuple-element.38), channel_id=1, source_target_pairs={{0,8},{4,12},{8,0},{12,4},{16,24},{20,28},{24,16},{28,20},{1,9},{5... | collective-permute-start | bytes 49160 | tf_op jit(solution)/shard_map/ppermute | solution.py:426
  59.9 5.8 %collective-permute-start.8 = (f32[32,128]{1,0:T(8,128)}, f32[32,128]{1,0:T(8,128)S(1)}, u32[]{:S(2)}, u32[]{:S(2)}) collective-permute-start(f32[32,128]{1,0:T(8,128)} %get-tuple-element.39), channel_id=1, source_target_pairs={{0,12},{4,8},{8,4},{12,0},{16,28},{20,24},{24,20},{28,16},{1,13},{... | collective-permute-start | bytes 49160 | tf_op jit(solution)/shard_map/ppermute | solution.py:426
  63.4 0.7 copy-start.19
  63.4 4.8 %collective-permute-start.9 = (f32[32,128]{1,0:T(8,128)}, f32[32,128]{1,0:T(8,128)S(1)}, u32[]{:S(2)}, u32[]{:S(2)}) collective-permute-start(f32[32,128]{1,0:T(8,128)} %get-tuple-element.40), channel_id=1, source_target_pairs={{0,16},{4,20},{8,24},{12,28},{16,0},{20,4},{24,8},{28,12},{1,17},{... | collective-permute-start | bytes 49160 | tf_op jit(solution)/shard_map/ppermute | solution.py:426
  68.2 0.9 copy-start.13
  69.1 0.9 copy-start.14
  70.1 2.3 %copy-start.20 = (f32[1024]{0:T(1024)S(1)}, f32[1024]{0:T(1024)}, u32[]{:S(2)}) copy-start(f32[1024]{0:T(1024)} %constant.30.clone) | copy-start | bytes 12292
  70.1 2.3 %copy-start.21 = (f32[1024]{0:T(1024)S(1)}, f32[1024]{0:T(1024)}, u32[]{:S(2)}) copy-start(f32[1024]{0:T(1024)} %constant.31.clone) | copy-start | bytes 12292
  70.1 3.1 %copy-start.15 = (f32[8,16,128]{2,1,0:T(8,128)S(1)}, f32[8,16,128]{2,1,0:T(8,128)}, u32[]{:S(2)}) copy-start(f32[8,16,128]{2,1,0:T(8,128)} %constant.23.clone.axial) | copy-start | bytes 196612
  71.6 1.5 %collective-permute-start.13 = (f32[48,1024]{1,0:T(8,128)S(1)}, f32[48,1024]{1,0:T(8,128)S(1)}, u32[]{:S(2)}, u32[]{:S(2)}) collective-permute-start(f32[48,1024]{1,0:T(8,128)S(1)} %get-tuple-element.45), channel_id=1, source_target_pairs={{0,1},{1,0},{2,3},{3,2},{4,5},{5,4},{6,7},{7,6},{8,9},{9,8},{10,11... | collective-permute-start | bytes 589832 | tf_op jit(solution)/shard_map/ppermute | solution.py:422
  71.7 1.4 %collective-permute-start.14 = (f32[48,1024]{1,0:T(8,128)S(1)}, f32[48,1024]{1,0:T(8,128)S(1)}, u32[]{:S(2)}, u32[]{:S(2)}) collective-permute-start(f32[48,1024]{1,0:T(8,128)S(1)} %get-tuple-element.46), channel_id=1, source_target_pairs={{1,2},{2,1},{5,6},{6,5},{9,10},{10,9},{13,14},{14,13},{17,18},{18,... | collective-permute-start | bytes 589832 | tf_op jit(solution)/shard_map/ppermute | solution.py:422

commit v5 on v4

--- a/solution.py
+++ b/solution.py
@@ -98,24 +98,13 @@
 NT = ((1,), (1,))
 
 
-def rim_kernel(density, pair, link, rim, sems):
-    cells_radius = density.shape[1]
-    odd = lax.axis_index("radial") % 2
-    copies = [
-        pltpu.make_async_copy(density.at[:, row, :], rim.at[side], sems.at[side])
-        for side, row in ((0, 0), (1, cells_radius - 1))
-    ]
-    for copy in copies:
-        copy.start()
-    for copy in copies:
-        copy.wait()
-    pair[...] = rim[1 - odd]
-    link[...] = rim[odd]
-
-
-def pack_kernel(density, swirl, acoustic, heat, pair, link, rho, spin, wave, sems):
+def edges_kernel(
+    density, swirl, heat_rate, acoustic, radial_pair, radial_link, sector_pair, sector_link, rho,
+    rate, spin, wave, rim, sems
+):
     cells_theta, cells_radius, _ = density.shape
-    odd = lax.axis_index("sector") % 2
+    radial_odd = lax.axis_index("radial") % 2
+    sector_odd = lax.axis_index("sector") % 2
     copies = []
 
     def fetch(source, target):
@@ -124,23 +113,29 @@
         copies.append(copy)
 
     for side, begin, row in ((0, 0, 0), (1, cells_theta - EDGE, cells_theta - 1)):
-        fetch(density.at[pl.ds(row, 1)], rho.at[side])
+        fetch(density.at[pl.ds(begin, EDGE)], rho.at[side])
+        fetch(heat_rate.at[pl.ds(begin, EDGE)], rate.at[side])
         fetch(swirl.at[pl.ds(row, 1)], spin.at[side])
         fetch(acoustic.at[:, pl.ds(begin, EDGE)], wave.at[side])
+    fetch(density.at[:, 0, :], rim.at[0])
+    fetch(density.at[:, cells_radius - 1, :], rim.at[1])
     for copy in copies:
         copy.wait()
-    for out, side in ((pair, 1 - odd), (link, odd)):
-        edge = rho[side, 0]
+    radial_pair[...] = rim[1 - radial_odd]
+    radial_link[...] = rim[radial_odd]
+    for out, side in ((sector_pair, 1 - sector_odd), (sector_link, sector_odd)):
+        edge = jnp.where(side == 0, rho[0, 0], rho[1, EDGE - 1])
         out[0:cells_radius] = edge
         out[cells_radius : 2 * cells_radius] = edge * spin[side, 0]
         at = 2 * cells_radius
         for k in range(3):
             out[at : at + EDGE] = wave[side, k]
             at += EDGE
-        out[at : at + EDGE] = jnp.where(side == 0, heat[:EDGE], heat[cells_theta - EDGE :])
-
-
-def flow_kernel(n_theta, mouth_azimuth, mouth_radius, density, swirl, heat_rate, forcing, heat):
+        heat = jnp.sum(rate[side] * rho[side] * rho[side], axis=1)
+        out[at : at + EDGE] = heat
+
+
+def flow_kernel(n_theta, mouth_azimuth, mouth_radius, density, swirl, forcing):
     sector = lax.axis_index("sector")
     radial = lax.axis_index("radial")
     cells_theta, cells_radius, cells_axial = density.shape
@@ -177,13 +172,6 @@
         laplace = (rho_up + rho_down - twice) + (r_up + r_down - twice) + (z_up + z_down - twice)
         forcing[t] = -0.5 * (flux_up - flux_down) + diffusion * laplace + gain * (1.0 - rho)
 
-    total = None
-    for r in range(cells_radius):
-        rho = density[:, r, :]
-        term = heat_rate[:, r, :] * rho * rho
-        total = term if total is None else total + term
-    heat[...] = total
-
 
 def sine_modes(basis, fields):
     high, low = split(basis)
@@ -196,57 +184,79 @@
     return out[:count] + out[count:]
 
 
-def spread_kernel(partial, partial_heat, pair, link, basis, forcing, heat, send):
+GROUP = 4
+
+
+def spread_kernel(
+    partial, density, radial_pair, radial_link, sector_pair, sector_link, basis, density_next, send,
+    forcing, following, staged, sems
+):
     radials = lax.axis_size("radial")
     radial = lax.axis_index("radial")
     cells_theta, cells_radius, cells_axial = partial.shape
     sectors = send.shape[0]
     own = cells_axial // sectors
+    odd = lax.axis_index("sector") % 2 == 1
+    above = jnp.where(odd, sector_link[...], sector_pair[...])
+    below = jnp.where(odd, sector_pair[...], sector_link[...])
     odd = radial % 2 == 1
-    inner = jnp.where(odd, pair[...], link[...]) * (diffusion * (radial > 0).astype(F32))
-    outer = jnp.where(odd, link[...], pair[...]) * (diffusion * (radial < radials - 1).astype(F32))
+    inner = jnp.where(odd, radial_pair[...], radial_link[...])
+    outer = jnp.where(odd, radial_link[...], radial_pair[...])
+    rho, flux = slice(0, cells_radius), slice(cells_radius, 2 * cells_radius)
+    end = cells_theta - 1
     forcing[...] = partial[...]
-    forcing[:, 0, :] = forcing[:, 0, :] + inner
-    forcing[:, cells_radius - 1, :] = forcing[:, cells_radius - 1, :] + outer
-    heat[...] = partial_heat[...]
+    forcing[0] = forcing[0] + (0.5 * below[flux] + diffusion * below[rho])
+    forcing[end] = forcing[end] + (diffusion * above[rho] - 0.5 * above[flux])
+    inside = diffusion * (radial > 0).astype(F32)
+    outside = diffusion * (radial < radials - 1).astype(F32)
+    forcing[:, 0, :] = forcing[:, 0, :] + inside * inner
+    forcing[:, cells_radius - 1, :] = forcing[:, cells_radius - 1, :] + outside * outer
+    following[...] = density[...] + time_step * forcing[...]
+    copies = [pltpu.make_async_copy(following, density_next, sems.at[0])]
+    copies[0].start()
     mine = basis[...]
-    for r in range(0, cells_radius, 2):
-        modes = sine_modes(mine, [forcing[:, r + i, :] for i in range(2)])
-        for i in range(2):
+    for r in range(0, cells_radius, GROUP):
+        modes = sine_modes(mine, [forcing[:, r + i, :] for i in range(GROUP)])
+        for i in range(GROUP):
             lane = slice(i * cells_theta, (i + 1) * cells_theta)
             for d in range(sectors):
-                send[d, (r + i) * own : (r + i + 1) * own, :] = modes[
+                staged[d, (r + i) * own : (r + i + 1) * own, :] = modes[
                     d * own : (d + 1) * own, lane
                 ]
-
-
-def late_kernel(
-    n_radius, density, forcing, heat, acoustic, pair, link, basis, density_next, acoustic_next,
-    *slots
+        rows = pl.ds(r * own, GROUP * own)
+        copy = pltpu.make_async_copy(
+            staged.at[:, rows, :], send.at[:, rows, :], sems.at[len(copies)]
+        )
+        copy.start()
+        copies.append(copy)
+    for copy in copies:
+        copy.wait()
+
+
+def acoustic_kernel(
+    n_radius, density, heat_rate, acoustic, pair, link, basis, state, *slots
 ):
     sector = lax.axis_index("sector")
     cells_theta, cells_radius, cells_axial = density.shape
     sectors = len(slots)
     own = cells_axial // sectors
+    share = (lax.axis_index("radial") == 0).astype(F32)
     odd = sector % 2 == 1
     above = jnp.where(odd, link[...], pair[...])
     below = jnp.where(odd, pair[...], link[...])
-    rho, flux = slice(0, cells_radius), slice(cells_radius, 2 * cells_radius)
-    first = 0.5 * below[flux] + diffusion * below[rho]
-    last = diffusion * above[rho] - 0.5 * above[flux]
-    density_next[...] = density[...] + time_step * forcing[...]
-    density_next[0] = density[0] + time_step * (forcing[0] + first)
-    end = cells_theta - 1
-    density_next[end] = density[end] + time_step * (forcing[end] + last)
-
+    heat = None
+    for r in range(cells_radius):
+        rho = density[:, r, :]
+        term = heat_rate[:, r, :] * rho * rho
+        heat = term if heat is None else heat + term
     skip = 2 * cells_radius
 
     def extended(k):
         rows = slice(skip + k * EDGE, skip + (k + 1) * EDGE)
-        middle = acoustic[k] if k < 3 else heat[...]
+        middle = acoustic[k] if k < 3 else heat
         return jnp.concatenate([below[rows], middle, above[rows]], 0)
 
-    press, along, axial = extended(0), extended(1), extended(2)
+    press, along, axial = extended(0) * share, extended(1) * share, extended(2) * share
     warm = extended(3) * (heat_coupling / n_radius)
     count = press.shape[0]
     lanes = lax.broadcasted_iota(jnp.int32, press.shape, 1)
@@ -259,69 +269,74 @@
         axial_down = jnp.where(lanes == 0, 0.0, pltpu.roll(axial, 1, 1))
         press = press - wave_speed * ((along - along_down) + (axial - axial_down)) + warm
     middle = slice(EDGE, EDGE + cells_theta)
-    acoustic_next[0] = press[middle]
-    acoustic_next[1] = along[middle]
-    acoustic_next[2] = axial[middle]
+    state[0] = press[middle]
+    state[1] = along[middle]
+    state[2] = axial[middle]
     mine = jnp.concatenate(
         [basis[pl.ds(pl.multiple_of((sector ^ k) * own, 8), own), :] for k in range(sectors)], 0
     )
-    blank = jnp.zeros((cells_theta - 2 * cells_radius, cells_axial), F32)
-    edges = jnp.concatenate([first, last, blank], 0)
-    modes = sine_modes(mine, [feedback * press[middle], edges])
+    modes = sine_modes(mine, [feedback * press[middle]])
     for k, slot in enumerate(slots):
-        rows = slice(k * own, (k + 1) * own)
-        slot[:own] = modes[rows, :cells_theta]
-        slot[own:] = modes[rows, cells_theta:]
-
-
-def forward_kernel(edge, received, *refs):
-    sectors, columns, cells_theta = received.shape
-    slots, refs = refs[:sectors], refs[sectors:]
-    tables, (modes, pair, link, wave), late = refs[:6], refs[6:10], refs[10]
-    own = wave.shape[0]
-    cells_radius = columns // own
-    sector = lax.axis_index("sector")
-    radial_odd = lax.axis_index("radial") % 2 == 1
-    for k in range(sectors):
-        late[sector ^ k] = slots[k][...]
-    lanes = lax.broadcasted_iota(jnp.int32, (own, cells_theta), 1)
-
-    def value(s):
-        extra = late[s, own:]
-        rows = []
-        for r in range(cells_radius):
-            first = jnp.where(lanes == 0, extra[:, r : r + 1], 0.0)
-            at = cells_radius + r
-            both = jnp.where(lanes == cells_theta - 1, extra[:, at : at + 1], first)
-            rows.append(received[s, r * own : (r + 1) * own, :] + both)
-        return jnp.concatenate(rows + [late[s, :own]], 0)
-
+        slot[...] = modes[k * own : (k + 1) * own]
+
+
+def transformed(values, table, store):
+    sectors = len(values)
     quarter, half = sectors // 4, sectors // 2
 
     def joined(parts):
         return jnp.concatenate(parts, 1) if len(parts) > 1 else parts[0]
 
-    values = [value(s) for s in range(sectors)]
     even = [values[s] + values[s + half] for s in range(half)]
     odd = [values[s] - values[s + half] for s in range(half)]
     both = [even[s] + even[s + quarter] for s in range(quarter)]
     apart = [even[s] - even[s + quarter] for s in range(quarter)]
     at = 0
-    for i, parts in enumerate((both, apart, odd)):
-        wh, wl = tables[2 * i : 2 * i + 2]
-        lane = slice(at, at + wh.shape[1])
-        out = product(split(joined(parts)), (wh[...], wl[...]), NN)
-        modes[:, lane] = out[:columns]
-        first, last = out[:edge], out[columns - edge : columns]
+    for parts, pieces in zip((both, apart, odd), table_parts(table)):
+        width = pieces[0].shape[1]
+        store(slice(at, at + width), product(split(joined(parts)), pieces, NN))
+        at += width
+
+
+def table_parts(table):
+    n_theta = table.shape[1]
+    quarter, half = n_theta // 4, n_theta // 2
+    top, bottom = slice(0, quarter), slice(quarter, quarter + half)
+    columns = [slice(i * quarter, (i + 1) * quarter) for i in range(4)]
+    return (
+        (table[top, columns[0]], table[top, columns[1]]),
+        (table[top, columns[2]], table[top, columns[3]]),
+        (table[bottom, :half], table[bottom, half:]),
+    )
+
+
+def forward_kernel(edge, received, table, modes, pair, link):
+    sectors, columns, _ = received.shape
+    radial_odd = lax.axis_index("radial") % 2 == 1
+
+    def store(lane, out):
+        modes[:, lane] = out
+        first, last = out[:edge], out[columns - edge :]
         pair[:, lane] = jnp.where(radial_odd, first, last)
         link[:, lane] = jnp.where(radial_odd, last, first)
-        wave[:, lane] = out[columns:]
-        at += wh.shape[1]
+
+    transformed([received[s] for s in range(sectors)], table, store)
+
+
+def wave_kernel(*refs):
+    slots, (table, wave, pieces) = refs[:-3], refs[-3:]
+    sector = lax.axis_index("sector")
+    for k, slot in enumerate(slots):
+        pieces[sector ^ k] = slot[...]
+
+    def store(lane, out):
+        wave[:, lane] = out
+
+    transformed([pieces[s] for s in range(len(slots))], table, store)
 
 
 def solve_kernel(
-    modes, pair, link, wave, inverse, scaled, axial, w0h, w0l, w1h, w1l, w2h, w2l,
-    send, solved
+    modes, pair, link, wave, inverse, scaled, axial, table, state_in, send, state, solved
 ):
     radials = lax.axis_size("radial")
     radial = lax.axis_index("radial")
@@ -368,10 +383,12 @@
             solved[i * each : (i + 1) * each, lane] = x[i + HALO]
 
     sectors, _, width = send.shape
-    n0, n1 = w0h.shape[1], w1h.shape[1]
-    both = product(split(solved[:, :n0]), (w0h[...], w0l[...]), NT)
-    apart = product(split(solved[:, n0 : n0 + n1]), (w1h[...], w1l[...]), NT)
-    odd = product(split(solved[:, n0 + n1 :]), (w2h[...], w2l[...]), NT)
+    outs, at = [], 0
+    for pieces in table_parts(table):
+        lane = slice(at, at + pieces[0].shape[1])
+        outs.append(product(split(solved[:, lane]), pieces, NT))
+        at = lane.stop
+    both, apart, odd = outs
     even = jnp.concatenate([both + apart, both - apart], 1)
     for s in range(sectors // 2):
         lane = slice(s * width, (s + 1) * width)
@@ -402,7 +419,7 @@
         kernel,
         out_shape=outs,
         in_specs=ins,
-        out_specs=[VMEM] * len(outs),
+        out_specs=more.pop("out_specs", [VMEM] * len(outs)),
         scratch_shapes=list(scratch),
         cost_estimate=pl.CostEstimate(flops=0, bytes_accessed=3 * moved, transcendentals=0),
         compiler_params=pltpu.CompilerParams(vmem_limit_bytes=limit),
@@ -453,67 +470,81 @@
     eigen = jnp.asarray(
         np.broadcast_to(eigen.reshape(sectors, own, 1), (sectors, own, 128)).astype(np.float32)
     )
-    tables = []
-    for table in azimuth_tables(n_theta):
-        tables += [jnp.asarray(t) for t in halves(table)]
+    parts = [halves(table) for table in azimuth_tables(n_theta)]
+    table = jnp.asarray(
+        np.concatenate(
+            [np.concatenate(parts[0] + parts[1], 1), np.concatenate(parts[2], 1)], 0
+        )
+    )
     fixed, weight = diagonal_tables(n_theta)
     inverse = (1.0 / (jnp.asarray(fixed) + mode_rows(mode_impedance)))[None, :]
     scaled = inverse * jnp.asarray(weight)[None, :]
 
     packed = 2 * cells_radius + 4 * EDGE
     row_block = shape(cells_theta, cells_axial)
-    pair, link = call(
-        rim_kernel,
-        [row_block] * 2,
-        [HBM],
-        [pltpu.VMEM((2, cells_theta, cells_axial), F32), pltpu.SemaphoreType.DMA((2,))],
-        limit=None,
-    )(density)
-    radial_halo = paired(pair, link, "radial", False)
-
-    partial, heat = call(
-        lambda *refs: flow_kernel(n_theta, *refs),
-        [shape(*density.shape), row_block],
-        [SMEM] * 2 + [VMEM] * 3,
-    )(mouth_azimuth, mouth_radius, density, swirl, heat_rate)
-    forcing, heat, send = call(
-        spread_kernel,
-        [shape(*density.shape), row_block, shape(sectors, columns, cells_theta)],
-        [VMEM] * 5,
-    )(partial, heat, *radial_halo, basis)
-    received = exchanged(send)
-
-    heat = summed(heat, "radial")
-    pair, link = call(
-        pack_kernel,
-        [shape(packed, cells_axial)] * 2,
-        [HBM] * 3 + [VMEM],
+    edges = call(
+        edges_kernel,
+        [row_block] * 2 + [shape(packed, cells_axial)] * 2,
+        [HBM] * 4,
         [
-            pltpu.VMEM((2, 1, cells_radius, cells_axial), F32),
+            pltpu.VMEM((2, EDGE, cells_radius, cells_axial), F32),
+            pltpu.VMEM((2, EDGE, cells_radius, cells_axial), F32),
             pltpu.VMEM((2, 1, cells_radius, cells_axial), F32),
             pltpu.VMEM((2, 3, EDGE, cells_axial), F32),
-            pltpu.SemaphoreType.DMA((6,)),
+            pltpu.VMEM((2, cells_theta, cells_axial), F32),
+            pltpu.SemaphoreType.DMA((10,)),
         ],
-    )(density, swirl, acoustic, heat)
-    density_next, acoustic_next, *slots = call(
-        lambda *refs: late_kernel(n_radius, *refs),
-        [shape(*density.shape), shape(*acoustic.shape)] + [shape(2 * own, cells_theta)] * sectors,
+        limit=None,
+    )(density, swirl, heat_rate, acoustic)
+    sector_halo = paired(edges[2], edges[3], "sector", True)
+    radial_halo = paired(edges[0], edges[1], "radial", False)
+
+    (partial,) = call(
+        lambda *refs: flow_kernel(n_theta, *refs),
+        [shape(*density.shape)],
+        [SMEM] * 2 + [VMEM] * 2,
+    )(mouth_azimuth, mouth_radius, density, swirl)
+    density_next, send = call(
+        spread_kernel,
+        [shape(*density.shape), shape(sectors, columns, cells_theta)],
         [VMEM] * 7,
-    )(density, forcing, heat, acoustic, *paired(pair, link, "sector", True), basis)
+        [pltpu.VMEM(density.shape, F32)] * 2
+        + [pltpu.VMEM((sectors, columns, cells_theta), F32)]
+        + [pltpu.SemaphoreType.DMA((1 + cells_radius // GROUP,))],
+        out_specs=[HBM] * 2,
+    )(partial, density, *radial_halo, *sector_halo, basis)
+    received = exchanged(send)
+
+    state, *slots = call(
+        lambda *refs: acoustic_kernel(n_radius, *refs),
+        [shape(*acoustic.shape)] + [shape(own, cells_theta)] * sectors,
+        [VMEM] * 6,
+    )(density, heat_rate, acoustic, *sector_halo, basis)
     slots = [slots[0]] + [swapped(slots[k], "sector", k) for k in range(1, sectors)]
 
-    modes, pair, link, wave = call(
+    modes, pair, link = call(
         lambda *refs: forward_kernel(edge, *refs),
-        [shape(columns, n_theta)] + [shape(edge, n_theta)] * 2 + [shape(own, n_theta)],
-        [VMEM] * (sectors + 7),
-        [pltpu.VMEM((sectors, 2 * own, cells_theta), F32)],
-    )(received, *slots, *tables)
-    (send,) = call(
+        [shape(columns, n_theta)] + [shape(edge, n_theta)] * 2,
+        [VMEM] * 2,
+    )(received, table)
+    (wave,) = call(
+        wave_kernel,
+        [shape(own, n_theta)],
+        [VMEM] * (sectors + 1),
+        [pltpu.VMEM((sectors, own, cells_theta), F32)],
+    )(*slots, table)
+    send, state = call(
         solve_kernel,
-        [shape(sectors, columns, cells_theta)],
-        [VMEM] * 13,
+        [shape(sectors, columns, cells_theta), shape(*acoustic.shape)],
+        [VMEM] * 8 + [HBM],
         [pltpu.VMEM((columns, n_theta), F32)],
-    )(modes, *paired(pair, link, "radial", False), wave, inverse, scaled, eigen, *tables)
+        out_specs=[VMEM, HBM],
+        input_output_aliases={8: 1},
+    )(
+        modes, *paired(pair, link, "radial", False), summed(wave, "radial"), inverse, scaled, eigen,
+        table, state,
+    )
+    acoustic_next = summed(state, "radial")
 
     (pressure,) = call(pressure_kernel, [shape(*density.shape)], [VMEM] * 2)(exchanged(send), basis)
     return density_next, pressure, acoustic_next

time: 106 us -> 92.8 us (0.88)
  the two profiles are of different devices: /device:TPU:0 before, /device:TPU:1 now
where the time goes in v5:
time: 92.8 us; the launch traced here: 92.4 us
  waiting for transfers between devices  35.9 us (39%)
  starting transfers between devices  35.5 us (38%)
  Pallas kernels  16.4 us (18%)
  local copies, waits for them, and re-layouts  2.95 us (3%)
    ppermute x11, waiting for transfers between devices, swapped(): lax.ppermute(value, axis, [(i, i ^ bits) for i in range(lax.axis_size(axi...  18 us
    ppermute x11, starting transfers between devices, swapped(): lax.ppermute(value, axis, [(i, i ^ bits) for i in range(lax.axis_size(axi...  14.2 us
    all_to_all x2, waiting for transfers between devices, exchanged(): lax.all_to_all(value, 'sector', split_axis=0, concat_axis=0, tiled=True)  13.6 us
    ppermute x6, starting transfers between devices, paired(): return (lax.ppermute(pair, axis, first), lax.ppermute(link, axis, second))  13.1 us
    all_to_all x2, starting transfers between devices, exchanged(): lax.all_to_all(value, 'sector', split_axis=0, concat_axis=0, tiled=True)  8.24 us
    ppermute x6, waiting for transfers between devices, paired(): return (lax.ppermute(pair, axis, first), lax.ppermute(link, axis, second))  4.33 us
    pallas_call x1, Pallas kernels, shards(): call(spread_kernel, [shape(*density.shape), shape(sectors, columns, cells...  4.22 us
    pallas_call x1, Pallas kernels, shards(): call(solve_kernel, [shape(sectors, columns, cells_theta), shape(*acoustic...  2.38 us
  transfers between devices with their start and end apart: 19, of which 9 were waited for; matrix products, arithmetic and copies ran while one was open for 3% of the time, Pallas kernels for 6%

profile of v5, /device:TPU:1, one launch (start us, length us, event | category | flops | bytes accessed | tf_op | source)
XLA Modules:
  0.0 92.4 jit_solution(3746838332562963910)
XLA Ops:
  0.7 1.9 %shard_map.140 = (f32[128,128]{1,0:T(8,128)}, f32[128,128]{1,0:T(8,128)}, f32[64,128]{1,0:T(8,128)}, f32[64,128]{1,0:T(8,128)}) custom-call(f32[128,16,128]{2,1,0:T(8,128)} %refs_0_.3, f32[128,16,128]{2,1,0:T(8,128)} %swirl.1, f32[128,16,128]{2,1,0:T(8,128)} %refs_1_.4, f32[3,128,128]{2,1,0:T(8,128)} %refs_2_.3), custom_call_target="tpu_custom_call" | custom-call | bytes 589824 | tf_op jit(solution)/shard_map/pallas_call | solution.py:485
  2.6 0.1 collective-permute-start
  2.7 4.5 %collective-permute-start.1 = (f32[128,128]{1,0:T(8,128)}, f32[128,128]{1,0:T(8,128)S(1)}, u32[]{:S(2)}, u32[]{:S(2)}) collective-permute-start(f32[128,128]{1,0:T(8,128)} %get-tuple-element.24), channel_id=1, source_target_pairs={{1,2},{2,1},{5,6},{6,5},{9,10},{10,9},{13,14},{14,13},{17,18},{18,... | collective-permute-start | bytes 196616 | tf_op jit(solution)/shard_map/ppermute | solution.py:439
  7.2 1.3 %collective-permute-start.2 = (f32[64,128]{1,0:T(8,128)}, f32[64,128]{1,0:T(8,128)S(1)}, u32[]{:S(2)}, u32[]{:S(2)}) collective-permute-start(f32[64,128]{1,0:T(8,128)} %get-tuple-element.25), channel_id=1, source_target_pairs={{0,4},{4,0},{8,12},{12,8},{16,20},{20,16},{24,28},{28,24},{1,5},{5... | collective-permute-start | bytes 98312 | tf_op jit(solution)/shard_map/ppermute | solution.py:439
  8.5 3.3 %collective-permute-start.3 = (f32[64,128]{1,0:T(8,128)}, f32[64,128]{1,0:T(8,128)S(1)}, u32[]{:S(2)}, u32[]{:S(2)}) collective-permute-start(f32[64,128]{1,0:T(8,128)} %get-tuple-element.26), channel_id=1, source_target_pairs={{4,8},{12,16},{20,24},{28,0},{8,4},{16,12},{24,20},{0,28},{5,9},{1... | collective-permute-start | bytes 98312 | tf_op jit(solution)/shard_map/ppermute | solution.py:439
  11.8 1.4 %shard_map.139.partial = f32[128,16,128]{2,1,0:T(8,128)S(1)} custom-call(s32[16]{0:T(128)S(1)} %copy-done.7, s32[16]{0:T(128)S(1)} %copy-done.8, f32[128,16,128]{2,1,0:T(8,128)S(1)} %copy-done, f32[128,16,128]{2,1,0:T(8,128)S(1)} %copy-done.3), custom_call_target="tpu_custom_call" | custom-call | bytes 3145728 | tf_op jit(solution)/shard_map/pallas_call | solution.py:502
  13.2 1.0 %collective-permute-done.3.sector_link.refs_4_ = f32[64,128]{1,0:T(8,128)S(1)} collective-permute-done((f32[64,128]{1,0:T(8,128)}, f32[64,128]{1,0:T(8,128)S(1)}, u32[]{:S(2)}, u32[]{:S(2)}) %collective-permute-start.3) | collective-permute-done | bytes 32800 | tf_op jit(solution)/shard_map/ppermute | solution.py:439
  14.2 0.0 collective-permute-done.radial_pair
  14.2 0.0 collective-permute-done.1.radial_link
  14.2 4.2 %shard_map.141 = (f32[128,16,128]{2,1,0:T(8,128)}, f32[8,256,128]{2,1,0:T(8,128)}) custom-call(f32[128,16,128]{2,1,0:T(8,128)S(1)} %shard_map.139.partial, f32[128,16,128]{2,1,0:T(8,128)S(1)} %copy-done, f32[128,128]{1,0:T(8,128)S(1)} %collective-permute-done.radial_pair, f32[128,128]{1,0:T(8,128)S(1)} %collective-permute-done.1.radial_link, ...), custom_call_target="tpu_custom_call" | custom-call | bytes 6291456 | tf_op jit(solution)/shard_map/pallas_call | solution.py:507
  18.4 0.0 copy-start.4
  18.4 4.7 %all-to-all-start = ((f32[8,256,128]{2,1,0:T(8,128)}), f32[8,256,128]{2,1,0:T(8,128)}, u32[]{:S(2)}, u32[]{:S(2)}) async-start(f32[8,256,128]{2,1,0:T(8,128)} %get-tuple-element.28), calls=%async_computation | async-start | bytes 2097152 | tf_op jit(solution)/shard_map/all_to_all | solution.py:455
  23.1 0.0 copy-start.2
  23.1 1.2 %copy-done.2 = f32[128,16,128]{2,1,0:T(8,128)S(1)} copy-done((f32[128,16,128]{2,1,0:T(8,128)S(1)}, f32[128,16,128]{2,1,0:T(8,128)}, u32[]{:S(2)}) %copy-start.2) | copy-done | bytes 1048600
  24.4 2.1 %shard_map.143 = (f32[3,128,128]{2,1,0:T(8,128)S(1)}, f32[16,128]{1,0:T(8,128)S(1)}, f32[16,128]{1,0:T(8,128)S(1)}, f32[16,128]{1,0:T(8,128)S(1)}, f32[16,128]{1...) custom-call(f32[128,16,128]{2,1,0:T(8,128)S(1)} %copy-done, ...), custom_call_target="tpu_custom_call" | custom-call | bytes 786432 | tf_op jit(solution)/shard_map/pallas_call | solution.py:518
  26.5 1.5 %collective-permute-start.6 = (f32[16,128]{1,0:T(8,128)S(1)}, f32[16,128]{1,0:T(8,128)S(1)}, u32[]{:S(2)}, u32[]{:S(2)}) collective-permute-start(f32[16,128]{1,0:T(8,128)S(1)} %get-tuple-element.33), channel_id=1, source_target_pairs={{0,4},{4,0},{8,12},{12,8},{16,20},{20,16},{24,28},{28,24},{1,5},{5... | collective-permute-start | bytes 24584 | tf_op jit(solution)/shard_map/ppermute | solution.py:443
  28.0 1.2 %collective-permute-start.7 = (f32[16,128]{1,0:T(8,128)S(1)}, f32[16,128]{1,0:T(8,128)S(1)}, u32[]{:S(2)}, u32[]{:S(2)}) collective-permute-start(f32[16,128]{1,0:T(8,128)S(1)} %get-tuple-element.34), channel_id=1, source_target_pairs={{0,8},{4,12},{8,0},{12,4},{16,24},{20,28},{24,16},{28,20},{1,9},{5... | collective-permute-start | bytes 24584 | tf_op jit(solution)/shard_map/ppermute | solution.py:443
  29.2 0.1 reshape.11
  29.3 0.1 collective-permute-start.8
  29.4 2.3 %collective-permute-start.9 = (f32[16,128]{1,0:T(8,128)S(1)}, f32[16,128]{1,0:T(8,128)S(1)}, u32[]{:S(2)}, u32[]{:S(2)}) collective-permute-start(f32[16,128]{1,0:T(8,128)S(1)} %get-tuple-element.36), channel_id=1, source_target_pairs={{0,16},{4,20},{8,24},{12,28},{16,0},{20,4},{24,8},{28,12},{1,17},{... | collective-permute-start | bytes 24584 | tf_op jit(solution)/shard_map/ppermute | solution.py:443
  31.7 1.2 %collective-permute-start.10 = (f32[16,128]{1,0:T(8,128)S(1)}, f32[16,128]{1,0:T(8,128)S(1)}, u32[]{:S(2)}, u32[]{:S(2)}) collective-permute-start(f32[16,128]{1,0:T(8,128)S(1)} %get-tuple-element.37), channel_id=1, source_target_pairs={{0,20},{4,16},{8,28},{12,24},{16,4},{20,0},{24,12},{28,8},{1,21},{... | collective-permute-start | bytes 24584 | tf_op jit(solution)/shard_map/ppermute | solution.py:443
  32.9 3.0 %collective-permute-start.11 = (f32[16,128]{1,0:T(8,128)S(1)}, f32[16,128]{1,0:T(8,128)S(1)}, u32[]{:S(2)}, u32[]{:S(2)}) collective-permute-start(f32[16,128]{1,0:T(8,128)S(1)} %get-tuple-element.38), channel_id=1, source_target_pairs={{0,24},{4,28},{8,16},{12,20},{16,8},{20,12},{24,0},{28,4},{1,25},{... | collective-permute-start | bytes 24584 | tf_op jit(solution)/shard_map/ppermute | solution.py:443
  35.9 6.4 %collective-permute-done.7.refs_2_ = f32[16,128]{1,0:T(8,128)S(1)} collective-permute-done((f32[16,128]{1,0:T(8,128)S(1)}, f32[16,128]{1,0:T(8,128)S(1)}, u32[]{:S(2)}, u32[]{:S(2)}) %collective-permute-start.7) | collective-permute-done | bytes 8224 | tf_op jit(solution)/shard_map/ppermute | solution.py:443
  42.3 2.9 %collective-permute-start.12 = (f32[16,128]{1,0:T(8,128)S(1)}, f32[16,128]{1,0:T(8,128)S(1)}, u32[]{:S(2)}, u32[]{:S(2)}) collective-permute-start(f32[16,128]{1,0:T(8,128)S(1)} %get-tuple-element.39), channel_id=1, source_target_pairs={{0,28},{4,24},{8,20},{12,16},{16,12},{20,8},{24,4},{28,0},{1,29},{... | collective-permute-start | bytes 24584 | tf_op jit(solution)/shard_map/ppermute | solution.py:443
  45.2 0.2 slice_reduce_fusion
  45.4 0.5 slice.27
  45.9 0.0 collective-permute-done.8.refs_3_
  45.9 4.8 %collective-permute-done.9.refs_4_ = f32[16,128]{1,0:T(8,128)S(1)} collective-permute-done((f32[16,128]{1,0:T(8,128)S(1)}, f32[16,128]{1,0:T(8,128)S(1)}, u32[]{:S(2)}, u32[]{:S(2)}) %collective-permute-start.9) | collective-permute-done | bytes 8224 | tf_op jit(solution)/shard_map/ppermute | solution.py:443
  50.7 0.4 collective-permute-done.10.refs_5_
  51.1 0.4 shard_map.144
  51.5 0.4 collective-permute-start.13
  51.9 0.1 slice_reduce_fusion.3
  52.0 0.7 concatenate.3
  52.8 0.1 collective-permute-done.13
  52.9 0.1 collective-permute-start.14
  52.9 2.0 %shard_map.142 = (f32[256,1024]{1,0:T(8,128)S(1)}, f32[48,1024]{1,0:T(8,128)S(1)}, f32[48,1024]{1,0:T(8,128)S(1)}) custom-call(f32[8,256,128]{2,1,0:T(8,128)} %all-to-all-done.refs_0_, bf16[768,1024]{1,0:T(8,128)(2,1)S(1)} %copy-done.1), custom_call_target="tpu_custom_call" | custom-call | bytes 4325376 | tf_op jit(solution)/shard_map/pallas_call | solution.py:525
  55.0 0.4 collective-permute-start.4
  55.4 3.5 %collective-permute-start.5 = (f32[48,1024]{1,0:T(8,128)S(1)}, f32[48,1024]{1,0:T(8,128)S(1)}, u32[]{:S(2)}, u32[]{:S(2)}) collective-permute-start(f32[48,1024]{1,0:T(8,128)S(1)} %get-tuple-element.31), channel_id=1, source_target_pairs={{1,2},{2,1},{5,6},{6,5},{9,10},{10,9},{13,14},{14,13},{17,18},{18,... | collective-permute-start | bytes 589832 | tf_op jit(solution)/shard_map/ppermute | solution.py:439
  59.0 3.4 %collective-permute-done.5.link = f32[48,1024]{1,0:T(8,128)S(1)} collective-permute-done((f32[48,1024]{1,0:T(8,128)S(1)}, f32[48,1024]{1,0:T(8,128)S(1)}, u32[]{:S(2)}, u32[]{:S(2)}) %collective-permute-start.5) | collective-permute-done | bytes 196640 | tf_op jit(solution)/shard_map/ppermute | solution.py:439
  62.4 2.4 %shard_map.145 = (f32[8,256,128]{2,1,0:T(8,128)}, f32[3,128,128]{2,1,0:T(8,128)S(1)}) custom-call(f32[256,1024]{1,0:T(8,128)S(1)} %get-tuple-element.29.modes, f32[48,1024]{1,0:T(8,128)S(1)} %collective-permute-done.4.pair, f32[48,1024]{1,0:T(8,128)S(1)} %collective-permute-done.5.link, f32[16,1024]{1,0:T(8,128)S(1)} %add.16.wave, ...), custom_call_target="tpu_custom_call", output_to_operand_aliasing={{1}: (8, {})} | custom-call | bytes 3735552 | tf_op jit(solution)/shard_map/pallas_call | solution.py:536
  64.8 3.6 %all-to-all-start.1 = ((f32[8,256,128]{2,1,0:T(8,128)}), f32[8,256,128]{2,1,0:T(8,128)S(1)}, u32[]{:S(2)}, u32[]{:S(2)}) async-start(f32[8,256,128]{2,1,0:T(8,128)} %get-tuple-element.41), calls=%async_computation.1 | async-start | bytes 2097152 | tf_op jit(solution)/shard_map/all_to_all | solution.py:455
  68.3 0.1 collective-permute-start.15
  68.4 1.4 %collective-permute-done.15 = f32[3,128,128]{2,1,0:T(8,128)S(1)} collective-permute-done((f32[3,128,128]{2,1,0:T(8,128)S(1)}, f32[3,128,128]{2,1,0:T(8,128)S(1)}, u32[]{:S(2)}, u32[]{:S(2)}) %collective-permute-start.15) | collective-permute-done | bytes 196640 | tf_op jit(solution)/shard_map/ppermute | solution.py:443
  69.9 1.5 %collective-permute-start.16 = (f32[3,128,128]{2,1,0:T(8,128)S(1)}, f32[3,128,128]{2,1,0:T(8,128)S(1)}, u32[]{:S(2)}, u32[]{:S(2)}) collective-permute-start(f32[3,128,128]{2,1,0:T(8,128)S(1)} %add.18), channel_id=1, source_target_pairs={{0,2},{1,3},{2,0},{3,1},{4,6},{5,7},{6,4},{7,5},{8,10},{9,11},{10,... | collective-permute-start | bytes 589832 | tf_op jit(solution)/shard_map/ppermute | solution.py:443
  71.3 4.9 %collective-permute-done.16 = f32[3,128,128]{2,1,0:T(8,128)S(1)} collective-permute-done((f32[3,128,128]{2,1,0:T(8,128)S(1)}, f32[3,128,128]{2,1,0:T(8,128)S(1)}, u32[]{:S(2)}, u32[]{:S(2)}) %collective-permute-start.16) | collective-permute-done | bytes 196640 | tf_op jit(solution)/shard_map/ppermute | solution.py:443
  76.2 0.7 add.19
  76.9 13.6 %all-to-all-done.1.received = f32[8,256,128]{2,1,0:T(8,128)S(1)} async-done(((f32[8,256,128]{2,1,0:T(8,128)}), f32[8,256,128]{2,1,0:T(8,128)S(1)}, u32[]{:S(2)}, u32[]{:S(2)}) %all-to-all-start.1) | async-done | bytes 1048608 | tf_op jit(solution)/shard_map/all_to_all | solution.py:455
  90.5 1.9 %shard_map.146 = f32[128,16,128]{2,1,0:T(8,128)} custom-call(f32[8,256,128]{2,1,0:T(8,128)S(1)} %all-to-all-done.1.received, f32[128,128]{1,0:T(8,128)S(1)} %copy-done.5), custom_call_target="tpu_custom_call" | custom-call | bytes 3145728 | tf_op jit(solution)/shard_map/pallas_call | solution.py:549
  (34 shorter events, 0.1 us)
Async XLA Ops:
  0.6 11.1 %copy-start = (f32[128,16,128]{2,1,0:T(8,128)S(1)}, f32[128,16,128]{2,1,0:T(8,128)}, u32[]{:S(2)}) copy-start(f32[128,16,128]{2,1,0:T(8,128)} %refs_0_.3) | copy-start | bytes 3145732
  0.6 11.1 %copy-start.3 = (f32[128,16,128]{2,1,0:T(8,128)S(1)}, f32[128,16,128]{2,1,0:T(8,128)}, u32[]{:S(2)}) copy-start(f32[128,16,128]{2,1,0:T(8,128)} %swirl.1) | copy-start | bytes 3145732
  0.7 11.1 %copy-start.8 = (s32[16]{0:T(128)S(1)}, s32[16]{0:T(128)}, u32[]{:S(2)}) copy-start(s32[16]{0:T(128)} %refs_1_.3) | copy-start | bytes 196
  0.7 11.1 %copy-start.7 = (s32[16]{0:T(128)S(1)}, s32[16]{0:T(128)}, u32[]{:S(2)}) copy-start(s32[16]{0:T(128)} %refs_0_.2) | copy-start | bytes 196
  2.6 11.6 %collective-permute-start = (f32[128,128]{1,0:T(8,128)}, f32[128,128]{1,0:T(8,128)S(1)}, u32[]{:S(2)}, u32[]{:S(2)}) collective-permute-start(f32[128,128]{1,0:T(8,128)} %get-tuple-element.23), channel_id=1, source_target_pairs={{0,1},{1,0},{2,3},{3,2},{4,5},{5,4},{6,7},{7,6},{8,9},{9,8},{10,11... | collective-permute-start | bytes 196616 | tf_op jit(solution)/shard_map/ppermute | solution.py:439
  2.7 11.5 %collective-permute-start.1 = (f32[128,128]{1,0:T(8,128)}, f32[128,128]{1,0:T(8,128)S(1)}, u32[]{:S(2)}, u32[]{:S(2)}) collective-permute-start(f32[128,128]{1,0:T(8,128)} %get-tuple-element.24), channel_id=1, source_target_pairs={{1,2},{2,1},{5,6},{6,5},{9,10},{10,9},{13,14},{14,13},{17,18},{18,... | collective-permute-start | bytes 196616 | tf_op jit(solution)/shard_map/ppermute | solution.py:439
  7.2 6.0 %collective-permute-start.2 = (f32[64,128]{1,0:T(8,128)}, f32[64,128]{1,0:T(8,128)S(1)}, u32[]{:S(2)}, u32[]{:S(2)}) collective-permute-start(f32[64,128]{1,0:T(8,128)} %get-tuple-element.25), channel_id=1, source_target_pairs={{0,4},{4,0},{8,12},{12,8},{16,20},{20,16},{24,28},{28,24},{1,5},{5... | collective-permute-start | bytes 98312 | tf_op jit(solution)/shard_map/ppermute | solution.py:439
  8.5 5.7 %copy-start.5 = (f32[128,128]{1,0:T(8,128)S(1)}, f32[128,128]{1,0:T(8,128)}, u32[]{:S(2)}) copy-start(f32[128,128]{1,0:T(8,128)} %constant.12.clone.basis.refs_5_) | copy-start | bytes 196612
  8.5 5.7 %collective-permute-start.3 = (f32[64,128]{1,0:T(8,128)}, f32[64,128]{1,0:T(8,128)S(1)}, u32[]{:S(2)}, u32[]{:S(2)}) collective-permute-start(f32[64,128]{1,0:T(8,128)} %get-tuple-element.26), channel_id=1, source_target_pairs={{4,8},{12,16},{20,24},{28,0},{8,4},{16,12},{24,20},{0,28},{5,9},{1... | collective-permute-start | bytes 98312 | tf_op jit(solution)/shard_map/ppermute | solution.py:439
  18.4 4.7 %copy-start.4 = (f32[3,128,128]{2,1,0:T(8,128)S(1)}, f32[3,128,128]{2,1,0:T(8,128)}, u32[]{:S(2)}) copy-start(f32[3,128,128]{2,1,0:T(8,128)} %refs_2_.3) | copy-start | bytes 589828
  18.4 34.5 %all-to-all-start = ((f32[8,256,128]{2,1,0:T(8,128)}), f32[8,256,128]{2,1,0:T(8,128)}, u32[]{:S(2)}, u32[]{:S(2)}) async-start(f32[8,256,128]{2,1,0:T(8,128)} %get-tuple-element.28), calls=%async_computation | async-start | bytes 2097152 | tf_op jit(solution)/shard_map/all_to_all | solution.py:455
  23.1 1.2 %copy-start.2 = (f32[128,16,128]{2,1,0:T(8,128)S(1)}, f32[128,16,128]{2,1,0:T(8,128)}, u32[]{:S(2)}) copy-start(f32[128,16,128]{2,1,0:T(8,128)} %refs_1_.4) | copy-start | bytes 3145732
  24.4 4.8 %slice-start = ((f32[513]{0:T(1024)}), f32[512]{0:T(512)S(1)}, s32[]{:S(2)}) async-start(f32[513]{0:T(1024)} %param.16), calls=%async_computation.2 | async-start | bytes 4096 | tf_op jit(solution)/shard_map/slice | solution.py:79
  24.4 21.0 %copy-start.9 = (f32[513]{0:T(1024)S(1)}, f32[513]{0:T(1024)}, u32[]{:S(2)}) copy-start(f32[513]{0:T(1024)} %param.16) | copy-start | bytes 6160
  24.4 26.7 %copy-start.1 = (bf16[768,1024]{1,0:T(8,128)(2,1)S(1)}, bf16[768,1024]{1,0:T(8,128)(2,1)}, u32[]{:S(2)}) copy-start(bf16[768,1024]{1,0:T(8,128)(2,1)} %constant.14.clone.refs_1_.refs_8_.table) | copy-start | bytes 4718596
  26.5 6.4 %collective-permute-start.6 = (f32[16,128]{1,0:T(8,128)S(1)}, f32[16,128]{1,0:T(8,128)S(1)}, u32[]{:S(2)}, u32[]{:S(2)}) collective-permute-start(f32[16,128]{1,0:T(8,128)S(1)} %get-tuple-element.33), channel_id=1, source_target_pairs={{0,4},{4,0},{8,12},{12,8},{16,20},{20,16},{24,28},{28,24},{1,5},{5... | collective-permute-start | bytes 24584 | tf_op jit(solution)/shard_map/ppermute | solution.py:443
  28.0 14.3 %collective-permute-start.7 = (f32[16,128]{1,0:T(8,128)S(1)}, f32[16,128]{1,0:T(8,128)S(1)}, u32[]{:S(2)}, u32[]{:S(2)}) collective-permute-start(f32[16,128]{1,0:T(8,128)S(1)} %get-tuple-element.34), channel_id=1, source_target_pairs={{0,8},{4,12},{8,0},{12,4},{16,24},{20,28},{24,16},{28,20},{1,9},{5... | collective-permute-start | bytes 24584 | tf_op jit(solution)/shard_map/ppermute | solution.py:443
  29.3 16.6 %collective-permute-start.8 = (f32[16,128]{1,0:T(8,128)S(1)}, f32[16,128]{1,0:T(8,128)S(1)}, u32[]{:S(2)}, u32[]{:S(2)}) collective-permute-start(f32[16,128]{1,0:T(8,128)S(1)} %get-tuple-element.35), channel_id=1, source_target_pairs={{0,12},{4,8},{8,4},{12,0},{16,28},{20,24},{24,20},{28,16},{1,13},{... | collective-permute-start | bytes 24584 | tf_op jit(solution)/shard_map/ppermute | solution.py:443
  29.4 21.3 %collective-permute-start.9 = (f32[16,128]{1,0:T(8,128)S(1)}, f32[16,128]{1,0:T(8,128)S(1)}, u32[]{:S(2)}, u32[]{:S(2)}) collective-permute-start(f32[16,128]{1,0:T(8,128)S(1)} %get-tuple-element.36), channel_id=1, source_target_pairs={{0,16},{4,20},{8,24},{12,28},{16,0},{20,4},{24,8},{28,12},{1,17},{... | collective-permute-start | bytes 24584 | tf_op jit(solution)/shard_map/ppermute | solution.py:443
  31.7 19.4 %collective-permute-start.10 = (f32[16,128]{1,0:T(8,128)S(1)}, f32[16,128]{1,0:T(8,128)S(1)}, u32[]{:S(2)}, u32[]{:S(2)}) collective-permute-start(f32[16,128]{1,0:T(8,128)S(1)} %get-tuple-element.37), channel_id=1, source_target_pairs={{0,20},{4,16},{8,28},{12,24},{16,4},{20,0},{24,12},{28,8},{1,21},{... | collective-permute-start | bytes 24584 | tf_op jit(solution)/shard_map/ppermute | solution.py:443
  32.9 18.2 %collective-permute-start.11 = (f32[16,128]{1,0:T(8,128)S(1)}, f32[16,128]{1,0:T(8,128)S(1)}, u32[]{:S(2)}, u32[]{:S(2)}) collective-permute-start(f32[16,128]{1,0:T(8,128)S(1)} %get-tuple-element.38), channel_id=1, source_target_pairs={{0,24},{4,28},{8,16},{12,20},{16,8},{20,12},{24,0},{28,4},{1,25},{... | collective-permute-start | bytes 24584 | tf_op jit(solution)/shard_map/ppermute | solution.py:443
  42.3 8.8 %collective-permute-start.12 = (f32[16,128]{1,0:T(8,128)S(1)}, f32[16,128]{1,0:T(8,128)S(1)}, u32[]{:S(2)}, u32[]{:S(2)}) collective-permute-start(f32[16,128]{1,0:T(8,128)S(1)} %get-tuple-element.39), channel_id=1, source_target_pairs={{0,28},{4,24},{8,20},{12,16},{16,12},{20,8},{24,4},{28,0},{1,29},{... | collective-permute-start | bytes 24584 | tf_op jit(solution)/shard_map/ppermute | solution.py:443
  51.5 7.4 %copy-start.10 = (f32[1024]{0:T(1024)S(1)}, f32[1024]{0:T(1024)}, u32[]{:S(2)}) copy-start(f32[1024]{0:T(1024)} %constant.16.clone) | copy-start | bytes 12292
  51.5 7.4 %copy-start.11 = (f32[1024]{0:T(1024)S(1)}, f32[1024]{0:T(1024)}, u32[]{:S(2)}) copy-start(f32[1024]{0:T(1024)} %constant.15.clone) | copy-start | bytes 12292
  51.5 10.9 %copy-start.6 = (f32[8,16,128]{2,1,0:T(8,128)S(1)}, f32[8,16,128]{2,1,0:T(8,128)}, u32[]{:S(2)}) copy-start(f32[8,16,128]{2,1,0:T(8,128)} %constant.13.clone.axial) | copy-start | bytes 196612
  51.5 1.3 %collective-permute-start.13 = (f32[16,1024]{1,0:T(8,128)S(1)}, f32[16,1024]{1,0:T(8,128)S(1)}, u32[]{:S(2)}, u32[]{:S(2)}) collective-permute-start(f32[16,1024]{1,0:T(8,128)S(1)} %shard_map.144), channel_id=1, source_target_pairs={{0,1},{1,0},{2,3},{3,2},{4,5},{5,4},{6,7},{7,6},{8,9},{9,8},{10,11... | collective-permute-start | bytes 196616 | tf_op jit(solution)/shard_map/ppermute | solution.py:443
  52.9 6.1 %collective-permute-start.14 = (f32[16,1024]{1,0:T(8,128)S(1)}, f32[16,1024]{1,0:T(8,128)S(1)}, u32[]{:S(2)}, u32[]{:S(2)}) collective-permute-start(f32[16,1024]{1,0:T(8,128)S(1)} %add.15), channel_id=1, source_target_pairs={{0,2},{1,3},{2,0},{3,1},{4,6},{5,7},{6,4},{7,5},{8,10},{9,11},{10,... | collective-permute-start | bytes 196616 | tf_op jit(solution)/shard_map/ppermute | solution.py:443
  55.0 4.0 %collective-permute-start.4 = (f32[48,1024]{1,0:T(8,128)S(1)}, f32[48,1024]{1,0:T(8,128)S(1)}, u32[]{:S(2)}, u32[]{:S(2)}) collective-permute-start(f32[48,1024]{1,0:T(8,128)S(1)} %get-tuple-element.30), channel_id=1, source_target_pairs={{0,1},{1,0},{2,3},{3,2},{4,5},{5,4},{6,7},{7,6},{8,9},{9,8},{10,11... | collective-permute-start | bytes 589832 | tf_op jit(solution)/shard_map/ppermute | solution.py:439
  55.4 7.0 %collective-permute-start.5 = (f32[48,1024]{1,0:T(8,128)S(1)}, f32[48,1024]{1,0:T(8,128)S(1)}, u32[]{:S(2)}, u32[]{:S(2)}) collective-permute-start(f32[48,1024]{1,0:T(8,128)S(1)} %get-tuple-element.31), channel_id=1, source_target_pairs={{1,2},{2,1},{5,6},{6,5},{9,10},{10,9},{13,14},{14,13},{17,18},{18,... | collective-permute-start | bytes 589832 | tf_op jit(solution)/shard_map/ppermute | solution.py:439
  64.8 25.8 %all-to-all-start.1 = ((f32[8,256,128]{2,1,0:T(8,128)}), f32[8,256,128]{2,1,0:T(8,128)S(1)}, u32[]{:S(2)}, u32[]{:S(2)}) async-start(f32[8,256,128]{2,1,0:T(8,128)} %get-tuple-element.41), calls=%async_computation.1 | async-start | bytes 2097152 | tf_op jit(solution)/shard_map/all_to_all | solution.py:455
  68.3 1.5 %collective-permute-start.15 = (f32[3,128,128]{2,1,0:T(8,128)S(1)}, f32[3,128,128]{2,1,0:T(8,128)S(1)}, u32[]{:S(2)}, u32[]{:S(2)}) collective-permute-start(f32[3,128,128]{2,1,0:T(8,128)S(1)} %get-tuple-element.42), channel_id=1, source_target_pairs={{0,1},{1,0},{2,3},{3,2},{4,5},{5,4},{6,7},{7,6},{8,9},{9,8},{10,11... | collective-permute-start | bytes 589832 | tf_op jit(solution)/shard_map/ppermute | solution.py:443
  69.9 6.4 %collective-permute-start.16 = (f32[3,128,128]{2,1,0:T(8,128)S(1)}, f32[3,128,128]{2,1,0:T(8,128)S(1)}, u32[]{:S(2)}, u32[]{:S(2)}) collective-permute-start(f32[3,128,128]{2,1,0:T(8,128)S(1)} %add.18), channel_id=1, source_target_pairs={{0,2},{1,3},{2,0},{3,1},{4,6},{5,7},{6,4},{7,5},{8,10},{9,11},{10,... | collective-permute-start | bytes 589832 | tf_op jit(solution)/shard_map/ppermute | solution.py:443

commit v6 on v5

--- a/solution.py
+++ b/solution.py
@@ -8,6 +8,7 @@
 from jax.experimental.pallas import tpu as pltpu
 from jax.sharding import PartitionSpec as P
 
+
 BURNERS = 16
 MOUTH = 8
 SWEEPS = 4
@@ -74,14 +75,6 @@
     return (4.0 + shifted).astype(np.float32), weight.astype(np.float32)
 
 
-def mode_rows(impedance):
-    half = impedance.shape[0] - 1
-    by_four = impedance[:half].reshape(half // 4, 4).T
-    q0, q1, q2, q3 = by_four[0], by_four[1], by_four[2], by_four[3]
-    first = jnp.concatenate([impedance[half:], q0[1:]])
-    return jnp.concatenate([q0, first, q2, q2, q1, q3, q1, q3])
-
-
 def split(value):
     high = value.astype(BF16)
     return high, (value - high.astype(F32)).astype(BF16)
@@ -98,13 +91,9 @@
 NT = ((1,), (1,))
 
 
-def edges_kernel(
-    density, swirl, heat_rate, acoustic, radial_pair, radial_link, sector_pair, sector_link, rho,
-    rate, spin, wave, rim, sems
-):
+def edges_kernel(density, swirl, heat_rate, acoustic, pair, link, rho, rate, spin, wave, sems):
     cells_theta, cells_radius, _ = density.shape
-    radial_odd = lax.axis_index("radial") % 2
-    sector_odd = lax.axis_index("sector") % 2
+    odd = lax.axis_index("sector") % 2
     copies = []
 
     def fetch(source, target):
@@ -117,13 +106,9 @@
         fetch(heat_rate.at[pl.ds(begin, EDGE)], rate.at[side])
         fetch(swirl.at[pl.ds(row, 1)], spin.at[side])
         fetch(acoustic.at[:, pl.ds(begin, EDGE)], wave.at[side])
-    fetch(density.at[:, 0, :], rim.at[0])
-    fetch(density.at[:, cells_radius - 1, :], rim.at[1])
     for copy in copies:
         copy.wait()
-    radial_pair[...] = rim[1 - radial_odd]
-    radial_link[...] = rim[radial_odd]
-    for out, side in ((sector_pair, 1 - sector_odd), (sector_link, sector_odd)):
+    for out, side in ((pair, 1 - odd), (link, odd)):
         edge = jnp.where(side == 0, rho[0, 0], rho[1, EDGE - 1])
         out[0:cells_radius] = edge
         out[cells_radius : 2 * cells_radius] = edge * spin[side, 0]
@@ -135,7 +120,7 @@
         out[at : at + EDGE] = heat
 
 
-def flow_kernel(n_theta, mouth_azimuth, mouth_radius, density, swirl, forcing):
+def flow_rows(n_theta, mouth_azimuth, mouth_radius, density, swirl, forcing):
     sector = lax.axis_index("sector")
     radial = lax.axis_index("radial")
     cells_theta, cells_radius, cells_axial = density.shape
@@ -173,29 +158,10 @@
         forcing[t] = -0.5 * (flux_up - flux_down) + diffusion * laplace + gain * (1.0 - rho)
 
 
-def sine_modes(basis, fields):
-    high, low = split(basis)
-    count = high.shape[0]
-    left = jnp.concatenate(
-        [jnp.concatenate([high, high], 1), jnp.concatenate([low, jnp.zeros_like(low)], 1)], 0
-    )
-    right = jnp.concatenate([jnp.concatenate(split(field), 1) for field in fields], 0)
-    out = lax.dot_general(left, right, (NT, ((), ())), preferred_element_type=F32)
-    return out[:count] + out[count:]
-
-
-GROUP = 4
-
-
-def spread_kernel(
-    partial, density, radial_pair, radial_link, sector_pair, sector_link, basis, density_next, send,
-    forcing, following, staged, sems
-):
+def add_halos(forcing, radial_pair, radial_link, sector_pair, sector_link):
     radials = lax.axis_size("radial")
     radial = lax.axis_index("radial")
-    cells_theta, cells_radius, cells_axial = partial.shape
-    sectors = send.shape[0]
-    own = cells_axial // sectors
+    cells_theta, cells_radius, _ = forcing.shape
     odd = lax.axis_index("sector") % 2 == 1
     above = jnp.where(odd, sector_link[...], sector_pair[...])
     below = jnp.where(odd, sector_pair[...], sector_link[...])
@@ -204,16 +170,63 @@
     outer = jnp.where(odd, radial_link[...], radial_pair[...])
     rho, flux = slice(0, cells_radius), slice(cells_radius, 2 * cells_radius)
     end = cells_theta - 1
-    forcing[...] = partial[...]
     forcing[0] = forcing[0] + (0.5 * below[flux] + diffusion * below[rho])
     forcing[end] = forcing[end] + (diffusion * above[rho] - 0.5 * above[flux])
     inside = diffusion * (radial > 0).astype(F32)
     outside = diffusion * (radial < radials - 1).astype(F32)
     forcing[:, 0, :] = forcing[:, 0, :] + inside * inner
     forcing[:, cells_radius - 1, :] = forcing[:, cells_radius - 1, :] + outside * outer
-    following[...] = density[...] + time_step * forcing[...]
-    copies = [pltpu.make_async_copy(following, density_next, sems.at[0])]
-    copies[0].start()
+    return above, below
+
+
+def flow_kernel(
+    n_theta, mouth_azimuth, mouth_radius, density, swirl, heat_rate, _, forcing, heat, pair, link
+):
+    cells_theta, cells_radius, _ = density.shape
+    odd = lax.axis_index("radial") % 2 == 1
+    first, last = density[:, 0, :], density[:, cells_radius - 1, :]
+    pair[...] = jnp.where(odd, first, last)
+    link[...] = jnp.where(odd, last, first)
+    flow_rows(n_theta, mouth_azimuth, mouth_radius, density, swirl, forcing)
+    for t in range(0, cells_theta, 8):
+        rho = density[t : t + 8]
+        heat[t : t + 8] = jnp.sum(heat_rate[t : t + 8] * rho * rho, axis=1)
+
+
+def sine_modes(basis, fields):
+    high, low = split(basis)
+    count = high.shape[0]
+    left = jnp.concatenate(
+        [jnp.concatenate([high, high], 1), jnp.concatenate([low, jnp.zeros_like(low)], 1)], 0
+    )
+    right = jnp.concatenate([jnp.concatenate(split(field), 1) for field in fields], 0)
+    out = lax.dot_general(left, right, (NT, ((), ())), preferred_element_type=F32)
+    return out[:count] + out[count:]
+
+
+GROUP = 4
+
+
+def first_kernel(
+    n_radius, partial, heat, acoustic, radial_pair, radial_link, sector_pair, sector_link, basis,
+    state, send, forcing, following, staged, sems
+):
+    radial = lax.axis_index("radial")
+    cells_theta, cells_radius, cells_axial = partial.shape
+    sectors = send.shape[0]
+    own = cells_axial // sectors
+    forcing[...] = partial[...]
+    above, below = add_halos(forcing, radial_pair, radial_link, sector_pair, sector_link)
+    copies = []
+
+    def leave(begin, count):
+        rows = pl.ds(begin, count)
+        copy = pltpu.make_async_copy(
+            staged.at[:, rows, :], send.at[:, rows, :], sems.at[len(copies)]
+        )
+        copy.start()
+        copies.append(copy)
+
     mine = basis[...]
     for r in range(0, cells_radius, GROUP):
         modes = sine_modes(mine, [forcing[:, r + i, :] for i in range(GROUP)])
@@ -223,37 +236,14 @@
                 staged[d, (r + i) * own : (r + i + 1) * own, :] = modes[
                     d * own : (d + 1) * own, lane
                 ]
-        rows = pl.ds(r * own, GROUP * own)
-        copy = pltpu.make_async_copy(
-            staged.at[:, rows, :], send.at[:, rows, :], sems.at[len(copies)]
-        )
-        copy.start()
-        copies.append(copy)
-    for copy in copies:
-        copy.wait()
-
-
-def acoustic_kernel(
-    n_radius, density, heat_rate, acoustic, pair, link, basis, state, *slots
-):
-    sector = lax.axis_index("sector")
-    cells_theta, cells_radius, cells_axial = density.shape
-    sectors = len(slots)
-    own = cells_axial // sectors
-    share = (lax.axis_index("radial") == 0).astype(F32)
-    odd = sector % 2 == 1
-    above = jnp.where(odd, link[...], pair[...])
-    below = jnp.where(odd, pair[...], link[...])
-    heat = None
-    for r in range(cells_radius):
-        rho = density[:, r, :]
-        term = heat_rate[:, r, :] * rho * rho
-        heat = term if heat is None else heat + term
+        leave(r * own, GROUP * own)
+
+    share = (radial == 0).astype(F32)
     skip = 2 * cells_radius
 
     def extended(k):
         rows = slice(skip + k * EDGE, skip + (k + 1) * EDGE)
-        middle = acoustic[k] if k < 3 else heat
+        middle = acoustic[k] if k < 3 else heat[...]
         return jnp.concatenate([below[rows], middle, above[rows]], 0)
 
     press, along, axial = extended(0) * share, extended(1) * share, extended(2) * share
@@ -269,15 +259,18 @@
         axial_down = jnp.where(lanes == 0, 0.0, pltpu.roll(axial, 1, 1))
         press = press - wave_speed * ((along - along_down) + (axial - axial_down)) + warm
     middle = slice(EDGE, EDGE + cells_theta)
-    state[0] = press[middle]
-    state[1] = along[middle]
-    state[2] = axial[middle]
-    mine = jnp.concatenate(
-        [basis[pl.ds(pl.multiple_of((sector ^ k) * own, 8), own), :] for k in range(sectors)], 0
-    )
+    following[0] = press[middle]
+    following[1] = along[middle]
+    following[2] = axial[middle]
+    copies.append(pltpu.make_async_copy(following, state, sems.at[len(copies)]))
+    copies[-1].start()
     modes = sine_modes(mine, [feedback * press[middle]])
-    for k, slot in enumerate(slots):
-        slot[...] = modes[k * own : (k + 1) * own]
+    columns = cells_radius * own
+    for d in range(sectors):
+        staged[d, columns : columns + own, :] = modes[d * own : (d + 1) * own]
+    leave(columns, own)
+    for copy in copies:
+        copy.wait()
 
 
 def transformed(values, table, store):
@@ -310,33 +303,24 @@
     )
 
 
-def forward_kernel(edge, received, table, modes, pair, link):
-    sectors, columns, _ = received.shape
+def forward_kernel(edge, received, table, *refs):
+    modes, pair, link, wave = refs[-4:]
+    sectors = received.shape[0]
+    columns = modes.shape[0]
     radial_odd = lax.axis_index("radial") % 2 == 1
 
     def store(lane, out):
-        modes[:, lane] = out
-        first, last = out[:edge], out[columns - edge :]
+        modes[:, lane] = out[:columns]
+        first, last = out[:edge], out[columns - edge : columns]
         pair[:, lane] = jnp.where(radial_odd, first, last)
         link[:, lane] = jnp.where(radial_odd, last, first)
+        wave[:, lane] = out[columns:]
 
     transformed([received[s] for s in range(sectors)], table, store)
 
 
-def wave_kernel(*refs):
-    slots, (table, wave, pieces) = refs[:-3], refs[-3:]
-    sector = lax.axis_index("sector")
-    for k, slot in enumerate(slots):
-        pieces[sector ^ k] = slot[...]
-
-    def store(lane, out):
-        wave[:, lane] = out
-
-    transformed([pieces[s] for s in range(len(slots))], table, store)
-
-
 def solve_kernel(
-    modes, pair, link, wave, inverse, scaled, axial, table, state_in, send, state, solved
+    modes, pair, link, wave, other_wave, impedance, fixed, weight, axial, table, send, solved
 ):
     radials = lax.axis_size("radial")
     radial = lax.axis_index("radial")
@@ -352,10 +336,11 @@
     total = cells_radius + 2 * HALO
     for block in range(n_theta // step):
         lane = slice(block * step, (block + 1) * step)
-        inv = jnp.broadcast_to(inverse[:, lane], (each, step))
+        row = 1.0 / (fixed[:, lane] + impedance[:, lane])
+        inv = jnp.broadcast_to(row, (each, step))
         inv_inner, inv_outer = inv * has_inner, inv * has_outer
-        last_scale = jnp.broadcast_to(scaled[:, lane], (each, step))
-        add = wave[:, lane]
+        last_scale = jnp.broadcast_to(row * weight[:, lane], (each, step))
+        add = wave[:, lane] + other_wave[:, lane]
 
         def row_of(i):
             i -= HALO
@@ -396,7 +381,7 @@
         send[s + sectors // 2] = even[:, lane] - odd[:, lane]
 
 
-def pressure_kernel(received, basis, pressure):
+def pressure_kernel(received, basis, pressure_out, pressure, sems):
     sectors = received.shape[0]
     cells_radius = pressure.shape[1]
     own = received.shape[1] // cells_radius
@@ -405,15 +390,62 @@
         [jnp.concatenate([high, low], 1), jnp.concatenate([high, jnp.zeros_like(low)], 1)], 0
     )
     cells_axial = high.shape[1]
+    copies = []
     for r in range(cells_radius):
         rows = [received[d, r * own : (r + 1) * own, :] for d in range(sectors)]
         modes = jnp.concatenate(rows, 0)
         left = jnp.concatenate(split(modes.T), 1)
         out = lax.dot_general(left, right, (NN, ((), ())), preferred_element_type=F32)
         pressure[:, r, :] = out[:, :cells_axial] + out[:, cells_axial:]
-
-
-def call(kernel, outs, ins, scratch=(), limit=24 * 1024 * 1024, **more):
+        if r % 8 == 7:
+            rows = pl.ds(r - 7, 8)
+            copy = pltpu.make_async_copy(
+                pressure.at[:, rows, :], pressure_out.at[:, rows, :], sems.at[r // 8]
+            )
+            copy.start()
+            copies.append(copy)
+    for copy in copies:
+        copy.wait()
+
+
+def impedance_kernel(impedance, _, rows):
+    half = impedance.shape[1] - 1
+    count = half // 4
+    pieces, rest = [], jnp.broadcast_to(impedance[:, :half], (8, half))
+    for _ in range(3):
+        piece = rest.astype(BF16)
+        pieces.append(piece)
+        rest = rest - piece.astype(F32)
+    index = lax.broadcasted_iota(jnp.int32, (half, count), 0)
+    target = 4 * lax.broadcasted_iota(jnp.int32, (half, count), 1)
+    by_four = []
+    for q in range(4):
+        pick = (index == target + q).astype(F32).astype(BF16)
+        parts = [
+            lax.dot_general(piece, pick, (NN, ((), ())), preferred_element_type=F32)
+            for piece in pieces
+        ]
+        by_four.append((parts[0] + (parts[1] + parts[2]))[:1])
+    q0, q1, q2, q3 = by_four
+    lanes = lax.broadcasted_iota(jnp.int32, (1, count), 1)
+    last = jnp.broadcast_to(impedance[:, half:], (1, count))
+    rows[...] = jnp.concatenate([q0, jnp.where(lanes == 0, last, q0), q2, q2, q1, q3, q1, q3], 1)
+
+
+def add_kernel(left, right, out):
+    out[...] = left[...] + right[...]
+
+
+def step_kernel(
+    n_theta, mouth_azimuth, mouth_radius, density, swirl, radial_pair, radial_link, sector_pair,
+    sector_link, density_next, forcing
+):
+    flow_rows(n_theta, mouth_azimuth, mouth_radius, density, swirl, forcing)
+    add_halos(forcing, radial_pair, radial_link, sector_pair, sector_link)
+    density_next[...] = density[...] + time_step * forcing[...]
+
+
+def call(kernel, outs, ins, scratch=(), limit=12 * 1024 * 1024, **more):
     moved = sum(math.prod(o.shape) * 4 for o in outs)
     return pl.pallas_call(
         kernel,
@@ -443,19 +475,33 @@
     return lax.ppermute(value, axis, [(i, i ^ bits) for i in range(lax.axis_size(axis))])
 
 
-def summed(value, axis):
+def halves_of_sum(value, axis):
     step = 1
-    while step < lax.axis_size(axis):
-        value = value + swapped(value, axis, step)
+    while True:
+        other = swapped(value, axis, step)
         step *= 2
-    return value
+        if step >= lax.axis_size(axis):
+            return value, other
+        value = added(value, other)
+
+
+def added(left, right):
+    return call(add_kernel, [shape(*left.shape)], [VMEM] * 2, limit=4 * 1024 * 1024)(left, right)[0]
+
+
+def in_hbm(value):
+    return pltpu.with_memory_space_constraint(value, pltpu.HBM)
+
+
+def in_vmem(value):
+    return pltpu.with_memory_space_constraint(value, pltpu.VMEM)
 
 
 def exchanged(value):
     return lax.all_to_all(value, "sector", split_axis=0, concat_axis=0, tiled=True)
 
 
-def shards(density, swirl, heat_rate, acoustic, mode_impedance, mouth_azimuth, mouth_radius):
+def section(density, swirl, heat_rate, acoustic, mode_impedance, mouth_azimuth, mouth_radius):
     sectors = lax.axis_size("sector")
     radials = lax.axis_size("radial")
     cells_theta, cells_radius, cells_axial = density.shape
@@ -477,82 +523,84 @@
         )
     )
     fixed, weight = diagonal_tables(n_theta)
-    inverse = (1.0 / (jnp.asarray(fixed) + mode_rows(mode_impedance)))[None, :]
-    scaled = inverse * jnp.asarray(weight)[None, :]
+    fixed, weight = jnp.asarray(fixed)[None, :], jnp.asarray(weight)[None, :]
+    (impedance,) = call(impedance_kernel, [shape(1, n_theta)], [VMEM] * 2)(
+        mode_impedance[None, :], table
+    )
 
     packed = 2 * cells_radius + 4 * EDGE
     row_block = shape(cells_theta, cells_axial)
-    edges = call(
+    pair, link = call(
         edges_kernel,
-        [row_block] * 2 + [shape(packed, cells_axial)] * 2,
+        [shape(packed, cells_axial)] * 2,
         [HBM] * 4,
         [
             pltpu.VMEM((2, EDGE, cells_radius, cells_axial), F32),
             pltpu.VMEM((2, EDGE, cells_radius, cells_axial), F32),
             pltpu.VMEM((2, 1, cells_radius, cells_axial), F32),
             pltpu.VMEM((2, 3, EDGE, cells_axial), F32),
-            pltpu.VMEM((2, cells_theta, cells_axial), F32),
-            pltpu.SemaphoreType.DMA((10,)),
+            pltpu.SemaphoreType.DMA((8,)),
         ],
-        limit=None,
-    )(density, swirl, heat_rate, acoustic)
-    sector_halo = paired(edges[2], edges[3], "sector", True)
-    radial_halo = paired(edges[0], edges[1], "radial", False)
-
-    (partial,) = call(
+    )(*[in_hbm(value) for value in (density, swirl, heat_rate, acoustic)])
+    sector_halo = paired(pair, link, "sector", True)
+    edge_rows = pair
+    partial, heat, pair, link = call(
         lambda *refs: flow_kernel(n_theta, *refs),
+        [shape(*density.shape)] + [row_block] * 3,
+        [SMEM] * 2 + [VMEM] * 3 + [HBM],
+    )(mouth_azimuth, mouth_radius, density, swirl, heat_rate, edge_rows)
+    radial_halo = paired(pair, link, "radial", False)
+    state, send = call(
+        lambda *refs: first_kernel(n_radius, *refs),
+        [
+            pltpu.HBM(acoustic.shape, F32),
+            pltpu.HBM((sectors, columns + own, cells_theta), F32),
+        ],
+        [VMEM] * 8,
+        [
+            pltpu.VMEM(density.shape, F32),
+            pltpu.VMEM(acoustic.shape, F32),
+            pltpu.VMEM((sectors, columns + own, cells_theta), F32),
+            pltpu.SemaphoreType.DMA((2 + cells_radius // GROUP,)),
+        ],
+        out_specs=[HBM, HBM],
+    )(partial, heat, acoustic, *radial_halo, *sector_halo, basis)
+    received = exchanged(send)
+    (density_next,) = call(
+        lambda *refs: step_kernel(n_theta, *refs),
         [shape(*density.shape)],
-        [SMEM] * 2 + [VMEM] * 2,
-    )(mouth_azimuth, mouth_radius, density, swirl)
-    density_next, send = call(
-        spread_kernel,
-        [shape(*density.shape), shape(sectors, columns, cells_theta)],
-        [VMEM] * 7,
-        [pltpu.VMEM(density.shape, F32)] * 2
-        + [pltpu.VMEM((sectors, columns, cells_theta), F32)]
-        + [pltpu.SemaphoreType.DMA((1 + cells_radius // GROUP,))],
-        out_specs=[HBM] * 2,
-    )(partial, density, *radial_halo, *sector_halo, basis)
-    received = exchanged(send)
-
-    state, *slots = call(
-        lambda *refs: acoustic_kernel(n_radius, *refs),
-        [shape(*acoustic.shape)] + [shape(own, cells_theta)] * sectors,
-        [VMEM] * 6,
-    )(density, heat_rate, acoustic, *sector_halo, basis)
-    slots = [slots[0]] + [swapped(slots[k], "sector", k) for k in range(1, sectors)]
-
-    modes, pair, link = call(
+        [SMEM] * 2 + [VMEM] * 6,
+        [pltpu.VMEM(density.shape, F32)],
+    )(mouth_azimuth, mouth_radius, density, swirl, *radial_halo, *sector_halo)
+    acoustic_next = added(*halves_of_sum(state, "radial"))
+
+    modes, pair, link, wave = call(
         lambda *refs: forward_kernel(edge, *refs),
-        [shape(columns, n_theta)] + [shape(edge, n_theta)] * 2,
+        [shape(columns, n_theta)] + [shape(edge, n_theta)] * 2 + [shape(own, n_theta)],
+        [VMEM] * 2 + [HBM] * 3,
+    )(in_vmem(received), table, in_hbm(density_next), in_hbm(acoustic_next), impedance)
+    (send,) = call(
+        solve_kernel,
+        [shape(sectors, columns, cells_theta)],
+        [VMEM] * 10,
+        [pltpu.VMEM((columns, n_theta), F32)],
+    )(
+        modes, *paired(pair, link, "radial", False), *halves_of_sum(wave, "radial"), impedance,
+        fixed, weight, eigen, table,
+    )
+    (pressure,) = call(
+        pressure_kernel,
+        [shape(*density.shape)],
         [VMEM] * 2,
-    )(received, table)
-    (wave,) = call(
-        wave_kernel,
-        [shape(own, n_theta)],
-        [VMEM] * (sectors + 1),
-        [pltpu.VMEM((sectors, own, cells_theta), F32)],
-    )(*slots, table)
-    send, state = call(
-        solve_kernel,
-        [shape(sectors, columns, cells_theta), shape(*acoustic.shape)],
-        [VMEM] * 8 + [HBM],
-        [pltpu.VMEM((columns, n_theta), F32)],
-        out_specs=[VMEM, HBM],
-        input_output_aliases={8: 1},
-    )(
-        modes, *paired(pair, link, "radial", False), summed(wave, "radial"), inverse, scaled, eigen,
-        table, state,
-    )
-    acoustic_next = summed(state, "radial")
-
-    (pressure,) = call(pressure_kernel, [shape(*density.shape)], [VMEM] * 2)(exchanged(send), basis)
+        [pltpu.VMEM(density.shape, F32), pltpu.SemaphoreType.DMA((cells_radius // 8,))],
+        out_specs=[HBM],
+    )(exchanged(send), basis)
     return density_next, pressure, acoustic_next
 
 
 def solution(mesh):
     return jax.shard_map(
-        shards,
+        section,
         mesh=mesh,
         in_specs=(
             P("sector", "radial", None),

time: 92.8 us -> 96.8 us (1.043)
  the two profiles are of different devices: /device:TPU:1 before, /device:TPU:0 now
where the time goes in v6:
time: 96.8 us; the launch traced here: 96.5 us
  waiting for transfers between devices  30.3 us (31%)
  blocking collectives  28.2 us (29%)
  starting transfers between devices  19.3 us (20%)
  Pallas kernels  17.1 us (18%)
    all_to_all x1, blocking collectives, exchanged(): lax.all_to_all(value, 'sector', split_axis=0, concat_axis=0, tiled=True)  28.2 us
    all_to_all x1, waiting for transfers between devices, exchanged(): lax.all_to_all(value, 'sector', split_axis=0, concat_axis=0, tiled=True)  18.3 us
    ppermute x6, starting transfers between devices, paired(): return (lax.ppermute(pair, axis, first), lax.ppermute(link, axis, second))  7.68 us
    ppermute x4, waiting for transfers between devices, swapped(): lax.ppermute(value, axis, [(i, i ^ bits) for i in range(lax.axis_size(axi...  7.66 us
    ppermute x4, starting transfers between devices, swapped(): lax.ppermute(value, axis, [(i, i ^ bits) for i in range(lax.axis_size(axi...  7.25 us
    pallas_call x1, Pallas kernels, section(): call(lambda *refs: first_kernel(n_radius, *refs), [pltpu.HBM(acoustic.sha...  4.84 us
    all_to_all x1, starting transfers between devices, exchanged(): lax.all_to_all(value, 'sector', split_axis=0, concat_axis=0, tiled=True)  4.39 us
    ppermute x6, waiting for transfers between devices, paired(): return (lax.ppermute(pair, axis, first), lax.ppermute(link, axis, second))  4.27 us
  transfers between devices with their start and end apart: 11, of which 7 were waited for; matrix products, arithmetic and copies ran while one was open for 0% of the time, Pallas kernels for 4%

profile of v6, /device:TPU:0, one launch (start us, length us, event | category | flops | bytes accessed | tf_op | source)
XLA Modules:
  0.0 96.5 jit_solution(12783418639123877326)
XLA Ops:
  0.6 0.0 copy-start.2
  0.6 0.0 copy-start.1
  0.7 0.0 copy-start.4
  0.7 0.0 copy-start.12
  0.7 0.0 copy-start.11
  0.7 1.2 %shard_map.139 = (f32[64,128]{1,0:T(8,128)S(1)}, f32[64,128]{1,0:T(8,128)S(1)}) custom-call(f32[128,16,128]{2,1,0:T(8,128)} %refs_2_.4, f32[128,16,128]{2,1,0:T(8,128)} %refs_3_.3, f32[128,16,128]{2,1,0:T(8,128)} %refs_4_.1, f32[3,128,128]{2,1,0:T(8,128)} %refs_2_.5), custom_call_target="tpu_custom_call" | custom-call | bytes 196608 | tf_op jit(solution)/shard_map/pallas_call | solution.py:533
  1.9 0.1 copy-done.2
  2.0 0.3 copy-done.1
  2.3 0.3 copy-done.4
  2.6 0.0 copy-done.12
  2.7 1.9 %shard_map.140 = (f32[128,16,128]{2,1,0:T(8,128)S(1)}, f32[128,128]{1,0:T(8,128)S(1)}, f32[128,128]{1,0:T(8,128)S(1)}, f32[128,128]{1,0:T(8,128)S(1)}) custom-call(s32[16]{0:T(128)S(1)} %copy-done.11, s32[16]{0:T(128)S(1)} %copy-done.12, f32[128,16,128]{2,1,0:T(8,128)S(1)} %copy-done.1, f32[128,16,128]{2,1,0:T(8,128)S(1)} %copy-done.2, ...), custom_call_target="tpu_custom_call" | custom-call | bytes 3735552 | tf_op jit(solution)/shard_map/pallas_call | solution.py:547
  4.5 0.6 collective-permute-start
  5.1 0.7 collective-permute-start.1
  5.7 5.6 %collective-permute-start.3 = (f32[64,128]{1,0:T(8,128)S(1)}, f32[64,128]{1,0:T(8,128)S(1)}, u32[]{:S(2)}, u32[]{:S(2)}) collective-permute-start(f32[64,128]{1,0:T(8,128)S(1)} %get-tuple-element.18), channel_id=1, source_target_pairs={{4,8},{12,16},{20,24},{28,0},{8,4},{16,12},{24,20},{0,28},{5,9},{1... | collective-permute-start | bytes 98312 | tf_op jit(solution)/shard_map/ppermute | solution.py:471
  11.4 0.0 collective-permute-start.2
  11.4 1.9 %collective-permute-done.3.refs_7_.refs_6_ = f32[64,128]{1,0:T(8,128)S(1)} collective-permute-done((f32[64,128]{1,0:T(8,128)S(1)}, f32[64,128]{1,0:T(8,128)S(1)}, u32[]{:S(2)}, u32[]{:S(2)}) %collective-permute-start.3) | collective-permute-done | bytes 32800 | tf_op jit(solution)/shard_map/ppermute | solution.py:471
  13.3 2.4 %collective-permute-done.2.refs_6_.refs_5_ = f32[64,128]{1,0:T(8,128)S(1)} collective-permute-done((f32[64,128]{1,0:T(8,128)S(1)}, f32[64,128]{1,0:T(8,128)S(1)}, u32[]{:S(2)}, u32[]{:S(2)}) %collective-permute-start.2) | collective-permute-done | bytes 32800 | tf_op jit(solution)/shard_map/ppermute | solution.py:471
  15.6 0.0 collective-permute-done.refs_4_.refs_3_
  15.6 0.0 collective-permute-done.1.refs_5_.refs_4_
  15.7 4.8 %shard_map.142 = (f32[3,128,128]{2,1,0:T(8,128)}, f32[8,272,128]{2,1,0:T(8,128)}) custom-call(f32[128,16,128]{2,1,0:T(8,128)S(1)} %get-tuple-element.19.refs_0_, f32[128,128]{1,0:T(8,128)S(1)} %get-tuple-element.20.refs_1_, f32[3,128,128]{2,1,0:T(8,128)S(1)} %copy-done.5, f32[128,128]{1,0:T(8,128)S(1)} %collective-permute-done.refs_4_.refs_3_, ...), custom_call_target="tpu_custom_call" | custom-call | bytes 3932160 | tf_op jit(solution)/shard_map/pallas_call | solution.py:553
  20.5 0.0 copy-start.7
  20.5 0.0 copy-start.13
  20.5 0.0 copy-start
  20.5 4.4 %all-to-all-start = ((f32[8,272,128]{2,1,0:T(8,128)}), f32[8,272,128]{2,1,0:T(8,128)}, u32[]{:S(2)}, u32[]{:S(2)}) async-start(f32[8,272,128]{2,1,0:T(8,128)} %get-tuple-element.21), calls=%async_computation | async-start | bytes 2228224 | tf_op jit(solution)/shard_map/all_to_all | solution.py:501
  24.9 0.0 copy-start.3
  24.9 0.0 copy-done.7
  25.0 1.1 %collective-permute-start.4 = (f32[3,128,128]{2,1,0:T(8,128)S(1)}, f32[3,128,128]{2,1,0:T(8,128)S(1)}, u32[]{:S(2)}, u32[]{:S(2)}) collective-permute-start(f32[3,128,128]{2,1,0:T(8,128)S(1)} %copy-done.7), channel_id=1, source_target_pairs={{0,1},{1,0},{2,3},{3,2},{4,5},{5,4},{6,7},{7,6},{8,9},{9,8},{10,11... | collective-permute-start | bytes 589832 | tf_op jit(solution)/shard_map/ppermute | solution.py:475
  26.1 1.1 %collective-permute-done.4.right = f32[3,128,128]{2,1,0:T(8,128)S(1)} collective-permute-done((f32[3,128,128]{2,1,0:T(8,128)S(1)}, f32[3,128,128]{2,1,0:T(8,128)S(1)}, u32[]{:S(2)}, u32[]{:S(2)}) %collective-permute-start.4) | collective-permute-done | bytes 196640 | tf_op jit(solution)/shard_map/ppermute | solution.py:475
  27.2 2.4 %collective-permute-start.5 = (f32[3,128,128]{2,1,0:T(8,128)S(1)}, f32[3,128,128]{2,1,0:T(8,128)S(1)}, u32[]{:S(2)}, u32[]{:S(2)}) collective-permute-start(f32[3,128,128]{2,1,0:T(8,128)S(1)} %shard_map.143.left), channel_id=1, source_target_pairs={{0,2},{1,3},{2,0},{3,1},{4,6},{5,7},{6,4},{7,5},{8,10},{9,11},{10,... | collective-permute-start | bytes 589832 | tf_op jit(solution)/shard_map/ppermute | solution.py:475
  29.6 0.0 copy-done
  29.6 0.3 shard_map.145.refs_4_.impedance
  29.9 2.8 %shard_map.141.refs_2_ = f32[128,16,128]{2,1,0:T(8,128)} custom-call(s32[16]{0:T(128)S(1)} %copy-done.11, s32[16]{0:T(128)S(1)} %copy-done.12, f32[128,16,128]{2,1,0:T(8,128)S(1)} %copy-done.1, f32[128,16,128]{2,1,0:T(8,128)S(1)} %copy-done.3, f32[128,128]{1,0:T(8,128)S(1)} %collective-permute-done.refs_4_.refs_3_, ...), custom_call_target="tpu_custom_call" | custom-call | bytes 3145728 | tf_op jit(solution)/shard_map/pallas_call | solution.py:569
  32.7 2.1 %collective-permute-done.5.right = f32[3,128,128]{2,1,0:T(8,128)S(1)} collective-permute-done((f32[3,128,128]{2,1,0:T(8,128)S(1)}, f32[3,128,128]{2,1,0:T(8,128)S(1)}, u32[]{:S(2)}, u32[]{:S(2)}) %collective-permute-start.5) | collective-permute-done | bytes 196640 | tf_op jit(solution)/shard_map/ppermute | solution.py:475
  34.8 0.7 shard_map.144.refs_3_
  35.5 18.3 %all-to-all-done.refs_0_ = f32[8,272,128]{2,1,0:T(8,128)} async-done(((f32[8,272,128]{2,1,0:T(8,128)}), f32[8,272,128]{2,1,0:T(8,128)}, u32[]{:S(2)}, u32[]{:S(2)}) %all-to-all-start) | async-done | bytes 1114144 | tf_op jit(solution)/shard_map/all_to_all | solution.py:501
  53.8 2.1 %shard_map.146 = (f32[256,1024]{1,0:T(8,128)S(1)}, f32[48,1024]{1,0:T(8,128)S(1)}, f32[48,1024]{1,0:T(8,128)S(1)}, f32[16,1024]{1,0:T(8,128)S(1)}) custom-call(f32[8,272,128]{2,1,0:T(8,128)} %all-to-all-done.refs_0_, bf16[768,1024]{1,0:T(8,128)(2,1)S(1)} %copy-done, f32[128,16,128]{2,1,0:T(8,128)} %shard_map.141.refs_2_, f32[3,128,128]{2,1,0:T(8,128)} %shard_map.144.refs_3_, ...), custom_call_target="tpu_custom_call" | custom-call | bytes 4521984 | tf_op jit(solution)/shard_map/pallas_call | solution.py:577
  55.9 0.2 collective-permute-start.6
  56.1 0.7 collective-permute-start.7
  56.8 1.7 %collective-permute-start.8 = (f32[16,1024]{1,0:T(8,128)S(1)}, f32[16,1024]{1,0:T(8,128)S(1)}, u32[]{:S(2)}, u32[]{:S(2)}) collective-permute-start(f32[16,1024]{1,0:T(8,128)S(1)} %get-tuple-element.26.left), channel_id=1, source_target_pairs={{0,1},{1,0},{2,3},{3,2},{4,5},{5,4},{6,7},{7,6},{8,9},{9,8},{10,11... | collective-permute-start | bytes 196616 | tf_op jit(solution)/shard_map/ppermute | solution.py:475
  58.5 0.9 collective-permute-done.8.right
  59.4 2.0 %collective-permute-start.9 = (f32[16,1024]{1,0:T(8,128)S(1)}, f32[16,1024]{1,0:T(8,128)S(1)}, u32[]{:S(2)}, u32[]{:S(2)}) collective-permute-start(f32[16,1024]{1,0:T(8,128)S(1)} %shard_map.147.wave), channel_id=1, source_target_pairs={{0,2},{1,3},{2,0},{3,1},{4,6},{5,7},{6,4},{7,5},{8,10},{9,11},{10,... | collective-permute-start | bytes 196616 | tf_op jit(solution)/shard_map/ppermute | solution.py:475
  61.4 3.6 %collective-permute-done.9.other_wave = f32[16,1024]{1,0:T(8,128)S(1)} collective-permute-done((f32[16,1024]{1,0:T(8,128)S(1)}, f32[16,1024]{1,0:T(8,128)S(1)}, u32[]{:S(2)}, u32[]{:S(2)}) %collective-permute-start.9) | collective-permute-done | bytes 65568 | tf_op jit(solution)/shard_map/ppermute | solution.py:475
  65.1 0.0 collective-permute-done.6.pair
  65.1 0.0 collective-permute-done.7.link
  65.1 0.0 copy-done.8
  65.1 1.5 %shard_map.148 = f32[8,256,128]{2,1,0:T(8,128)S(1)} custom-call(f32[256,1024]{1,0:T(8,128)S(1)} %get-tuple-element.23.modes, f32[48,1024]{1,0:T(8,128)S(1)} %collective-permute-done.6.pair, f32[48,1024]{1,0:T(8,128)S(1)} %collective-permute-done.7.link, f32[16,1024]{1,0:T(8,128)S(1)} %shard_map.147.wave, f32[16,1024]{1,0:T(8,128)S(1)} %collective-permute-done.9.other_wave, ...), custom_call_target="tpu_custom_call" | custom-call | bytes 3145728 | tf_op jit(solution)/shard_map/pallas_call | solution.py:582
  66.6 28.2 %all_to_all.10.received = f32[8,256,128]{2,1,0:T(8,128)S(1)} all-to-all(f32[8,256,128]{2,1,0:T(8,128)S(1)} %shard_map.148), channel_id=1, replica_groups=mesh['sector'=8,'radial'=4] {'sector'}, dimensions={0} | all-to-all | bytes 2097152 | tf_op jit(solution)/shard_map/all_to_all | solution.py:501
  94.8 1.7 %shard_map.149 = f32[128,16,128]{2,1,0:T(8,128)} custom-call(f32[8,256,128]{2,1,0:T(8,128)S(1)} %all_to_all.10.received, f32[128,128]{1,0:T(8,128)S(1)} %copy-done.6), custom_call_target="tpu_custom_call" | custom-call | bytes 3145728 | tf_op jit(solution)/shard_map/pallas_call | solution.py:591
  (15 shorter events, 0.1 us)
Async XLA Ops:
  0.6 1.4 %copy-start.2 = (f32[128,16,128]{2,1,0:T(8,128)S(1)}, f32[128,16,128]{2,1,0:T(8,128)}, u32[]{:S(2)}) copy-start(f32[128,16,128]{2,1,0:T(8,128)} %refs_3_.3) | copy-start | bytes 3145732
  0.6 1.7 %copy-start.1 = (f32[128,16,128]{2,1,0:T(8,128)S(1)}, f32[128,16,128]{2,1,0:T(8,128)}, u32[]{:S(2)}) copy-start(f32[128,16,128]{2,1,0:T(8,128)} %refs_2_.4) | copy-start | bytes 3145732
  0.7 2.0 %copy-start.4 = (f32[128,16,128]{2,1,0:T(8,128)S(1)}, f32[128,16,128]{2,1,0:T(8,128)}, u32[]{:S(2)}) copy-start(f32[128,16,128]{2,1,0:T(8,128)} %refs_4_.1) | copy-start | bytes 3145732
  0.7 2.0 %copy-start.12 = (s32[16]{0:T(128)S(1)}, s32[16]{0:T(128)}, u32[]{:S(2)}) copy-start(s32[16]{0:T(128)} %refs_1_.4) | copy-start | bytes 196
  0.7 2.0 %copy-start.11 = (s32[16]{0:T(128)S(1)}, s32[16]{0:T(128)}, u32[]{:S(2)}) copy-start(s32[16]{0:T(128)} %refs_0_.3) | copy-start | bytes 196
  2.7 13.0 %copy-start.5 = (f32[3,128,128]{2,1,0:T(8,128)S(1)}, f32[3,128,128]{2,1,0:T(8,128)}, u32[]{:S(2)}) copy-start(f32[3,128,128]{2,1,0:T(8,128)} %refs_2_.5) | copy-start | bytes 589828
  2.7 13.0 %copy-start.6 = (f32[128,128]{1,0:T(8,128)S(1)}, f32[128,128]{1,0:T(8,128)}, u32[]{:S(2)}) copy-start(f32[128,128]{1,0:T(8,128)} %constant.10.clone.refs_7_.basis) | copy-start | bytes 196612
  4.5 11.1 %collective-permute-start = (f32[128,128]{1,0:T(8,128)S(1)}, f32[128,128]{1,0:T(8,128)S(1)}, u32[]{:S(2)}, u32[]{:S(2)}) collective-permute-start(f32[128,128]{1,0:T(8,128)S(1)} %get-tuple-element.16), channel_id=1, source_target_pairs={{0,1},{1,0},{2,3},{3,2},{4,5},{5,4},{6,7},{7,6},{8,9},{9,8},{10,11... | collective-permute-start | bytes 196616 | tf_op jit(solution)/shard_map/ppermute | solution.py:471
  5.1 10.6 %collective-permute-start.1 = (f32[128,128]{1,0:T(8,128)S(1)}, f32[128,128]{1,0:T(8,128)S(1)}, u32[]{:S(2)}, u32[]{:S(2)}) collective-permute-start(f32[128,128]{1,0:T(8,128)S(1)} %get-tuple-element.17), channel_id=1, source_target_pairs={{1,2},{2,1},{5,6},{6,5},{9,10},{10,9},{13,14},{14,13},{17,18},{18,... | collective-permute-start | bytes 196616 | tf_op jit(solution)/shard_map/ppermute | solution.py:471
  5.7 7.5 %collective-permute-start.3 = (f32[64,128]{1,0:T(8,128)S(1)}, f32[64,128]{1,0:T(8,128)S(1)}, u32[]{:S(2)}, u32[]{:S(2)}) collective-permute-start(f32[64,128]{1,0:T(8,128)S(1)} %get-tuple-element.18), channel_id=1, source_target_pairs={{4,8},{12,16},{20,24},{28,0},{8,4},{16,12},{24,20},{0,28},{5,9},{1... | collective-permute-start | bytes 98312 | tf_op jit(solution)/shard_map/ppermute | solution.py:471
  11.4 4.3 %collective-permute-start.2 = (f32[64,128]{1,0:T(8,128)S(1)}, f32[64,128]{1,0:T(8,128)S(1)}, u32[]{:S(2)}, u32[]{:S(2)}) collective-permute-start(f32[64,128]{1,0:T(8,128)S(1)} %get-tuple-element.15.refs_5_), channel_id=1, source_target_pairs={{0,4},{4,0},{8,12},{12,8},{16,20},{20,16},{24,28},{28,24},{1,5},{5... | collective-permute-start | bytes 98312 | tf_op jit(solution)/shard_map/ppermute | solution.py:471
  20.5 4.4 %copy-start.7 = (f32[3,128,128]{2,1,0:T(8,128)S(1)}, f32[3,128,128]{2,1,0:T(8,128)}, u32[]{:S(2)}) copy-start(f32[3,128,128]{2,1,0:T(8,128)} %get-tuple-element.22.left) | copy-start | bytes 589828
  20.5 9.0 %copy-start.13 = (f32[513]{0:T(1024)S(1)}, f32[513]{0:T(1024)}, u32[]{:S(2)}) copy-start(f32[513]{0:T(1024)} %param.16) | copy-start | bytes 6160
  20.5 9.0 %copy-start = (bf16[768,1024]{1,0:T(8,128)(2,1)S(1)}, bf16[768,1024]{1,0:T(8,128)(2,1)}, u32[]{:S(2)}) copy-start(bf16[768,1024]{1,0:T(8,128)(2,1)} %constant.12.clone._.refs_1_.table) | copy-start | bytes 4718596
  20.5 33.3 %all-to-all-start = ((f32[8,272,128]{2,1,0:T(8,128)}), f32[8,272,128]{2,1,0:T(8,128)}, u32[]{:S(2)}, u32[]{:S(2)}) async-start(f32[8,272,128]{2,1,0:T(8,128)} %get-tuple-element.21), calls=%async_computation | async-start | bytes 2228224 | tf_op jit(solution)/shard_map/all_to_all | solution.py:501
  24.9 5.0 %copy-start.3 = (f32[128,16,128]{2,1,0:T(8,128)S(1)}, f32[128,16,128]{2,1,0:T(8,128)}, u32[]{:S(2)}) copy-start(f32[128,16,128]{2,1,0:T(8,128)} %refs_3_.3) | copy-start | bytes 3145732
  25.0 2.2 %collective-permute-start.4 = (f32[3,128,128]{2,1,0:T(8,128)S(1)}, f32[3,128,128]{2,1,0:T(8,128)S(1)}, u32[]{:S(2)}, u32[]{:S(2)}) collective-permute-start(f32[3,128,128]{2,1,0:T(8,128)S(1)} %copy-done.7), channel_id=1, source_target_pairs={{0,1},{1,0},{2,3},{3,2},{4,5},{5,4},{6,7},{7,6},{8,9},{9,8},{10,11... | collective-permute-start | bytes 589832 | tf_op jit(solution)/shard_map/ppermute | solution.py:475
  27.2 7.6 %collective-permute-start.5 = (f32[3,128,128]{2,1,0:T(8,128)S(1)}, f32[3,128,128]{2,1,0:T(8,128)S(1)}, u32[]{:S(2)}, u32[]{:S(2)}) collective-permute-start(f32[3,128,128]{2,1,0:T(8,128)S(1)} %shard_map.143.left), channel_id=1, source_target_pairs={{0,2},{1,3},{2,0},{3,1},{4,6},{5,7},{6,4},{7,5},{8,10},{9,11},{10,... | collective-permute-start | bytes 589832 | tf_op jit(solution)/shard_map/ppermute | solution.py:475
  35.5 29.6 %copy-start.8 = (f32[8,16,128]{2,1,0:T(8,128)S(1)}, f32[8,16,128]{2,1,0:T(8,128)}, u32[]{:S(2)}) copy-start(f32[8,16,128]{2,1,0:T(8,128)} %constant.11.clone.axial) | copy-start | bytes 196612
  35.5 29.6 %copy-start.9 = (f32[1,1024]{1,0:T(1,128)S(1)}, f32[1,1024]{1,0:T(1,128)}, u32[]{:S(2)}) copy-start(f32[1,1024]{1,0:T(1,128)} %constant.16.weight) | copy-start | bytes 12292
  35.5 29.6 %copy-start.10 = (f32[1,1024]{1,0:T(1,128)S(1)}, f32[1,1024]{1,0:T(1,128)}, u32[]{:S(2)}) copy-start(f32[1,1024]{1,0:T(1,128)} %constant.15.fixed) | copy-start | bytes 12292
  55.9 9.1 %collective-permute-start.6 = (f32[48,1024]{1,0:T(8,128)S(1)}, f32[48,1024]{1,0:T(8,128)S(1)}, u32[]{:S(2)}, u32[]{:S(2)}) collective-permute-start(f32[48,1024]{1,0:T(8,128)S(1)} %get-tuple-element.24), channel_id=1, source_target_pairs={{0,1},{1,0},{2,3},{3,2},{4,5},{5,4},{6,7},{7,6},{8,9},{9,8},{10,11... | collective-permute-start | bytes 589832 | tf_op jit(solution)/shard_map/ppermute | solution.py:471
  56.1 9.0 %collective-permute-start.7 = (f32[48,1024]{1,0:T(8,128)S(1)}, f32[48,1024]{1,0:T(8,128)S(1)}, u32[]{:S(2)}, u32[]{:S(2)}) collective-permute-start(f32[48,1024]{1,0:T(8,128)S(1)} %get-tuple-element.25), channel_id=1, source_target_pairs={{1,2},{2,1},{5,6},{6,5},{9,10},{10,9},{13,14},{14,13},{17,18},{18,... | collective-permute-start | bytes 589832 | tf_op jit(solution)/shard_map/ppermute | solution.py:471
  56.8 2.6 %collective-permute-start.8 = (f32[16,1024]{1,0:T(8,128)S(1)}, f32[16,1024]{1,0:T(8,128)S(1)}, u32[]{:S(2)}, u32[]{:S(2)}) collective-permute-start(f32[16,1024]{1,0:T(8,128)S(1)} %get-tuple-element.26.left), channel_id=1, source_target_pairs={{0,1},{1,0},{2,3},{3,2},{4,5},{5,4},{6,7},{7,6},{8,9},{9,8},{10,11... | collective-permute-start | bytes 196616 | tf_op jit(solution)/shard_map/ppermute | solution.py:475
  59.4 5.7 %collective-permute-start.9 = (f32[16,1024]{1,0:T(8,128)S(1)}, f32[16,1024]{1,0:T(8,128)S(1)}, u32[]{:S(2)}, u32[]{:S(2)}) collective-permute-start(f32[16,1024]{1,0:T(8,128)S(1)} %shard_map.147.wave), channel_id=1, source_target_pairs={{0,2},{1,3},{2,0},{3,1},{4,6},{5,7},{6,4},{7,5},{8,10},{9,11},{10,... | collective-permute-start | bytes 196616 | tf_op jit(solution)/shard_map/ppermute | solution.py:475

commit v7 on v6

--- a/solution.py
+++ b/solution.py
@@ -312,9 +312,12 @@
     def store(lane, out):
         modes[:, lane] = out[:columns]
         first, last = out[:edge], out[columns - edge : columns]
-        pair[:, lane] = jnp.where(radial_odd, first, last)
-        link[:, lane] = jnp.where(radial_odd, last, first)
+        pair[:edge, lane] = jnp.where(radial_odd, first, last)
+        link[:edge, lane] = jnp.where(radial_odd, last, first)
         wave[:, lane] = out[columns:]
+        if pair.shape[0] > edge:
+            pair[edge:, lane] = out[columns:]
+            link[edge:, lane] = out[columns:]
 
     transformed([received[s] for s in range(sectors)], table, store)
 
@@ -341,6 +344,9 @@
         inv_inner, inv_outer = inv * has_inner, inv * has_outer
         last_scale = jnp.broadcast_to(row * weight[:, lane], (each, step))
         add = wave[:, lane] + other_wave[:, lane]
+        edge = HALO * each
+        if pair.shape[0] > edge:
+            add = add + (pair[edge:, lane] + link[edge:, lane])
 
         def row_of(i):
             i -= HALO
@@ -574,20 +580,21 @@
     )(mouth_azimuth, mouth_radius, density, swirl, *radial_halo, *sector_halo)
     acoustic_next = added(*halves_of_sum(state, "radial"))
 
+    direct = radials == 4
+    message = edge + own if direct else edge
     modes, pair, link, wave = call(
         lambda *refs: forward_kernel(edge, *refs),
-        [shape(columns, n_theta)] + [shape(edge, n_theta)] * 2 + [shape(own, n_theta)],
+        [shape(columns, n_theta)] + [shape(message, n_theta)] * 2 + [shape(own, n_theta)],
         [VMEM] * 2 + [HBM] * 3,
     )(in_vmem(received), table, in_hbm(density_next), in_hbm(acoustic_next), impedance)
+    halo = paired(pair, link, "radial", direct)
+    waves = (wave, swapped(wave, "radial", 2)) if direct else halves_of_sum(wave, "radial")
     (send,) = call(
         solve_kernel,
         [shape(sectors, columns, cells_theta)],
         [VMEM] * 10,
         [pltpu.VMEM((columns, n_theta), F32)],
-    )(
-        modes, *paired(pair, link, "radial", False), *halves_of_sum(wave, "radial"), impedance,
-        fixed, weight, eigen, table,
-    )
+    )(modes, *halo, *waves, impedance, fixed, weight, eigen, table)
     (pressure,) = call(
         pressure_kernel,
         [shape(*density.shape)],

time: 96.8 us -> 98.2 us (1.014)
  waiting for transfers between devices: 30.3 us -> 33.7 us
  starting transfers between devices: 19.3 us -> 17 us
    ppermute x4 -> x3, waiting for transfers between devices: 7.66 us -> 11.1 us  [swapped(): lax.ppermute(value, axis, [(i, i ^ bits) for i in range(lax.axis_size(axi...]
    ppermute x4 -> x3, starting transfers between devices: 7.25 us -> 5.53 us  [swapped(): lax.ppermute(value, axis, [(i, i ^ bits) for i in range(lax.axis_size(axi...]
  transfers between devices with their start and end apart: 11 -> 10, of which waited for: 7 -> 6; matrix products, arithmetic and copies ran while one was open for 0% -> 0% of each run, Pallas kernels for 4% -> 4%
where the time goes in v7:
time: 98.2 us; the launch traced here: 98 us
  waiting for transfers between devices  33.7 us (34%)
  blocking collectives  28.6 us (29%)
  Pallas kernels  17 us (17%)
  starting transfers between devices  17 us (17%)
    all_to_all x1, blocking collectives, exchanged(): lax.all_to_all(value, 'sector', split_axis=0, concat_axis=0, tiled=True)  28.6 us
    all_to_all x1, waiting for transfers between devices, exchanged(): lax.all_to_all(value, 'sector', split_axis=0, concat_axis=0, tiled=True)  18.3 us
    ppermute x3, waiting for transfers between devices, swapped(): lax.ppermute(value, axis, [(i, i ^ bits) for i in range(lax.axis_size(axi...  11.1 us
    ppermute x6, starting transfers between devices, paired(): return (lax.ppermute(pair, axis, first), lax.ppermute(link, axis, second))  7.03 us
    ppermute x3, starting transfers between devices, swapped(): lax.ppermute(value, axis, [(i, i ^ bits) for i in range(lax.axis_size(axi...  5.53 us
    pallas_call x1, Pallas kernels, section(): call(lambda *refs: first_kernel(n_radius, *refs), [pltpu.HBM(acoustic.sha...  4.83 us
    all_to_all x1, starting transfers between devices, exchanged(): lax.all_to_all(value, 'sector', split_axis=0, concat_axis=0, tiled=True)  4.4 us
    ppermute x6, waiting for transfers between devices, paired(): return (lax.ppermute(pair, axis, first), lax.ppermute(link, axis, second))  4.27 us
  transfers between devices with their start and end apart: 10, of which 6 were waited for; matrix products, arithmetic and copies ran while one was open for 0% of the time, Pallas kernels for 4%

profile of v7, /device:TPU:0, one launch (start us, length us, event | category | flops | bytes accessed | tf_op | source)
XLA Modules:
  0.0 98.0 jit_solution(5592531015359034824)
XLA Ops:
  0.6 0.0 copy-start.2
  0.6 0.0 copy-start.1
  0.7 0.0 copy-start.4
  0.7 0.0 copy-start.12
  0.7 0.0 copy-start.11
  0.7 1.2 %shard_map.139 = (f32[64,128]{1,0:T(8,128)S(1)}, f32[64,128]{1,0:T(8,128)S(1)}) custom-call(f32[128,16,128]{2,1,0:T(8,128)} %refs_2_.4, f32[128,16,128]{2,1,0:T(8,128)} %refs_3_.3, f32[128,16,128]{2,1,0:T(8,128)} %refs_4_.1, f32[3,128,128]{2,1,0:T(8,128)} %refs_2_.5), custom_call_target="tpu_custom_call" | custom-call | bytes 196608 | tf_op jit(solution)/shard_map/pallas_call | solution.py:539
  1.9 0.1 copy-done.2
  2.0 0.3 copy-done.1
  2.3 0.3 copy-done.4
  2.6 0.0 copy-done.12
  2.6 0.0 copy-done.11
  2.7 1.8 %shard_map.140 = (f32[128,16,128]{2,1,0:T(8,128)S(1)}, f32[128,128]{1,0:T(8,128)S(1)}, f32[128,128]{1,0:T(8,128)S(1)}, f32[128,128]{1,0:T(8,128)S(1)}) custom-call(s32[16]{0:T(128)S(1)} %copy-done.11, s32[16]{0:T(128)S(1)} %copy-done.12, f32[128,16,128]{2,1,0:T(8,128)S(1)} %copy-done.1, f32[128,16,128]{2,1,0:T(8,128)S(1)} %copy-done.2, ...), custom_call_target="tpu_custom_call" | custom-call | bytes 3735552 | tf_op jit(solution)/shard_map/pallas_call | solution.py:553
  4.5 0.6 collective-permute-start
  5.0 0.7 collective-permute-start.1
  5.7 5.6 %collective-permute-start.3 = (f32[64,128]{1,0:T(8,128)S(1)}, f32[64,128]{1,0:T(8,128)S(1)}, u32[]{:S(2)}, u32[]{:S(2)}) collective-permute-start(f32[64,128]{1,0:T(8,128)S(1)} %get-tuple-element.18), channel_id=1, source_target_pairs={{4,8},{12,16},{20,24},{28,0},{8,4},{16,12},{24,20},{0,28},{5,9},{1... | collective-permute-start | bytes 98312 | tf_op jit(solution)/shard_map/ppermute | solution.py:477
  11.3 0.0 collective-permute-start.2
  11.3 1.9 %collective-permute-done.3.refs_7_.refs_6_ = f32[64,128]{1,0:T(8,128)S(1)} collective-permute-done((f32[64,128]{1,0:T(8,128)S(1)}, f32[64,128]{1,0:T(8,128)S(1)}, u32[]{:S(2)}, u32[]{:S(2)}) %collective-permute-start.3) | collective-permute-done | bytes 32800 | tf_op jit(solution)/shard_map/ppermute | solution.py:477
  13.2 2.4 %collective-permute-done.2.refs_6_.refs_5_ = f32[64,128]{1,0:T(8,128)S(1)} collective-permute-done((f32[64,128]{1,0:T(8,128)S(1)}, f32[64,128]{1,0:T(8,128)S(1)}, u32[]{:S(2)}, u32[]{:S(2)}) %collective-permute-start.2) | collective-permute-done | bytes 32800 | tf_op jit(solution)/shard_map/ppermute | solution.py:477
  15.6 0.0 collective-permute-done.refs_4_.refs_3_
  15.6 0.0 collective-permute-done.1.refs_5_.refs_4_
  15.6 0.0 copy-done.5
  15.6 0.0 copy-done.6
  15.6 4.8 %shard_map.142 = (f32[3,128,128]{2,1,0:T(8,128)}, f32[8,272,128]{2,1,0:T(8,128)}) custom-call(f32[128,16,128]{2,1,0:T(8,128)S(1)} %get-tuple-element.19.refs_0_, f32[128,128]{1,0:T(8,128)S(1)} %get-tuple-element.20.refs_1_, f32[3,128,128]{2,1,0:T(8,128)S(1)} %copy-done.5, f32[128,128]{1,0:T(8,128)S(1)} %collective-permute-done.refs_4_.refs_3_, ...), custom_call_target="tpu_custom_call" | custom-call | bytes 3932160 | tf_op jit(solution)/shard_map/pallas_call | solution.py:559
  20.5 0.0 copy-start.7
  20.5 0.0 copy-start.13
  20.5 0.0 copy-start
  20.5 4.4 %all-to-all-start = ((f32[8,272,128]{2,1,0:T(8,128)}), f32[8,272,128]{2,1,0:T(8,128)}, u32[]{:S(2)}, u32[]{:S(2)}) async-start(f32[8,272,128]{2,1,0:T(8,128)} %get-tuple-element.21), calls=%async_computation | async-start | bytes 2228224 | tf_op jit(solution)/shard_map/all_to_all | solution.py:507
  24.9 0.0 copy-start.3
  24.9 0.0 copy-done.7
  24.9 1.1 %collective-permute-start.4 = (f32[3,128,128]{2,1,0:T(8,128)S(1)}, f32[3,128,128]{2,1,0:T(8,128)S(1)}, u32[]{:S(2)}, u32[]{:S(2)}) collective-permute-start(f32[3,128,128]{2,1,0:T(8,128)S(1)} %copy-done.7), channel_id=1, source_target_pairs={{0,1},{1,0},{2,3},{3,2},{4,5},{5,4},{6,7},{7,6},{8,9},{9,8},{10,11... | collective-permute-start | bytes 589832 | tf_op jit(solution)/shard_map/ppermute | solution.py:481
  26.1 1.1 %collective-permute-done.4.right = f32[3,128,128]{2,1,0:T(8,128)S(1)} collective-permute-done((f32[3,128,128]{2,1,0:T(8,128)S(1)}, f32[3,128,128]{2,1,0:T(8,128)S(1)}, u32[]{:S(2)}, u32[]{:S(2)}) %collective-permute-start.4) | collective-permute-done | bytes 196640 | tf_op jit(solution)/shard_map/ppermute | solution.py:481
  27.2 2.4 %collective-permute-start.5 = (f32[3,128,128]{2,1,0:T(8,128)S(1)}, f32[3,128,128]{2,1,0:T(8,128)S(1)}, u32[]{:S(2)}, u32[]{:S(2)}) collective-permute-start(f32[3,128,128]{2,1,0:T(8,128)S(1)} %shard_map.143.left), channel_id=1, source_target_pairs={{0,2},{1,3},{2,0},{3,1},{4,6},{5,7},{6,4},{7,5},{8,10},{9,11},{10,... | collective-permute-start | bytes 589832 | tf_op jit(solution)/shard_map/ppermute | solution.py:481
  29.5 0.0 copy-done
  29.6 0.3 shard_map.145.refs_4_.impedance
  29.9 2.8 %shard_map.141.refs_2_ = f32[128,16,128]{2,1,0:T(8,128)} custom-call(s32[16]{0:T(128)S(1)} %copy-done.11, s32[16]{0:T(128)S(1)} %copy-done.12, f32[128,16,128]{2,1,0:T(8,128)S(1)} %copy-done.1, f32[128,16,128]{2,1,0:T(8,128)S(1)} %copy-done.3, f32[128,128]{1,0:T(8,128)S(1)} %collective-permute-done.refs_4_.refs_3_, ...), custom_call_target="tpu_custom_call" | custom-call | bytes 3145728 | tf_op jit(solution)/shard_map/pallas_call | solution.py:575
  32.7 2.1 %collective-permute-done.5.right = f32[3,128,128]{2,1,0:T(8,128)S(1)} collective-permute-done((f32[3,128,128]{2,1,0:T(8,128)S(1)}, f32[3,128,128]{2,1,0:T(8,128)S(1)}, u32[]{:S(2)}, u32[]{:S(2)}) %collective-permute-start.5) | collective-permute-done | bytes 196640 | tf_op jit(solution)/shard_map/ppermute | solution.py:481
  34.7 0.7 shard_map.144.refs_3_
  35.5 18.3 %all-to-all-done.refs_0_ = f32[8,272,128]{2,1,0:T(8,128)} async-done(((f32[8,272,128]{2,1,0:T(8,128)}), f32[8,272,128]{2,1,0:T(8,128)}, u32[]{:S(2)}, u32[]{:S(2)}) %all-to-all-start) | async-done | bytes 1114144 | tf_op jit(solution)/shard_map/all_to_all | solution.py:507
  53.8 2.1 %shard_map.146 = (f32[256,1024]{1,0:T(8,128)S(1)}, f32[64,1024]{1,0:T(8,128)S(1)}, f32[64,1024]{1,0:T(8,128)S(1)}, f32[16,1024]{1,0:T(8,128)S(1)}) custom-call(f32[8,272,128]{2,1,0:T(8,128)} %all-to-all-done.refs_0_, bf16[768,1024]{1,0:T(8,128)(2,1)S(1)} %copy-done, f32[128,16,128]{2,1,0:T(8,128)} %shard_map.141.refs_2_, f32[3,128,128]{2,1,0:T(8,128)} %shard_map.144.refs_3_, ...), custom_call_target="tpu_custom_call" | custom-call | bytes 4915200 | tf_op jit(solution)/shard_map/pallas_call | solution.py:585
  55.9 0.2 collective-permute-start.6
  56.1 0.0 collective-permute-start.7
  56.1 2.0 %collective-permute-start.8 = (f32[16,1024]{1,0:T(8,128)S(1)}, f32[16,1024]{1,0:T(8,128)S(1)}, u32[]{:S(2)}, u32[]{:S(2)}) collective-permute-start(f32[16,1024]{1,0:T(8,128)S(1)} %get-tuple-element.26.wave), channel_id=1, source_target_pairs={{0,2},{1,3},{2,0},{3,1},{4,6},{5,7},{6,4},{7,5},{8,10},{9,11},{10,... | collective-permute-start | bytes 196616 | tf_op jit(solution)/shard_map/ppermute | solution.py:481
  58.1 8.0 %collective-permute-done.8.other_wave = f32[16,1024]{1,0:T(8,128)S(1)} collective-permute-done((f32[16,1024]{1,0:T(8,128)S(1)}, f32[16,1024]{1,0:T(8,128)S(1)}, u32[]{:S(2)}, u32[]{:S(2)}) %collective-permute-start.8) | collective-permute-done | bytes 65568 | tf_op jit(solution)/shard_map/ppermute | solution.py:481
  66.1 0.0 collective-permute-done.6.pair
  66.1 0.0 collective-permute-done.7.link
  66.1 1.5 %shard_map.147 = f32[8,256,128]{2,1,0:T(8,128)S(1)} custom-call(f32[256,1024]{1,0:T(8,128)S(1)} %get-tuple-element.23.modes, f32[64,1024]{1,0:T(8,128)S(1)} %collective-permute-done.6.pair, f32[64,1024]{1,0:T(8,128)S(1)} %collective-permute-done.7.link, f32[16,1024]{1,0:T(8,128)S(1)} %get-tuple-element.26.wave, ...), custom_call_target="tpu_custom_call" | custom-call | bytes 3145728 | tf_op jit(solution)/shard_map/pallas_call | solution.py:592
  67.6 28.6 %all_to_all.10.received = f32[8,256,128]{2,1,0:T(8,128)S(1)} all-to-all(f32[8,256,128]{2,1,0:T(8,128)S(1)} %shard_map.147), channel_id=1, replica_groups=mesh['sector'=8,'radial'=4] {'sector'}, dimensions={0} | all-to-all | bytes 2097152 | tf_op jit(solution)/shard_map/all_to_all | solution.py:507
  96.2 1.7 %shard_map.148 = f32[128,16,128]{2,1,0:T(8,128)} custom-call(f32[8,256,128]{2,1,0:T(8,128)S(1)} %all_to_all.10.received, f32[128,128]{1,0:T(8,128)S(1)} %copy-done.6), custom_call_target="tpu_custom_call" | custom-call | bytes 3145728 | tf_op jit(solution)/shard_map/pallas_call | solution.py:598
  (12 shorter events, 0.0 us)
Async XLA Ops:
  0.6 1.4 %copy-start.2 = (f32[128,16,128]{2,1,0:T(8,128)S(1)}, f32[128,16,128]{2,1,0:T(8,128)}, u32[]{:S(2)}) copy-start(f32[128,16,128]{2,1,0:T(8,128)} %refs_3_.3) | copy-start | bytes 3145732
  0.6 1.7 %copy-start.1 = (f32[128,16,128]{2,1,0:T(8,128)S(1)}, f32[128,16,128]{2,1,0:T(8,128)}, u32[]{:S(2)}) copy-start(f32[128,16,128]{2,1,0:T(8,128)} %refs_2_.4) | copy-start | bytes 3145732
  0.7 2.0 %copy-start.4 = (f32[128,16,128]{2,1,0:T(8,128)S(1)}, f32[128,16,128]{2,1,0:T(8,128)}, u32[]{:S(2)}) copy-start(f32[128,16,128]{2,1,0:T(8,128)} %refs_4_.1) | copy-start | bytes 3145732
  0.7 2.0 %copy-start.12 = (s32[16]{0:T(128)S(1)}, s32[16]{0:T(128)}, u32[]{:S(2)}) copy-start(s32[16]{0:T(128)} %refs_1_.4) | copy-start | bytes 196
  0.7 2.0 %copy-start.11 = (s32[16]{0:T(128)S(1)}, s32[16]{0:T(128)}, u32[]{:S(2)}) copy-start(s32[16]{0:T(128)} %refs_0_.3) | copy-start | bytes 196
  2.7 13.0 %copy-start.5 = (f32[3,128,128]{2,1,0:T(8,128)S(1)}, f32[3,128,128]{2,1,0:T(8,128)}, u32[]{:S(2)}) copy-start(f32[3,128,128]{2,1,0:T(8,128)} %refs_2_.5) | copy-start | bytes 589828
  2.7 13.0 %copy-start.6 = (f32[128,128]{1,0:T(8,128)S(1)}, f32[128,128]{1,0:T(8,128)}, u32[]{:S(2)}) copy-start(f32[128,128]{1,0:T(8,128)} %constant.10.clone.refs_7_.basis) | copy-start | bytes 196612
  4.5 11.1 %collective-permute-start = (f32[128,128]{1,0:T(8,128)S(1)}, f32[128,128]{1,0:T(8,128)S(1)}, u32[]{:S(2)}, u32[]{:S(2)}) collective-permute-start(f32[128,128]{1,0:T(8,128)S(1)} %get-tuple-element.16), channel_id=1, source_target_pairs={{0,1},{1,0},{2,3},{3,2},{4,5},{5,4},{6,7},{7,6},{8,9},{9,8},{10,11... | collective-permute-start | bytes 196616 | tf_op jit(solution)/shard_map/ppermute | solution.py:477
  5.0 10.6 %collective-permute-start.1 = (f32[128,128]{1,0:T(8,128)S(1)}, f32[128,128]{1,0:T(8,128)S(1)}, u32[]{:S(2)}, u32[]{:S(2)}) collective-permute-start(f32[128,128]{1,0:T(8,128)S(1)} %get-tuple-element.17), channel_id=1, source_target_pairs={{1,2},{2,1},{5,6},{6,5},{9,10},{10,9},{13,14},{14,13},{17,18},{18,... | collective-permute-start | bytes 196616 | tf_op jit(solution)/shard_map/ppermute | solution.py:477
  5.7 7.5 %collective-permute-start.3 = (f32[64,128]{1,0:T(8,128)S(1)}, f32[64,128]{1,0:T(8,128)S(1)}, u32[]{:S(2)}, u32[]{:S(2)}) collective-permute-start(f32[64,128]{1,0:T(8,128)S(1)} %get-tuple-element.18), channel_id=1, source_target_pairs={{4,8},{12,16},{20,24},{28,0},{8,4},{16,12},{24,20},{0,28},{5,9},{1... | collective-permute-start | bytes 98312 | tf_op jit(solution)/shard_map/ppermute | solution.py:477
  11.3 4.3 %collective-permute-start.2 = (f32[64,128]{1,0:T(8,128)S(1)}, f32[64,128]{1,0:T(8,128)S(1)}, u32[]{:S(2)}, u32[]{:S(2)}) collective-permute-start(f32[64,128]{1,0:T(8,128)S(1)} %get-tuple-element.15.refs_5_), channel_id=1, source_target_pairs={{0,4},{4,0},{8,12},{12,8},{16,20},{20,16},{24,28},{28,24},{1,5},{5... | collective-permute-start | bytes 98312 | tf_op jit(solution)/shard_map/ppermute | solution.py:477
  20.5 4.5 %copy-start.7 = (f32[3,128,128]{2,1,0:T(8,128)S(1)}, f32[3,128,128]{2,1,0:T(8,128)}, u32[]{:S(2)}) copy-start(f32[3,128,128]{2,1,0:T(8,128)} %get-tuple-element.22.left) | copy-start | bytes 589828
  20.5 9.1 %copy-start.13 = (f32[513]{0:T(1024)S(1)}, f32[513]{0:T(1024)}, u32[]{:S(2)}) copy-start(f32[513]{0:T(1024)} %param.16) | copy-start | bytes 6160
  20.5 9.1 %copy-start = (bf16[768,1024]{1,0:T(8,128)(2,1)S(1)}, bf16[768,1024]{1,0:T(8,128)(2,1)}, u32[]{:S(2)}) copy-start(bf16[768,1024]{1,0:T(8,128)(2,1)} %constant.12.clone._.refs_1_.table) | copy-start | bytes 4718596
  20.5 33.3 %all-to-all-start = ((f32[8,272,128]{2,1,0:T(8,128)}), f32[8,272,128]{2,1,0:T(8,128)}, u32[]{:S(2)}, u32[]{:S(2)}) async-start(f32[8,272,128]{2,1,0:T(8,128)} %get-tuple-element.21), calls=%async_computation | async-start | bytes 2228224 | tf_op jit(solution)/shard_map/all_to_all | solution.py:507
  24.9 5.0 %copy-start.3 = (f32[128,16,128]{2,1,0:T(8,128)S(1)}, f32[128,16,128]{2,1,0:T(8,128)}, u32[]{:S(2)}) copy-start(f32[128,16,128]{2,1,0:T(8,128)} %refs_3_.3) | copy-start | bytes 3145732
  24.9 2.2 %collective-permute-start.4 = (f32[3,128,128]{2,1,0:T(8,128)S(1)}, f32[3,128,128]{2,1,0:T(8,128)S(1)}, u32[]{:S(2)}, u32[]{:S(2)}) collective-permute-start(f32[3,128,128]{2,1,0:T(8,128)S(1)} %copy-done.7), channel_id=1, source_target_pairs={{0,1},{1,0},{2,3},{3,2},{4,5},{5,4},{6,7},{7,6},{8,9},{9,8},{10,11... | collective-permute-start | bytes 589832 | tf_op jit(solution)/shard_map/ppermute | solution.py:481
  27.2 7.6 %collective-permute-start.5 = (f32[3,128,128]{2,1,0:T(8,128)S(1)}, f32[3,128,128]{2,1,0:T(8,128)S(1)}, u32[]{:S(2)}, u32[]{:S(2)}) collective-permute-start(f32[3,128,128]{2,1,0:T(8,128)S(1)} %shard_map.143.left), channel_id=1, source_target_pairs={{0,2},{1,3},{2,0},{3,1},{4,6},{5,7},{6,4},{7,5},{8,10},{9,11},{10,... | collective-permute-start | bytes 589832 | tf_op jit(solution)/shard_map/ppermute | solution.py:481
  35.4 30.7 %copy-start.8 = (f32[8,16,128]{2,1,0:T(8,128)S(1)}, f32[8,16,128]{2,1,0:T(8,128)}, u32[]{:S(2)}) copy-start(f32[8,16,128]{2,1,0:T(8,128)} %constant.11.clone.axial) | copy-start | bytes 196612
  35.4 30.7 %copy-start.9 = (f32[1,1024]{1,0:T(1,128)S(1)}, f32[1,1024]{1,0:T(1,128)}, u32[]{:S(2)}) copy-start(f32[1,1024]{1,0:T(1,128)} %constant.16.weight) | copy-start | bytes 12292
  35.4 30.7 %copy-start.10 = (f32[1,1024]{1,0:T(1,128)S(1)}, f32[1,1024]{1,0:T(1,128)}, u32[]{:S(2)}) copy-start(f32[1,1024]{1,0:T(1,128)} %constant.15.fixed) | copy-start | bytes 12292
  55.9 10.2 %collective-permute-start.6 = (f32[64,1024]{1,0:T(8,128)S(1)}, f32[64,1024]{1,0:T(8,128)S(1)}, u32[]{:S(2)}, u32[]{:S(2)}) collective-permute-start(f32[64,1024]{1,0:T(8,128)S(1)} %get-tuple-element.24), channel_id=1, source_target_pairs={{0,1},{1,0},{2,3},{3,2},{4,5},{5,4},{6,7},{7,6},{8,9},{9,8},{10,11... | collective-permute-start | bytes 786440 | tf_op jit(solution)/shard_map/ppermute | solution.py:477
  56.1 10.0 %collective-permute-start.7 = (f32[64,1024]{1,0:T(8,128)S(1)}, f32[64,1024]{1,0:T(8,128)S(1)}, u32[]{:S(2)}, u32[]{:S(2)}) collective-permute-start(f32[64,1024]{1,0:T(8,128)S(1)} %get-tuple-element.25), channel_id=1, source_target_pairs={{1,2},{3,0},{2,1},{0,3},{5,6},{7,4},{6,5},{4,7},{9,10},{11,8},{10,... | collective-permute-start | bytes 786440 | tf_op jit(solution)/shard_map/ppermute | solution.py:477
  56.1 10.0 %collective-permute-start.8 = (f32[16,1024]{1,0:T(8,128)S(1)}, f32[16,1024]{1,0:T(8,128)S(1)}, u32[]{:S(2)}, u32[]{:S(2)}) collective-permute-start(f32[16,1024]{1,0:T(8,128)S(1)} %get-tuple-element.26.wave), channel_id=1, source_target_pairs={{0,2},{1,3},{2,0},{3,1},{4,6},{5,7},{6,4},{7,5},{8,10},{9,11},{10,... | collective-permute-start | bytes 196616 | tf_op jit(solution)/shard_map/ppermute | solution.py:481

commit v8 on v6

--- a/solution.py
+++ b/solution.py
@@ -118,6 +118,15 @@
             at += EDGE
         heat = jnp.sum(rate[side] * rho[side] * rho[side], axis=1)
         out[at : at + EDGE] = heat
+
+
+def flat(ref):
+    cells_theta, cells_radius, cells_axial = ref.shape
+    return ref.reshape(cells_theta * cells_radius, cells_axial)
+
+
+def plane(shape, r):
+    return pl.ds(r, shape[0], stride=shape[1])
 
 
 def flow_rows(n_theta, mouth_azimuth, mouth_radius, density, swirl, forcing):
@@ -174,8 +183,10 @@
     forcing[end] = forcing[end] + (diffusion * above[rho] - 0.5 * above[flux])
     inside = diffusion * (radial > 0).astype(F32)
     outside = diffusion * (radial < radials - 1).astype(F32)
-    forcing[:, 0, :] = forcing[:, 0, :] + inside * inner
-    forcing[:, cells_radius - 1, :] = forcing[:, cells_radius - 1, :] + outside * outer
+    rows = flat(forcing)
+    for r, term in ((0, inside * inner), (cells_radius - 1, outside * outer)):
+        at = plane(forcing.shape, r)
+        rows[at, :] = rows[at, :] + term
     return above, below
 
 
@@ -184,7 +195,8 @@
 ):
     cells_theta, cells_radius, _ = density.shape
     odd = lax.axis_index("radial") % 2 == 1
-    first, last = density[:, 0, :], density[:, cells_radius - 1, :]
+    rows = flat(density)
+    first, last = (rows[plane(density.shape, r), :] for r in (0, cells_radius - 1))
     pair[...] = jnp.where(odd, first, last)
     link[...] = jnp.where(odd, last, first)
     flow_rows(n_theta, mouth_azimuth, mouth_radius, density, swirl, forcing)
@@ -220,16 +232,16 @@
     copies = []
 
     def leave(begin, count):
-        rows = pl.ds(begin, count)
+        part = pl.ds(begin, count)
         copy = pltpu.make_async_copy(
-            staged.at[:, rows, :], send.at[:, rows, :], sems.at[len(copies)]
+            staged.at[:, part, :], send.at[:, part, :], sems.at[len(copies)]
         )
         copy.start()
         copies.append(copy)
 
-    mine = basis[...]
+    mine, rows = basis[...], flat(forcing)
     for r in range(0, cells_radius, GROUP):
-        modes = sine_modes(mine, [forcing[:, r + i, :] for i in range(GROUP)])
+        modes = sine_modes(mine, [rows[plane(forcing.shape, r + i), :] for i in range(GROUP)])
         for i in range(GROUP):
             lane = slice(i * cells_theta, (i + 1) * cells_theta)
             for d in range(sectors):
@@ -312,7 +324,8 @@
     def store(lane, out):
         modes[:, lane] = out[:columns]
         first, last = out[:edge], out[columns - edge : columns]
-        pair[:, lane] = jnp.where(radial_odd, first, last)
+        pair[:edge, lane] = jnp.where(radial_odd, first, last)
+        pair[edge:, lane] = out[columns:]
         link[:, lane] = jnp.where(radial_odd, last, first)
         wave[:, lane] = out[columns:]
 
@@ -396,7 +409,7 @@
         modes = jnp.concatenate(rows, 0)
         left = jnp.concatenate(split(modes.T), 1)
         out = lax.dot_general(left, right, (NN, ((), ())), preferred_element_type=F32)
-        pressure[:, r, :] = out[:, :cells_axial] + out[:, cells_axial:]
+        flat(pressure)[plane(pressure.shape, r), :] = out[:, :cells_axial] + out[:, cells_axial:]
         if r % 8 == 7:
             rows = pl.ds(r - 7, 8)
             copy = pltpu.make_async_copy(
@@ -432,6 +445,10 @@
     rows[...] = jnp.concatenate([q0, jnp.where(lanes == 0, last, q0), q2, q2, q1, q3, q1, q3], 1)
 
 
+def partner_kernel(edge, wave, pair, out):
+    out[...] = wave[...] + pair[edge:, :]
+
+
 def add_kernel(left, right, out):
     out[...] = left[...] + right[...]
 
@@ -475,8 +492,9 @@
     return lax.ppermute(value, axis, [(i, i ^ bits) for i in range(lax.axis_size(axis))])
 
 
-def halves_of_sum(value, axis):
-    step = 1
+def halves_of_sum(value, axis, step=1):
+    if step >= lax.axis_size(axis):
+        return value, jnp.zeros_like(value)
     while True:
         other = swapped(value, axis, step)
         step *= 2
@@ -576,18 +594,24 @@
 
     modes, pair, link, wave = call(
         lambda *refs: forward_kernel(edge, *refs),
-        [shape(columns, n_theta)] + [shape(edge, n_theta)] * 2 + [shape(own, n_theta)],
+        [
+            shape(columns, n_theta),
+            shape(edge + own, n_theta),
+            shape(edge, n_theta),
+            shape(own, n_theta),
+        ],
         [VMEM] * 2 + [HBM] * 3,
     )(in_vmem(received), table, in_hbm(density_next), in_hbm(acoustic_next), impedance)
+    halo = paired(pair, link, "radial", False)
+    (wave,) = call(
+        lambda *refs: partner_kernel(edge, *refs), [shape(own, n_theta)], [VMEM] * 2
+    )(wave, halo[0])
     (send,) = call(
         solve_kernel,
         [shape(sectors, columns, cells_theta)],
         [VMEM] * 10,
         [pltpu.VMEM((columns, n_theta), F32)],
-    )(
-        modes, *paired(pair, link, "radial", False), *halves_of_sum(wave, "radial"), impedance,
-        fixed, weight, eigen, table,
-    )
+    )(modes, *halo, *halves_of_sum(wave, "radial", 2), impedance, fixed, weight, eigen, table)
     (pressure,) = call(
         pressure_kernel,
         [shape(*density.shape)],

time: 96.8 us -> 93.5 us (0.966)
  Pallas kernels: 17.1 us -> 14 us
  starting transfers between devices: 19.3 us -> 18.2 us
    pallas_call x1, Pallas kernels: 4.84 us -> 2.45 us  [section(): call(lambda *refs: first_kernel(n_radius, *refs), [pltpu.HBM(acoustic.sha...]
    ppermute x4 -> x3, starting transfers between devices: 7.25 us -> 6.1 us  [swapped(): lax.ppermute(value, axis, [(i, i ^ bits) for i in range(lax.axis_size(axi...]
    ppermute x4 -> x3, waiting for transfers between devices: 7.66 us -> 7.81 us  [swapped(): lax.ppermute(value, axis, [(i, i ^ bits) for i in range(lax.axis_size(axi...]
    pallas_call x1 -> x2, Pallas kernels: 2.11 us -> 2.12 us  [the longest x1 2.11 us: section(): call(lambda *refs: forward_kernel(edge, *refs), [shape(columns, n_theta),...]
  transfers between devices with their start and end apart: 11 -> 10, of which waited for: 7 -> 7; matrix products, arithmetic and copies ran while one was open for 0% -> 0% of each run, Pallas kernels for 4% -> 4%
where the time goes in v8:
time: 93.5 us; the launch traced here: 93.2 us
  waiting for transfers between devices  31.2 us (33%)
  blocking collectives  28.2 us (30%)
  starting transfers between devices  18.2 us (19%)
  Pallas kernels  14 us (15%)
    all_to_all x1, blocking collectives, exchanged(): lax.all_to_all(value, 'sector', split_axis=0, concat_axis=0, tiled=True)  28.2 us
    all_to_all x1, waiting for transfers between devices, exchanged(): lax.all_to_all(value, 'sector', split_axis=0, concat_axis=0, tiled=True)  18.3 us
    ppermute x3, waiting for transfers between devices, swapped(): lax.ppermute(value, axis, [(i, i ^ bits) for i in range(lax.axis_size(axi...  7.81 us
    ppermute x6, starting transfers between devices, paired(): return (lax.ppermute(pair, axis, first), lax.ppermute(link, axis, second))  7.69 us
    ppermute x3, starting transfers between devices, swapped(): lax.ppermute(value, axis, [(i, i ^ bits) for i in range(lax.axis_size(axi...  6.1 us
    ppermute x6, waiting for transfers between devices, paired(): return (lax.ppermute(pair, axis, first), lax.ppermute(link, axis, second))  5.02 us
    all_to_all x1, starting transfers between devices, exchanged(): lax.all_to_all(value, 'sector', split_axis=0, concat_axis=0, tiled=True)  4.4 us
    pallas_call x1, Pallas kernels, section(): call(lambda *refs: step_kernel(n_theta, *refs), [shape(*density.shape)],...  2.6 us
  transfers between devices with their start and end apart: 10, of which 7 were waited for; matrix products, arithmetic and copies ran while one was open for 0% of the time, Pallas kernels for 4%

profile of v8, /device:TPU:0, one launch (start us, length us, event | category | flops | bytes accessed | tf_op | source)
XLA Modules:
  0.0 93.2 jit_solution(14081375489977891073)
XLA Ops:
  0.6 0.0 copy-start.2
  0.6 0.0 copy-start.1
  0.7 0.0 copy-start.4
  0.7 0.0 copy-start.12
  0.7 0.0 copy-start.11
  0.7 1.2 %shard_map.139 = (f32[64,128]{1,0:T(8,128)S(1)}, f32[64,128]{1,0:T(8,128)S(1)}) custom-call(f32[128,16,128]{2,1,0:T(8,128)} %refs_2_.4, f32[128,16,128]{2,1,0:T(8,128)} %refs_3_.3, f32[128,16,128]{2,1,0:T(8,128)} %refs_4_.1, f32[3,128,128]{2,1,0:T(8,128)} %refs_2_.5), custom_call_target="tpu_custom_call" | custom-call | bytes 196608 | tf_op jit(solution)/shard_map/pallas_call | solution.py:551
  1.9 0.1 copy-done.2
  2.0 0.3 copy-done.1
  2.3 0.3 copy-done.4
  2.6 0.0 copy-done.12
  2.6 0.0 copy-done.11
  2.7 1.7 %shard_map.140 = (f32[128,16,128]{2,1,0:T(8,128)S(1)}, f32[128,128]{1,0:T(8,128)S(1)}, f32[128,128]{1,0:T(8,128)S(1)}, f32[128,128]{1,0:T(8,128)S(1)}) custom-call(s32[16]{0:T(128)S(1)} %copy-done.11, s32[16]{0:T(128)S(1)} %copy-done.12, f32[128,16,128]{2,1,0:T(8,128)S(1)} %copy-done.1, f32[128,16,128]{2,1,0:T(8,128)S(1)} %copy-done.2, ...), custom_call_target="tpu_custom_call" | custom-call | bytes 3735552 | tf_op jit(solution)/shard_map/pallas_call | solution.py:565
  4.4 0.6 collective-permute-start
  4.9 0.7 collective-permute-start.1
  5.6 5.6 %collective-permute-start.3 = (f32[64,128]{1,0:T(8,128)S(1)}, f32[64,128]{1,0:T(8,128)S(1)}, u32[]{:S(2)}, u32[]{:S(2)}) collective-permute-start(f32[64,128]{1,0:T(8,128)S(1)} %get-tuple-element.18), channel_id=1, source_target_pairs={{4,8},{12,16},{20,24},{28,0},{8,4},{16,12},{24,20},{0,28},{5,9},{1... | collective-permute-start | bytes 98312 | tf_op jit(solution)/shard_map/ppermute | solution.py:488
  11.2 0.0 collective-permute-start.2
  11.2 1.9 %collective-permute-done.3.refs_7_.refs_6_ = f32[64,128]{1,0:T(8,128)S(1)} collective-permute-done((f32[64,128]{1,0:T(8,128)S(1)}, f32[64,128]{1,0:T(8,128)S(1)}, u32[]{:S(2)}, u32[]{:S(2)}) %collective-permute-start.3) | collective-permute-done | bytes 32800 | tf_op jit(solution)/shard_map/ppermute | solution.py:488
  13.1 2.4 %collective-permute-done.2.refs_6_.refs_5_ = f32[64,128]{1,0:T(8,128)S(1)} collective-permute-done((f32[64,128]{1,0:T(8,128)S(1)}, f32[64,128]{1,0:T(8,128)S(1)}, u32[]{:S(2)}, u32[]{:S(2)}) %collective-permute-start.2) | collective-permute-done | bytes 32800 | tf_op jit(solution)/shard_map/ppermute | solution.py:488
  15.5 0.0 collective-permute-done.refs_4_.refs_3_
  15.5 0.0 collective-permute-done.1.refs_5_.refs_4_
  15.5 0.0 copy-done.5
  15.5 0.0 copy-done.6
  15.5 2.4 %shard_map.142 = (f32[3,128,128]{2,1,0:T(8,128)}, f32[8,272,128]{2,1,0:T(8,128)}) custom-call(f32[128,16,128]{2,1,0:T(8,128)S(1)} %get-tuple-element.19.refs_0_, f32[128,128]{1,0:T(8,128)S(1)} %get-tuple-element.20.refs_1_, f32[3,128,128]{2,1,0:T(8,128)S(1)} %copy-done.5, f32[128,128]{1,0:T(8,128)S(1)} %collective-permute-done.refs_4_.refs_3_, ...), custom_call_target="tpu_custom_call" | custom-call | bytes 3932160 | tf_op jit(solution)/shard_map/pallas_call | solution.py:571
  17.9 0.0 copy-start.7
  18.0 0.0 copy-start.13
  18.0 0.0 copy-start
  18.0 4.4 %all-to-all-start = ((f32[8,272,128]{2,1,0:T(8,128)}), f32[8,272,128]{2,1,0:T(8,128)}, u32[]{:S(2)}, u32[]{:S(2)}) async-start(f32[8,272,128]{2,1,0:T(8,128)} %get-tuple-element.21), calls=%async_computation | async-start | bytes 2228224 | tf_op jit(solution)/shard_map/all_to_all | solution.py:519
  22.4 0.0 copy-start.3
  22.4 1.1 %collective-permute-start.4 = (f32[3,128,128]{2,1,0:T(8,128)S(1)}, f32[3,128,128]{2,1,0:T(8,128)S(1)}, u32[]{:S(2)}, u32[]{:S(2)}) collective-permute-start(f32[3,128,128]{2,1,0:T(8,128)S(1)} %copy-done.7), channel_id=1, source_target_pairs={{0,1},{1,0},{2,3},{3,2},{4,5},{5,4},{6,7},{7,6},{8,9},{9,8},{10,11... | collective-permute-start | bytes 589832 | tf_op jit(solution)/shard_map/ppermute | solution.py:492
  23.6 1.1 %collective-permute-done.4.right = f32[3,128,128]{2,1,0:T(8,128)S(1)} collective-permute-done((f32[3,128,128]{2,1,0:T(8,128)S(1)}, f32[3,128,128]{2,1,0:T(8,128)S(1)}, u32[]{:S(2)}, u32[]{:S(2)}) %collective-permute-start.4) | collective-permute-done | bytes 196640 | tf_op jit(solution)/shard_map/ppermute | solution.py:492
  24.6 2.4 %collective-permute-start.5 = (f32[3,128,128]{2,1,0:T(8,128)S(1)}, f32[3,128,128]{2,1,0:T(8,128)S(1)}, u32[]{:S(2)}, u32[]{:S(2)}) collective-permute-start(f32[3,128,128]{2,1,0:T(8,128)S(1)} %shard_map.143.left), channel_id=1, source_target_pairs={{0,2},{1,3},{2,0},{3,1},{4,6},{5,7},{6,4},{7,5},{8,10},{9,11},{10,... | collective-permute-start | bytes 589832 | tf_op jit(solution)/shard_map/ppermute | solution.py:492
  27.0 0.0 copy-done
  27.0 0.3 shard_map.145.refs_4_.impedance
  27.4 2.6 %shard_map.141.refs_2_ = f32[128,16,128]{2,1,0:T(8,128)} custom-call(s32[16]{0:T(128)S(1)} %copy-done.11, s32[16]{0:T(128)S(1)} %copy-done.12, f32[128,16,128]{2,1,0:T(8,128)S(1)} %copy-done.1, f32[128,16,128]{2,1,0:T(8,128)S(1)} %copy-done.3, f32[128,128]{1,0:T(8,128)S(1)} %collective-permute-done.refs_4_.refs_3_, ...), custom_call_target="tpu_custom_call" | custom-call | bytes 3145728 | tf_op jit(solution)/shard_map/pallas_call | solution.py:587
  30.0 2.3 %collective-permute-done.5.right = f32[3,128,128]{2,1,0:T(8,128)S(1)} collective-permute-done((f32[3,128,128]{2,1,0:T(8,128)S(1)}, f32[3,128,128]{2,1,0:T(8,128)S(1)}, u32[]{:S(2)}, u32[]{:S(2)}) %collective-permute-start.5) | collective-permute-done | bytes 196640 | tf_op jit(solution)/shard_map/ppermute | solution.py:492
  32.2 0.7 shard_map.144.refs_3_
  32.9 18.3 %all-to-all-done.refs_0_ = f32[8,272,128]{2,1,0:T(8,128)} async-done(((f32[8,272,128]{2,1,0:T(8,128)}), f32[8,272,128]{2,1,0:T(8,128)}, u32[]{:S(2)}, u32[]{:S(2)}) %all-to-all-start) | async-done | bytes 1114144 | tf_op jit(solution)/shard_map/all_to_all | solution.py:519
  51.3 2.1 %shard_map.146 = (f32[256,1024]{1,0:T(8,128)S(1)}, f32[64,1024]{1,0:T(8,128)S(1)}, f32[48,1024]{1,0:T(8,128)S(1)}, f32[16,1024]{1,0:T(8,128)S(1)}) custom-call(f32[8,272,128]{2,1,0:T(8,128)} %all-to-all-done.refs_0_, bf16[768,1024]{1,0:T(8,128)(2,1)S(1)} %copy-done, f32[128,16,128]{2,1,0:T(8,128)} %shard_map.141.refs_2_, f32[3,128,128]{2,1,0:T(8,128)} %shard_map.144.refs_3_, ...), custom_call_target="tpu_custom_call" | custom-call | bytes 4718592 | tf_op jit(solution)/shard_map/pallas_call | solution.py:595
  53.4 0.2 collective-permute-start.6
  53.6 0.7 collective-permute-start.7
  54.2 0.8 collective-permute-done.6.refs_1_.pair
  55.0 2.6 %collective-permute-start.8 = (f32[16,1024]{1,0:T(8,128)S(1)}, f32[16,1024]{1,0:T(8,128)S(1)}, u32[]{:S(2)}, u32[]{:S(2)}) collective-permute-start(f32[16,1024]{1,0:T(8,128)S(1)} %shard_map.147.wave), channel_id=1, source_target_pairs={{0,2},{1,3},{2,0},{3,1},{4,6},{5,7},{6,4},{7,5},{8,10},{9,11},{10,... | collective-permute-start | bytes 196616 | tf_op jit(solution)/shard_map/ppermute | solution.py:492
  57.6 0.0 collective-permute-done.7.link
  57.6 4.5 %collective-permute-done.8.other_wave = f32[16,1024]{1,0:T(8,128)S(1)} collective-permute-done((f32[16,1024]{1,0:T(8,128)S(1)}, f32[16,1024]{1,0:T(8,128)S(1)}, u32[]{:S(2)}, u32[]{:S(2)}) %collective-permute-start.8) | collective-permute-done | bytes 65568 | tf_op jit(solution)/shard_map/ppermute | solution.py:492
  62.1 0.0 copy-done.8
  62.1 1.5 %shard_map.148 = f32[8,256,128]{2,1,0:T(8,128)S(1)} custom-call(f32[256,1024]{1,0:T(8,128)S(1)} %get-tuple-element.23.modes, f32[64,1024]{1,0:T(8,128)S(1)} %collective-permute-done.6.refs_1_.pair, f32[48,1024]{1,0:T(8,128)S(1)} %collective-permute-done.7.link, f32[16,1024]{1,0:T(8,128)S(1)} %shard_map.147.wave, ...), custom_call_target="tpu_custom_call" | custom-call | bytes 3145728 | tf_op jit(solution)/shard_map/pallas_call | solution.py:609
  63.5 28.2 %all_to_all.10.received = f32[8,256,128]{2,1,0:T(8,128)S(1)} all-to-all(f32[8,256,128]{2,1,0:T(8,128)S(1)} %shard_map.148), channel_id=1, replica_groups=mesh['sector'=8,'radial'=4] {'sector'}, dimensions={0} | all-to-all | bytes 2097152 | tf_op jit(solution)/shard_map/all_to_all | solution.py:519
  91.8 1.5 %shard_map.149 = f32[128,16,128]{2,1,0:T(8,128)} custom-call(f32[8,256,128]{2,1,0:T(8,128)S(1)} %all_to_all.10.received, f32[128,128]{1,0:T(8,128)S(1)} %copy-done.6), custom_call_target="tpu_custom_call" | custom-call | bytes 3145728 | tf_op jit(solution)/shard_map/pallas_call | solution.py:615
  (13 shorter events, 0.1 us)
Async XLA Ops:
  0.6 1.4 %copy-start.2 = (f32[128,16,128]{2,1,0:T(8,128)S(1)}, f32[128,16,128]{2,1,0:T(8,128)}, u32[]{:S(2)}) copy-start(f32[128,16,128]{2,1,0:T(8,128)} %refs_3_.3) | copy-start | bytes 3145732
  0.6 1.7 %copy-start.1 = (f32[128,16,128]{2,1,0:T(8,128)S(1)}, f32[128,16,128]{2,1,0:T(8,128)}, u32[]{:S(2)}) copy-start(f32[128,16,128]{2,1,0:T(8,128)} %refs_2_.4) | copy-start | bytes 3145732
  0.7 2.0 %copy-start.4 = (f32[128,16,128]{2,1,0:T(8,128)S(1)}, f32[128,16,128]{2,1,0:T(8,128)}, u32[]{:S(2)}) copy-start(f32[128,16,128]{2,1,0:T(8,128)} %refs_4_.1) | copy-start | bytes 3145732
  0.7 2.0 %copy-start.12 = (s32[16]{0:T(128)S(1)}, s32[16]{0:T(128)}, u32[]{:S(2)}) copy-start(s32[16]{0:T(128)} %refs_1_.4) | copy-start | bytes 196
  0.7 2.0 %copy-start.11 = (s32[16]{0:T(128)S(1)}, s32[16]{0:T(128)}, u32[]{:S(2)}) copy-start(s32[16]{0:T(128)} %refs_0_.3) | copy-start | bytes 196
  2.7 12.8 %copy-start.5 = (f32[3,128,128]{2,1,0:T(8,128)S(1)}, f32[3,128,128]{2,1,0:T(8,128)}, u32[]{:S(2)}) copy-start(f32[3,128,128]{2,1,0:T(8,128)} %refs_2_.5) | copy-start | bytes 589828
  2.7 12.8 %copy-start.6 = (f32[128,128]{1,0:T(8,128)S(1)}, f32[128,128]{1,0:T(8,128)}, u32[]{:S(2)}) copy-start(f32[128,128]{1,0:T(8,128)} %constant.10.clone.refs_7_.basis) | copy-start | bytes 196612
  4.4 11.1 %collective-permute-start = (f32[128,128]{1,0:T(8,128)S(1)}, f32[128,128]{1,0:T(8,128)S(1)}, u32[]{:S(2)}, u32[]{:S(2)}) collective-permute-start(f32[128,128]{1,0:T(8,128)S(1)} %get-tuple-element.16), channel_id=1, source_target_pairs={{0,1},{1,0},{2,3},{3,2},{4,5},{5,4},{6,7},{7,6},{8,9},{9,8},{10,11... | collective-permute-start | bytes 196616 | tf_op jit(solution)/shard_map/ppermute | solution.py:488
  4.9 10.6 %collective-permute-start.1 = (f32[128,128]{1,0:T(8,128)S(1)}, f32[128,128]{1,0:T(8,128)S(1)}, u32[]{:S(2)}, u32[]{:S(2)}) collective-permute-start(f32[128,128]{1,0:T(8,128)S(1)} %get-tuple-element.17), channel_id=1, source_target_pairs={{1,2},{2,1},{5,6},{6,5},{9,10},{10,9},{13,14},{14,13},{17,18},{18,... | collective-permute-start | bytes 196616 | tf_op jit(solution)/shard_map/ppermute | solution.py:488
  5.6 7.5 %collective-permute-start.3 = (f32[64,128]{1,0:T(8,128)S(1)}, f32[64,128]{1,0:T(8,128)S(1)}, u32[]{:S(2)}, u32[]{:S(2)}) collective-permute-start(f32[64,128]{1,0:T(8,128)S(1)} %get-tuple-element.18), channel_id=1, source_target_pairs={{4,8},{12,16},{20,24},{28,0},{8,4},{16,12},{24,20},{0,28},{5,9},{1... | collective-permute-start | bytes 98312 | tf_op jit(solution)/shard_map/ppermute | solution.py:488
  11.2 4.3 %collective-permute-start.2 = (f32[64,128]{1,0:T(8,128)S(1)}, f32[64,128]{1,0:T(8,128)S(1)}, u32[]{:S(2)}, u32[]{:S(2)}) collective-permute-start(f32[64,128]{1,0:T(8,128)S(1)} %get-tuple-element.15.refs_5_), channel_id=1, source_target_pairs={{0,4},{4,0},{8,12},{12,8},{16,20},{20,16},{24,28},{28,24},{1,5},{5... | collective-permute-start | bytes 98312 | tf_op jit(solution)/shard_map/ppermute | solution.py:488
  17.9 4.5 %copy-start.7 = (f32[3,128,128]{2,1,0:T(8,128)S(1)}, f32[3,128,128]{2,1,0:T(8,128)}, u32[]{:S(2)}) copy-start(f32[3,128,128]{2,1,0:T(8,128)} %get-tuple-element.22.left) | copy-start | bytes 589828
  18.0 9.1 %copy-start.13 = (f32[513]{0:T(1024)S(1)}, f32[513]{0:T(1024)}, u32[]{:S(2)}) copy-start(f32[513]{0:T(1024)} %param.16) | copy-start | bytes 6160
  18.0 9.1 %copy-start = (bf16[768,1024]{1,0:T(8,128)(2,1)S(1)}, bf16[768,1024]{1,0:T(8,128)(2,1)}, u32[]{:S(2)}) copy-start(bf16[768,1024]{1,0:T(8,128)(2,1)} %constant.12.clone._.refs_1_.table) | copy-start | bytes 4718596
  18.0 33.3 %all-to-all-start = ((f32[8,272,128]{2,1,0:T(8,128)}), f32[8,272,128]{2,1,0:T(8,128)}, u32[]{:S(2)}, u32[]{:S(2)}) async-start(f32[8,272,128]{2,1,0:T(8,128)} %get-tuple-element.21), calls=%async_computation | async-start | bytes 2228224 | tf_op jit(solution)/shard_map/all_to_all | solution.py:519
  22.4 5.0 %copy-start.3 = (f32[128,16,128]{2,1,0:T(8,128)S(1)}, f32[128,16,128]{2,1,0:T(8,128)}, u32[]{:S(2)}) copy-start(f32[128,16,128]{2,1,0:T(8,128)} %refs_3_.3) | copy-start | bytes 3145732
  22.4 2.2 %collective-permute-start.4 = (f32[3,128,128]{2,1,0:T(8,128)S(1)}, f32[3,128,128]{2,1,0:T(8,128)S(1)}, u32[]{:S(2)}, u32[]{:S(2)}) collective-permute-start(f32[3,128,128]{2,1,0:T(8,128)S(1)} %copy-done.7), channel_id=1, source_target_pairs={{0,1},{1,0},{2,3},{3,2},{4,5},{5,4},{6,7},{7,6},{8,9},{9,8},{10,11... | collective-permute-start | bytes 589832 | tf_op jit(solution)/shard_map/ppermute | solution.py:492
  24.6 7.6 %collective-permute-start.5 = (f32[3,128,128]{2,1,0:T(8,128)S(1)}, f32[3,128,128]{2,1,0:T(8,128)S(1)}, u32[]{:S(2)}, u32[]{:S(2)}) collective-permute-start(f32[3,128,128]{2,1,0:T(8,128)S(1)} %shard_map.143.left), channel_id=1, source_target_pairs={{0,2},{1,3},{2,0},{3,1},{4,6},{5,7},{6,4},{7,5},{8,10},{9,11},{10,... | collective-permute-start | bytes 589832 | tf_op jit(solution)/shard_map/ppermute | solution.py:492
  32.9 29.1 %copy-start.8 = (f32[8,16,128]{2,1,0:T(8,128)S(1)}, f32[8,16,128]{2,1,0:T(8,128)}, u32[]{:S(2)}) copy-start(f32[8,16,128]{2,1,0:T(8,128)} %constant.11.clone.axial) | copy-start | bytes 196612
  32.9 29.1 %copy-start.9 = (f32[1,1024]{1,0:T(1,128)S(1)}, f32[1,1024]{1,0:T(1,128)}, u32[]{:S(2)}) copy-start(f32[1,1024]{1,0:T(1,128)} %constant.16.weight) | copy-start | bytes 12292
  32.9 29.1 %copy-start.10 = (f32[1,1024]{1,0:T(1,128)S(1)}, f32[1,1024]{1,0:T(1,128)}, u32[]{:S(2)}) copy-start(f32[1,1024]{1,0:T(1,128)} %constant.15.fixed) | copy-start | bytes 12292
  53.4 1.6 %collective-permute-start.6 = (f32[64,1024]{1,0:T(8,128)S(1)}, f32[64,1024]{1,0:T(8,128)S(1)}, u32[]{:S(2)}, u32[]{:S(2)}) collective-permute-start(f32[64,1024]{1,0:T(8,128)S(1)} %get-tuple-element.24), channel_id=1, source_target_pairs={{0,1},{1,0},{2,3},{3,2},{4,5},{5,4},{6,7},{7,6},{8,9},{9,8},{10,11... | collective-permute-start | bytes 786440 | tf_op jit(solution)/shard_map/ppermute | solution.py:488
  53.6 4.0 %collective-permute-start.7 = (f32[48,1024]{1,0:T(8,128)S(1)}, f32[48,1024]{1,0:T(8,128)S(1)}, u32[]{:S(2)}, u32[]{:S(2)}) collective-permute-start(f32[48,1024]{1,0:T(8,128)S(1)} %get-tuple-element.25), channel_id=1, source_target_pairs={{1,2},{2,1},{5,6},{6,5},{9,10},{10,9},{13,14},{14,13},{17,18},{18,... | collective-permute-start | bytes 589832 | tf_op jit(solution)/shard_map/ppermute | solution.py:488
  55.0 7.1 %collective-permute-start.8 = (f32[16,1024]{1,0:T(8,128)S(1)}, f32[16,1024]{1,0:T(8,128)S(1)}, u32[]{:S(2)}, u32[]{:S(2)}) collective-permute-start(f32[16,1024]{1,0:T(8,128)S(1)} %shard_map.147.wave), channel_id=1, source_target_pairs={{0,2},{1,3},{2,0},{3,1},{4,6},{5,7},{6,4},{7,5},{8,10},{9,11},{10,... | collective-permute-start | bytes 196616 | tf_op jit(solution)/shard_map/ppermute | solution.py:492

commit v9 on v8

--- a/solution.py
+++ b/solution.py
@@ -187,7 +187,6 @@
     for r, term in ((0, inside * inner), (cells_radius - 1, outside * outer)):
         at = plane(forcing.shape, r)
         rows[at, :] = rows[at, :] + term
-    return above, below
 
 
 def flow_kernel(
@@ -220,15 +219,13 @@
 
 
 def first_kernel(
-    n_radius, partial, heat, acoustic, radial_pair, radial_link, sector_pair, sector_link, basis,
-    state, send, forcing, following, staged, sems
+    partial, radial_pair, radial_link, sector_pair, sector_link, basis, send, forcing, staged, sems
 ):
-    radial = lax.axis_index("radial")
     cells_theta, cells_radius, cells_axial = partial.shape
     sectors = send.shape[0]
     own = cells_axial // sectors
     forcing[...] = partial[...]
-    above, below = add_halos(forcing, radial_pair, radial_link, sector_pair, sector_link)
+    add_halos(forcing, radial_pair, radial_link, sector_pair, sector_link)
     copies = []
 
     def leave(begin, count):
@@ -250,8 +247,18 @@
                 ]
         leave(r * own, GROUP * own)
 
+    for copy in copies:
+        copy.wait()
+
+
+def acoustic_kernel(n_radius, heat, acoustic, pair, link, share_press, share_rest, following, sem):
+    radial = lax.axis_index("radial")
+    cells_theta, cells_axial = heat.shape
+    odd = lax.axis_index("sector") % 2 == 1
+    above = jnp.where(odd, link[...], pair[...])
+    below = jnp.where(odd, pair[...], link[...])
     share = (radial == 0).astype(F32)
-    skip = 2 * cells_radius
+    skip = above.shape[0] - 4 * EDGE
 
     def extended(k):
         rows = slice(skip + k * EDGE, skip + (k + 1) * EDGE)
@@ -271,18 +278,42 @@
         axial_down = jnp.where(lanes == 0, 0.0, pltpu.roll(axial, 1, 1))
         press = press - wave_speed * ((along - along_down) + (axial - axial_down)) + warm
     middle = slice(EDGE, EDGE + cells_theta)
-    following[0] = press[middle]
-    following[1] = along[middle]
-    following[2] = axial[middle]
-    copies.append(pltpu.make_async_copy(following, state, sems.at[len(copies)]))
-    copies[-1].start()
-    modes = sine_modes(mine, [feedback * press[middle]])
-    columns = cells_radius * own
-    for d in range(sectors):
-        staged[d, columns : columns + own, :] = modes[d * own : (d + 1) * own]
-    leave(columns, own)
-    for copy in copies:
-        copy.wait()
+    share_press[...] = press[middle]
+    following[0] = along[middle]
+    following[1] = axial[middle]
+    copy = pltpu.make_async_copy(following, share_rest, sem)
+    copy.start()
+    copy.wait()
+
+
+def part_kernel(press, basis, *parts):
+    count, own = len(parts), parts[0].shape[1]
+    sector, radial = lax.axis_index("sector"), lax.axis_index("radial")
+    rows = [
+        basis[pl.ds(pl.multiple_of((sector ^ (radial * count + j)) * own, 8), own), :]
+        for j in range(count)
+    ]
+    modes = sine_modes(jnp.concatenate(rows, 0), [feedback * press[...]])
+    for j in range(count):
+        parts[j][0] = modes[j * own : (j + 1) * own]
+
+
+def acoustic_next_kernel(press, left, right, acoustic_next):
+    acoustic_next[0] = press[...]
+    acoustic_next[1:] = left[...] + right[...]
+
+
+def wave_kernel(count, *refs):
+    parts, (table, wave, pieces) = refs[:-3], refs[-3:]
+    sector, radial = lax.axis_index("sector"), lax.axis_index("radial")
+    for i, part in enumerate(parts):
+        offset, j = divmod(i, count)
+        pieces[sector ^ ((radial ^ offset) * count + j)] = part[...].reshape(part.shape[-2:])
+
+    def store(lane, out):
+        wave[:, lane] = out
+
+    transformed([pieces[s] for s in range(pieces.shape[0])], table, store)
 
 
 def transformed(values, table, store):
@@ -316,24 +347,21 @@
 
 
 def forward_kernel(edge, received, table, *refs):
-    modes, pair, link, wave = refs[-4:]
-    sectors = received.shape[0]
-    columns = modes.shape[0]
+    modes, pair, link = refs[-3:]
+    sectors, columns, _ = received.shape
     radial_odd = lax.axis_index("radial") % 2 == 1
 
     def store(lane, out):
-        modes[:, lane] = out[:columns]
-        first, last = out[:edge], out[columns - edge : columns]
-        pair[:edge, lane] = jnp.where(radial_odd, first, last)
-        pair[edge:, lane] = out[columns:]
+        modes[:, lane] = out
+        first, last = out[:edge], out[columns - edge :]
+        pair[:, lane] = jnp.where(radial_odd, first, last)
         link[:, lane] = jnp.where(radial_odd, last, first)
-        wave[:, lane] = out[columns:]
 
     transformed([received[s] for s in range(sectors)], table, store)
 
 
 def solve_kernel(
-    modes, pair, link, wave, other_wave, impedance, fixed, weight, axial, table, send, solved
+    modes, pair, link, wave, impedance, fixed, weight, axial, table, send, solved
 ):
     radials = lax.axis_size("radial")
     radial = lax.axis_index("radial")
@@ -353,7 +381,7 @@
         inv = jnp.broadcast_to(row, (each, step))
         inv_inner, inv_outer = inv * has_inner, inv * has_outer
         last_scale = jnp.broadcast_to(row * weight[:, lane], (each, step))
-        add = wave[:, lane] + other_wave[:, lane]
+        add = wave[:, lane]
 
         def row_of(i):
             i -= HALO
@@ -445,10 +473,6 @@
     rows[...] = jnp.concatenate([q0, jnp.where(lanes == 0, last, q0), q2, q2, q1, q3, q1, q3], 1)
 
 
-def partner_kernel(edge, wave, pair, out):
-    out[...] = wave[...] + pair[edge:, :]
-
-
 def add_kernel(left, right, out):
     out[...] = left[...] + right[...]
 
@@ -501,6 +525,16 @@
         if step >= lax.axis_size(axis):
             return value, other
         value = added(value, other)
+
+
+def spread_part(part, j, count):
+    sectors, radials = lax.axis_size("sector"), lax.axis_size("radial")
+    pairs = [
+        (s * radials + r, (s ^ (r * count + j)) * radials + r)
+        for s in range(sectors)
+        for r in range(radials)
+    ]
+    return lax.ppermute(part, ("sector", "radial"), pairs)
 
 
 def added(left, right):
@@ -568,50 +602,63 @@
         [SMEM] * 2 + [VMEM] * 3 + [HBM],
     )(mouth_azimuth, mouth_radius, density, swirl, heat_rate, edge_rows)
     radial_halo = paired(pair, link, "radial", False)
-    state, send = call(
-        lambda *refs: first_kernel(n_radius, *refs),
-        [
-            pltpu.HBM(acoustic.shape, F32),
-            pltpu.HBM((sectors, columns + own, cells_theta), F32),
-        ],
-        [VMEM] * 8,
+    (send,) = call(
+        first_kernel,
+        [pltpu.HBM((sectors, columns, cells_theta), F32)],
+        [VMEM] * 6,
         [
             pltpu.VMEM(density.shape, F32),
-            pltpu.VMEM(acoustic.shape, F32),
-            pltpu.VMEM((sectors, columns + own, cells_theta), F32),
-            pltpu.SemaphoreType.DMA((2 + cells_radius // GROUP,)),
+            pltpu.VMEM((sectors, columns, cells_theta), F32),
+            pltpu.SemaphoreType.DMA((cells_radius // GROUP,)),
         ],
-        out_specs=[HBM, HBM],
-    )(partial, heat, acoustic, *radial_halo, *sector_halo, basis)
+        out_specs=[HBM],
+    )(partial, *radial_halo, *sector_halo, basis)
     received = exchanged(send)
+
+    rest_shape = (2, cells_theta, cells_axial)
+    press, rest = call(
+        lambda *refs: acoustic_kernel(n_radius, *refs),
+        [row_block, pltpu.HBM(rest_shape, F32)],
+        [VMEM] * 4,
+        [pltpu.VMEM(rest_shape, F32), pltpu.SemaphoreType.DMA],
+        out_specs=[VMEM, HBM],
+    )(heat, acoustic, *sector_halo)
+    press = added(*halves_of_sum(press, "radial"))
+    count = sectors // radials
+    parts = call(part_kernel, [shape(1, own, cells_theta)] * count, [VMEM] * 2)(press, basis)
+    parts = [spread_part(part, j, count) for j, part in enumerate(parts)]
+    step = 1
+    while step < radials:
+        parts += [swapped(value, "radial", step) for value in parts]
+        step *= 2
+    (wave,) = call(
+        lambda *refs: wave_kernel(count, *refs),
+        [shape(own, n_theta)],
+        [VMEM] * (sectors + 1),
+        [pltpu.VMEM((sectors, own, cells_theta), F32)],
+    )(*parts, table)
+    rest = halves_of_sum(rest, "radial")
+    (acoustic_next,) = call(acoustic_next_kernel, [shape(*acoustic.shape)], [VMEM] * 3)(
+        press, *rest
+    )
     (density_next,) = call(
         lambda *refs: step_kernel(n_theta, *refs),
         [shape(*density.shape)],
         [SMEM] * 2 + [VMEM] * 6,
         [pltpu.VMEM(density.shape, F32)],
     )(mouth_azimuth, mouth_radius, density, swirl, *radial_halo, *sector_halo)
-    acoustic_next = added(*halves_of_sum(state, "radial"))
-
-    modes, pair, link, wave = call(
+
+    modes, pair, link = call(
         lambda *refs: forward_kernel(edge, *refs),
-        [
-            shape(columns, n_theta),
-            shape(edge + own, n_theta),
-            shape(edge, n_theta),
-            shape(own, n_theta),
-        ],
-        [VMEM] * 2 + [HBM] * 3,
-    )(in_vmem(received), table, in_hbm(density_next), in_hbm(acoustic_next), impedance)
-    halo = paired(pair, link, "radial", False)
-    (wave,) = call(
-        lambda *refs: partner_kernel(edge, *refs), [shape(own, n_theta)], [VMEM] * 2
-    )(wave, halo[0])
+        [shape(columns, n_theta), shape(edge, n_theta), shape(edge, n_theta)],
+        [VMEM] * 2 + [HBM] * 4,
+    )(in_vmem(received), table, in_hbm(density_next), in_hbm(acoustic_next), impedance, wave)
     (send,) = call(
         solve_kernel,
         [shape(sectors, columns, cells_theta)],
-        [VMEM] * 10,
+        [VMEM] * 9,
         [pltpu.VMEM((columns, n_theta), F32)],
-    )(modes, *halo, *halves_of_sum(wave, "radial", 2), impedance, fixed, weight, eigen, table)
+    )(modes, *paired(pair, link, "radial", False), wave, impedance, fixed, weight, eigen, table)
     (pressure,) = call(
         pressure_kernel,
         [shape(*density.shape)],

time: 93.5 us -> 92.8 us (level)
  the two profiles are of different devices: /device:TPU:0 before, /device:TPU:1 now
where the time goes in v9:
time: 92.8 us; the launch traced here: 92.5 us
  starting transfers between devices  34.2 us (37%)
  blocking collectives  24 us (26%)
  waiting for transfers between devices  16.3 us (18%)
  Pallas kernels  15.4 us (17%)
  local copies, waits for them, and re-layouts  1.7 us (2%)
    all_to_all x1, blocking collectives, exchanged(): lax.all_to_all(value, 'sector', split_axis=0, concat_axis=0, tiled=True)  24 us
    ppermute x6, starting transfers between devices, paired(): return (lax.ppermute(pair, axis, first), lax.ppermute(link, axis, second))  13.3 us
    ppermute x10, starting transfers between devices, swapped(): lax.ppermute(value, axis, [(i, i ^ bits) for i in range(lax.axis_size(axi...  11.8 us
    ppermute x6, waiting for transfers between devices, paired(): return (lax.ppermute(pair, axis, first), lax.ppermute(link, axis, second))  6.85 us
    ppermute x10, waiting for transfers between devices, swapped(): lax.ppermute(value, axis, [(i, i ^ bits) for i in range(lax.axis_size(axi...  5.98 us
    ppermute x2, starting transfers between devices, spread_part(): return lax.ppermute(part, ('sector', 'radial'), pairs)  4.76 us
    all_to_all x1, starting transfers between devices, exchanged(): lax.all_to_all(value, 'sector', split_axis=0, concat_axis=0, tiled=True)  4.38 us
    ppermute x2, waiting for transfers between devices, spread_part(): return lax.ppermute(part, ('sector', 'radial'), pairs)  3.42 us
  transfers between devices with their start and end apart: 19, of which 7 were waited for; matrix products, arithmetic and copies ran while one was open for 0% of the time, Pallas kernels for 7%

profile of v9, /device:TPU:1, one launch (start us, length us, event | category | flops | bytes accessed | tf_op | source)
XLA Modules:
  0.0 92.5 jit_solution(3538484041725946631)
XLA Ops:
  0.6 0.0 copy-start.2
  0.7 1.2 %shard_map.139 = (f32[64,128]{1,0:T(8,128)S(1)}, f32[64,128]{1,0:T(8,128)S(1)}) custom-call(f32[128,16,128]{2,1,0:T(8,128)} %refs_2_.3, f32[128,16,128]{2,1,0:T(8,128)} %refs_3_.3, f32[128,16,128]{2,1,0:T(8,128)} %refs_4_.1, f32[3,128,128]{2,1,0:T(8,128)} %refs_1_.6), custom_call_target="tpu_custom_call" | custom-call | bytes 196608 | tf_op jit(solution)/shard_map/pallas_call | solution.py:585
  1.9 0.1 copy-done.2
  2.0 0.3 copy-done.1
  2.3 0.3 copy-done.4
  2.7 1.7 %shard_map.140 = (f32[128,16,128]{2,1,0:T(8,128)S(1)}, f32[128,128]{1,0:T(8,128)S(1)}, f32[128,128]{1,0:T(8,128)S(1)}, f32[128,128]{1,0:T(8,128)S(1)}) custom-call(s32[16]{0:T(128)S(1)} %copy-done.11, s32[16]{0:T(128)S(1)} %copy-done.12, f32[128,16,128]{2,1,0:T(8,128)S(1)} %copy-done.1, f32[128,16,128]{2,1,0:T(8,128)S(1)} %copy-done.2, ...), custom_call_target="tpu_custom_call" | custom-call | bytes 3735552 | tf_op jit(solution)/shard_map/pallas_call | solution.py:599
  4.3 0.1 collective-permute-start
  4.4 4.5 %collective-permute-start.1 = (f32[128,128]{1,0:T(8,128)S(1)}, f32[128,128]{1,0:T(8,128)S(1)}, u32[]{:S(2)}, u32[]{:S(2)}) collective-permute-start(f32[128,128]{1,0:T(8,128)S(1)} %get-tuple-element.18), channel_id=1, source_target_pairs={{1,2},{2,1},{5,6},{6,5},{9,10},{10,9},{13,14},{14,13},{17,18},{18,... | collective-permute-start | bytes 196616 | tf_op jit(solution)/shard_map/ppermute | solution.py:512
  8.9 4.3 %collective-permute-start.3 = (f32[64,128]{1,0:T(8,128)S(1)}, f32[64,128]{1,0:T(8,128)S(1)}, u32[]{:S(2)}, u32[]{:S(2)}) collective-permute-start(f32[64,128]{1,0:T(8,128)S(1)} %get-tuple-element.19), channel_id=1, source_target_pairs={{4,8},{12,16},{20,24},{28,0},{8,4},{16,12},{24,20},{0,28},{5,9},{1... | collective-permute-start | bytes 98312 | tf_op jit(solution)/shard_map/ppermute | solution.py:512
  13.3 1.4 %collective-permute-done.3.refs_7_.sector_link.refs_3_ = f32[64,128]{1,0:T(8,128)S(1)} collective-permute-done((f32[64,128]{1,0:T(8,128)S(1)}, f32[64,128]{1,0:T(8,128)S(1)}, u32[]{:S(2)}, u32[]{:S(2)}) %collective-permute-start.3) | collective-permute-done | bytes 32800 | tf_op jit(solution)/shard_map/ppermute | solution.py:512
  14.7 1.4 %collective-permute-done.2.refs_6_.sector_pair.refs_2_ = f32[64,128]{1,0:T(8,128)S(1)} collective-permute-done((f32[64,128]{1,0:T(8,128)S(1)}, f32[64,128]{1,0:T(8,128)S(1)}, u32[]{:S(2)}, u32[]{:S(2)}) %collective-permute-start.2) | collective-permute-done | bytes 32800 | tf_op jit(solution)/shard_map/ppermute | solution.py:512
  16.0 0.0 collective-permute-done.refs_4_.radial_pair
  16.0 0.0 collective-permute-done.1.refs_5_.radial_link
  16.0 1.5 %shard_map.142 = f32[8,256,128]{2,1,0:T(8,128)} custom-call(f32[128,16,128]{2,1,0:T(8,128)S(1)} %get-tuple-element.20.partial, f32[128,128]{1,0:T(8,128)S(1)} %collective-permute-done.refs_4_.radial_pair, f32[128,128]{1,0:T(8,128)S(1)} %collective-permute-done.1.refs_5_.radial_link, f32[64,128]{1,0:T(8,128)S(1)} %collective-permute-done.2.refs_6_.sector_pair.refs_2_, ...), custom_call_target="tpu_custom_call" | custom-call | bytes 3145728 | tf_op jit(solution)/shard_map/pallas_call | solution.py:605
  17.6 0.0 copy-start.5
  17.6 0.0 copy-start.13
  17.6 0.0 copy-start
  17.6 4.4 %all-to-all-start = ((f32[8,256,128]{2,1,0:T(8,128)}), f32[8,256,128]{2,1,0:T(8,128)}, u32[]{:S(2)}, u32[]{:S(2)}) async-start(f32[8,256,128]{2,1,0:T(8,128)} %shard_map.142), calls=%async_computation | async-start | bytes 2097152 | tf_op jit(solution)/shard_map/all_to_all | solution.py:553
  22.0 0.0 copy-start.3
  22.0 1.8 %shard_map.143 = (f32[128,128]{1,0:T(8,128)S(1)}, f32[2,128,128]{2,1,0:T(8,128)}) custom-call(f32[128,128]{1,0:T(8,128)S(1)} %get-tuple-element.21.refs_0_, f32[3,128,128]{2,1,0:T(8,128)S(1)} %copy-done.5, f32[64,128]{1,0:T(8,128)S(1)} %collective-permute-done.2.refs_6_.sector_pair.refs_2_, f32[64,128]{1,0:T(8,128)S(1)} %collective-permute-done.3.refs_7_.sector_link.refs_3_), custom_call_target="tpu_custom_call" | custom-call | bytes 589824 | tf_op jit(solution)/shard_map/pallas_call | solution.py:619
  23.8 0.1 collective-permute-start.6
  23.9 0.5 collective-permute-start.4
  24.4 1.0 %collective-permute-done.6.right = f32[2,128,128]{2,1,0:T(8,128)S(1)} collective-permute-done((f32[2,128,128]{2,1,0:T(8,128)}, f32[2,128,128]{2,1,0:T(8,128)S(1)}, u32[]{:S(2)}, u32[]{:S(2)}) %collective-permute-start.6) | collective-permute-done | bytes 131104 | tf_op jit(solution)/shard_map/ppermute | solution.py:516
  25.4 0.9 copy-done.7
  26.4 1.9 %collective-permute-start.7 = (f32[2,128,128]{2,1,0:T(8,128)S(1)}, f32[2,128,128]{2,1,0:T(8,128)S(1)}, u32[]{:S(2)}, u32[]{:S(2)}) collective-permute-start(f32[2,128,128]{2,1,0:T(8,128)S(1)} %shard_map.146.left), channel_id=1, source_target_pairs={{0,2},{1,3},{2,0},{3,1},{4,6},{5,7},{6,4},{7,5},{8,10},{9,11},{10,... | collective-permute-start | bytes 393224 | tf_op jit(solution)/shard_map/ppermute | solution.py:516
  28.2 0.0 collective-permute-done.4.right
  28.3 0.1 collective-permute-start.5
  28.3 4.9 %collective-permute-done.5.right = f32[128,128]{1,0:T(8,128)S(1)} collective-permute-done((f32[128,128]{1,0:T(8,128)S(1)}, f32[128,128]{1,0:T(8,128)S(1)}, u32[]{:S(2)}, u32[]{:S(2)}) %collective-permute-start.5) | collective-permute-done | bytes 65568 | tf_op jit(solution)/shard_map/ppermute | solution.py:516
  33.3 0.1 shard_map.149
  33.4 3.5 %collective-permute-start.8 = (f32[1,16,128]{2,1,0:T(8,128)S(1)}, f32[1,16,128]{2,1,0:T(8,128)S(1)}, u32[]{:S(2)}, u32[]{:S(2)}) collective-permute-start(f32[1,16,128]{2,1,0:T(8,128)S(1)} %get-tuple-element.24), channel_id=1, source_target_pairs={{0,0},{1,9},{2,18},{3,27},{4,4},{5,13},{6,22},{7,31},{8,8},{9,1},{... | collective-permute-start | bytes 24584 | tf_op jit(solution)/shard_map/ppermute | solution.py:537
  36.9 1.2 %collective-permute-start.9 = (f32[1,16,128]{2,1,0:T(8,128)S(1)}, f32[1,16,128]{2,1,0:T(8,128)S(1)}, u32[]{:S(2)}, u32[]{:S(2)}) collective-permute-start(f32[1,16,128]{2,1,0:T(8,128)S(1)} %get-tuple-element.25), channel_id=1, source_target_pairs={{0,4},{1,13},{2,22},{3,31},{4,0},{5,9},{6,18},{7,27},{8,12},{9,5},... | collective-permute-start | bytes 24584 | tf_op jit(solution)/shard_map/ppermute | solution.py:537
  38.2 2.6 %collective-permute-done.8.refs_0_ = f32[1,16,128]{2,1,0:T(8,128)S(1)} collective-permute-done((f32[1,16,128]{2,1,0:T(8,128)S(1)}, f32[1,16,128]{2,1,0:T(8,128)S(1)}, u32[]{:S(2)}, u32[]{:S(2)}) %collective-permute-start.8) | collective-permute-done | bytes 8224 | tf_op jit(solution)/shard_map/ppermute | solution.py:537
  40.8 0.8 collective-permute-done.9.refs_1_
  41.6 7.7 %collective-permute-start.12 = (f32[1,16,128]{2,1,0:T(8,128)S(1)}, f32[1,16,128]{2,1,0:T(8,128)S(1)}, u32[]{:S(2)}, u32[]{:S(2)}) collective-permute-start(f32[1,16,128]{2,1,0:T(8,128)S(1)} %collective-permute-done.8.refs_0_), channel_id=1, source_target_pairs={{0,2},{1,3},{2,0},{3,1},{4,6},{5,7},{6,4},{7,5},{8,10},{9,11},{10,... | collective-permute-start | bytes 24584 | tf_op jit(solution)/shard_map/ppermute | solution.py:516
  49.3 0.0 collective-permute-start.13
  49.3 1.4 %collective-permute-start.14 = (f32[1,16,128]{2,1,0:T(8,128)S(1)}, f32[1,16,128]{2,1,0:T(8,128)S(1)}, u32[]{:S(2)}, u32[]{:S(2)}) collective-permute-start(f32[1,16,128]{2,1,0:T(8,128)S(1)} %collective-permute-done.10.refs_2_), channel_id=1, source_target_pairs={{0,2},{1,3},{2,0},{3,1},{4,6},{5,7},{6,4},{7,5},{8,10},{9,11},{10,... | collective-permute-start | bytes 24584 | tf_op jit(solution)/shard_map/ppermute | solution.py:516
  50.8 0.1 collective-permute-start.15
  50.9 0.3 shard_map.148.refs_4_.impedance
  51.2 2.6 %shard_map.141.refs_2_ = f32[128,16,128]{2,1,0:T(8,128)} custom-call(s32[16]{0:T(128)S(1)} %copy-done.11, s32[16]{0:T(128)S(1)} %copy-done.12, f32[128,16,128]{2,1,0:T(8,128)S(1)} %copy-done.1, f32[128,16,128]{2,1,0:T(8,128)S(1)} %copy-done.3, f32[128,128]{1,0:T(8,128)S(1)} %collective-permute-done.refs_4_.radial_pair, ...), custom_call_target="tpu_custom_call" | custom-call | bytes 3145728 | tf_op jit(solution)/shard_map/pallas_call | solution.py:644
  53.8 0.4 shard_map.150.refs_5_.wave
  54.2 0.7 shard_map.147.refs_3_
  55.0 2.1 %shard_map.151 = (f32[256,1024]{1,0:T(8,128)S(1)}, f32[48,1024]{1,0:T(8,128)S(1)}, f32[48,1024]{1,0:T(8,128)S(1)}) custom-call(f32[8,256,128]{2,1,0:T(8,128)} %all-to-all-done.refs_0_, bf16[768,1024]{1,0:T(8,128)(2,1)S(1)} %copy-done, f32[128,16,128]{2,1,0:T(8,128)} %shard_map.141.refs_2_, f32[3,128,128]{2,1,0:T(8,128)} %shard_map.147.refs_3_, ...), custom_call_target="tpu_custom_call" | custom-call | bytes 4325376 | tf_op jit(solution)/shard_map/pallas_call | solution.py:651
  57.1 1.5 %collective-permute-start.16 = (f32[48,1024]{1,0:T(8,128)S(1)}, f32[48,1024]{1,0:T(8,128)S(1)}, u32[]{:S(2)}, u32[]{:S(2)}) collective-permute-start(f32[48,1024]{1,0:T(8,128)S(1)} %get-tuple-element.27), channel_id=1, source_target_pairs={{0,1},{1,0},{2,3},{3,2},{4,5},{5,4},{6,7},{7,6},{8,9},{9,8},{10,11... | collective-permute-start | bytes 589832 | tf_op jit(solution)/shard_map/ppermute | solution.py:512
  58.6 2.9 %collective-permute-start.17 = (f32[48,1024]{1,0:T(8,128)S(1)}, f32[48,1024]{1,0:T(8,128)S(1)}, u32[]{:S(2)}, u32[]{:S(2)}) collective-permute-start(f32[48,1024]{1,0:T(8,128)S(1)} %get-tuple-element.28), channel_id=1, source_target_pairs={{1,2},{2,1},{5,6},{6,5},{9,10},{10,9},{13,14},{14,13},{17,18},{18,... | collective-permute-start | bytes 589832 | tf_op jit(solution)/shard_map/ppermute | solution.py:512
  61.5 4.1 %collective-permute-done.17.link = f32[48,1024]{1,0:T(8,128)S(1)} collective-permute-done((f32[48,1024]{1,0:T(8,128)S(1)}, f32[48,1024]{1,0:T(8,128)S(1)}, u32[]{:S(2)}, u32[]{:S(2)}) %collective-permute-start.17) | collective-permute-done | bytes 196640 | tf_op jit(solution)/shard_map/ppermute | solution.py:512
  65.6 1.4 %shard_map.152 = f32[8,256,128]{2,1,0:T(8,128)S(1)} custom-call(f32[256,1024]{1,0:T(8,128)S(1)} %get-tuple-element.26.modes, f32[48,1024]{1,0:T(8,128)S(1)} %collective-permute-done.16.pair, f32[48,1024]{1,0:T(8,128)S(1)} %collective-permute-done.17.link, f32[16,1024]{1,0:T(8,128)S(1)} %shard_map.150.refs_5_.wave, ...), custom_call_target="tpu_custom_call" | custom-call | bytes 3145728 | tf_op jit(solution)/shard_map/pallas_call | solution.py:656
  67.0 24.0 %all_to_all.10.received = f32[8,256,128]{2,1,0:T(8,128)S(1)} all-to-all(f32[8,256,128]{2,1,0:T(8,128)S(1)} %shard_map.152), channel_id=1, replica_groups=mesh['sector'=8,'radial'=4] {'sector'}, dimensions={0} | all-to-all | bytes 2097152 | tf_op jit(solution)/shard_map/all_to_all | solution.py:553
  91.0 1.5 %shard_map.153 = f32[128,16,128]{2,1,0:T(8,128)} custom-call(f32[8,256,128]{2,1,0:T(8,128)S(1)} %all_to_all.10.received, f32[128,128]{1,0:T(8,128)S(1)} %copy-done.6), custom_call_target="tpu_custom_call" | custom-call | bytes 3145728 | tf_op jit(solution)/shard_map/pallas_call | solution.py:662
  (35 shorter events, 0.1 us)
Async XLA Ops:
  0.6 1.4 %copy-start.2 = (f32[128,16,128]{2,1,0:T(8,128)S(1)}, f32[128,16,128]{2,1,0:T(8,128)}, u32[]{:S(2)}) copy-start(f32[128,16,128]{2,1,0:T(8,128)} %refs_3_.3) | copy-start | bytes 3145732
  0.6 1.7 %copy-start.1 = (f32[128,16,128]{2,1,0:T(8,128)S(1)}, f32[128,16,128]{2,1,0:T(8,128)}, u32[]{:S(2)}) copy-start(f32[128,16,128]{2,1,0:T(8,128)} %refs_2_.3) | copy-start | bytes 3145732
  0.7 2.0 %copy-start.4 = (f32[128,16,128]{2,1,0:T(8,128)S(1)}, f32[128,16,128]{2,1,0:T(8,128)}, u32[]{:S(2)}) copy-start(f32[128,16,128]{2,1,0:T(8,128)} %refs_4_.1) | copy-start | bytes 3145732
  0.7 2.0 %copy-start.12 = (s32[16]{0:T(128)S(1)}, s32[16]{0:T(128)}, u32[]{:S(2)}) copy-start(s32[16]{0:T(128)} %refs_1_.5) | copy-start | bytes 196
  0.7 2.0 %copy-start.11 = (s32[16]{0:T(128)S(1)}, s32[16]{0:T(128)}, u32[]{:S(2)}) copy-start(s32[16]{0:T(128)} %refs_0_.3) | copy-start | bytes 196
  2.7 13.4 %copy-start.6 = (f32[128,128]{1,0:T(8,128)S(1)}, f32[128,128]{1,0:T(8,128)}, u32[]{:S(2)}) copy-start(f32[128,128]{1,0:T(8,128)} %constant.10.clone.basis) | copy-start | bytes 196612
  4.3 11.7 %collective-permute-start = (f32[128,128]{1,0:T(8,128)S(1)}, f32[128,128]{1,0:T(8,128)S(1)}, u32[]{:S(2)}, u32[]{:S(2)}) collective-permute-start(f32[128,128]{1,0:T(8,128)S(1)} %get-tuple-element.17), channel_id=1, source_target_pairs={{0,1},{1,0},{2,3},{3,2},{4,5},{5,4},{6,7},{7,6},{8,9},{9,8},{10,11... | collective-permute-start | bytes 196616 | tf_op jit(solution)/shard_map/ppermute | solution.py:512
  4.4 11.6 %collective-permute-start.1 = (f32[128,128]{1,0:T(8,128)S(1)}, f32[128,128]{1,0:T(8,128)S(1)}, u32[]{:S(2)}, u32[]{:S(2)}) collective-permute-start(f32[128,128]{1,0:T(8,128)S(1)} %get-tuple-element.18), channel_id=1, source_target_pairs={{1,2},{2,1},{5,6},{6,5},{9,10},{10,9},{13,14},{14,13},{17,18},{18,... | collective-permute-start | bytes 196616 | tf_op jit(solution)/shard_map/ppermute | solution.py:512
  8.9 5.7 %collective-permute-start.3 = (f32[64,128]{1,0:T(8,128)S(1)}, f32[64,128]{1,0:T(8,128)S(1)}, u32[]{:S(2)}, u32[]{:S(2)}) collective-permute-start(f32[64,128]{1,0:T(8,128)S(1)} %get-tuple-element.19), channel_id=1, source_target_pairs={{4,8},{12,16},{20,24},{28,0},{8,4},{16,12},{24,20},{0,28},{5,9},{1... | collective-permute-start | bytes 98312 | tf_op jit(solution)/shard_map/ppermute | solution.py:512
  13.3 2.8 %collective-permute-start.2 = (f32[64,128]{1,0:T(8,128)S(1)}, f32[64,128]{1,0:T(8,128)S(1)}, u32[]{:S(2)}, u32[]{:S(2)}) collective-permute-start(f32[64,128]{1,0:T(8,128)S(1)} %get-tuple-element.16.refs_5_), channel_id=1, source_target_pairs={{0,4},{4,0},{8,12},{12,8},{16,20},{20,16},{24,28},{28,24},{1,5},{5... | collective-permute-start | bytes 98312 | tf_op jit(solution)/shard_map/ppermute | solution.py:512
  17.6 4.4 %copy-start.5 = (f32[3,128,128]{2,1,0:T(8,128)S(1)}, f32[3,128,128]{2,1,0:T(8,128)}, u32[]{:S(2)}) copy-start(f32[3,128,128]{2,1,0:T(8,128)} %refs_1_.6) | copy-start | bytes 589828
  17.6 33.3 %copy-start.13 = (f32[513]{0:T(1024)S(1)}, f32[513]{0:T(1024)}, u32[]{:S(2)}) copy-start(f32[513]{0:T(1024)} %param.16) | copy-start | bytes 6160
  17.6 33.3 %copy-start = (bf16[768,1024]{1,0:T(8,128)(2,1)S(1)}, bf16[768,1024]{1,0:T(8,128)(2,1)}, u32[]{:S(2)}) copy-start(bf16[768,1024]{1,0:T(8,128)(2,1)} %constant.12.clone._.refs_8_.refs_1_.table) | copy-start | bytes 4718596
  17.6 37.4 %all-to-all-start = ((f32[8,256,128]{2,1,0:T(8,128)}), f32[8,256,128]{2,1,0:T(8,128)}, u32[]{:S(2)}, u32[]{:S(2)}) async-start(f32[8,256,128]{2,1,0:T(8,128)} %shard_map.142), calls=%async_computation | async-start | bytes 2097152 | tf_op jit(solution)/shard_map/all_to_all | solution.py:553
  22.0 29.2 %copy-start.3 = (f32[128,16,128]{2,1,0:T(8,128)S(1)}, f32[128,16,128]{2,1,0:T(8,128)}, u32[]{:S(2)}) copy-start(f32[128,16,128]{2,1,0:T(8,128)} %refs_3_.3) | copy-start | bytes 3145732
  23.8 1.6 %collective-permute-start.6 = (f32[2,128,128]{2,1,0:T(8,128)}, f32[2,128,128]{2,1,0:T(8,128)S(1)}, u32[]{:S(2)}, u32[]{:S(2)}) collective-permute-start(f32[2,128,128]{2,1,0:T(8,128)} %get-tuple-element.23.left), channel_id=1, source_target_pairs={{0,1},{1,0},{2,3},{3,2},{4,5},{5,4},{6,7},{7,6},{8,9},{9,8},{10,11... | collective-permute-start | bytes 393224 | tf_op jit(solution)/shard_map/ppermute | solution.py:516
  23.9 4.3 %collective-permute-start.4 = (f32[128,128]{1,0:T(8,128)S(1)}, f32[128,128]{1,0:T(8,128)S(1)}, u32[]{:S(2)}, u32[]{:S(2)}) collective-permute-start(f32[128,128]{1,0:T(8,128)S(1)} %get-tuple-element.22.left), channel_id=1, source_target_pairs={{0,1},{1,0},{2,3},{3,2},{4,5},{5,4},{6,7},{7,6},{8,9},{9,8},{10,11... | collective-permute-start | bytes 196616 | tf_op jit(solution)/shard_map/ppermute | solution.py:516
  25.4 0.9 copy-start.7
  26.4 27.9 %collective-permute-start.7 = (f32[2,128,128]{2,1,0:T(8,128)S(1)}, f32[2,128,128]{2,1,0:T(8,128)S(1)}, u32[]{:S(2)}, u32[]{:S(2)}) collective-permute-start(f32[2,128,128]{2,1,0:T(8,128)S(1)} %shard_map.146.left), channel_id=1, source_target_pairs={{0,2},{1,3},{2,0},{3,1},{4,6},{5,7},{6,4},{7,5},{8,10},{9,11},{10,... | collective-permute-start | bytes 393224 | tf_op jit(solution)/shard_map/ppermute | solution.py:516
  28.3 5.0 %collective-permute-start.5 = (f32[128,128]{1,0:T(8,128)S(1)}, f32[128,128]{1,0:T(8,128)S(1)}, u32[]{:S(2)}, u32[]{:S(2)}) collective-permute-start(f32[128,128]{1,0:T(8,128)S(1)} %shard_map.144.left), channel_id=1, source_target_pairs={{0,2},{1,3},{2,0},{3,1},{4,6},{5,7},{6,4},{7,5},{8,10},{9,11},{10,... | collective-permute-start | bytes 196616 | tf_op jit(solution)/shard_map/ppermute | solution.py:516
  33.4 7.4 %collective-permute-start.8 = (f32[1,16,128]{2,1,0:T(8,128)S(1)}, f32[1,16,128]{2,1,0:T(8,128)S(1)}, u32[]{:S(2)}, u32[]{:S(2)}) collective-permute-start(f32[1,16,128]{2,1,0:T(8,128)S(1)} %get-tuple-element.24), channel_id=1, source_target_pairs={{0,0},{1,9},{2,18},{3,27},{4,4},{5,13},{6,22},{7,31},{8,8},{9,1},{... | collective-permute-start | bytes 24584 | tf_op jit(solution)/shard_map/ppermute | solution.py:537
  36.9 4.7 %collective-permute-start.9 = (f32[1,16,128]{2,1,0:T(8,128)S(1)}, f32[1,16,128]{2,1,0:T(8,128)S(1)}, u32[]{:S(2)}, u32[]{:S(2)}) collective-permute-start(f32[1,16,128]{2,1,0:T(8,128)S(1)} %get-tuple-element.25), channel_id=1, source_target_pairs={{0,4},{1,13},{2,22},{3,31},{4,0},{5,9},{6,18},{7,27},{8,12},{9,5},... | collective-permute-start | bytes 24584 | tf_op jit(solution)/shard_map/ppermute | solution.py:537
  40.8 8.6 %collective-permute-start.10 = (f32[1,16,128]{2,1,0:T(8,128)S(1)}, f32[1,16,128]{2,1,0:T(8,128)S(1)}, u32[]{:S(2)}, u32[]{:S(2)}) collective-permute-start(f32[1,16,128]{2,1,0:T(8,128)S(1)} %collective-permute-done.8.refs_0_), channel_id=1, source_target_pairs={{0,1},{1,0},{2,3},{3,2},{4,5},{5,4},{6,7},{7,6},{8,9},{9,8},{10,11... | collective-permute-start | bytes 24584 | tf_op jit(solution)/shard_map/ppermute | solution.py:516
  41.6 9.2 %collective-permute-start.11 = (f32[1,16,128]{2,1,0:T(8,128)S(1)}, f32[1,16,128]{2,1,0:T(8,128)S(1)}, u32[]{:S(2)}, u32[]{:S(2)}) collective-permute-start(f32[1,16,128]{2,1,0:T(8,128)S(1)} %collective-permute-done.9.refs_1_), channel_id=1, source_target_pairs={{0,1},{1,0},{2,3},{3,2},{4,5},{5,4},{6,7},{7,6},{8,9},{9,8},{10,11... | collective-permute-start | bytes 24584 | tf_op jit(solution)/shard_map/ppermute | solution.py:516
  41.6 12.2 %collective-permute-start.12 = (f32[1,16,128]{2,1,0:T(8,128)S(1)}, f32[1,16,128]{2,1,0:T(8,128)S(1)}, u32[]{:S(2)}, u32[]{:S(2)}) collective-permute-start(f32[1,16,128]{2,1,0:T(8,128)S(1)} %collective-permute-done.8.refs_0_), channel_id=1, source_target_pairs={{0,2},{1,3},{2,0},{3,1},{4,6},{5,7},{6,4},{7,5},{8,10},{9,11},{10,... | collective-permute-start | bytes 24584 | tf_op jit(solution)/shard_map/ppermute | solution.py:516
  49.3 4.5 %collective-permute-start.13 = (f32[1,16,128]{2,1,0:T(8,128)S(1)}, f32[1,16,128]{2,1,0:T(8,128)S(1)}, u32[]{:S(2)}, u32[]{:S(2)}) collective-permute-start(f32[1,16,128]{2,1,0:T(8,128)S(1)} %collective-permute-done.9.refs_1_), channel_id=1, source_target_pairs={{0,2},{1,3},{2,0},{3,1},{4,6},{5,7},{6,4},{7,5},{8,10},{9,11},{10,... | collective-permute-start | bytes 24584 | tf_op jit(solution)/shard_map/ppermute | solution.py:516
  49.3 4.5 %collective-permute-start.14 = (f32[1,16,128]{2,1,0:T(8,128)S(1)}, f32[1,16,128]{2,1,0:T(8,128)S(1)}, u32[]{:S(2)}, u32[]{:S(2)}) collective-permute-start(f32[1,16,128]{2,1,0:T(8,128)S(1)} %collective-permute-done.10.refs_2_), channel_id=1, source_target_pairs={{0,2},{1,3},{2,0},{3,1},{4,6},{5,7},{6,4},{7,5},{8,10},{9,11},{10,... | collective-permute-start | bytes 24584 | tf_op jit(solution)/shard_map/ppermute | solution.py:516
  50.8 3.0 %collective-permute-start.15 = (f32[1,16,128]{2,1,0:T(8,128)S(1)}, f32[1,16,128]{2,1,0:T(8,128)S(1)}, u32[]{:S(2)}, u32[]{:S(2)}) collective-permute-start(f32[1,16,128]{2,1,0:T(8,128)S(1)} %collective-permute-done.11.refs_3_), channel_id=1, source_target_pairs={{0,2},{1,3},{2,0},{3,1},{4,6},{5,7},{6,4},{7,5},{8,10},{9,11},{10,... | collective-permute-start | bytes 24584 | tf_op jit(solution)/shard_map/ppermute | solution.py:516
  55.0 10.6 %copy-start.8 = (f32[8,16,128]{2,1,0:T(8,128)S(1)}, f32[8,16,128]{2,1,0:T(8,128)}, u32[]{:S(2)}) copy-start(f32[8,16,128]{2,1,0:T(8,128)} %constant.11.clone.axial) | copy-start | bytes 196612
  55.0 10.6 %copy-start.9 = (f32[1,1024]{1,0:T(1,128)S(1)}, f32[1,1024]{1,0:T(1,128)}, u32[]{:S(2)}) copy-start(f32[1,1024]{1,0:T(1,128)} %constant.16.weight) | copy-start | bytes 12292
  55.0 10.6 %copy-start.10 = (f32[1,1024]{1,0:T(1,128)S(1)}, f32[1,1024]{1,0:T(1,128)}, u32[]{:S(2)}) copy-start(f32[1,1024]{1,0:T(1,128)} %constant.15.fixed) | copy-start | bytes 12292
  57.1 4.4 %collective-permute-start.16 = (f32[48,1024]{1,0:T(8,128)S(1)}, f32[48,1024]{1,0:T(8,128)S(1)}, u32[]{:S(2)}, u32[]{:S(2)}) collective-permute-start(f32[48,1024]{1,0:T(8,128)S(1)} %get-tuple-element.27), channel_id=1, source_target_pairs={{0,1},{1,0},{2,3},{3,2},{4,5},{5,4},{6,7},{7,6},{8,9},{9,8},{10,11... | collective-permute-start | bytes 589832 | tf_op jit(solution)/shard_map/ppermute | solution.py:512
  58.6 7.0 %collective-permute-start.17 = (f32[48,1024]{1,0:T(8,128)S(1)}, f32[48,1024]{1,0:T(8,128)S(1)}, u32[]{:S(2)}, u32[]{:S(2)}) collective-permute-start(f32[48,1024]{1,0:T(8,128)S(1)} %get-tuple-element.28), channel_id=1, source_target_pairs={{1,2},{2,1},{5,6},{6,5},{9,10},{10,9},{13,14},{14,13},{17,18},{18,... | collective-permute-start | bytes 589832 | tf_op jit(solution)/shard_map/ppermute | solution.py:512

commit v10 on v8

--- a/solution.py
+++ b/solution.py
@@ -316,20 +316,27 @@
 
 
 def forward_kernel(edge, received, table, *refs):
-    modes, pair, link, wave = refs[-4:]
+    modes, pair, link = refs[-3:]
     sectors = received.shape[0]
     columns = modes.shape[0]
     radial_odd = lax.axis_index("radial") % 2 == 1
 
     def store(lane, out):
-        modes[:, lane] = out[:columns]
-        first, last = out[:edge], out[columns - edge : columns]
-        pair[:edge, lane] = jnp.where(radial_odd, first, last)
-        pair[edge:, lane] = out[columns:]
+        modes[:, lane] = out
+        first, last = out[:edge], out[columns - edge :]
+        pair[:, lane] = jnp.where(radial_odd, first, last)
         link[:, lane] = jnp.where(radial_odd, last, first)
-        wave[:, lane] = out[columns:]
-
-    transformed([received[s] for s in range(sectors)], table, store)
+
+    transformed([received[s, :columns, :] for s in range(sectors)], table, store)
+
+
+def wave_kernel(received, table, wave):
+    columns = received.shape[1] - wave.shape[0]
+
+    def store(lane, out):
+        wave[:, lane] = out
+
+    transformed([received[s, columns:, :] for s in range(received.shape[0])], table, store)
 
 
 def solve_kernel(
@@ -443,10 +450,6 @@
     lanes = lax.broadcasted_iota(jnp.int32, (1, count), 1)
     last = jnp.broadcast_to(impedance[:, half:], (1, count))
     rows[...] = jnp.concatenate([q0, jnp.where(lanes == 0, last, q0), q2, q2, q1, q3, q1, q3], 1)
-
-
-def partner_kernel(edge, wave, pair, out):
-    out[...] = wave[...] + pair[edge:, :]
 
 
 def add_kernel(left, right, out):
@@ -592,26 +595,22 @@
     )(mouth_azimuth, mouth_radius, density, swirl, *radial_halo, *sector_halo)
     acoustic_next = added(*halves_of_sum(state, "radial"))
 
-    modes, pair, link, wave = call(
+    received = in_vmem(received)
+    (wave,) = call(wave_kernel, [shape(own, n_theta)], [VMEM] * 2)(received, table)
+    partner = swapped(wave, "radial", 1)
+    modes, pair, link = call(
         lambda *refs: forward_kernel(edge, *refs),
-        [
-            shape(columns, n_theta),
-            shape(edge + own, n_theta),
-            shape(edge, n_theta),
-            shape(own, n_theta),
-        ],
-        [VMEM] * 2 + [HBM] * 3,
-    )(in_vmem(received), table, in_hbm(density_next), in_hbm(acoustic_next), impedance)
+        [shape(columns, n_theta), shape(edge, n_theta), shape(edge, n_theta)],
+        [VMEM] * 2 + [HBM] * 4,
+    )(received, table, in_hbm(density_next), in_hbm(acoustic_next), impedance, wave)
+    wave = halves_of_sum(added(wave, partner), "radial", 2)
     halo = paired(pair, link, "radial", False)
-    (wave,) = call(
-        lambda *refs: partner_kernel(edge, *refs), [shape(own, n_theta)], [VMEM] * 2
-    )(wave, halo[0])
     (send,) = call(
         solve_kernel,
         [shape(sectors, columns, cells_theta)],
         [VMEM] * 10,
         [pltpu.VMEM((columns, n_theta), F32)],
-    )(modes, *halo, *halves_of_sum(wave, "radial", 2), impedance, fixed, weight, eigen, table)
+    )(modes, *halo, *wave, impedance, fixed, weight, eigen, table)
     (pressure,) = call(
         pressure_kernel,
         [shape(*density.shape)],

time: 93.5 us -> 92.9 us (level)
  starting transfers between devices: 18.2 us -> 20.8 us
  waiting for transfers between devices: 31.2 us -> 28.8 us
    ppermute x6, waiting for transfers between devices: 5.02 us -> 3.08 us  [paired(): return (lax.ppermute(pair, axis, first), lax.ppermute(link, axis, second))]
    ppermute x3 -> x4, starting transfers between devices: 6.1 us -> 7.6 us  [swapped(): lax.ppermute(value, axis, [(i, i ^ bits) for i in range(lax.axis_size(axi...]
    pallas_call x1, Pallas kernels: 2.11 us -> 0.84 us  [section(): call(lambda *refs: forward_kernel(edge, *refs), [shape(columns, n_theta),...]
    ppermute x3 -> x4, waiting for transfers between devices: 7.81 us -> 7.82 us  [swapped(): lax.ppermute(value, axis, [(i, i ^ bits) for i in range(lax.axis_size(axi...]
  transfers between devices with their start and end apart: 10 -> 11, of which waited for: 7 -> 6; matrix products, arithmetic and copies ran while one was open for 0% -> 0% of each run, Pallas kernels for 4% -> 4%
where the time goes in v10:
time: 92.9 us; the launch traced here: 92.7 us
  waiting for transfers between devices  28.8 us (31%)
  blocking collectives  28.3 us (30%)
  starting transfers between devices  20.8 us (22%)
  Pallas kernels  13.2 us (14%)
    all_to_all x1, blocking collectives, exchanged(): lax.all_to_all(value, 'sector', split_axis=0, concat_axis=0, tiled=True)  28.3 us
    all_to_all x1, waiting for transfers between devices, exchanged(): lax.all_to_all(value, 'sector', split_axis=0, concat_axis=0, tiled=True)  17.9 us
    ppermute x6, starting transfers between devices, paired(): return (lax.ppermute(pair, axis, first), lax.ppermute(link, axis, second))  8.19 us
    ppermute x4, waiting for transfers between devices, swapped(): lax.ppermute(value, axis, [(i, i ^ bits) for i in range(lax.axis_size(axi...  7.82 us
    ppermute x4, starting transfers between devices, swapped(): lax.ppermute(value, axis, [(i, i ^ bits) for i in range(lax.axis_size(axi...  7.6 us
    all_to_all x1, starting transfers between devices, exchanged(): lax.all_to_all(value, 'sector', split_axis=0, concat_axis=0, tiled=True)  4.97 us
    ppermute x6, waiting for transfers between devices, paired(): return (lax.ppermute(pair, axis, first), lax.ppermute(link, axis, second))  3.08 us
    pallas_call x1, Pallas kernels, section(): call(lambda *refs: step_kernel(n_theta, *refs), [shape(*density.shape)],...  2.62 us
  transfers between devices with their start and end apart: 11, of which 6 were waited for; matrix products, arithmetic and copies ran while one was open for 0% of the time, Pallas kernels for 4%

profile of v10, /device:TPU:0, one launch (start us, length us, event | category | flops | bytes accessed | tf_op | source)
XLA Modules:
  0.0 92.7 jit_solution(9099863822462061803)
XLA Ops:
  0.6 0.0 copy-start.1
  0.6 0.0 copy-start.3
  0.7 0.0 copy-start.5
  0.7 0.0 copy-start.12
  0.7 0.0 copy-start.13
  0.7 1.2 %shard_map.139 = (f32[64,128]{1,0:T(8,128)S(1)}, f32[64,128]{1,0:T(8,128)S(1)}) custom-call(f32[128,16,128]{2,1,0:T(8,128)} %refs_2_.4, f32[128,16,128]{2,1,0:T(8,128)} %refs_3_.3, f32[128,16,128]{2,1,0:T(8,128)} %refs_4_.1, f32[3,128,128]{2,1,0:T(8,128)} %refs_2_.5), custom_call_target="tpu_custom_call" | custom-call | bytes 196608 | tf_op jit(solution)/shard_map/pallas_call | solution.py:554
  1.9 0.1 copy-done.1
  2.0 0.3 copy-done.3
  2.3 0.3 copy-done.5
  2.7 1.7 %shard_map.140 = (f32[128,16,128]{2,1,0:T(8,128)S(1)}, f32[128,128]{1,0:T(8,128)S(1)}, f32[128,128]{1,0:T(8,128)S(1)}, f32[128,128]{1,0:T(8,128)S(1)}) custom-call(s32[16]{0:T(128)S(1)} %copy-done.12, s32[16]{0:T(128)S(1)} %copy-done.13, f32[128,16,128]{2,1,0:T(8,128)S(1)} %copy-done.1, f32[128,16,128]{2,1,0:T(8,128)S(1)} %copy-done.3, ...), custom_call_target="tpu_custom_call" | custom-call | bytes 3735552 | tf_op jit(solution)/shard_map/pallas_call | solution.py:568
  4.3 0.6 collective-permute-start
  4.9 0.7 collective-permute-start.1
  5.6 2.6 %collective-permute-start.2 = (f32[64,128]{1,0:T(8,128)S(1)}, f32[64,128]{1,0:T(8,128)S(1)}, u32[]{:S(2)}, u32[]{:S(2)}) collective-permute-start(f32[64,128]{1,0:T(8,128)S(1)} %get-tuple-element.14.refs_5_), channel_id=1, source_target_pairs={{0,4},{4,0},{8,12},{12,8},{16,20},{20,16},{24,28},{28,24},{1,5},{5... | collective-permute-start | bytes 98312 | tf_op jit(solution)/shard_map/ppermute | solution.py:491
  8.1 3.5 %collective-permute-start.3 = (f32[64,128]{1,0:T(8,128)S(1)}, f32[64,128]{1,0:T(8,128)S(1)}, u32[]{:S(2)}, u32[]{:S(2)}) collective-permute-start(f32[64,128]{1,0:T(8,128)S(1)} %get-tuple-element.17), channel_id=1, source_target_pairs={{4,8},{12,16},{20,24},{28,0},{8,4},{16,12},{24,20},{0,28},{5,9},{1... | collective-permute-start | bytes 98312 | tf_op jit(solution)/shard_map/ppermute | solution.py:491
  11.7 0.0 collective-permute-done.2.refs_6_.refs_5_
  11.7 3.1 %collective-permute-done.3.refs_7_.refs_6_ = f32[64,128]{1,0:T(8,128)S(1)} collective-permute-done((f32[64,128]{1,0:T(8,128)S(1)}, f32[64,128]{1,0:T(8,128)S(1)}, u32[]{:S(2)}, u32[]{:S(2)}) %collective-permute-start.3) | collective-permute-done | bytes 32800 | tf_op jit(solution)/shard_map/ppermute | solution.py:491
  14.8 0.0 collective-permute-done.refs_4_.refs_3_
  14.8 0.0 collective-permute-done.1.refs_5_.refs_4_
  14.8 2.4 %shard_map.142 = (f32[3,128,128]{2,1,0:T(8,128)}, f32[8,272,128]{2,1,0:T(8,128)}) custom-call(f32[128,16,128]{2,1,0:T(8,128)S(1)} %get-tuple-element.18.refs_0_, f32[128,128]{1,0:T(8,128)S(1)} %get-tuple-element.19.refs_1_, f32[3,128,128]{2,1,0:T(8,128)S(1)} %copy-done.6, f32[128,128]{1,0:T(8,128)S(1)} %collective-permute-done.refs_4_.refs_3_, ...), custom_call_target="tpu_custom_call" | custom-call | bytes 3932160 | tf_op jit(solution)/shard_map/pallas_call | solution.py:574
  17.2 0.0 copy-start.8
  17.2 0.0 copy-start.14
  17.2 0.0 copy-start
  17.3 5.0 %all-to-all-start = ((f32[8,272,128]{2,1,0:T(8,128)}), f32[8,272,128]{2,1,0:T(8,128)S(1)}, u32[]{:S(2)}, u32[]{:S(2)}) async-start(f32[8,272,128]{2,1,0:T(8,128)} %get-tuple-element.20), calls=%async_computation | async-start | bytes 2228224 | tf_op jit(solution)/shard_map/all_to_all | solution.py:522
  22.2 0.0 copy-start.4
  22.3 1.2 %collective-permute-start.4 = (f32[3,128,128]{2,1,0:T(8,128)S(1)}, f32[3,128,128]{2,1,0:T(8,128)S(1)}, u32[]{:S(2)}, u32[]{:S(2)}) collective-permute-start(f32[3,128,128]{2,1,0:T(8,128)S(1)} %copy-done.8), channel_id=1, source_target_pairs={{0,1},{1,0},{2,3},{3,2},{4,5},{5,4},{6,7},{7,6},{8,9},{9,8},{10,11... | collective-permute-start | bytes 589832 | tf_op jit(solution)/shard_map/ppermute | solution.py:495
  23.5 1.1 %collective-permute-done.4.right = f32[3,128,128]{2,1,0:T(8,128)S(1)} collective-permute-done((f32[3,128,128]{2,1,0:T(8,128)S(1)}, f32[3,128,128]{2,1,0:T(8,128)S(1)}, u32[]{:S(2)}, u32[]{:S(2)}) %collective-permute-start.4) | collective-permute-done | bytes 196640 | tf_op jit(solution)/shard_map/ppermute | solution.py:495
  24.6 2.7 %collective-permute-start.5 = (f32[3,128,128]{2,1,0:T(8,128)S(1)}, f32[3,128,128]{2,1,0:T(8,128)S(1)}, u32[]{:S(2)}, u32[]{:S(2)}) collective-permute-start(f32[3,128,128]{2,1,0:T(8,128)S(1)} %shard_map.143.left), channel_id=1, source_target_pairs={{0,2},{1,3},{2,0},{3,1},{4,6},{5,7},{6,4},{7,5},{8,10},{9,11},{10,... | collective-permute-start | bytes 589832 | tf_op jit(solution)/shard_map/ppermute | solution.py:495
  27.2 0.3 shard_map.145.refs_4_.impedance
  27.6 0.0 copy-done.2
  27.6 0.0 copy-done.4
  27.6 2.6 %shard_map.141.refs_2_ = f32[128,16,128]{2,1,0:T(8,128)} custom-call(s32[16]{0:T(128)S(1)} %copy-done.12, s32[16]{0:T(128)S(1)} %copy-done.13, f32[128,16,128]{2,1,0:T(8,128)S(1)} %copy-done.2, f32[128,16,128]{2,1,0:T(8,128)S(1)} %copy-done.4, f32[128,128]{1,0:T(8,128)S(1)} %collective-permute-done.refs_4_.refs_3_, ...), custom_call_target="tpu_custom_call" | custom-call | bytes 3145728 | tf_op jit(solution)/shard_map/pallas_call | solution.py:590
  30.2 2.2 %collective-permute-done.5.right = f32[3,128,128]{2,1,0:T(8,128)S(1)} collective-permute-done((f32[3,128,128]{2,1,0:T(8,128)S(1)}, f32[3,128,128]{2,1,0:T(8,128)S(1)}, u32[]{:S(2)}, u32[]{:S(2)}) %collective-permute-start.5) | collective-permute-done | bytes 196640 | tf_op jit(solution)/shard_map/ppermute | solution.py:495
  32.4 0.7 shard_map.144.refs_3_
  33.1 17.9 %all-to-all-done.received.refs_0_ = f32[8,272,128]{2,1,0:T(8,128)S(1)} async-done(((f32[8,272,128]{2,1,0:T(8,128)}), f32[8,272,128]{2,1,0:T(8,128)S(1)}, u32[]{:S(2)}, u32[]{:S(2)}) %all-to-all-start) | async-done | bytes 1114144 | tf_op jit(solution)/shard_map/all_to_all | solution.py:522
  51.0 0.4 shard_map.146.refs_5_.left
  51.5 0.8 shard_map.147
  52.3 0.2 collective-permute-start.6
  52.5 0.7 collective-permute-start.7
  53.2 1.7 %collective-permute-start.8 = (f32[16,1024]{1,0:T(8,128)S(1)}, f32[16,1024]{1,0:T(8,128)S(1)}, u32[]{:S(2)}, u32[]{:S(2)}) collective-permute-start(f32[16,1024]{1,0:T(8,128)S(1)} %shard_map.146.refs_5_.left), channel_id=1, source_target_pairs={{0,1},{1,0},{2,3},{3,2},{4,5},{5,4},{6,7},{7,6},{8,9},{9,8},{10,11... | collective-permute-start | bytes 196616 | tf_op jit(solution)/shard_map/ppermute | solution.py:495
  54.9 0.9 collective-permute-done.8.right
  55.8 2.0 %collective-permute-start.9 = (f32[16,1024]{1,0:T(8,128)S(1)}, f32[16,1024]{1,0:T(8,128)S(1)}, u32[]{:S(2)}, u32[]{:S(2)}) collective-permute-start(f32[16,1024]{1,0:T(8,128)S(1)} %shard_map.148.wave), channel_id=1, source_target_pairs={{0,2},{1,3},{2,0},{3,1},{4,6},{5,7},{6,4},{7,5},{8,10},{9,11},{10,... | collective-permute-start | bytes 196616 | tf_op jit(solution)/shard_map/ppermute | solution.py:495
  57.8 3.6 %collective-permute-done.9.other_wave = f32[16,1024]{1,0:T(8,128)S(1)} collective-permute-done((f32[16,1024]{1,0:T(8,128)S(1)}, f32[16,1024]{1,0:T(8,128)S(1)}, u32[]{:S(2)}, u32[]{:S(2)}) %collective-permute-start.9) | collective-permute-done | bytes 65568 | tf_op jit(solution)/shard_map/ppermute | solution.py:495
  61.4 0.0 collective-permute-done.6.pair
  61.5 0.0 collective-permute-done.7.link
  61.5 0.0 copy-done.9
  61.5 1.5 %shard_map.149 = f32[8,256,128]{2,1,0:T(8,128)S(1)} custom-call(f32[256,1024]{1,0:T(8,128)S(1)} %get-tuple-element.22.modes, f32[48,1024]{1,0:T(8,128)S(1)} %collective-permute-done.6.pair, f32[48,1024]{1,0:T(8,128)S(1)} %collective-permute-done.7.link, f32[16,1024]{1,0:T(8,128)S(1)} %shard_map.148.wave, f32[16,1024]{1,0:T(8,128)S(1)} %collective-permute-done.9.other_wave, ...), custom_call_target="tpu_custom_call" | custom-call | bytes 3145728 | tf_op jit(solution)/shard_map/pallas_call | solution.py:608
  63.0 28.3 %all_to_all.10.received = f32[8,256,128]{2,1,0:T(8,128)S(1)} all-to-all(f32[8,256,128]{2,1,0:T(8,128)S(1)} %shard_map.149), channel_id=1, replica_groups=mesh['sector'=8,'radial'=4] {'sector'}, dimensions={0} | all-to-all | bytes 2097152 | tf_op jit(solution)/shard_map/all_to_all | solution.py:522
  91.2 1.5 %shard_map.150 = f32[128,16,128]{2,1,0:T(8,128)} custom-call(f32[8,256,128]{2,1,0:T(8,128)S(1)} %all_to_all.10.received, f32[128,128]{1,0:T(8,128)S(1)} %copy-done.7), custom_call_target="tpu_custom_call" | custom-call | bytes 3145728 | tf_op jit(solution)/shard_map/pallas_call | solution.py:614
  (18 shorter events, 0.1 us)
Async XLA Ops:
  0.6 1.4 %copy-start.1 = (f32[128,16,128]{2,1,0:T(8,128)S(1)}, f32[128,16,128]{2,1,0:T(8,128)}, u32[]{:S(2)}) copy-start(f32[128,16,128]{2,1,0:T(8,128)} %refs_2_.4) | copy-start | bytes 3145732
  0.6 1.7 %copy-start.3 = (f32[128,16,128]{2,1,0:T(8,128)S(1)}, f32[128,16,128]{2,1,0:T(8,128)}, u32[]{:S(2)}) copy-start(f32[128,16,128]{2,1,0:T(8,128)} %refs_3_.3) | copy-start | bytes 3145732
  0.7 2.0 %copy-start.5 = (f32[128,16,128]{2,1,0:T(8,128)S(1)}, f32[128,16,128]{2,1,0:T(8,128)}, u32[]{:S(2)}) copy-start(f32[128,16,128]{2,1,0:T(8,128)} %refs_4_.1) | copy-start | bytes 3145732
  0.7 2.0 %copy-start.12 = (s32[16]{0:T(128)S(1)}, s32[16]{0:T(128)}, u32[]{:S(2)}) copy-start(s32[16]{0:T(128)} %refs_0_.3) | copy-start | bytes 196
  0.7 2.0 %copy-start.13 = (s32[16]{0:T(128)S(1)}, s32[16]{0:T(128)}, u32[]{:S(2)}) copy-start(s32[16]{0:T(128)} %refs_1_.4) | copy-start | bytes 196
  2.7 12.1 %copy-start.6 = (f32[3,128,128]{2,1,0:T(8,128)S(1)}, f32[3,128,128]{2,1,0:T(8,128)}, u32[]{:S(2)}) copy-start(f32[3,128,128]{2,1,0:T(8,128)} %refs_2_.5) | copy-start | bytes 589828
  2.7 12.1 %copy-start.7 = (f32[128,128]{1,0:T(8,128)S(1)}, f32[128,128]{1,0:T(8,128)}, u32[]{:S(2)}) copy-start(f32[128,128]{1,0:T(8,128)} %constant.10.clone.refs_7_.basis) | copy-start | bytes 196612
  4.3 10.4 %collective-permute-start = (f32[128,128]{1,0:T(8,128)S(1)}, f32[128,128]{1,0:T(8,128)S(1)}, u32[]{:S(2)}, u32[]{:S(2)}) collective-permute-start(f32[128,128]{1,0:T(8,128)S(1)} %get-tuple-element.15), channel_id=1, source_target_pairs={{0,1},{1,0},{2,3},{3,2},{4,5},{5,4},{6,7},{7,6},{8,9},{9,8},{10,11... | collective-permute-start | bytes 196616 | tf_op jit(solution)/shard_map/ppermute | solution.py:491
  4.9 9.9 %collective-permute-start.1 = (f32[128,128]{1,0:T(8,128)S(1)}, f32[128,128]{1,0:T(8,128)S(1)}, u32[]{:S(2)}, u32[]{:S(2)}) collective-permute-start(f32[128,128]{1,0:T(8,128)S(1)} %get-tuple-element.16), channel_id=1, source_target_pairs={{1,2},{2,1},{5,6},{6,5},{9,10},{10,9},{13,14},{14,13},{17,18},{18,... | collective-permute-start | bytes 196616 | tf_op jit(solution)/shard_map/ppermute | solution.py:491
  5.6 6.1 %collective-permute-start.2 = (f32[64,128]{1,0:T(8,128)S(1)}, f32[64,128]{1,0:T(8,128)S(1)}, u32[]{:S(2)}, u32[]{:S(2)}) collective-permute-start(f32[64,128]{1,0:T(8,128)S(1)} %get-tuple-element.14.refs_5_), channel_id=1, source_target_pairs={{0,4},{4,0},{8,12},{12,8},{16,20},{20,16},{24,28},{28,24},{1,5},{5... | collective-permute-start | bytes 98312 | tf_op jit(solution)/shard_map/ppermute | solution.py:491
  8.1 6.6 %collective-permute-start.3 = (f32[64,128]{1,0:T(8,128)S(1)}, f32[64,128]{1,0:T(8,128)S(1)}, u32[]{:S(2)}, u32[]{:S(2)}) collective-permute-start(f32[64,128]{1,0:T(8,128)S(1)} %get-tuple-element.17), channel_id=1, source_target_pairs={{4,8},{12,16},{20,24},{28,0},{8,4},{16,12},{24,20},{0,28},{5,9},{1... | collective-permute-start | bytes 98312 | tf_op jit(solution)/shard_map/ppermute | solution.py:491
  17.2 5.0 %copy-start.8 = (f32[3,128,128]{2,1,0:T(8,128)S(1)}, f32[3,128,128]{2,1,0:T(8,128)}, u32[]{:S(2)}) copy-start(f32[3,128,128]{2,1,0:T(8,128)} %get-tuple-element.21.left) | copy-start | bytes 589828
  17.2 10.0 %copy-start.14 = (f32[513]{0:T(1024)S(1)}, f32[513]{0:T(1024)}, u32[]{:S(2)}) copy-start(f32[513]{0:T(1024)} %param.16) | copy-start | bytes 6160
  17.2 10.0 %copy-start = (bf16[768,1024]{1,0:T(8,128)(2,1)S(1)}, bf16[768,1024]{1,0:T(8,128)(2,1)}, u32[]{:S(2)}) copy-start(bf16[768,1024]{1,0:T(8,128)(2,1)} %constant.12.clone._.table.refs_1_) | copy-start | bytes 4718596
  17.3 33.8 %all-to-all-start = ((f32[8,272,128]{2,1,0:T(8,128)}), f32[8,272,128]{2,1,0:T(8,128)S(1)}, u32[]{:S(2)}, u32[]{:S(2)}) async-start(f32[8,272,128]{2,1,0:T(8,128)} %get-tuple-element.20), calls=%async_computation | async-start | bytes 2228224 | tf_op jit(solution)/shard_map/all_to_all | solution.py:522
  22.2 5.3 %copy-start.2 = (f32[128,16,128]{2,1,0:T(8,128)S(1)}, f32[128,16,128]{2,1,0:T(8,128)}, u32[]{:S(2)}) copy-start(f32[128,16,128]{2,1,0:T(8,128)} %refs_2_.4) | copy-start | bytes 3145732
  22.2 5.3 %copy-start.4 = (f32[128,16,128]{2,1,0:T(8,128)S(1)}, f32[128,16,128]{2,1,0:T(8,128)}, u32[]{:S(2)}) copy-start(f32[128,16,128]{2,1,0:T(8,128)} %refs_3_.3) | copy-start | bytes 3145732
  22.3 2.3 %collective-permute-start.4 = (f32[3,128,128]{2,1,0:T(8,128)S(1)}, f32[3,128,128]{2,1,0:T(8,128)S(1)}, u32[]{:S(2)}, u32[]{:S(2)}) collective-permute-start(f32[3,128,128]{2,1,0:T(8,128)S(1)} %copy-done.8), channel_id=1, source_target_pairs={{0,1},{1,0},{2,3},{3,2},{4,5},{5,4},{6,7},{7,6},{8,9},{9,8},{10,11... | collective-permute-start | bytes 589832 | tf_op jit(solution)/shard_map/ppermute | solution.py:495
  24.6 7.9 %collective-permute-start.5 = (f32[3,128,128]{2,1,0:T(8,128)S(1)}, f32[3,128,128]{2,1,0:T(8,128)S(1)}, u32[]{:S(2)}, u32[]{:S(2)}) collective-permute-start(f32[3,128,128]{2,1,0:T(8,128)S(1)} %shard_map.143.left), channel_id=1, source_target_pairs={{0,2},{1,3},{2,0},{3,1},{4,6},{5,7},{6,4},{7,5},{8,10},{9,11},{10,... | collective-permute-start | bytes 589832 | tf_op jit(solution)/shard_map/ppermute | solution.py:495
  51.5 10.0 %copy-start.9 = (f32[8,16,128]{2,1,0:T(8,128)S(1)}, f32[8,16,128]{2,1,0:T(8,128)}, u32[]{:S(2)}) copy-start(f32[8,16,128]{2,1,0:T(8,128)} %constant.11.clone.axial) | copy-start | bytes 196612
  51.5 10.0 %copy-start.10 = (f32[1,1024]{1,0:T(1,128)S(1)}, f32[1,1024]{1,0:T(1,128)}, u32[]{:S(2)}) copy-start(f32[1,1024]{1,0:T(1,128)} %constant.15.fixed) | copy-start | bytes 12292
  51.5 10.0 %copy-start.11 = (f32[1,1024]{1,0:T(1,128)S(1)}, f32[1,1024]{1,0:T(1,128)}, u32[]{:S(2)}) copy-start(f32[1,1024]{1,0:T(1,128)} %constant.16.weight) | copy-start | bytes 12292
  52.3 9.1 %collective-permute-start.6 = (f32[48,1024]{1,0:T(8,128)S(1)}, f32[48,1024]{1,0:T(8,128)S(1)}, u32[]{:S(2)}, u32[]{:S(2)}) collective-permute-start(f32[48,1024]{1,0:T(8,128)S(1)} %get-tuple-element.23), channel_id=1, source_target_pairs={{0,1},{1,0},{2,3},{3,2},{4,5},{5,4},{6,7},{7,6},{8,9},{9,8},{10,11... | collective-permute-start | bytes 589832 | tf_op jit(solution)/shard_map/ppermute | solution.py:491
  52.5 9.0 %collective-permute-start.7 = (f32[48,1024]{1,0:T(8,128)S(1)}, f32[48,1024]{1,0:T(8,128)S(1)}, u32[]{:S(2)}, u32[]{:S(2)}) collective-permute-start(f32[48,1024]{1,0:T(8,128)S(1)} %get-tuple-element.24), channel_id=1, source_target_pairs={{1,2},{2,1},{5,6},{6,5},{9,10},{10,9},{13,14},{14,13},{17,18},{18,... | collective-permute-start | bytes 589832 | tf_op jit(solution)/shard_map/ppermute | solution.py:491
  53.2 2.6 %collective-permute-start.8 = (f32[16,1024]{1,0:T(8,128)S(1)}, f32[16,1024]{1,0:T(8,128)S(1)}, u32[]{:S(2)}, u32[]{:S(2)}) collective-permute-start(f32[16,1024]{1,0:T(8,128)S(1)} %shard_map.146.refs_5_.left), channel_id=1, source_target_pairs={{0,1},{1,0},{2,3},{3,2},{4,5},{5,4},{6,7},{7,6},{8,9},{9,8},{10,11... | collective-permute-start | bytes 196616 | tf_op jit(solution)/shard_map/ppermute | solution.py:495
  55.8 5.7 %collective-permute-start.9 = (f32[16,1024]{1,0:T(8,128)S(1)}, f32[16,1024]{1,0:T(8,128)S(1)}, u32[]{:S(2)}, u32[]{:S(2)}) collective-permute-start(f32[16,1024]{1,0:T(8,128)S(1)} %shard_map.148.wave), channel_id=1, source_target_pairs={{0,2},{1,3},{2,0},{3,1},{4,6},{5,7},{6,4},{7,5},{8,10},{9,11},{10,... | collective-permute-start | bytes 196616 | tf_op jit(solution)/shard_map/ppermute | solution.py:495
